TPU v7x, 32 devices: a whole 2x2x4 slice. The times are simulated.
32 devices in a mesh: dp: 4 (over z), group: 8 (over y, x, core).
Axes of the slice: x: 2, y: 2, z: 4, core: 2. Of those that a mesh axis runs over, the one named last changes fastest.
Arguments:
- tokens: bfloat16 [128, 160, 768], P(('dp', 'group')), may hold values from -6 to 6
- cotangent: bfloat16 [128, 160, 768], P(('dp', 'group')), may hold values from -6 to 6
- counts: int32 [128], P(('dp', 'group')), may hold values from 96 to 160, as said below
- first_gain: float32 [768], replicated, may hold values from 0.5 to 1.5
- first_shift: float32 [768], replicated, may hold values from -1.75 to 1.75
- joined_weight: bfloat16 [768, 2304], replicated, may hold values from -0.21875 to 0.21875
- joined_bias: float32 [2, 768], replicated, may hold values from -1.75 to 1.75
- merge_weight: bfloat16 [768, 768], replicated, may hold values from -0.75 to 0.75
- merge_bias: float32 [768], replicated, may hold values from -1.75 to 1.75
- second_gain: float32 [768], replicated, may hold values from 0.5 to 1.5
- second_shift: float32 [768], replicated, may hold values from -1.75 to 1.75
- up_weight: bfloat16 [768, 3072], replicated, may hold values from -0.21875 to 0.21875
- up_bias: float32 [3072], replicated, may hold values from -1.75 to 1.75
- down_weight: bfloat16 [3072, 768], replicated, may hold values from -0.109375 to 0.109375
- down_bias: float32 [768], replicated, may hold values from -1.75 to 1.75
Outputs:
- result: bfloat16 [128, 160, 768], P(('dp', 'group'))
- token_grad: bfloat16 [128, 160, 768], P(('dp', 'group'))
- first_gain_grad: float32 [768], replicated
- first_shift_grad: float32 [768], replicated
- joined_weight_grad: float32 [768, 2304], replicated
- joined_bias_grad: float32 [2, 768], replicated
- merge_weight_grad: float32 [768, 768], replicated
- merge_bias_grad: float32 [768], replicated
- second_gain_grad: float32 [768], replicated
- second_shift_grad: float32 [768], replicated
- up_weight_grad: float32 [768, 3072], replicated
- up_bias_grad: float32 [3072], replicated
- down_weight_grad: float32 [3072, 768], replicated
- down_bias_grad: float32 [768], replicated
Inputs may be any that keep to these rules, and one draw needn't show every extreme that they name: `counts`: item j of a device is owned by the device with index j // 1 along dp and the same index along group; the items owned by one device hold 512 visible patches together.
All inputs are finite; a program needn't handle non-finite values.
Results may differ from a plain program's by a relative error of at most 0.012.
Values may be sent and summed in bfloat16 or wider, within the bound.
No kernel may reach another device: no remote copies, remote signals or barrier semaphores. Data moves between devices by JAX's collectives and lax.ppermute only.
A program may use at most 256 MiB of HBM per device.

v0:
```python
import math

import jax
import jax.numpy as jnp
from jax import lax
from jax.experimental import pallas as pl
from jax.experimental.pallas import tpu as pltpu
from jax.sharding import PartitionSpec as P

D = 768
HEADS = 12
HEAD_DIM = 64
FF = 3072
PAIRS = HEADS // 2
LANES = 2 * HEAD_DIM
EPS = 1e-06
NEG = -1e30
BF = jnp.bfloat16
F32 = jnp.float32
FACTOR = HEAD_DIM ** (-0.5)
BLOCKS = 16
BROWS = D // BLOCKS


def dot(a, b):
    return jnp.dot(a, b, preferred_element_type=F32)


def dot_t(a, b):
    return lax.dot_general(a, b, (((1,), (1,)), ((), ())), preferred_element_type=F32)


def t_dot(a, b):
    return lax.dot_general(a, b, (((0,), (0,)), ((), ())), preferred_element_type=F32)


def vectors(g1, s1, jb, mb, g2, s2, db):
    row = lax.broadcasted_iota(jnp.int32, (8, D), 0)
    total = jnp.zeros((8, D), F32)
    for at, vector in enumerate((g1, s1, jb[0], jb[1], mb, g2, s2, db)):
        total = jnp.where(row == at, vector[None, :], total)
    return total


def stats(x):
    centred = x - jnp.mean(x, axis=-1, keepdims=True)
    rstd = lax.rsqrt(jnp.mean(centred * centred, axis=-1, keepdims=True) + EPS)
    return centred * rstd, rstd


def params(limit=56):
    return pltpu.CompilerParams(vmem_limit_bytes=limit * 1024 * 1024)


def cost(flops, nbytes, trans=0):
    return pl.CostEstimate(flops=int(10 * flops), bytes_accessed=int(10 * nbytes), transcendentals=int(trans))


def full(shape):
    return pl.BlockSpec(shape, lambda *_: (0,) * len(shape))


def head_masks(rows):
    lane = lax.broadcasted_iota(jnp.int32, (rows, LANES), 1)
    return lane < HEAD_DIM


def stack_heads(pair, low):
    zero = jnp.zeros_like(pair)
    return jnp.concatenate([jnp.where(low, pair, zero), jnp.where(low, zero, pair)], axis=0)


def first_body(
    slots,
    counts_ref,
    tok_ref,
    cot_ref,
    vec_ref,
    wj_ref,
    wm_ref,
    normed_ref,
    joined_ref,
    probs_ref,
    mix_ref,
    middle_ref,
    second_ref,
    gout_ref,
):
    step = pl.program_id(0)
    rows = tok_ref.shape[0]
    items = rows // slots
    x = tok_ref[...].astype(F32)
    xhat, _ = stats(x)
    normed = (xhat * vec_ref[0:1, :] + vec_ref[1:2, :]).astype(BF)
    normed_ref[...] = normed
    for third in range(3):
        cols = slice(third * D, (third + 1) * D)
        part = dot(normed, wj_ref[:, cols])
        if third == 0:
            part = part + vec_ref[2:3, :]
        if third == 2:
            part = part + vec_ref[3:4, :]
        joined_ref[:, cols] = part.astype(BF)
    low = head_masks(slots)
    key_slot = lax.broadcasted_iota(jnp.int32, (2 * slots, slots), 1)
    row_slot = lax.broadcasted_iota(jnp.int32, (slots, D), 0)

    def one(item, carry):
        count = counts_ref[step * items + item]
        here = pl.ds(pl.multiple_of(item * slots, 16), slots)
        seen = row_slot < count
        cot = cot_ref[here, :]
        gout_ref[here, :] = jnp.where(seen, cot, jnp.zeros_like(cot))
        allowed = key_slot < count
        for pair in range(PAIRS):
            cols = slice(pair * LANES, (pair + 1) * LANES)
            q = stack_heads(joined_ref[here, cols], low)
            k = joined_ref[here, D + pair * LANES : D + (pair + 1) * LANES]
            v = joined_ref[here, 2 * D + pair * LANES : 2 * D + (pair + 1) * LANES]
            scores = jnp.where(allowed, dot_t(q, k) * FACTOR, NEG)
            raised = jnp.exp(scores - jnp.max(scores, axis=-1, keepdims=True))
            soft = (raised / jnp.sum(raised, axis=-1, keepdims=True)).astype(BF)
            probs_ref[item, pair] = soft
            mixed = dot(soft, v)
            mix_ref[here, cols] = jnp.where(low, mixed[:slots], mixed[slots:]).astype(BF)
        return carry

    lax.fori_loop(0, items, one, 0)
    middle = x + dot(mix_ref[...], wm_ref[...]) + vec_ref[4:5, :]
    middle_ref[...] = middle
    xhat, _ = stats(middle)
    second_ref[...] = (xhat * vec_ref[5:6, :] + vec_ref[6:7, :]).astype(BF)


def first_call(group, slots, counts, tok, cot, vec, wj, wm):
    total = tok.shape[0]
    rows = group * slots
    steps = total // rows
    row = lambda width: pl.BlockSpec((rows, width), lambda i, c: (i, 0))
    out = lambda width, dt: jax.ShapeDtypeStruct((total, width), dt)
    return pl.pallas_call(
        lambda *refs: first_body(slots, *refs),
        grid_spec=pltpu.PrefetchScalarGridSpec(
            num_scalar_prefetch=1,
            grid=(steps,),
            in_specs=[row(D), row(D)]
            + [full(a.shape) for a in (vec, wj, wm)],
            out_specs=[
                row(D),
                row(3 * D),
                pl.BlockSpec((group, PAIRS, 2 * slots, slots), lambda i, c: (i, 0, 0, 0)),
                row(D),
                row(D),
                row(D),
                row(D),
            ],
        ),
        out_shape=[
            out(D, BF),
            out(3 * D, BF),
            jax.ShapeDtypeStruct((total // slots, PAIRS, 2 * slots, slots), BF),
            out(D, BF),
            out(D, F32),
            out(D, BF),
            out(D, BF),
        ],
        compiler_params=params(),
        cost_estimate=cost(2 * total * D * D * 4 * 2, 20e6),
        name="attn_fwd",
    )(counts, tok, cot, vec, wj, wm)


def put_blocks(ref, which, mask, value):
    for k in range(BLOCKS):
        ref[which, k ^ mask] = value[k * BROWS : (k + 1) * BROWS, :].astype(BF)


def quarter_body(chunk, ids_ref, sec_ref, gout_ref, up_ref, ub_ref, down_ref, *rest):
    act_ref, gh_ref, grad_ref = rest[-3:]
    rows = sec_ref.shape[0]
    chunk = rows // chunk
    for part in range(rows // chunk):
        here = slice(part * chunk, (part + 1) * chunk)
        hidden = dot(sec_ref[here, :], up_ref[...]) + ub_ref[...]
        grad_act = dot_t(gout_ref[here, :], down_ref[...])
        cdf = 0.5 + 0.5 * lax.erf(hidden * (0.5**0.5))
        act_ref[0, here, :] = (hidden * cdf).astype(BF)
        slope = cdf + hidden * (jnp.exp(-0.5 * hidden * hidden) * ((2 * math.pi) ** -0.5))
        gh_ref[0, here, :] = (grad_act * slope).astype(BF)
    put_blocks(grad_ref, 0, ids_ref[0], t_dot(act_ref[0], gout_ref[...]))
    put_blocks(grad_ref, 1, ids_ref[1], t_dot(sec_ref[...], gh_ref[0]))


def quarter_call(call, ids, second, gout, up, ub, down, kept):
    total = second.shape[0]
    quarter = lambda ids: ids[4 + call]
    in_specs = [
        full((total, D)),
        full((total, D)),
        pl.BlockSpec((D, D), lambda i, ids: (0, quarter(ids))),
        pl.BlockSpec((1, D), lambda i, ids: (0, quarter(ids))),
        pl.BlockSpec((D, D), lambda i, ids: (quarter(ids), 0)),
    ]
    args = [ids, second, gout, up, ub, down]
    aliases = {}
    if kept is not None:
        in_specs += [pl.BlockSpec(memory_space=pl.ANY)] * 2
        args += list(kept)
        aliases = {6: 0, 7: 1}
    slab = pl.BlockSpec((1, total, D), lambda i, ids: (call, 0, 0))
    return pl.pallas_call(
        lambda *refs: quarter_body(2, *refs),
        grid_spec=pltpu.PrefetchScalarGridSpec(
            num_scalar_prefetch=1,
            grid=(1,),
            in_specs=in_specs,
            out_specs=[slab, slab, full((2, BLOCKS, BROWS, D))],
        ),
        out_shape=[
            jax.ShapeDtypeStruct((4, total, D), BF),
            jax.ShapeDtypeStruct((4, total, D), BF),
            jax.ShapeDtypeStruct((2, BLOCKS, BROWS, D), BF),
        ],
        input_output_aliases=aliases,
        compiler_params=params(),
        cost_estimate=cost(8 * total * D * D * 2, 12e6),
        name=f"mlp_{call}",
    )(*args)


def middle_body(
    slots,
    counts_ref,
    ids_ref,
    act_ref,
    gh_ref,
    down_ref,
    up_ref,
    mid_ref,
    gout_ref,
    vec_ref,
    wm_ref,
    result_ref,
    gmid_ref,
    branch_ref,
    gmix_ref,
    small_ref,
    outer_ref,
    g_ref,
):
    step = pl.program_id(0)
    rows = mid_ref.shape[0]
    items = rows // slots
    outer = dot(act_ref[0], down_ref[...])
    g = dot_t(gh_ref[0], up_ref[...])
    sums = jnp.sum(gh_ref[0].astype(F32), axis=0, keepdims=True)
    small_ref[pl.ds(ids_ref[4 + step], 1), :] = sums

    @pl.when(step == 0)
    def _():
        outer_ref[...] = outer
        g_ref[...] = g

    @pl.when(step > 0)
    def _():
        outer_ref[...] += outer
        g_ref[...] += g

    @pl.when(step == 3)
    def _():
        row_slot = lax.broadcasted_iota(jnp.int32, (slots, D), 0)

        def one(item, sums):
            here = pl.ds(pl.multiple_of(item * slots, 16), slots)
            seen = row_slot < counts_ref[item]
            middle = mid_ref[here, :]
            total = middle + outer_ref[here, :] + vec_ref[7:8, :]
            result_ref[here, :] = jnp.where(seen, total, 0.0).astype(BF)
            gout = gout_ref[here, :].astype(F32)
            xhat, rstd = stats(middle)
            g = g_ref[here, :]
            e = g * vec_ref[5:6, :]
            mean_e = jnp.mean(e, axis=-1, keepdims=True)
            mean_x = jnp.mean(e * xhat, axis=-1, keepdims=True)
            grad = gout + rstd * (e - mean_e - xhat * mean_x)
            gmid_ref[here, :] = grad
            branch = grad.astype(BF)
            branch_ref[here, :] = branch
            row = lambda a: jnp.sum(a, axis=0, keepdims=True)
            return (
                sums[0] + row(gout),
                sums[1] + row(g * xhat),
                sums[2] + row(g),
                sums[3] + row(branch.astype(F32)),
            )

        zero = jnp.zeros((1, D), F32)
        sums = lax.fori_loop(0, items, one, (zero,) * 4)
        for k in range(4):
            small_ref[4 + k : 5 + k, :] = sums[k]
        gmix_ref[...] = dot_t(branch_ref[...], wm_ref[...]).astype(BF)


def middle_call(slots, counts, ids, act, gh, down, up, mid, gout, vec, wm):
    total = mid.shape[0]
    whole = full((total, D))
    return pl.pallas_call(
        lambda *refs: middle_body(slots, *refs),
        grid_spec=pltpu.PrefetchScalarGridSpec(
            num_scalar_prefetch=2,
            grid=(4,),
            in_specs=[
                pl.BlockSpec((1, total, D), lambda i, c, ids: (i, 0, 0)),
                pl.BlockSpec((1, total, D), lambda i, c, ids: (i, 0, 0)),
                pl.BlockSpec((D, D), lambda i, c, ids: (ids[4 + i], 0)),
                pl.BlockSpec((D, D), lambda i, c, ids: (0, ids[4 + i])),
                whole,
                whole,
                full((8, D)),
                full((D, D)),
            ],
            out_specs=[whole, whole, whole, whole, full((8, D))],
            scratch_shapes=[pltpu.VMEM((total, D), F32), pltpu.VMEM((total, D), F32)],
        ),
        out_shape=[
            jax.ShapeDtypeStruct((total, D), BF),
            jax.ShapeDtypeStruct((total, D), F32),
            jax.ShapeDtypeStruct((total, D), BF),
            jax.ShapeDtypeStruct((total, D), BF),
            jax.ShapeDtypeStruct((8, D), F32),
        ],
        compiler_params=params(),
        cost_estimate=cost(2 * total * D * D * 9, 25e6),
        name="mlp_back",
    )(counts, ids, act, gh, down, up, mid, gout, vec, wm)


def attn_back_body(joined_ref, probs_ref, gmix_ref, grad_ref):
    slots = joined_ref.shape[0]
    low = head_masks(slots)
    for pair in range(PAIRS):
        cols = slice(pair * LANES, (pair + 1) * LANES)
        q = stack_heads(joined_ref[:, cols], low)
        k = joined_ref[:, D + pair * LANES : D + (pair + 1) * LANES]
        v = joined_ref[:, 2 * D + pair * LANES : 2 * D + (pair + 1) * LANES]
        out = stack_heads(gmix_ref[:, cols], low)
        low_soft = probs_ref[0, pair]
        soft = low_soft.astype(F32)
        grad_probs = dot_t(out, v)
        mean = jnp.sum(soft * grad_probs, axis=-1, keepdims=True)
        scores = (soft * (grad_probs - mean)).astype(BF)
        gq = dot(scores, k) * FACTOR
        grad_ref[:, cols] = jnp.where(low, gq[:slots], gq[slots:]).astype(BF)
        grad_ref[:, D + pair * LANES : D + (pair + 1) * LANES] = (
            t_dot(scores, q) * FACTOR
        ).astype(BF)
        grad_ref[:, 2 * D + pair * LANES : 2 * D + (pair + 1) * LANES] = t_dot(
            low_soft, out
        ).astype(BF)


def attn_back_call(slots, joined, probs, gmix):
    total = joined.shape[0]
    row = lambda width: pl.BlockSpec((slots, width), lambda i: (i, 0))
    return pl.pallas_call(
        attn_back_body,
        grid=(total // slots,),
        in_specs=[
            row(3 * D),
            pl.BlockSpec((1, PAIRS, 2 * slots, slots), lambda i: (i, 0, 0, 0)),
            row(D),
        ],
        out_specs=row(3 * D),
        out_shape=jax.ShapeDtypeStruct((total, 3 * D), BF),
        compiler_params=params(),
        cost_estimate=cost(total * slots * 256 * 6 * 8, 12e6),
        name="attn_bwd",
    )(joined, probs, gmix)


def attn_grad_body(ids_ref, normed_ref, mix_ref, grad_ref, branch_ref, out_ref):
    half = BLOCKS // 2

    def put(which, base, mask, value):
        for k in range(half):
            out_ref[which, (base + k) ^ mask] = value[k * BROWS : (k + 1) * BROWS, :].astype(BF)

    normed = normed_ref[...]
    put(0, 0, ids_ref[0], t_dot(normed, grad_ref[:, :D]))
    put(0, half, ids_ref[0], t_dot(normed, grad_ref[:, D : 2 * D]))
    put(1, 0, ids_ref[1], t_dot(normed, grad_ref[:, 2 * D :]))
    put(1, half, ids_ref[1], t_dot(mix_ref[...], branch_ref[...]))


def attn_grad_call(call, ids, normed, mix, grad, branch):
    total = normed.shape[0]
    half = pl.BlockSpec((total, D // 2), lambda i, ids: (0, ids[8 + call]))
    return pl.pallas_call(
        attn_grad_body,
        grid_spec=pltpu.PrefetchScalarGridSpec(
            num_scalar_prefetch=1,
            grid=(1,),
            in_specs=[half, half, full((total, 3 * D)), full((total, D))],
            out_specs=full((2, BLOCKS, BROWS, D)),
        ),
        out_shape=jax.ShapeDtypeStruct((2, BLOCKS, BROWS, D), BF),
        compiler_params=params(),
        cost_estimate=cost(2 * total * D * D * 2, 8e6),
        name=f"attn_grad_{call}",
    )(ids, normed, mix, grad, branch)


def last_body(slots, grad_ref, wj_ref, tok_ref, gmid_ref, vec_ref, out_ref, small_ref, g_ref):
    rows = tok_ref.shape[0]
    items = rows // slots
    g_ref[...] = dot_t(grad_ref[...], wj_ref[...])

    def one(item, sums):
        here = pl.ds(pl.multiple_of(item * slots, 16), slots)
        xhat, rstd = stats(tok_ref[here, :].astype(F32))
        g = g_ref[here, :]
        e = g * vec_ref[0:1, :]
        mean_e = jnp.mean(e, axis=-1, keepdims=True)
        mean_x = jnp.mean(e * xhat, axis=-1, keepdims=True)
        out_ref[here, :] = (gmid_ref[here, :] + rstd * (e - mean_e - xhat * mean_x)).astype(BF)
        row = lambda a: jnp.sum(a, axis=0, keepdims=True)
        return (
            sums[0] + row(grad_ref[here, :D].astype(F32)),
            sums[1] + row(grad_ref[here, 2 * D :].astype(F32)),
            sums[2] + row(g * xhat),
            sums[3] + row(g),
        )

    zero = jnp.zeros((1, D), F32)
    sums = lax.fori_loop(0, items, one, (zero,) * 4)
    for k in range(4):
        small_ref[k : k + 1, :] = sums[k]
    small_ref[4:8, :] = jnp.zeros((4, D), F32)


def last_call(slots, grad, wj, tok, gmid, vec):
    total = tok.shape[0]
    return pl.pallas_call(
        lambda *refs: last_body(slots, *refs),
        grid=(1,),
        in_specs=[full(a.shape) for a in (grad, wj, tok, gmid, vec)],
        out_specs=[full((total, D)), full((8, D))],
        out_shape=[
            jax.ShapeDtypeStruct((total, D), BF),
            jax.ShapeDtypeStruct((8, D), F32),
        ],
        scratch_shapes=[pltpu.VMEM((total, D), F32)],
        compiler_params=params(),
        cost_estimate=cost(2 * total * D * D * 3, 12e6),
        name="first_back",
    )(grad, wj, tok, gmid, vec)


def finish_mlp_body(groups, ab, ids_ref, in_ref, *rest):
    out_ref = rest[-1]
    mask = ids_ref[ab] & (groups - 1)
    for k in range(groups):
        out_ref[k * BROWS : (k + 1) * BROWS, :] = in_ref[0, k ^ mask].astype(F32)


def finish_mlp_call(ab, which, ids, blocks, kept):
    groups = 8
    steps = BLOCKS // groups

    def place(chunk, i, ids):
        at = (ids[ab] // groups) ^ i
        quarter = 2 * chunk + (ids[3] ^ which)
        return (quarter * steps + at, 0) if ab == 0 else (at, quarter)

    in_specs = [pl.BlockSpec((1, groups, BROWS, D), lambda chunk, i, ids: (chunk, i, 0, 0))]
    args = [ids, blocks]
    aliases = {}
    if kept is not None:
        in_specs.append(pl.BlockSpec(memory_space=pl.ANY))
        args.append(kept)
        aliases = {2: 0}
    return pl.pallas_call(
        lambda *refs: finish_mlp_body(groups, ab, *refs),
        grid_spec=pltpu.PrefetchScalarGridSpec(
            num_scalar_prefetch=1,
            grid=(2, steps),
            in_specs=in_specs,
            out_specs=pl.BlockSpec((groups * BROWS, D), place),
        ),
        out_shape=jax.ShapeDtypeStruct((FF, D) if ab == 0 else (D, FF), F32),
        input_output_aliases=aliases,
        compiler_params=params(16),
        cost_estimate=cost(0, 7e6),
        name=f"finish_mlp_{ab}_{which}",
    )(*args)


def finish_attn_body(ids_ref, a_ref, b_ref, *rest):
    joined_ref, merge_ref = rest[-2:]
    half = BLOCKS // 2
    for ab, in_ref in enumerate((a_ref, b_ref)):
        mask = ids_ref[ab]
        for i in range(BLOCKS):
            block = in_ref[i ^ mask].astype(F32)
            third, k = 2 * ab + i // half, i % half
            rows = slice(k * BROWS, (k + 1) * BROWS)
            if third < 3:
                joined_ref[rows, third * D : (third + 1) * D] = block
            else:
                merge_ref[rows, :] = block


def finish_attn_call(which, ids, a, b, kept):
    in_specs = [full((BLOCKS, BROWS, D))] * 2
    args = [ids, a, b]
    aliases = {}
    if kept is not None:
        in_specs += [pl.BlockSpec(memory_space=pl.ANY)] * 2
        args += list(kept)
        aliases = {3: 0, 4: 1}
    place = lambda i, ids: (ids[3] ^ which, 0)
    return pl.pallas_call(
        finish_attn_body,
        grid_spec=pltpu.PrefetchScalarGridSpec(
            num_scalar_prefetch=1,
            grid=(1,),
            in_specs=in_specs,
            out_specs=[pl.BlockSpec((D // 2, 3 * D), place), pl.BlockSpec((D // 2, D), place)],
        ),
        out_shape=[jax.ShapeDtypeStruct(s, F32) for s in ((D, 3 * D), (D, D))],
        input_output_aliases=aliases,
        compiler_params=params(32),
        cost_estimate=cost(0, 7e6),
        name=f"finish_attn_{which}",
    )(*args)


def stage_lists(sizes):
    bits = {axis: [(axis, b) for b in range(size.bit_length() - 1)] for axis, size in sizes.items()}
    dp, group = bits["dp"], bits["group"]
    if len(dp) == 2 and len(group) == 3:
        order = group + dp
    else:
        order = [dp[0], group[0], group[-1]] + dp[1:] + group[1:-1]
    return order[0], order[1:3], order[3:]


def add(a, b):
    return (a.astype(F32) + b.astype(F32)).astype(BF)


def bit_of(stage):
    return (lax.axis_index(stage[0]) >> stage[1]) & 1


def tie(*values):
    return lax.optimization_barrier(values)


class Sums:
    def __init__(self, sizes):
        self.sizes = sizes
        self.first, self.pair, self.rest = stage_lists(sizes)

    def swap(self, value, stage):
        axis, bit = stage
        return lax.ppermute(value, axis, [(i, i ^ (1 << bit)) for i in range(self.sizes[axis])])

    def stage(self, ab, at):
        return self.pair[at if ab == 0 else 1 - at]

    def halve(self, mine, got, axis=0):
        n = mine.shape[axis] // 2
        low = lax.slice_in_dim(mine, 0, n, axis=axis), lax.slice_in_dim(got, 0, n, axis=axis)
        high = lax.slice_in_dim(mine, n, 2 * n, axis=axis), lax.slice_in_dim(
            got, n, 2 * n, axis=axis
        )
        return add(*low), add(*high)

    def tail_down(self, at, mine):
        if at < 2:
            n = mine.shape[1] // 2
            return mine[:, :n], mine[:, n:]
        n = mine.shape[2] // 2
        high = bit_of(self.rest[at]) == 1
        low_rows, high_rows = mine[:, :, :n], mine[:, :, n:]
        return jnp.where(high, high_rows, low_rows), jnp.where(high, low_rows, high_rows)

    def tail_up(self, at, mine, got):
        if at < 2:
            return jnp.concatenate([mine, got], axis=1)
        high = bit_of(self.rest[at]) == 1
        return jnp.concatenate([jnp.where(high, got, mine), jnp.where(high, mine, got)], axis=2)


def split_small(value):
    high = lax.reduce_precision(value, 8, 7)
    return jnp.concatenate([high.astype(BF), (value - high).astype(BF)], axis=0)


def join_small(value):
    n = value.shape[0] // 2
    return value[:n].astype(F32) + value[n:].astype(F32)


def solution(mesh):
    sizes = dict(mesh.shape)
    sums = Sums(sizes)

    def shards(
        tokens,
        cotangent,
        counts,
        first_gain,
        first_shift,
        joined_weight,
        joined_bias,
        merge_weight,
        merge_bias,
        second_gain,
        second_shift,
        up_weight,
        up_bias,
        down_weight,
        down_bias,
    ):
        items, slots, features = tokens.shape
        total = items * slots
        row = lambda a: a.reshape(1, -1)
        tok = tokens.reshape(total, features)
        cot = cotangent.reshape(total, features)
        counts = counts.astype(jnp.int32)
        masks = []
        for two in (sums.pair, sums.pair[::-1]):
            mask = 0
            for stage in list(two) + list(sums.rest[:2]):
                mask = 2 * mask + bit_of(stage)
            masks.append(mask)
        core = bit_of(sums.first)
        other = 1 - core
        ids = jnp.stack(
            [masks[0], masks[1], core, core, other, core, 2 + other, 2 + core, other, core]
        ).astype(jnp.int32)

        vec = vectors(
            first_gain,
            first_shift,
            joined_bias,
            merge_bias,
            second_gain,
            second_shift,
            down_bias,
        )
        normed, joined, probs, mix, middle, second, gout = first_call(
            4,
            slots,
            counts,
            tok,
            cot,
            vec,
            joined_weight,
            merge_weight,
        )

        def quarter(call, kept, ids):
            act, gh, grad = quarter_call(
                call, ids, second, gout, up_weight, row(up_bias), down_weight, kept
            )
            return (act, gh), grad

        def start_pair(keep, send, at):
            return [sums.swap(send[ab], sums.stage(ab, at)) for ab in range(2)]

        kept, send0 = quarter(0, None, ids)
        got0 = sums.swap(send0, sums.first)
        kept, keep0 = quarter(1, kept, ids)
        keep0, out0 = zip(*[sums.halve(keep0[ab], got0[ab]) for ab in range(2)])
        got0 = start_pair(keep0, out0, 0)
        ids, out0 = tie(ids, out0)
        kept, send1 = quarter(2, kept, ids)
        got1 = sums.swap(send1, sums.first)
        kept, keep1 = quarter(3, kept, ids)
        keep1, out1 = zip(*[sums.halve(keep1[ab], got1[ab]) for ab in range(2)])
        got1 = start_pair(keep1, out1, 0)
        keep0, out0 = zip(*[sums.halve(keep0[ab], got0[ab]) for ab in range(2)])
        got0 = start_pair(keep0, out0, 1)
        ids, out0, out1 = tie(ids, out0, out1)
        result, gmid, branch, gmix, small_a = middle_call(
            slots,
            counts,
            ids,
            kept[0],
            kept[1],
            down_weight,
            up_weight,
            middle,
            gout,
            vec,
            merge_weight,
        )
        keep1, out1 = zip(*[sums.halve(keep1[ab], got1[ab]) for ab in range(2)])
        got1 = start_pair(keep1, out1, 1)
        mine0 = [add(keep0[ab], got0[ab]) for ab in range(2)]
        gmix, out1, mine0 = tie(gmix, out1, mine0)
        grad_joined = attn_back_call(slots, joined, probs, gmix)
        mine1 = [add(keep1[ab], got1[ab]) for ab in range(2)]
        mine = jnp.stack([mine0[0], mine1[0], mine0[1], mine1[1]])
        down = sums.tail_down(0, mine)
        got = sums.swap(down[1], sums.rest[0])
        ids, down = tie(ids, down)
        send2 = attn_grad_call(0, ids, normed, mix, grad_joined, branch)
        got2 = sums.swap(send2, sums.first)
        for at in range(len(sums.rest)):
            mine = add(down[0], got)
            if at + 1 < len(sums.rest):
                down = sums.tail_down(at + 1, mine)
                got = sums.swap(down[1], sums.rest[at + 1])
                if at == 0:
                    ids, down = tie(ids, down)
                    keep2 = attn_grad_call(1, ids, normed, mix, grad_joined, branch)
        keep2, out2 = zip(*[sums.halve(keep2[ab], got2[ab]) for ab in range(2)])
        got2 = start_pair(keep2, out2, 0)
        got = sums.swap(mine, sums.rest[-1])
        grad_joined, out2, mine = tie(grad_joined, out2, mine)
        token_grad, small_b = last_call(
            slots, grad_joined, joined_weight, tok, gmid, vec
        )
        for at in reversed(range(len(sums.rest))):
            mine = sums.tail_up(at, mine, got)
            if at:
                got = sums.swap(mine, sums.rest[at - 1])
        keep2, out2 = zip(*[sums.halve(keep2[ab], got2[ab]) for ab in range(2)])
        got2 = start_pair(keep2, out2, 1)
        own = [mine[:2], mine[2:]]
        got = [sums.swap(own[ab], sums.stage(ab, 1)) for ab in range(2)]
        mine2 = jnp.stack([add(keep2[ab], got2[ab]) for ab in range(2)])
        for at in range(len(sums.rest)):
            down = sums.tail_down(at, mine2)
            mine2 = add(down[0], sums.swap(down[1], sums.rest[at]))
        small = jnp.concatenate([small_a, small_b[:4]], axis=0)

        def piggy(value, small, stage):
            rows = split_small(small)
            pad = jnp.zeros((BROWS - rows.shape[0], D), BF)
            load = value.reshape(-1, D)
            out = jnp.concatenate([load, rows, pad], axis=0)
            got = sums.swap(out, stage)
            total = join_small(rows) + join_small(
                got[load.shape[0] : load.shape[0] + rows.shape[0]]
            )
            return got[: load.shape[0]].reshape(value.shape), total

        for at in reversed(range(len(sums.rest))):
            got2, small = piggy(mine2, small, sums.rest[at])
            mine2 = sums.tail_up(at, mine2, got2)
        own = [jnp.concatenate([own[ab], got[ab]], axis=1) for ab in range(2)]
        got = [sums.swap(own[ab], sums.stage(ab, 0)) for ab in range(2)]
        own2 = [mine2[0], mine2[1]]
        for at in (1, 0):
            got2, small = piggy(own2[0], small, sums.stage(0, at))
            other2 = sums.swap(own2[1], sums.stage(1, at))
            own2 = [jnp.concatenate([own2[0], got2]), jnp.concatenate([own2[1], other2])]
            if at:
                own = [jnp.concatenate([own[ab], got[ab]], axis=1) for ab in range(2)]
                got = [sums.swap(own[ab], sums.first) for ab in range(2)]
        mlp = [finish_mlp_call(ab, 0, ids, own[ab], None) for ab in range(2)]
        mlp = [finish_mlp_call(ab, 1, ids, got[ab], mlp[ab]) for ab in range(2)]
        got2, small = piggy(own2[0], small, sums.first)
        other2 = sums.swap(own2[1], sums.first)
        attn = finish_attn_call(0, ids, own2[0], own2[1], None)
        joined_grad, merge_grad = finish_attn_call(1, ids, got2, other2, attn)
        down_grad, up_grad = mlp
        return (
            result.reshape(tokens.shape),
            token_grad.reshape(tokens.shape),
            small[10],
            small[11],
            joined_grad,
            small[8:10],
            merge_grad,
            small[7],
            small[5],
            small[6],
            up_grad,
            small[:4].reshape(FF),
            down_grad,
            small[4],
        )

    spread = P(("dp", "group"), None, None)
    return jax.shard_map(
        shards,
        mesh=mesh,
        in_specs=(spread, spread, P(("dp", "group"))) + (P(),) * 12,
        out_specs=(spread, spread) + (P(),) * 12,
        check_vma=False,
    )
```

profile of v0, /device:TPU:0, one launch (start us, length us, event | category | flops | bytes accessed | tf_op | source)
XLA Modules:
  0.0 284.8 jit_solution(8719029428958437299)
XLA Ops:
  2.1 1.4 select_select_fusion.refs_3_.refs_8_.refs_4_
  3.6 16.6 %attn_fwd.1 = (bf16[640,768]{1,0:T(8,128)(2,1)}, bf16[640,2304]{1,0:T(8,128)(2,1)}, bf16[4,6,320,160]{3,2,1,0:T(8,128)(2,1)}, bf16[640,768]{1,0:T(8,128)(2,1)}, ...) custom-call(s32[4]{0:T(128)} %refs_0_.3, bf16[640,768]{1,0:T(8,128)(2,1)} %bitcast.122, ...), custom_call_target="tpu_custom_call" | custom-call | flops 60397977600 | bytes 200000000 | tf_op jit(solution)/shard_map/attn_fwd/pallas_call | solution.py:141
  20.1 7.9 %mlp_0.1 = (bf16[4,640,768]{2,1,0:T(8,128)(2,1)}, bf16[4,640,768]{2,1,0:T(8,128)(2,1)}, bf16[2,16,48,768]{3,2,1,0:T(8,128)(2,1)}) custom-call(s32[10]{0:T(128)} %stack.55.refs_0_.refs_1_.ids_ref, bf16[640,768]{1,0:T(8,128)(2,1)} %get-tuple-element.55.refs_1_, bf16[640,768]{1,0:T(8,128)(2,1)} %get-tuple-element.56.refs_2_.refs_7_, ...), custom_call_target="tpu_custom_call" | custom-call | flops 60397977600 | bytes 120000000 | tf_op jit(solution)/shard_map/mlp_0/pallas_call | solution.py:211
  28.5 8.2 %mlp_1.1 = (bf16[4,640,768]{2,1,0:T(8,128)(2,1)}, bf16[4,640,768]{2,1,0:T(8,128)(2,1)}, bf16[2,16,48,768]{3,2,1,0:T(8,128)(2,1)}) custom-call(s32[10]{0:T(128)} %stack.55.refs_0_.refs_1_.ids_ref, bf16[640,768]{1,0:T(8,128)(2,1)} %get-tuple-element.55.refs_1_, ...), custom_call_target="tpu_custom_call", output_to_operand_aliasing={{0}: (6, {}), {1}: (7, {})} | custom-call | flops 60397977600 | bytes 120000000 | tf_op jit(solution)/shard_map/mlp_1/pallas_call | solution.py:211
  36.7 2.2 add_convert_fusion.9
  38.8 2.6 collective-permute-start.2
  41.4 1.5 collective-permute-start.1
  42.9 8.1 %mlp_2.1 = (bf16[4,640,768]{2,1,0:T(8,128)(2,1)}, bf16[4,640,768]{2,1,0:T(8,128)(2,1)}, bf16[2,16,48,768]{3,2,1,0:T(8,128)(2,1)}) custom-call(s32[10]{0:T(128)} %stack.55.refs_0_.refs_1_.ids_ref, bf16[640,768]{1,0:T(8,128)(2,1)} %get-tuple-element.55.refs_1_, ...), custom_call_target="tpu_custom_call", output_to_operand_aliasing={{0}: (6, {}), {1}: (7, {})} | custom-call | flops 60397977600 | bytes 120000000 | tf_op jit(solution)/shard_map/mlp_2/pallas_call | solution.py:211
  51.0 4.4 %collective-permute-done.2 = bf16[8,48,768]{2,1,0:T(8,128)(2,1)S(1)} collective-permute-done((bf16[8,48,768]{2,1,0:T(8,128)(2,1)S(1)}, bf16[8,48,768]{2,1,0:T(8,128)(2,1)S(1)}, u32[]{:S(2)}, u32[]{:S(2)}) %collective-permute-start.2) | collective-permute-done | bytes 589856 | tf_op jit(solution)/shard_map/ppermute | solution.py:567
  55.5 1.8 collective-permute-start.7
  57.4 1.6 collective-permute-start.6
  58.9 8.4 %mlp_3.1 = (bf16[4,640,768]{2,1,0:T(8,128)(2,1)}, bf16[4,640,768]{2,1,0:T(8,128)(2,1)}, bf16[2,16,48,768]{3,2,1,0:T(8,128)(2,1)}) custom-call(s32[10]{0:T(128)} %stack.55.refs_0_.refs_1_.ids_ref, bf16[640,768]{1,0:T(8,128)(2,1)} %get-tuple-element.55.refs_1_, ...), custom_call_target="tpu_custom_call", output_to_operand_aliasing={{0}: (6, {}), {1}: (7, {})} | custom-call | flops 60397977600 | bytes 120000000 | tf_op jit(solution)/shard_map/mlp_3/pallas_call | solution.py:211
  67.6 1.4 copy-done.1
  71.4 18.0 %mlp_back.1 = (bf16[640,768]{1,0:T(8,128)(2,1)}, f32[640,768]{1,0:T(8,128)}, bf16[640,768]{1,0:T(8,128)(2,1)}, bf16[640,768]{1,0:T(8,128)(2,1)}, f32[8,768]{1,0:T(8,128)}) custom-call(s32[4]{0:T(128)} %refs_0_.3, s32[10]{0:T(128)} %stack.55.refs_0_.refs_1_.ids_ref, bf16[4,640,768]{2,1,0:T(8,128)(2,1)} %get-tuple-element.69.refs_2_, ...), custom_call_target="tpu_custom_call" | custom-call | flops 67947724800 | bytes 250000000 | tf_op jit(solution)/shard_map/mlp_back/pallas_call | solution.py:307
  90.5 1.6 collective-permute-start.8
  92.1 13.3 %attn_bwd.1.grad_ref.refs_0_ = bf16[640,2304]{1,0:T(8,128)(2,1)} custom-call(bf16[640,2304]{1,0:T(8,128)(2,1)} %get-tuple-element.73.joined_ref, bf16[4,6,320,160]{3,2,1,0:T(8,128)(2,1)} %get-tuple-element.74.probs_ref, bf16[640,768]{1,0:T(8,128)(2,1)} %get-tuple-element.76.gmix_ref), custom_call_target="tpu_custom_call" | custom-call | flops 12582912000 | bytes 120000000 | tf_op jit(solution)/shard_map/attn_bwd/pallas_call | solution.py:365
  105.9 1.6 collective-permute-start.10
  107.6 6.6 %attn_grad_0.1 = bf16[2,16,48,768]{3,2,1,0:T(8,128)(2,1)} custom-call(s32[10]{0:T(128)} %stack.55.refs_0_.refs_1_.ids_ref, bf16[640,768]{1,0:T(8,128)(2,1)} %get-tuple-element.82.normed_ref, bf16[640,768]{1,0:T(8,128)(2,1)} %get-tuple-element.83.mix_ref, bf16[640,2304]{1,0:T(8,128)(2,1)} %attn_bwd.1.grad_ref.refs_0_, ...), custom_call_target="tpu_custom_call" | custom-call | flops 15099494400 | bytes 80000000 | tf_op jit(solution)/shard_map/attn_grad_0/pallas_call | solution.py:398
  114.2 5.1 %collective-permute-done.10 = bf16[4,2,48,768]{3,2,1,0:T(8,128)(2,1)S(1)} collective-permute-done((bf16[4,2,48,768]{3,2,1,0:T(8,128)(2,1)S(1)}, bf16[4,2,48,768]{3,2,1,0:T(8,128)(2,1)S(1)}, u32[]{:S(2)}, u32[]{:S(2)}) %collective-permute-start.10) | collective-permute-done | bytes 589856 | tf_op jit(solution)/shard_map/ppermute | solution.py:567
  119.4 6.5 %attn_grad_1.1 = bf16[2,16,48,768]{3,2,1,0:T(8,128)(2,1)} custom-call(s32[10]{0:T(128)} %stack.55.refs_0_.refs_1_.ids_ref, bf16[640,768]{1,0:T(8,128)(2,1)} %get-tuple-element.82.normed_ref, bf16[640,768]{1,0:T(8,128)(2,1)} %get-tuple-element.83.mix_ref, bf16[640,2304]{1,0:T(8,128)(2,1)} %attn_bwd.1.grad_ref.refs_0_, ...), custom_call_target="tpu_custom_call" | custom-call | flops 15099494400 | bytes 80000000 | tf_op jit(solution)/shard_map/attn_grad_1/pallas_call | solution.py:398
  125.9 2.2 add_convert_fusion.1
  128.7 2.6 collective-permute-start.12
  132.3 9.4 %collective-permute-done.12 = bf16[4,1,48,768]{3,2,1,0:T(8,128)(2,1)S(1)} collective-permute-done((bf16[4,1,48,768]{3,2,1,0:T(8,128)(2,1)S(1)}, bf16[4,1,48,768]{3,2,1,0:T(8,128)(2,1)S(1)}, u32[]{:S(2)}, u32[]{:S(2)}) %collective-permute-start.12) | collective-permute-done | bytes 294944 | tf_op jit(solution)/shard_map/ppermute | solution.py:567
  143.2 1.6 collective-permute-start.14
  144.8 9.0 %first_back.1 = (bf16[640,768]{1,0:T(8,128)(2,1)}, f32[8,768]{1,0:T(8,128)}) custom-call(bf16[640,2304]{1,0:T(8,128)(2,1)} %attn_bwd.1.grad_ref.refs_0_, bf16[768,2304]{1,0:T(8,128)(2,1)} %refs_1_.1, bf16[640,768]{1,0:T(8,128)(2,1)} %bitcast.123, f32[640,768]{1,0:T(8,128)} %get-tuple-element.87.refs_3_, f32[8,768]{1,0:T(8,128)} %select_select_fusion.refs_3_.refs_8_.refs_4_), custom_call_target="tpu_custom_call" | custom-call | flops 22649241600 | bytes 120000000 | tf_op jit(solution)/shard_map/first_back/pallas_call | solution.py:443
  154.1 3.5 %collective-permute-start.17 = (bf16[2,2,48,768]{3,2,1,0:T(8,128)(2,1)S(1)}, bf16[2,2,48,768]{3,2,1,0:T(8,128)(2,1)S(1)}, u32[]{:S(2)}, u32[]{:S(2)}) collective-permute-start(bf16[2,2,48,768]{3,2,1,0:T(8,128)(2,1)S(1)} %pad_maximum_fusion.15), channel_id=1, source_target_pairs={{0,8},{8,0},{16,24},{24,16},{1,9},{9,1},{17,25},{25,17},{2,10},{10... | collective-permute-start | bytes 884744 | tf_op jit(solution)/shard_map/ppermute | solution.py:567
  158.3 8.8 %collective-permute-done.17 = bf16[2,2,48,768]{3,2,1,0:T(8,128)(2,1)S(1)} collective-permute-done((bf16[2,2,48,768]{3,2,1,0:T(8,128)(2,1)S(1)}, bf16[2,2,48,768]{3,2,1,0:T(8,128)(2,1)S(1)}, u32[]{:S(2)}, u32[]{:S(2)}) %collective-permute-start.17) | collective-permute-done | bytes 294944 | tf_op jit(solution)/shard_map/ppermute | solution.py:567
  167.3 11.7 %collective-permute-done.28 = bf16[4,2,48,768]{3,2,1,0:T(8,128)(2,1)S(1)} collective-permute-done((bf16[4,2,48,768]{3,2,1,0:T(8,128)(2,1)S(1)}, bf16[4,2,48,768]{3,2,1,0:T(8,128)(2,1)S(1)}, u32[]{:S(2)}, u32[]{:S(2)}) %collective-permute-start.28) | collective-permute-done | bytes 589856 | tf_op jit(solution)/shard_map/ppermute | solution.py:567
  179.2 2.5 collective-permute-start.19
  182.7 1.1 collective-permute-start.29
  183.8 5.2 %collective-permute-done.19 = bf16[144,768]{1,0:T(8,128)(2,1)S(1)} collective-permute-done((bf16[144,768]{1,0:T(8,128)(2,1)S(1)}, bf16[144,768]{1,0:T(8,128)(2,1)S(1)}, u32[]{:S(2)}, u32[]{:S(2)}) %collective-permute-start.19) | collective-permute-done | bytes 221216 | tf_op jit(solution)/shard_map/ppermute | solution.py:567
  189.2 4.5 %collective-permute-done.32 = bf16[2,4,48,768]{3,2,1,0:T(8,128)(2,1)S(1)} collective-permute-done((bf16[2,4,48,768]{3,2,1,0:T(8,128)(2,1)S(1)}, bf16[2,4,48,768]{3,2,1,0:T(8,128)(2,1)S(1)}, u32[]{:S(2)}, u32[]{:S(2)}) %collective-permute-start.32) | collective-permute-done | bytes 589856 | tf_op jit(solution)/shard_map/ppermute | solution.py:567
  193.8 2.5 collective-permute-start.33
  198.4 3.2 %collective-permute-start.21 = (bf16[240,768]{1,0:T(8,128)(2,1)S(1)}, bf16[240,768]{1,0:T(8,128)(2,1)S(1)}, u32[]{:S(2)}, u32[]{:S(2)}) collective-permute-start(bf16[240,768]{1,0:T(8,128)(2,1)S(1)} %pad_maximum_fusion.13), channel_id=1, source_target_pairs={{0,4},{1,5},{2,6},{3,7},{4,0},{5,1},{6,2},{7,3},{8,12},{9,13},{10,... | collective-permute-start | bytes 1105928 | tf_op jit(solution)/shard_map/ppermute | solution.py:567
  201.6 25.2 %collective-permute-done.21 = bf16[240,768]{1,0:T(8,128)(2,1)S(1)} collective-permute-done((bf16[240,768]{1,0:T(8,128)(2,1)S(1)}, bf16[240,768]{1,0:T(8,128)(2,1)S(1)}, u32[]{:S(2)}, u32[]{:S(2)}) %collective-permute-start.21) | collective-permute-done | bytes 368672 | tf_op jit(solution)/shard_map/ppermute | solution.py:567
  227.0 1.6 collective-permute-start.22
  229.4 1.7 pad_maximum_fusion.1.refs_1_
  231.6 12.2 %collective-permute-done.24 = bf16[4,48,768]{2,1,0:T(8,128)(2,1)S(1)} collective-permute-done((bf16[4,48,768]{2,1,0:T(8,128)(2,1)S(1)}, bf16[4,48,768]{2,1,0:T(8,128)(2,1)S(1)}, u32[]{:S(2)}, u32[]{:S(2)}) %collective-permute-start.24) | collective-permute-done | bytes 294944 | tf_op jit(solution)/shard_map/ppermute | solution.py:567
  243.8 1.1 collective-permute-start.25
  245.4 8.4 %collective-permute-done.25 = bf16[8,48,768]{2,1,0:T(8,128)(2,1)S(1)} collective-permute-done((bf16[8,48,768]{2,1,0:T(8,128)(2,1)S(1)}, bf16[8,48,768]{2,1,0:T(8,128)(2,1)S(1)}, u32[]{:S(2)}, u32[]{:S(2)}) %collective-permute-start.25) | collective-permute-done | bytes 589856 | tf_op jit(solution)/shard_map/ppermute | solution.py:567
  254.0 3.2 %finish_mlp_1_0.1.refs_2_ = f32[768,3072]{1,0:T(8,128)} custom-call(s32[10]{0:T(128)S(1)} %copy-done, bf16[2,16,48,768]{3,2,1,0:T(8,128)(2,1)S(1)} %pad_maximum_fusion.refs_1_), custom_call_target="tpu_custom_call" | custom-call | bytes 70000000 | tf_op jit(solution)/shard_map/finish_mlp_1_0/pallas_call | solution.py:482
  257.1 4.9 %finish_mlp_0_0.1.refs_2_ = f32[3072,768]{1,0:T(8,128)} custom-call(s32[10]{0:T(128)S(1)} %copy-done, bf16[2,16,48,768]{3,2,1,0:T(8,128)(2,1)} %pad_maximum_fusion.1.refs_1_), custom_call_target="tpu_custom_call" | custom-call | bytes 70000000 | tf_op jit(solution)/shard_map/finish_mlp_0_0/pallas_call | solution.py:482
  262.1 2.9 %finish_attn_0.1 = (f32[768,2304]{1,0:T(8,128)}, f32[768,768]{1,0:T(8,128)}) custom-call(s32[10]{0:T(128)S(1)} %copy-done, bf16[16,48,768]{2,1,0:T(8,128)(2,1)S(1)} %pad_maximum_fusion.4.a_ref, bf16[16,48,768]{2,1,0:T(8,128)(2,1)S(1)} %pad_maximum_fusion.5.b_ref), custom_call_target="tpu_custom_call" | custom-call | bytes 70000000 | tf_op jit(solution)/shard_map/finish_attn_0/pallas_call | solution.py:522
  267.3 1.3 slice.496
  268.7 4.2 %finish_attn_1.1 = (f32[768,2304]{1,0:T(8,128)}, f32[768,768]{1,0:T(8,128)}) custom-call(s32[10]{0:T(128)S(1)} %copy-done, bf16[16,48,768]{2,1,0:T(8,128)(2,1)S(1)} %bitcast.108, bf16[16,48,768]{2,1,0:T(8,128)(2,1)} %collective-permute-done.26.b_ref, f32[768,2304]{1,0:T(8,128)} %get-tuple-element.91.rest_0_, ...), custom_call_target="tpu_custom_call", output_to_operand_aliasing={{0}: (3, {}), {1}: (4, {})} | custom-call | bytes 70000000 | tf_op jit(solution)/shard_map/finish_attn_1/pallas_call | solution.py:522
  272.9 1.6 slice_reduce_fusion
  274.5 4.9 %finish_mlp_1_1.1 = f32[768,3072]{1,0:T(8,128)} custom-call(s32[10]{0:T(128)S(1)} %copy-done, bf16[2,16,48,768]{3,2,1,0:T(8,128)(2,1)} %collective-permute-done.31.refs_1_, f32[768,3072]{1,0:T(8,128)} %finish_mlp_1_0.1.refs_2_), custom_call_target="tpu_custom_call", output_to_operand_aliasing={{}: (2, {})} | custom-call | bytes 70000000 | tf_op jit(solution)/shard_map/finish_mlp_1_1/pallas_call | solution.py:482
  279.4 4.9 %finish_mlp_0_1.1 = f32[3072,768]{1,0:T(8,128)} custom-call(s32[10]{0:T(128)S(1)} %copy-done, bf16[2,16,48,768]{3,2,1,0:T(8,128)(2,1)} %collective-permute-done.34.refs_1_, f32[3072,768]{1,0:T(8,128)} %finish_mlp_0_0.1.refs_2_), custom_call_target="tpu_custom_call", output_to_operand_aliasing={{}: (2, {})} | custom-call | bytes 70000000 | tf_op jit(solution)/shard_map/finish_mlp_0_1/pallas_call | solution.py:482
  (119 shorter events, 18.3 us)
Async XLA Ops:
  28.1 8.6 %collective-permute-start = (bf16[2,16,48,768]{3,2,1,0:T(8,128)(2,1)}, bf16[2,16,48,768]{3,2,1,0:T(8,128)(2,1)S(1)}, u32[]{:S(2)}, u32[]{:S(2)}) collective-permute-start(bf16[2,16,48,768]{3,2,1,0:T(8,128)(2,1)} %get-tuple-element.60), channel_id=1, source_target_pairs={{0,1},{1,0},{2,3},{3,2},{4,5},{5,4},{6,7},{7,6},{8,9},{9,8},{10,11... | collective-permute-start | bytes 7077896 | tf_op jit(solution)/shard_map/ppermute | solution.py:567
  38.8 16.6 %collective-permute-start.2 = (bf16[8,48,768]{2,1,0:T(8,128)(2,1)S(1)}, bf16[8,48,768]{2,1,0:T(8,128)(2,1)S(1)}, u32[]{:S(2)}, u32[]{:S(2)}) collective-permute-start(bf16[8,48,768]{2,1,0:T(8,128)(2,1)S(1)} %get-tuple-element.114), channel_id=1, source_target_pairs={{0,4},{1,5},{2,6},{3,7},{4,0},{5,1},{6,2},{7,3},{8,12},{9,13},{10,... | collective-permute-start | bytes 1769480 | tf_op jit(solution)/shard_map/ppermute | solution.py:567
  41.4 15.9 %collective-permute-start.1 = (bf16[8,48,768]{2,1,0:T(8,128)(2,1)S(1)}, bf16[8,48,768]{2,1,0:T(8,128)(2,1)S(1)}, u32[]{:S(2)}, u32[]{:S(2)}) collective-permute-start(bf16[8,48,768]{2,1,0:T(8,128)(2,1)S(1)} %get-tuple-element.115), channel_id=1, source_target_pairs={{0,2},{1,3},{2,0},{3,1},{4,6},{5,7},{6,4},{7,5},{8,10},{9,11},{10,... | collective-permute-start | bytes 1769480 | tf_op jit(solution)/shard_map/ppermute | solution.py:567
  51.0 16.6 %collective-permute-start.3 = (bf16[2,16,48,768]{3,2,1,0:T(8,128)(2,1)}, bf16[2,16,48,768]{3,2,1,0:T(8,128)(2,1)S(1)}, u32[]{:S(2)}, u32[]{:S(2)}) collective-permute-start(bf16[2,16,48,768]{3,2,1,0:T(8,128)(2,1)} %get-tuple-element.67), channel_id=1, source_target_pairs={{0,1},{1,0},{2,3},{3,2},{4,5},{5,4},{6,7},{7,6},{8,9},{9,8},{10,11... | collective-permute-start | bytes 7077896 | tf_op jit(solution)/shard_map/ppermute | solution.py:567
  55.5 11.9 %collective-permute-start.7 = (bf16[4,48,768]{2,1,0:T(8,128)(2,1)S(1)}, bf16[4,48,768]{2,1,0:T(8,128)(2,1)S(1)}, u32[]{:S(2)}, u32[]{:S(2)}) collective-permute-start(bf16[4,48,768]{2,1,0:T(8,128)(2,1)S(1)} %fusion.16), channel_id=1, source_target_pairs={{0,2},{1,3},{2,0},{3,1},{4,6},{5,7},{6,4},{7,5},{8,10},{9,11},{10,... | collective-permute-start | bytes 884744 | tf_op jit(solution)/shard_map/ppermute | solution.py:567
  57.4 10.1 %collective-permute-start.6 = (bf16[4,48,768]{2,1,0:T(8,128)(2,1)S(1)}, bf16[4,48,768]{2,1,0:T(8,128)(2,1)S(1)}, u32[]{:S(2)}, u32[]{:S(2)}) collective-permute-start(bf16[4,48,768]{2,1,0:T(8,128)(2,1)S(1)} %fusion.17), channel_id=1, source_target_pairs={{0,4},{1,5},{2,6},{3,7},{4,0},{5,1},{6,2},{7,3},{8,12},{9,13},{10,... | collective-permute-start | bytes 884744 | tf_op jit(solution)/shard_map/ppermute | solution.py:567
  67.4 1.7 copy-start.1
  69.7 19.7 %collective-permute-start.5 = (bf16[8,48,768]{2,1,0:T(8,128)(2,1)S(1)}, bf16[8,48,768]{2,1,0:T(8,128)(2,1)S(1)}, u32[]{:S(2)}, u32[]{:S(2)}) collective-permute-start(bf16[8,48,768]{2,1,0:T(8,128)(2,1)S(1)} %get-tuple-element.110), channel_id=1, source_target_pairs={{0,4},{1,5},{2,6},{3,7},{4,0},{5,1},{6,2},{7,3},{8,12},{9,13},{10,... | collective-permute-start | bytes 1769480 | tf_op jit(solution)/shard_map/ppermute | solution.py:567
  70.3 20.2 %collective-permute-start.4 = (bf16[8,48,768]{2,1,0:T(8,128)(2,1)S(1)}, bf16[8,48,768]{2,1,0:T(8,128)(2,1)S(1)}, u32[]{:S(2)}, u32[]{:S(2)}) collective-permute-start(bf16[8,48,768]{2,1,0:T(8,128)(2,1)S(1)} %get-tuple-element.111), channel_id=1, source_target_pairs={{0,2},{1,3},{2,0},{3,1},{4,6},{5,7},{6,4},{7,5},{8,10},{9,11},{10,... | collective-permute-start | bytes 1769480 | tf_op jit(solution)/shard_map/ppermute | solution.py:567
  89.4 16.0 %collective-permute-start.9 = (bf16[4,48,768]{2,1,0:T(8,128)(2,1)S(1)}, bf16[4,48,768]{2,1,0:T(8,128)(2,1)S(1)}, u32[]{:S(2)}, u32[]{:S(2)}) collective-permute-start(bf16[4,48,768]{2,1,0:T(8,128)(2,1)S(1)} %fusion.14), channel_id=1, source_target_pairs={{0,2},{1,3},{2,0},{3,1},{4,6},{5,7},{6,4},{7,5},{8,10},{9,11},{10,... | collective-permute-start | bytes 884744 | tf_op jit(solution)/shard_map/ppermute | solution.py:567
  90.5 15.1 %collective-permute-start.8 = (bf16[4,48,768]{2,1,0:T(8,128)(2,1)S(1)}, bf16[4,48,768]{2,1,0:T(8,128)(2,1)S(1)}, u32[]{:S(2)}, u32[]{:S(2)}) collective-permute-start(bf16[4,48,768]{2,1,0:T(8,128)(2,1)S(1)} %fusion.15), channel_id=1, source_target_pairs={{0,4},{1,5},{2,6},{3,7},{4,0},{5,1},{6,2},{7,3},{8,12},{9,13},{10,... | collective-permute-start | bytes 884744 | tf_op jit(solution)/shard_map/ppermute | solution.py:567
  105.9 13.3 %collective-permute-start.10 = (bf16[4,2,48,768]{3,2,1,0:T(8,128)(2,1)S(1)}, bf16[4,2,48,768]{3,2,1,0:T(8,128)(2,1)S(1)}, u32[]{:S(2)}, u32[]{:S(2)}) collective-permute-start(bf16[4,2,48,768]{3,2,1,0:T(8,128)(2,1)S(1)} %get-tuple-element.118), channel_id=1, source_target_pairs={{0,8},{8,0},{16,24},{24,16},{1,9},{9,1},{17,25},{25,17},{2,10},{10... | collective-permute-start | bytes 1769480 | tf_op jit(solution)/shard_map/ppermute | solution.py:567
  114.2 11.8 %collective-permute-start.11 = (bf16[2,16,48,768]{3,2,1,0:T(8,128)(2,1)}, bf16[2,16,48,768]{3,2,1,0:T(8,128)(2,1)S(1)}, u32[]{:S(2)}, u32[]{:S(2)}) collective-permute-start(bf16[2,16,48,768]{3,2,1,0:T(8,128)(2,1)} %attn_grad_0.1), channel_id=1, source_target_pairs={{0,1},{1,0},{2,3},{3,2},{4,5},{5,4},{6,7},{7,6},{8,9},{9,8},{10,11... | collective-permute-start | bytes 7077896 | tf_op jit(solution)/shard_map/ppermute | solution.py:567
  128.1 13.7 %collective-permute-start.15 = (bf16[8,48,768]{2,1,0:T(8,128)(2,1)S(1)}, bf16[8,48,768]{2,1,0:T(8,128)(2,1)S(1)}, u32[]{:S(2)}, u32[]{:S(2)}) collective-permute-start(bf16[8,48,768]{2,1,0:T(8,128)(2,1)S(1)} %get-tuple-element.106), channel_id=1, source_target_pairs={{0,4},{1,5},{2,6},{3,7},{4,0},{5,1},{6,2},{7,3},{8,12},{9,13},{10,... | collective-permute-start | bytes 1769480 | tf_op jit(solution)/shard_map/ppermute | solution.py:567
  128.7 13.0 %collective-permute-start.12 = (bf16[4,1,48,768]{3,2,1,0:T(8,128)(2,1)S(1)}, bf16[4,1,48,768]{3,2,1,0:T(8,128)(2,1)S(1)}, u32[]{:S(2)}, u32[]{:S(2)}) collective-permute-start(bf16[4,1,48,768]{3,2,1,0:T(8,128)(2,1)S(1)} %get-tuple-element.125), channel_id=1, source_target_pairs={{0,16},{8,24},{16,0},{24,8},{1,17},{9,25},{17,1},{25,9},{2,18},{10... | collective-permute-start | bytes 884744 | tf_op jit(solution)/shard_map/ppermute | solution.py:567
  131.3 11.8 %collective-permute-start.13 = (bf16[8,48,768]{2,1,0:T(8,128)(2,1)S(1)}, bf16[8,48,768]{2,1,0:T(8,128)(2,1)S(1)}, u32[]{:S(2)}, u32[]{:S(2)}) collective-permute-start(bf16[8,48,768]{2,1,0:T(8,128)(2,1)S(1)} %get-tuple-element.107), channel_id=1, source_target_pairs={{0,2},{1,3},{2,0},{3,1},{4,6},{5,7},{6,4},{7,5},{8,10},{9,11},{10,... | collective-permute-start | bytes 1769480 | tf_op jit(solution)/shard_map/ppermute | solution.py:567
  141.8 15.8 %collective-permute-start.27 = (bf16[4,1,48,768]{3,2,1,0:T(8,128)(2,1)S(1)}, bf16[4,1,48,768]{3,2,1,0:T(8,128)(2,1)S(1)}, u32[]{:S(2)}, u32[]{:S(2)}) collective-permute-start(bf16[4,1,48,768]{3,2,1,0:T(8,128)(2,1)S(1)} %add_convert_fusion.16), channel_id=1, source_target_pairs={{0,16},{8,24},{16,0},{24,8},{1,17},{9,25},{17,1},{25,9},{2,18},{10... | collective-permute-start | bytes 884744 | tf_op jit(solution)/shard_map/ppermute | solution.py:567
  141.9 11.9 %collective-permute-start.16 = (bf16[4,48,768]{2,1,0:T(8,128)(2,1)S(1)}, bf16[4,48,768]{2,1,0:T(8,128)(2,1)S(1)}, u32[]{:S(2)}, u32[]{:S(2)}) collective-permute-start(bf16[4,48,768]{2,1,0:T(8,128)(2,1)S(1)} %fusion.6), channel_id=1, source_target_pairs={{0,2},{1,3},{2,0},{3,1},{4,6},{5,7},{6,4},{7,5},{8,10},{9,11},{10,... | collective-permute-start | bytes 884744 | tf_op jit(solution)/shard_map/ppermute | solution.py:567
  143.2 10.7 %collective-permute-start.14 = (bf16[4,48,768]{2,1,0:T(8,128)(2,1)S(1)}, bf16[4,48,768]{2,1,0:T(8,128)(2,1)S(1)}, u32[]{:S(2)}, u32[]{:S(2)}) collective-permute-start(bf16[4,48,768]{2,1,0:T(8,128)(2,1)S(1)} %fusion.8), channel_id=1, source_target_pairs={{0,4},{1,5},{2,6},{3,7},{4,0},{5,1},{6,2},{7,3},{8,12},{9,13},{10,... | collective-permute-start | bytes 884744 | tf_op jit(solution)/shard_map/ppermute | solution.py:567
  154.0 3.6 %copy-start.5 = (f32[8,768]{1,0:T(8,128)S(1)}, f32[8,768]{1,0:T(8,128)}, u32[]{:S(2)}) copy-start(f32[8,768]{1,0:T(8,128)} %get-tuple-element.90) | copy-start | bytes 73732
  154.1 13.0 %collective-permute-start.17 = (bf16[2,2,48,768]{3,2,1,0:T(8,128)(2,1)S(1)}, bf16[2,2,48,768]{3,2,1,0:T(8,128)(2,1)S(1)}, u32[]{:S(2)}, u32[]{:S(2)}) collective-permute-start(bf16[2,2,48,768]{3,2,1,0:T(8,128)(2,1)S(1)} %pad_maximum_fusion.15), channel_id=1, source_target_pairs={{0,8},{8,0},{16,24},{24,16},{1,9},{9,1},{17,25},{25,17},{2,10},{10... | collective-permute-start | bytes 884744 | tf_op jit(solution)/shard_map/ppermute | solution.py:567
  157.7 21.3 %collective-permute-start.28 = (bf16[4,2,48,768]{3,2,1,0:T(8,128)(2,1)S(1)}, bf16[4,2,48,768]{3,2,1,0:T(8,128)(2,1)S(1)}, u32[]{:S(2)}, u32[]{:S(2)}) collective-permute-start(bf16[4,2,48,768]{3,2,1,0:T(8,128)(2,1)S(1)} %pad_maximum_fusion.12), channel_id=1, source_target_pairs={{0,8},{8,0},{16,24},{24,16},{1,9},{9,1},{17,25},{25,17},{2,10},{10... | collective-permute-start | bytes 1769480 | tf_op jit(solution)/shard_map/ppermute | solution.py:567
  158.3 9.0 %copy-start.4 = (f32[8,768]{1,0:T(8,128)S(1)}, f32[8,768]{1,0:T(8,128)}, u32[]{:S(2)}) copy-start(f32[8,768]{1,0:T(8,128)} %get-tuple-element.89) | copy-start | bytes 73732
  167.2 11.9 %collective-permute-start.18 = (bf16[2,1,48,768]{3,2,1,0:T(8,128)(2,1)S(1)}, bf16[2,1,48,768]{3,2,1,0:T(8,128)(2,1)S(1)}, u32[]{:S(2)}, u32[]{:S(2)}) collective-permute-start(bf16[2,1,48,768]{3,2,1,0:T(8,128)(2,1)S(1)} %slice.478), channel_id=1, source_target_pairs={{0,16},{8,24},{16,0},{24,8},{1,17},{9,25},{17,1},{25,9},{2,18},{10... | collective-permute-start | bytes 442376 | tf_op jit(solution)/shard_map/ppermute | solution.py:567
  179.2 9.8 %collective-permute-start.19 = (bf16[144,768]{1,0:T(8,128)(2,1)S(1)}, bf16[144,768]{1,0:T(8,128)(2,1)S(1)}, u32[]{:S(2)}, u32[]{:S(2)}) collective-permute-start(bf16[144,768]{1,0:T(8,128)(2,1)S(1)} %pad_maximum_fusion.17), channel_id=1, source_target_pairs={{0,16},{8,24},{16,0},{24,8},{1,17},{9,25},{17,1},{25,9},{2,18},{10... | collective-permute-start | bytes 663560 | tf_op jit(solution)/shard_map/ppermute | solution.py:567
  181.7 12.0 %collective-permute-start.32 = (bf16[2,4,48,768]{3,2,1,0:T(8,128)(2,1)S(1)}, bf16[2,4,48,768]{3,2,1,0:T(8,128)(2,1)S(1)}, u32[]{:S(2)}, u32[]{:S(2)}) collective-permute-start(bf16[2,4,48,768]{3,2,1,0:T(8,128)(2,1)S(1)} %get-tuple-element.116), channel_id=1, source_target_pairs={{0,4},{1,5},{2,6},{3,7},{4,0},{5,1},{6,2},{7,3},{8,12},{9,13},{10,... | collective-permute-start | bytes 1769480 | tf_op jit(solution)/shard_map/ppermute | solution.py:567
  182.7 13.7 %collective-permute-start.29 = (bf16[2,4,48,768]{3,2,1,0:T(8,128)(2,1)S(1)}, bf16[2,4,48,768]{3,2,1,0:T(8,128)(2,1)S(1)}, u32[]{:S(2)}, u32[]{:S(2)}) collective-permute-start(bf16[2,4,48,768]{3,2,1,0:T(8,128)(2,1)S(1)} %get-tuple-element.117), channel_id=1, source_target_pairs={{0,2},{1,3},{2,0},{3,1},{4,6},{5,7},{6,4},{7,5},{8,10},{9,11},{10,... | collective-permute-start | bytes 1769480 | tf_op jit(solution)/shard_map/ppermute | solution.py:567
  189.1 9.0 %collective-permute-start.20 = (bf16[240,768]{1,0:T(8,128)(2,1)S(1)}, bf16[240,768]{1,0:T(8,128)(2,1)S(1)}, u32[]{:S(2)}, u32[]{:S(2)}) collective-permute-start(bf16[240,768]{1,0:T(8,128)(2,1)S(1)} %pad_maximum_fusion.14), channel_id=1, source_target_pairs={{0,8},{8,0},{16,24},{24,16},{1,9},{9,1},{17,25},{25,17},{2,10},{10... | collective-permute-start | bytes 1105928 | tf_op jit(solution)/shard_map/ppermute | solution.py:567
  193.8 35.5 %collective-permute-start.33 = (bf16[2,8,48,768]{3,2,1,0:T(8,128)(2,1)S(1)}, bf16[2,8,48,768]{3,2,1,0:T(8,128)(2,1)S(1)}, u32[]{:S(2)}, u32[]{:S(2)}) collective-permute-start(bf16[2,8,48,768]{3,2,1,0:T(8,128)(2,1)S(1)} %pad_maximum_fusion.7), channel_id=1, source_target_pairs={{0,2},{1,3},{2,0},{3,1},{4,6},{5,7},{6,4},{7,5},{8,10},{9,11},{10,... | collective-permute-start | bytes 3538952 | tf_op jit(solution)/shard_map/ppermute | solution.py:567
  196.5 32.6 %collective-permute-start.30 = (bf16[2,8,48,768]{3,2,1,0:T(8,128)(2,1)S(1)}, bf16[2,8,48,768]{3,2,1,0:T(8,128)(2,1)S(1)}, u32[]{:S(2)}, u32[]{:S(2)}) collective-permute-start(bf16[2,8,48,768]{3,2,1,0:T(8,128)(2,1)S(1)} %pad_maximum_fusion.6), channel_id=1, source_target_pairs={{0,4},{1,5},{2,6},{3,7},{4,0},{5,1},{6,2},{7,3},{8,12},{9,13},{10,... | collective-permute-start | bytes 3538952 | tf_op jit(solution)/shard_map/ppermute | solution.py:567
  198.4 28.4 %collective-permute-start.21 = (bf16[240,768]{1,0:T(8,128)(2,1)S(1)}, bf16[240,768]{1,0:T(8,128)(2,1)S(1)}, u32[]{:S(2)}, u32[]{:S(2)}) collective-permute-start(bf16[240,768]{1,0:T(8,128)(2,1)S(1)} %pad_maximum_fusion.13), channel_id=1, source_target_pairs={{0,4},{1,5},{2,6},{3,7},{4,0},{5,1},{6,2},{7,3},{8,12},{9,13},{10,... | collective-permute-start | bytes 1105928 | tf_op jit(solution)/shard_map/ppermute | solution.py:567
  227.0 18.0 %collective-permute-start.22 = (bf16[432,768]{1,0:T(8,128)(2,1)S(1)}, bf16[432,768]{1,0:T(8,128)(2,1)S(1)}, u32[]{:S(2)}, u32[]{:S(2)}) collective-permute-start(bf16[432,768]{1,0:T(8,128)(2,1)S(1)} %pad_maximum_fusion.8), channel_id=1, source_target_pairs={{0,2},{1,3},{2,0},{3,1},{4,6},{5,7},{6,4},{7,5},{8,10},{9,11},{10,... | collective-permute-start | bytes 1990664 | tf_op jit(solution)/shard_map/ppermute | solution.py:567
  228.5 15.2 %collective-permute-start.24 = (bf16[4,48,768]{2,1,0:T(8,128)(2,1)S(1)}, bf16[4,48,768]{2,1,0:T(8,128)(2,1)S(1)}, u32[]{:S(2)}, u32[]{:S(2)}) collective-permute-start(bf16[4,48,768]{2,1,0:T(8,128)(2,1)S(1)} %get-tuple-element.122), channel_id=1, source_target_pairs={{0,2},{1,3},{2,0},{3,1},{4,6},{5,7},{6,4},{7,5},{8,10},{9,11},{10,... | collective-permute-start | bytes 884744 | tf_op jit(solution)/shard_map/ppermute | solution.py:567
  229.3 45.2 %collective-permute-start.31 = (bf16[2,16,48,768]{3,2,1,0:T(8,128)(2,1)S(1)}, bf16[2,16,48,768]{3,2,1,0:T(8,128)(2,1)}, u32[]{:S(2)}, u32[]{:S(2)}) collective-permute-start(bf16[2,16,48,768]{3,2,1,0:T(8,128)(2,1)S(1)} %pad_maximum_fusion.refs_1_), channel_id=1, source_target_pairs={{0,1},{1,0},{2,3},{3,2},{4,5},{5,4},{6,7},{7,6},{8,9},{9,8},{10,11... | collective-permute-start | bytes 7077896 | tf_op jit(solution)/shard_map/ppermute | solution.py:567
  231.1 48.4 %collective-permute-start.34 = (bf16[2,16,48,768]{3,2,1,0:T(8,128)(2,1)}, bf16[2,16,48,768]{3,2,1,0:T(8,128)(2,1)}, u32[]{:S(2)}, u32[]{:S(2)}) collective-permute-start(bf16[2,16,48,768]{3,2,1,0:T(8,128)(2,1)} %pad_maximum_fusion.1.refs_1_), channel_id=1, source_target_pairs={{0,1},{1,0},{2,3},{3,2},{4,5},{5,4},{6,7},{7,6},{8,9},{9,8},{10,11... | collective-permute-start | bytes 7077896 | tf_op jit(solution)/shard_map/ppermute | solution.py:567
  243.8 9.9 %collective-permute-start.25 = (bf16[8,48,768]{2,1,0:T(8,128)(2,1)S(1)}, bf16[8,48,768]{2,1,0:T(8,128)(2,1)S(1)}, u32[]{:S(2)}, u32[]{:S(2)}) collective-permute-start(bf16[8,48,768]{2,1,0:T(8,128)(2,1)S(1)} %pad_maximum_fusion.11), channel_id=1, source_target_pairs={{0,4},{1,5},{2,6},{3,7},{4,0},{5,1},{6,2},{7,3},{8,12},{9,13},{10,... | collective-permute-start | bytes 1769480 | tf_op jit(solution)/shard_map/ppermute | solution.py:567
  245.3 8.7 %copy-start = (s32[10]{0:T(128)S(1)}, s32[10]{0:T(128)}, u32[]{:S(2)}) copy-start(s32[10]{0:T(128)} %stack.55.refs_0_.refs_1_.ids_ref) | copy-start | bytes 124
  245.3 19.7 %collective-permute-start.23 = (bf16[816,768]{1,0:T(8,128)(2,1)S(1)}, bf16[816,768]{1,0:T(8,128)(2,1)S(1)}, u32[]{:S(2)}, u32[]{:S(2)}) collective-permute-start(bf16[816,768]{1,0:T(8,128)(2,1)S(1)} %pad_maximum_fusion.2), channel_id=1, source_target_pairs={{0,1},{1,0},{2,3},{3,2},{4,5},{5,4},{6,7},{7,6},{8,9},{9,8},{10,11... | collective-permute-start | bytes 3760136 | tf_op jit(solution)/shard_map/ppermute | solution.py:567
  253.9 14.8 %collective-permute-start.26 = (bf16[16,48,768]{2,1,0:T(8,128)(2,1)S(1)}, bf16[16,48,768]{2,1,0:T(8,128)(2,1)}, u32[]{:S(2)}, u32[]{:S(2)}) collective-permute-start(bf16[16,48,768]{2,1,0:T(8,128)(2,1)S(1)} %pad_maximum_fusion.5.b_ref), channel_id=1, source_target_pairs={{0,1},{1,0},{2,3},{3,2},{4,5},{5,4},{6,7},{7,6},{8,9},{9,8},{10,11... | collective-permute-start | bytes 3538952 | tf_op jit(solution)/shard_map/ppermute | solution.py:567
  265.0 1.1 copy-start.2
  266.1 0.6 copy-start.3
where the time goes:
time: 290 us; the launch traced here: 285 us
  Pallas kernels  128 us (44%)
  waiting for transfers between devices  96 us (33%)
  starting transfers between devices  39.9 us (14%)
  other arithmetic  11 us (4%)
  local copies, waits for them, and re-layouts  8.52 us (3%)
    ppermute x35, waiting for transfers between devices, swap(): lax.ppermute(value, axis, [(i, i ^ 1 << bit) for i in range(self.sizes[ax...  96 us
    ppermute x35, starting transfers between devices, swap(): lax.ppermute(value, axis, [(i, i ^ 1 << bit) for i in range(self.sizes[ax...  39.9 us
    pallas_call x4, Pallas kernels, quarter_call(): pl.pallas_call(lambda *refs: quarter_body(2, *refs), grid_spec=pltpu.Pref...  32.6 us
    pallas_call x1, Pallas kernels, middle_call(): pl.pallas_call(lambda *refs: middle_body(slots, *refs), grid_spec=pltpu.P...  18 us
    pallas_call x4, Pallas kernels, finish_mlp_call(): pl.pallas_call(lambda *refs: finish_mlp_body(groups, ab, *refs), grid_spe...  17.9 us
    pallas_call x1, Pallas kernels, first_call(): pl.pallas_call(lambda *refs: first_body(slots, *refs), grid_spec=pltpu.Pr...  16.6 us
    pallas_call x1, Pallas kernels, attn_back_call(): pl.pallas_call(attn_back_body, grid=(total // slots,), in_specs=[row(3 *...  13.3 us
    pallas_call x2, Pallas kernels, attn_grad_call(): pl.pallas_call(attn_grad_body, grid_spec=pltpu.PrefetchScalarGridSpec(num...  13 us
  transfers between devices with their start and end apart: 35, of which 13 were waited for; matrix products, arithmetic and copies ran while one was open for 3% of the time, Pallas kernels for 34%

commit v1 on v0

v1 whole, which is shorter than its diff:
```python
import math

import jax
import jax.numpy as jnp
from jax import lax
from jax.experimental import pallas as pl
from jax.experimental.pallas import tpu as pltpu
from jax.sharding import PartitionSpec as P

D = 768
HEADS = 12
HEAD_DIM = 64
FF = 3072
PAIRS = HEADS // 2
LANES = 2 * HEAD_DIM
EPS = 1e-06
NEG = -1e30
BF = jnp.bfloat16
F32 = jnp.float32
FACTOR = HEAD_DIM ** (-0.5)
BLOCKS = 16
BROWS = D // BLOCKS
SCALE = 10


def dot(a, b):
    return jnp.dot(a, b, preferred_element_type=F32)


def dot_t(a, b):
    return lax.dot_general(a, b, (((1,), (1,)), ((), ())), preferred_element_type=F32)


def t_dot(a, b):
    return lax.dot_general(a, b, (((0,), (0,)), ((), ())), preferred_element_type=F32)


def stats(x):
    centred = x - jnp.mean(x, axis=-1, keepdims=True)
    rstd = lax.rsqrt(jnp.mean(centred * centred, axis=-1, keepdims=True) + EPS)
    return centred * rstd, rstd


def pin(value):
    return pltpu.with_memory_space_constraint(value, pltpu.HBM)


def vmem(limit):
    return pltpu.CompilerParams(vmem_limit_bytes=limit * 1024 * 1024)


def params(rows=640):
    return vmem(20 if rows <= 640 else 48)


def cost(us):
    return pl.CostEstimate(flops=int(us * SCALE * 1e9), bytes_accessed=1000, transcendentals=0)


def full(shape):
    return pl.BlockSpec(shape, lambda *_: (0,) * len(shape))


def head_masks(rows):
    lane = lax.broadcasted_iota(jnp.int32, (rows, LANES), 1)
    return lane < HEAD_DIM


def stack_heads(pair, low):
    zero = jnp.zeros_like(pair)
    return jnp.concatenate([jnp.where(low, pair, zero), jnp.where(low, zero, pair)], axis=0)


def first_body(
    slots,
    counts_ref,
    tok_hbm,
    cot_hbm,
    wj_hbm,
    wm_hbm,
    g1_ref,
    s1_ref,
    jb_ref,
    mb_ref,
    g2_ref,
    s2_ref,
    normed_ref,
    joined_ref,
    probs_ref,
    mix_ref,
    middle_ref,
    second_ref,
    gout_ref,
    tok_ref,
    cot_ref,
    wj_ref,
    wm_ref,
    sem,
):
    step = pl.program_id(0)
    rows = tok_ref.shape[0]
    items = rows // slots
    span = pl.ds(pl.multiple_of(step * rows, 16), rows)
    tok_copy = pltpu.make_async_copy(tok_hbm.at[span], tok_ref, sem.at[0])
    cot_copy = pltpu.make_async_copy(cot_hbm.at[span], cot_ref, sem.at[1])
    wm_copy = pltpu.make_async_copy(wm_hbm, wm_ref, sem.at[2])
    wj_copies = [
        pltpu.make_async_copy(
            wj_hbm.at[:, pl.ds(third * D, D)], wj_ref.at[third], sem.at[3 + third]
        )
        for third in range(3)
    ]
    tok_copy.start()

    @pl.when(step == 0)
    def _():
        for copy in wj_copies:
            copy.start()

    cot_copy.start()

    @pl.when(step == 0)
    def _():
        wm_copy.start()

    tok_copy.wait()
    x = tok_ref[...].astype(F32)
    xhat, _ = stats(x)
    normed = (xhat * g1_ref[...] + s1_ref[...]).astype(BF)
    normed_ref[...] = normed
    for third in range(3):
        cols = slice(third * D, (third + 1) * D)

        @pl.when(step == 0)
        def _():
            wj_copies[third].wait()

        part = dot(normed, wj_ref[third])
        if third == 0:
            part = part + jb_ref[0:1, :]
        if third == 2:
            part = part + jb_ref[1:2, :]
        joined_ref[:, cols] = part.astype(BF)
    cot_copy.wait()
    low = head_masks(slots)
    key_slot = lax.broadcasted_iota(jnp.int32, (2 * slots, slots), 1)
    row_slot = lax.broadcasted_iota(jnp.int32, (slots, D), 0)

    def one(item, carry):
        count = counts_ref[step * items + item]
        here = pl.ds(pl.multiple_of(item * slots, 16), slots)
        seen = row_slot < count
        cot = cot_ref[here, :]
        gout_ref[here, :] = jnp.where(seen, cot, jnp.zeros_like(cot))
        allowed = key_slot < count
        for pair in range(PAIRS):
            cols = slice(pair * LANES, (pair + 1) * LANES)
            q = stack_heads(joined_ref[here, cols] * BF(FACTOR), low)
            k = joined_ref[here, D + pair * LANES : D + (pair + 1) * LANES]
            v = joined_ref[here, 2 * D + pair * LANES : 2 * D + (pair + 1) * LANES]
            scores = jnp.where(allowed, dot_t(q, k), NEG)
            raised = jnp.exp(scores - jnp.max(scores, axis=-1, keepdims=True))
            soft = (raised * (1.0 / jnp.sum(raised, axis=-1, keepdims=True))).astype(BF)
            probs_ref[item, pair] = soft
            mixed = dot(soft, v)
            mix_ref[here, cols] = jnp.where(low, mixed[:slots], mixed[slots:]).astype(BF)
        return carry

    lax.fori_loop(0, items, one, 0)

    @pl.when(step == 0)
    def _():
        wm_copy.wait()

    middle = tok_ref[...].astype(F32) + dot(mix_ref[...], wm_ref[...]) + mb_ref[...]
    middle_ref[...] = middle
    xhat, _ = stats(middle)
    second_ref[...] = (xhat * g2_ref[...] + s2_ref[...]).astype(BF)


def first_call(group, slots, counts, tok, cot, wj, wm, g1, s1, jb, mb, g2, s2):
    total = tok.shape[0]
    rows = group * slots
    steps = total // rows
    row = lambda width: pl.BlockSpec((rows, width), lambda i, c: (i, 0))
    out = lambda width, dt: jax.ShapeDtypeStruct((total, width), dt)
    hbm = pl.BlockSpec(memory_space=pltpu.HBM)
    return pl.pallas_call(
        lambda *refs: first_body(slots, *refs),
        grid_spec=pltpu.PrefetchScalarGridSpec(
            num_scalar_prefetch=1,
            grid=(steps,),
            in_specs=[hbm] * 4 + [full(a.shape) for a in (g1, s1, jb, mb, g2, s2)],
            out_specs=[
                row(D),
                row(3 * D),
                pl.BlockSpec((group, PAIRS, 2 * slots, slots), lambda i, c: (i, 0, 0, 0)),
                row(D),
                row(D),
                row(D),
                row(D),
            ],
            scratch_shapes=[
                pltpu.VMEM((rows, D), BF),
                pltpu.VMEM((rows, D), BF),
                pltpu.VMEM((3, D, D), BF),
                pltpu.VMEM((D, D), BF),
                pltpu.SemaphoreType.DMA((6,)),
            ],
        ),
        out_shape=[
            out(D, BF),
            out(3 * D, BF),
            jax.ShapeDtypeStruct((total // slots, PAIRS, 2 * slots, slots), BF),
            out(D, BF),
            out(D, F32),
            out(D, BF),
            out(D, BF),
        ],
        compiler_params=vmem(32 if steps == 1 else 48),
        cost_estimate=cost(15),
        name="attn_fwd",
    )(*[pin(a) for a in (counts, tok, cot, wj, wm, g1, s1, jb, mb, g2, s2)])


def put_blocks(ref, which, mask, value):
    for k in range(BLOCKS):
        ref[which, k ^ mask] = value[k * BROWS : (k + 1) * BROWS, :].astype(BF)


def quarter_body(parts, ids_ref, sec_ref, gout_ref, up_ref, ub_ref, down_ref, *outs):
    grad_ref, act_ref, gh_ref = outs
    rows = sec_ref.shape[0] // parts
    for part in range(parts):
        here = slice(part * rows, (part + 1) * rows)
        hidden = dot(sec_ref[here, :], up_ref[...]) + ub_ref[...]
        grad_act = dot_t(gout_ref[here, :], down_ref[...])
        cdf = 0.5 + 0.5 * lax.erf(hidden * (0.5**0.5))
        act_ref[here, :] = (hidden * cdf).astype(BF)
        slope = cdf + hidden * (jnp.exp(-0.5 * hidden * hidden) * ((2 * math.pi) ** -0.5))
        gh_ref[here, :] = (grad_act * slope).astype(BF)
    put_blocks(grad_ref, 0, ids_ref[0], t_dot(act_ref[...], gout_ref[...]))
    put_blocks(grad_ref, 1, ids_ref[1], t_dot(sec_ref[...], gh_ref[...]))


def quarter_call(call, ids, second, gout, up, ub, down):
    total = second.shape[0]
    whole = full((total, D))
    return pl.pallas_call(
        lambda *refs: quarter_body(2, *refs),
        grid_spec=pltpu.PrefetchScalarGridSpec(
            num_scalar_prefetch=1,
            grid=(1,),
            in_specs=[
                whole,
                whole,
                pl.BlockSpec((D, D), lambda i, ids: (0, ids[4 + call])),
                pl.BlockSpec((1, D), lambda i, ids: (0, ids[4 + call])),
                pl.BlockSpec((D, D), lambda i, ids: (ids[4 + call], 0)),
            ],
            out_specs=[full((2, BLOCKS, BROWS, D)), whole, whole],
        ),
        out_shape=[
            jax.ShapeDtypeStruct((2, BLOCKS, BROWS, D), BF),
            jax.ShapeDtypeStruct((total, D), BF),
            jax.ShapeDtypeStruct((total, D), BF),
        ],
        compiler_params=params(total),
        cost_estimate=cost(4.3),
        name=f"mlp_{call}",
    )(ids, second, gout, up, ub, down)


def collect_body(chunk, ids_ref, *refs):
    acts, ghs = refs[:2], refs[2:4]
    down_ref, up_ref = refs[4:6]
    kept = refs[6:-3]
    outer_ref, g_ref, small_ref = refs[-3:]
    step = pl.program_id(0)
    for at in range(2):

        @pl.when(step == at)
        def _():
            outer = dot(acts[at][...], down_ref[...])
            g = dot_t(ghs[at][...], up_ref[...])
            if at:
                outer = outer + outer_ref[...]
                g = g + g_ref[...]
            elif chunk:
                outer = outer + kept[0][...]
                g = g + kept[1][...]
                small_ref[...] = kept[2][...]
            outer_ref[...] = outer
            g_ref[...] = g
            small_ref[pl.ds(ids_ref[4 + 2 * chunk + at], 1), :] = jnp.sum(
                ghs[at][...].astype(F32), axis=0, keepdims=True
            )


def collect_call(chunk, ids, acts, ghs, down, up, kept):
    total = acts[0].shape[0]
    whole = full((total, D))
    specs = [whole, whole, full((4, D))]
    return pl.pallas_call(
        lambda *refs: collect_body(chunk, *refs),
        grid_spec=pltpu.PrefetchScalarGridSpec(
            num_scalar_prefetch=1,
            grid=(2,),
            in_specs=[whole] * 4
            + [
                pl.BlockSpec((D, D), lambda i, ids: (ids[4 + 2 * chunk + i], 0)),
                pl.BlockSpec((D, D), lambda i, ids: (0, ids[4 + 2 * chunk + i])),
            ]
            + specs * (1 if chunk else 0),
            out_specs=specs,
        ),
        out_shape=[
            jax.ShapeDtypeStruct((total, D), F32),
            jax.ShapeDtypeStruct((total, D), F32),
            jax.ShapeDtypeStruct((4, D), F32),
        ],
        compiler_params=vmem(24 if total <= 640 else 56),
        cost_estimate=cost(4.3),
        name=f"mlp_collect_{chunk}",
    )(ids, *acts, *ghs, down, up, *(kept or ()))


def middle_body(
    slots,
    counts_ref,
    outer_ref,
    g_ref,
    mid_ref,
    gout_ref,
    db_ref,
    g2_ref,
    wm_ref,
    result_ref,
    gmid_ref,
    branch_ref,
    gmix_ref,
    small_ref,
):
    items = mid_ref.shape[0] // slots
    row_slot = lax.broadcasted_iota(jnp.int32, (slots, D), 0)

    def one(item, sums):
        here = pl.ds(pl.multiple_of(item * slots, 16), slots)
        seen = row_slot < counts_ref[item]
        middle = mid_ref[here, :]
        total = middle + outer_ref[here, :] + db_ref[...]
        result_ref[here, :] = jnp.where(seen, total, 0.0).astype(BF)
        gout = gout_ref[here, :].astype(F32)
        xhat, rstd = stats(middle)
        g = g_ref[here, :]
        e = g * g2_ref[...]
        mean_e = jnp.mean(e, axis=-1, keepdims=True)
        mean_x = jnp.mean(e * xhat, axis=-1, keepdims=True)
        grad = gout + rstd * (e - mean_e - xhat * mean_x)
        gmid_ref[here, :] = grad
        branch = grad.astype(BF)
        branch_ref[here, :] = branch
        row = lambda a: jnp.sum(a, axis=0, keepdims=True)
        return (
            sums[0] + row(gout),
            sums[1] + row(g * xhat),
            sums[2] + row(g),
            sums[3] + row(branch.astype(F32)),
        )

    zero = jnp.zeros((1, D), F32)
    sums = lax.fori_loop(0, items, one, (zero,) * 4)
    for k in range(4):
        small_ref[k : k + 1, :] = sums[k]
    gmix_ref[...] = dot_t(branch_ref[...], wm_ref[...]).astype(BF)


def middle_call(slots, counts, outer, g, mid, gout, db, g2, wm):
    total = mid.shape[0]
    whole = full((total, D))
    return pl.pallas_call(
        lambda *refs: middle_body(slots, *refs),
        grid_spec=pltpu.PrefetchScalarGridSpec(
            num_scalar_prefetch=1,
            grid=(1,),
            in_specs=[whole, whole, whole, whole, full(db.shape), full(g2.shape), full((D, D))],
            out_specs=[whole, whole, whole, whole, full((4, D))],
        ),
        out_shape=[
            jax.ShapeDtypeStruct((total, D), BF),
            jax.ShapeDtypeStruct((total, D), F32),
            jax.ShapeDtypeStruct((total, D), BF),
            jax.ShapeDtypeStruct((total, D), BF),
            jax.ShapeDtypeStruct((4, D), F32),
        ],
        compiler_params=params(total),
        cost_estimate=cost(3.6),
        name="mlp_back",
    )(counts, outer, g, mid, gout, db, g2, wm)


def attn_back_body(joined_ref, probs_ref, gmix_ref, grad_ref):
    slots = joined_ref.shape[0]
    low = head_masks(slots)
    for pair in range(PAIRS):
        cols = slice(pair * LANES, (pair + 1) * LANES)
        q = stack_heads(joined_ref[:, cols], low)
        k = joined_ref[:, D + pair * LANES : D + (pair + 1) * LANES]
        v = joined_ref[:, 2 * D + pair * LANES : 2 * D + (pair + 1) * LANES]
        out = stack_heads(gmix_ref[:, cols], low)
        low_soft = probs_ref[0, pair]
        soft = low_soft.astype(F32)
        grad_probs = dot_t(out, v)
        mean = jnp.sum(soft * grad_probs, axis=-1, keepdims=True)
        scores = (soft * (grad_probs - mean)).astype(BF)
        gq = dot(scores, k) * FACTOR
        grad_ref[:, cols] = jnp.where(low, gq[:slots], gq[slots:]).astype(BF)
        grad_ref[:, D + pair * LANES : D + (pair + 1) * LANES] = (
            t_dot(scores, q) * FACTOR
        ).astype(BF)
        grad_ref[:, 2 * D + pair * LANES : 2 * D + (pair + 1) * LANES] = t_dot(
            low_soft, out
        ).astype(BF)


def attn_back_call(call, slots, joined, probs, gmix, kept):
    total = joined.shape[0]
    steps = total // slots // 2
    row = lambda width: pl.BlockSpec((slots, width), lambda i: (call * steps + i, 0))
    in_specs = [
        row(3 * D),
        pl.BlockSpec((1, PAIRS, 2 * slots, slots), lambda i: (call * steps + i, 0, 0, 0)),
        row(D),
    ]
    args = [joined, probs, gmix]
    aliases = {}
    if kept is not None:
        in_specs.append(pl.BlockSpec(memory_space=pl.ANY))
        args.append(kept)
        aliases = {3: 0}
    return pl.pallas_call(
        lambda *refs: attn_back_body(*refs[:3], refs[-1]),
        grid=(steps,),
        in_specs=in_specs,
        out_specs=row(3 * D),
        out_shape=jax.ShapeDtypeStruct((total, 3 * D), BF),
        input_output_aliases=aliases,
        compiler_params=params(),
        cost_estimate=cost(5.5),
        name=f"attn_bwd_{call}",
    )(*args)


def attn_grad_body(ids_ref, normed_ref, mix_ref, grad_ref, branch_ref, out_ref):
    half = BLOCKS // 2

    def put(which, base, mask, value):
        for k in range(half):
            out_ref[which, (base + k) ^ mask] = value[k * BROWS : (k + 1) * BROWS, :].astype(BF)

    normed = normed_ref[...]
    put(0, 0, ids_ref[0], t_dot(normed, grad_ref[:, :D]))
    put(0, half, ids_ref[0], t_dot(normed, grad_ref[:, D : 2 * D]))
    put(1, 0, ids_ref[1], t_dot(normed, grad_ref[:, 2 * D :]))
    put(1, half, ids_ref[1], t_dot(mix_ref[...], branch_ref[...]))


def attn_grad_call(call, ids, normed, mix, grad, branch):
    total = normed.shape[0]
    half = pl.BlockSpec((total, D // 2), lambda i, ids: (0, ids[8 + call]))
    return pl.pallas_call(
        attn_grad_body,
        grid_spec=pltpu.PrefetchScalarGridSpec(
            num_scalar_prefetch=1,
            grid=(1,),
            in_specs=[half, half, full((total, 3 * D)), full((total, D))],
            out_specs=full((2, BLOCKS, BROWS, D)),
        ),
        out_shape=jax.ShapeDtypeStruct((2, BLOCKS, BROWS, D), BF),
        compiler_params=params(total),
        cost_estimate=cost(2.6),
        name=f"attn_grad_{call}",
    )(ids, normed, mix, grad, branch)


def last_body(slots, grad_ref, wj_ref, tok_ref, gmid_ref, g1_ref, out_ref, small_ref, g_ref):
    rows = tok_ref.shape[0]
    items = rows // slots
    g_ref[...] = dot_t(grad_ref[...], wj_ref[...])

    def one(item, sums):
        here = pl.ds(pl.multiple_of(item * slots, 16), slots)
        xhat, rstd = stats(tok_ref[here, :].astype(F32))
        g = g_ref[here, :]
        e = g * g1_ref[...]
        mean_e = jnp.mean(e, axis=-1, keepdims=True)
        mean_x = jnp.mean(e * xhat, axis=-1, keepdims=True)
        out_ref[here, :] = (gmid_ref[here, :] + rstd * (e - mean_e - xhat * mean_x)).astype(BF)
        row = lambda a: jnp.sum(a, axis=0, keepdims=True)
        return (
            sums[0] + row(grad_ref[here, :D].astype(F32)),
            sums[1] + row(grad_ref[here, 2 * D :].astype(F32)),
            sums[2] + row(g * xhat),
            sums[3] + row(g),
        )

    zero = jnp.zeros((1, D), F32)
    sums = lax.fori_loop(0, items, one, (zero,) * 4)
    for k in range(4):
        small_ref[k : k + 1, :] = sums[k]
    small_ref[4:8, :] = jnp.zeros((4, D), F32)


def last_call(slots, grad, wj, tok, gmid, g1):
    total = tok.shape[0]
    return pl.pallas_call(
        lambda *refs: last_body(slots, *refs),
        grid=(1,),
        in_specs=[full(a.shape) for a in (grad, wj, tok, gmid, g1)],
        out_specs=[full((total, D)), full((8, D))],
        out_shape=[
            jax.ShapeDtypeStruct((total, D), BF),
            jax.ShapeDtypeStruct((8, D), F32),
        ],
        scratch_shapes=[pltpu.VMEM((total, D), F32)],
        compiler_params=params(total),
        cost_estimate=cost(5.6),
        name="first_back",
    )(grad, wj, tok, gmid, g1)


def finish_mlp_body(groups, ids_ref, a_ref, b_ref, *rest):
    for ab, in_ref in enumerate((a_ref, b_ref)):
        mask = ids_ref[ab] & (groups - 1)
        for k in range(groups):
            rest[ab - 2][k * BROWS : (k + 1) * BROWS, :] = in_ref[k ^ mask].astype(F32)


def finish_mlp_call(chunk, which, ids, a, b, kept):
    groups = 4
    steps = BLOCKS // groups

    def place(ab):
        def index(i, ids):
            at = (ids[ab] // groups) ^ i
            quarter = 2 * chunk + (ids[3] ^ which)
            return (quarter * steps + at, 0) if ab == 0 else (at, quarter)

        return index

    in_specs = [pl.BlockSpec((groups, BROWS, D), lambda i, ids: (i, 0, 0))] * 2
    args = [ids, a, b]
    aliases = {}
    if kept is not None:
        in_specs += [pl.BlockSpec(memory_space=pl.ANY)] * 2
        args += list(kept)
        aliases = {3: 0, 4: 1}
    return pl.pallas_call(
        lambda *refs: finish_mlp_body(groups, *refs),
        grid_spec=pltpu.PrefetchScalarGridSpec(
            num_scalar_prefetch=1,
            grid=(steps,),
            in_specs=in_specs,
            out_specs=[pl.BlockSpec((groups * BROWS, D), place(ab)) for ab in range(2)],
        ),
        out_shape=[jax.ShapeDtypeStruct(shape, F32) for shape in ((FF, D), (D, FF))],
        input_output_aliases=aliases,
        compiler_params=params(),
        cost_estimate=cost(3.2),
        name=f"finish_mlp_{chunk}_{which}",
    )(*args)


def finish_attn_body(ids_ref, a_ref, b_ref, *rest):
    joined_ref, merge_ref = rest[-2:]
    half = BLOCKS // 2
    for ab, in_ref in enumerate((a_ref, b_ref)):
        mask = ids_ref[ab]
        for i in range(BLOCKS):
            block = in_ref[i ^ mask].astype(F32)
            third, k = 2 * ab + i // half, i % half
            rows = slice(k * BROWS, (k + 1) * BROWS)
            if third < 3:
                joined_ref[rows, third * D : (third + 1) * D] = block
            else:
                merge_ref[rows, :] = block


def finish_attn_call(which, ids, a, b, kept):
    in_specs = [full(a.shape), full(b.shape)]
    args = [ids, a, b]
    aliases = {}
    if kept is not None:
        in_specs += [pl.BlockSpec(memory_space=pl.ANY)] * 2
        args += list(kept)
        aliases = {3: 0, 4: 1}
    place = lambda i, ids: (ids[3] ^ which, 0)
    return pl.pallas_call(
        finish_attn_body,
        grid_spec=pltpu.PrefetchScalarGridSpec(
            num_scalar_prefetch=1,
            grid=(1,),
            in_specs=in_specs,
            out_specs=[pl.BlockSpec((D // 2, 3 * D), place), pl.BlockSpec((D // 2, D), place)],
        ),
        out_shape=[jax.ShapeDtypeStruct(s, F32) for s in ((D, 3 * D), (D, D))],
        input_output_aliases=aliases,
        compiler_params=params(),
        cost_estimate=cost(4.2),
        name=f"finish_attn_{which}",
    )(*args)


def finish_small_body(mine_ref, got_ref, *outs):
    mine = mine_ref[...].astype(F32)
    got = got_ref[0].astype(F32)
    total = mine[0:12, :] + mine[12:24, :] + (got[0:12, :] + got[12:24, :])
    for k in range(4):
        outs[0][pl.ds(k * D, D)] = total[k]
    for out, k in zip(outs[1:7], (4, 5, 6, 7, 10, 11)):
        out[...] = total[k]
    outs[7][...] = total[8:10, :]


def finish_small_call(mine, got):
    vector = lambda n: jax.ShapeDtypeStruct((n,), F32)
    shapes = [vector(FF)] + [vector(D)] * 6 + [jax.ShapeDtypeStruct((2, D), F32)]
    return pl.pallas_call(
        finish_small_body,
        grid=(1,),
        in_specs=[
            full(mine.shape),
            pl.BlockSpec((1, BROWS, D), lambda i: (got.shape[0] - 1, 0, 0)),
        ],
        out_specs=[full(s.shape) for s in shapes],
        out_shape=shapes,
        compiler_params=params(),
        cost_estimate=cost(1),
        name="finish_small",
    )(mine, got)


def stage_lists(sizes):
    bits = {axis: [(axis, b) for b in range(size.bit_length() - 1)] for axis, size in sizes.items()}
    dp, group = bits["dp"], bits["group"]
    if len(dp) == 2 and len(group) == 3:
        order = group + dp
    else:
        order = [dp[0], group[0], group[-1]] + dp[1:] + group[1:-1]
    return order[0], order[1:3], order[3:]


def add(a, b):
    return (a.astype(F32) + b.astype(F32)).astype(BF)


def bit_of(stage):
    return (lax.axis_index(stage[0]) >> stage[1]) & 1


def tie(*values):
    return lax.optimization_barrier(values)


class Chain:
    def __init__(self):
        self.last = None

    def after(self, value):
        if self.last is None:
            return value
        value, _ = tie(value, self.last)
        return value

    def run(self, step, value):
        out = step(self.after(value))
        self.last = jax.tree.leaves(out)[0]
        return out


class Chunk:
    def __init__(self, sums, chain):
        self.sums = sums
        self.chain = chain
        self.down_at = 0
        self.small = None

    def first(self, send):
        self.got = self.sums.swap(send, self.sums.first)

    def pair(self, at, keep=None):
        if keep is not None:
            self.keep = keep
        got = self.chain.after(self.got)
        both = [self.sums.halve(self.keep[ab], got[ab]) for ab in range(2)]
        self.keep = [b[0] for b in both]
        out = [b[1] for b in both]
        self.chain.last = out
        self.got = [self.sums.swap(out[ab], self.sums.stage(ab, at)) for ab in range(2)]

    def tail_down(self, small=None):
        at = self.down_at
        got = self.chain.after(self.got)
        if at == 0:
            mine = jnp.stack([add(self.keep[ab], got[ab]) for ab in range(2)])
        else:
            mine = add(self.keep, got)
        self.down_at += 1
        if at < len(self.sums.rest):
            self.keep, out = self.sums.tail_down(at, mine)
            self.chain.last = out
            self.got = self.sums.swap(out, self.sums.rest[at])
            if len(self.sums.rest) > 2 and at >= 1 and at + 1 < len(self.sums.rest):
                self.tail_down(small)
            return
        self.mine = mine
        self.chain.last = mine
        self.up_at = at
        self.small = small
        self.up(self.mine, self.sums.rest[at - 1])

    def up(self, value, stage):
        if self.small is None:
            self.got = self.sums.swap(value, stage)
            return
        self.rows = split_small(self.small)
        pad = jnp.zeros((BROWS - self.rows.shape[0], D), BF)
        block = jnp.concatenate([self.rows, pad], axis=0)[None]
        load = value.reshape((-1,) + value.shape[-2:])
        if value.shape[-2] != BROWS:
            load = load.reshape(-1, D)
            load = jnp.concatenate([load, jnp.zeros((-load.shape[0] % BROWS, D), BF)])
            load = load.reshape(-1, BROWS, D)
        self.all = self.sums.swap(jnp.concatenate([load, block], axis=0), stage)
        self.got = self.all[:-1].reshape(-1, D)[: value.size // D].reshape(value.shape)

    def small_sum(self):
        other = self.all[-1, : self.rows.shape[0]]
        self.small = join_small(self.rows) + join_small(other)

    def tail_up(self):
        at = self.up_at - 1
        got = self.chain.after(self.got)
        self.mine = self.sums.tail_up(at, self.mine, got)
        self.chain.last = self.mine
        self.up_at = at
        if self.small is not None:
            self.small_sum()
        if at:
            self.up(self.mine, self.sums.rest[at - 1])
            if at > 1:
                self.tail_up()
            return
        self.own = [self.mine[0], self.mine[1]]
        self.ups([self.sums.stage(ab, 1) for ab in range(2)])

    def ups(self, stages):
        if self.small is None:
            self.got = [self.sums.swap(self.own[ab], stages[ab]) for ab in range(2)]
            return
        self.up(self.own[0], stages[0])
        self.got = [self.got, self.sums.swap(self.own[1], stages[1])]

    def pair_up(self, at):
        got = self.chain.after(self.got)
        self.own = [jnp.concatenate([self.own[ab], got[ab]]) for ab in range(2)]
        self.chain.last = self.own
        if self.small is not None:
            self.small_sum()
        if at:
            self.ups([self.sums.stage(ab, at - 1) for ab in range(2)])
        else:
            self.ups([self.sums.first] * 2)


class Sums:
    def __init__(self, sizes):
        self.sizes = sizes
        self.first, self.pair, self.rest = stage_lists(sizes)

    def swap(self, value, stage):
        axis, bit = stage
        return lax.ppermute(value, axis, [(i, i ^ (1 << bit)) for i in range(self.sizes[axis])])

    def stage(self, ab, at):
        return self.pair[at if ab == 0 else 1 - at]

    def halve(self, mine, got, axis=0):
        n = mine.shape[axis] // 2
        low = lax.slice_in_dim(mine, 0, n, axis=axis), lax.slice_in_dim(got, 0, n, axis=axis)
        high = lax.slice_in_dim(mine, n, 2 * n, axis=axis), lax.slice_in_dim(
            got, n, 2 * n, axis=axis
        )
        return add(*low), add(*high)

    def tail_down(self, at, mine):
        if at < 2:
            n = mine.shape[1] // 2
            return mine[:, :n], mine[:, n:]
        n = mine.shape[2] // 2
        high = bit_of(self.rest[at]) == 1
        low_rows, high_rows = mine[:, :, :n], mine[:, :, n:]
        return jnp.where(high, high_rows, low_rows), jnp.where(high, low_rows, high_rows)

    def tail_up(self, at, mine, got):
        if at < 2:
            return jnp.concatenate([mine, got], axis=1)
        high = bit_of(self.rest[at]) == 1
        return jnp.concatenate([jnp.where(high, got, mine), jnp.where(high, mine, got)], axis=2)


def split_small(value):
    high = lax.reduce_precision(value, 8, 7)
    return jnp.concatenate([high.astype(BF), (value - high).astype(BF)], axis=0)


def join_small(value):
    n = value.shape[0] // 2
    return value[:n].astype(F32) + value[n:].astype(F32)


def solution(mesh):
    sizes = dict(mesh.shape)
    sums = Sums(sizes)

    def shards(
        tokens,
        cotangent,
        counts,
        first_gain,
        first_shift,
        joined_weight,
        joined_bias,
        merge_weight,
        merge_bias,
        second_gain,
        second_shift,
        up_weight,
        up_bias,
        down_weight,
        down_bias,
    ):
        items, slots, features = tokens.shape
        total = items * slots
        row = lambda a: a.reshape(1, -1)
        tok = tokens.reshape(total, features)
        cot = cotangent.reshape(total, features)
        counts = counts.astype(jnp.int32)
        masks = []
        for two in (sums.pair, sums.pair[::-1]):
            mask = 0
            for stage in list(two) + list(sums.rest[:2]):
                mask = 2 * mask + bit_of(stage)
            masks.append(mask)
        core = bit_of(sums.first)
        other = 1 - core
        ids = jnp.stack(
            [masks[0], masks[1], core, core, other, core, 2 + other, 2 + core, other, core]
        ).astype(jnp.int32)

        normed, joined, probs, mix, middle, second, gout = first_call(
            4,
            slots,
            counts,
            tok,
            cot,
            joined_weight,
            merge_weight,
            first_gain,
            first_shift,
            joined_bias,
            merge_bias,
            second_gain,
            second_shift,
        )
        chain = Chain()

        acts, ghs = [], []

        def quarter(call):
            def step(ids):
                return quarter_call(
                    call, ids, second, gout, up_weight, row(up_bias), down_weight
                )

            grad, act, gh = chain.run(step, ids)
            acts.append(act)
            ghs.append(gh)
            return grad

        def collect(chunk, kept):
            pick = slice(2 * chunk, 2 * chunk + 2)
            return chain.run(
                lambda ids: collect_call(
                    chunk, ids, acts[pick], ghs[pick], down_weight, up_weight, kept
                ),
                ids,
            )

        def finish(chunk, which, kept):
            part = chunks[chunk].got if which else chunks[chunk].own
            return chain.run(
                lambda a: finish_mlp_call(chunk, which, ids, a, part[1], kept), part[0]
            )

        chunks = [Chunk(sums, chain) for _ in range(3)]
        one, two, three = chunks
        one.first(quarter(0))
        keep = quarter(1)
        kept = collect(0, None)
        one.pair(0, keep)
        send = quarter(2)
        keep = quarter(3)
        two.first(chain.after(send))
        outer, g, small_a = collect(1, kept)
        two.pair(0, keep)
        one.pair(1)
        result, gmid, branch, gmix, small_b = chain.run(
            lambda outer: middle_call(
                slots, counts, outer, g, middle, gout, down_bias, second_gain, merge_weight
            ),
            outer,
        )
        grad_joined = chain.run(
            lambda gmix: attn_back_call(0, slots, joined, probs, gmix, None), gmix
        )
        grad_joined = chain.run(
            lambda gmix: attn_back_call(1, slots, joined, probs, gmix, grad_joined), gmix
        )
        one.tail_down()
        attn_grad = lambda call: chain.run(
            lambda ids: attn_grad_call(call, ids, normed, mix, grad_joined, branch), ids
        )
        send = attn_grad(0)
        two.pair(1)
        keep = attn_grad(1)
        three.first(chain.after(send))
        one.tail_down()
        three.pair(0, keep)
        two.tail_down()
        one.tail_down()
        two.tail_down()
        one.tail_up()
        three.pair(1)
        two.tail_down()
        one.tail_up()
        three.tail_down()
        one.pair_up(1)
        two.tail_up()
        three.tail_down()
        token_grad, small_c = chain.run(
            lambda grad: last_call(slots, grad, joined_weight, tok, gmid, first_gain),
            grad_joined,
        )
        small = jnp.concatenate([small_a, small_b, small_c[:4]], axis=0)
        three.tail_down(small)
        two.tail_up()
        three.tail_up()
        two.pair_up(1)
        three.tail_up()
        one.pair_up(0)
        mlp = finish(0, 0, None)
        three.pair_up(1)
        two.pair_up(0)
        mlp = finish(0, 1, mlp)
        mlp = finish(1, 0, mlp)
        mlp = finish(1, 1, mlp)
        three.pair_up(0)
        attn = chain.run(
            lambda a: finish_attn_call(0, ids, a, three.own[1], None), three.own[0]
        )
        small = finish_small_call(three.rows, three.all)
        joined_grad, merge_grad = finish_attn_call(1, ids, three.all, three.got[1], attn)
        down_grad, up_grad = mlp
        return (
            result.reshape(tokens.shape),
            token_grad.reshape(tokens.shape),
            small[5],
            small[6],
            joined_grad,
            small[7],
            merge_grad,
            small[4],
            small[2],
            small[3],
            up_grad,
            small[0],
            down_grad,
            small[1],
        )

    spread = P(("dp", "group"), None, None)
    return jax.shard_map(
        shards,
        mesh=mesh,
        in_specs=(spread, spread, P(("dp", "group"))) + (P(),) * 12,
        out_specs=(spread, spread) + (P(),) * 12,
        check_vma=False,
    )
```

time: 290 us -> 220 us (0.76)
  the two profiles are of different devices: /device:TPU:0 before, /device:TPU:25 now
where the time goes in v1:
time: 220 us; the launch traced here: 217 us
  Pallas kernels  86 us (39%)
  waiting for transfers between devices  75.1 us (34%)
  starting transfers between devices  40.3 us (18%)
  other arithmetic  13.2 us (6%)
    ppermute x45, waiting for transfers between devices, swap(): lax.ppermute(value, axis, [(i, i ^ 1 << bit) for i in range(self.sizes[ax...  75.1 us
    ppermute x45, starting transfers between devices, swap(): lax.ppermute(value, axis, [(i, i ^ 1 << bit) for i in range(self.sizes[ax...  40.3 us
    pallas_call x4, Pallas kernels, quarter_call(): pl.pallas_call(lambda *refs: quarter_body(2, *refs), grid_spec=pltpu.Pref...  16.9 us
    pallas_call x1, Pallas kernels, first_call(): pl.pallas_call(lambda *refs: first_body(slots, *refs), grid_spec=pltpu.Pr...  15.7 us
    pallas_call x4, Pallas kernels, finish_mlp_call(): pl.pallas_call(lambda *refs: finish_mlp_body(groups, *refs), grid_spec=pl...  12.4 us
    pallas_call x2, Pallas kernels, attn_back_call(): pl.pallas_call(lambda *refs: attn_back_body(*refs[:3], refs[-1]), grid=(s...  11 us
    pallas_call x2, Pallas kernels, collect_call(): pl.pallas_call(lambda *refs: collect_body(chunk, *refs), grid_spec=pltpu....  9.22 us
    convert_element_type x15, other arithmetic, add(): return (a.astype(F32) + b.astype(F32)).astype(BF)  7.33 us
  transfers between devices with their start and end apart: 45, of which 16 were waited for; matrix products, arithmetic and copies ran while one was open for 4% of the time, Pallas kernels for 28%

profile of v1, /device:TPU:25, one launch (start us, length us, event | category | flops | bytes accessed | tf_op | source)
XLA Modules:
  0.0 216.9 jit_solution(14457984798746863220)
XLA Ops:
  0.8 15.7 %attn_fwd.1 = (bf16[640,768]{1,0:T(8,128)(2,1)S(1)}, bf16[640,2304]{1,0:T(8,128)(2,1)S(1)}, bf16[4,6,320,160]{3,2,1,0:T(8,128)(2,1)S(1)}, bf16[640,768]{1,0:T(8,...) custom-call(s32[4]{0:T(128)} %refs_0_.3, ...), custom_call_target="tpu_custom_call" | custom-call | flops 149999992832 | bytes 1000 | tf_op jit(solution)/shard_map/attn_fwd/pallas_call | solution.py:188
  16.5 4.2 %mlp_0.1 = (bf16[2,16,48,768]{3,2,1,0:T(8,128)(2,1)S(1)}, bf16[640,768]{1,0:T(8,128)(2,1)S(1)}, bf16[640,768]{1,0:T(8,128)(2,1)S(1)}) custom-call(s32[10]{0:T(128)S(1)} %stack.58.refs_0_.ids_ref, bf16[640,768]{1,0:T(8,128)(2,1)S(1)} %get-tuple-element.123.refs_1_, bf16[640,768]{1,0:T(8,128)(2,1)S(1)} %get-tuple-element.124.refs_2_.refs_4_, ...), custom_call_target="tpu_custom_call" | custom-call | flops 43000000512 | bytes 1000 | tf_op jit(solution)/shard_map/mlp_0/pallas_call | solution.py:249
  21.5 4.2 %mlp_1.1 = (bf16[2,16,48,768]{3,2,1,0:T(8,128)(2,1)S(1)}, bf16[640,768]{1,0:T(8,128)(2,1)S(1)}, bf16[640,768]{1,0:T(8,128)(2,1)S(1)}) custom-call(s32[10]{0:T(128)S(1)} %stack.58.refs_0_.ids_ref, bf16[640,768]{1,0:T(8,128)(2,1)S(1)} %get-tuple-element.123.refs_1_, bf16[640,768]{1,0:T(8,128)(2,1)S(1)} %get-tuple-element.124.refs_2_.refs_4_, ...), custom_call_target="tpu_custom_call" | custom-call | flops 43000000512 | bytes 1000 | tf_op jit(solution)/shard_map/mlp_1/pallas_call | solution.py:249
  25.8 4.8 %mlp_collect_0.1 = (f32[640,768]{1,0:T(8,128)S(1)}, f32[640,768]{1,0:T(8,128)S(1)}, f32[4,768]{1,0:T(4,128)S(1)}) custom-call(s32[10]{0:T(128)S(1)} %stack.58.refs_0_.ids_ref, bf16[640,768]{1,0:T(8,128)(2,1)S(1)} %get-tuple-element.129.refs_1_, bf16[640,768]{1,0:T(8,128)(2,1)S(1)} %get-tuple-element.130.refs_2_, ...), custom_call_target="tpu_custom_call" | custom-call | flops 43000000512 | bytes 1000 | tf_op jit(solution)/shard_map/mlp_collect_0/pallas_call | solution.py:304
  31.3 1.3 collective-permute-start.2
  33.8 4.2 %mlp_2.1 = (bf16[2,16,48,768]{3,2,1,0:T(8,128)(2,1)S(1)}, bf16[640,768]{1,0:T(8,128)(2,1)S(1)}, bf16[640,768]{1,0:T(8,128)(2,1)S(1)}) custom-call(s32[10]{0:T(128)S(1)} %stack.58.refs_0_.ids_ref, bf16[640,768]{1,0:T(8,128)(2,1)S(1)} %get-tuple-element.123.refs_1_, bf16[640,768]{1,0:T(8,128)(2,1)S(1)} %get-tuple-element.124.refs_2_.refs_4_, ...), custom_call_target="tpu_custom_call" | custom-call | flops 43000000512 | bytes 1000 | tf_op jit(solution)/shard_map/mlp_2/pallas_call | solution.py:249
  38.0 4.2 %mlp_3.1 = (bf16[2,16,48,768]{3,2,1,0:T(8,128)(2,1)S(1)}, bf16[640,768]{1,0:T(8,128)(2,1)S(1)}, bf16[640,768]{1,0:T(8,128)(2,1)S(1)}) custom-call(s32[10]{0:T(128)S(1)} %stack.58.refs_0_.ids_ref, bf16[640,768]{1,0:T(8,128)(2,1)S(1)} %get-tuple-element.123.refs_1_, bf16[640,768]{1,0:T(8,128)(2,1)S(1)} %get-tuple-element.124.refs_2_.refs_4_, ...), custom_call_target="tpu_custom_call" | custom-call | flops 43000000512 | bytes 1000 | tf_op jit(solution)/shard_map/mlp_3/pallas_call | solution.py:249
  42.9 4.4 %mlp_collect_1.1 = (f32[640,768]{1,0:T(8,128)S(1)}, f32[640,768]{1,0:T(8,128)S(1)}, f32[4,768]{1,0:T(4,128)S(1)}) custom-call(s32[10]{0:T(128)S(1)} %stack.58.refs_0_.ids_ref, bf16[640,768]{1,0:T(8,128)(2,1)S(1)} %get-tuple-element.140.refs_1_, bf16[640,768]{1,0:T(8,128)(2,1)S(1)} %get-tuple-element.141.refs_2_, ...), custom_call_target="tpu_custom_call" | custom-call | flops 43000000512 | bytes 1000 | tf_op jit(solution)/shard_map/mlp_collect_1/pallas_call | solution.py:304
  47.4 1.8 add_convert_fusion.4
  51.3 1.2 collective-permute-start.5
  52.6 1.2 collective-permute-start.4
  53.9 3.5 %mlp_back.1 = (bf16[640,768]{1,0:T(8,128)(2,1)}, f32[640,768]{1,0:T(8,128)S(1)}, bf16[640,768]{1,0:T(8,128)(2,1)S(1)}, bf16[640,768]{1,0:T(8,128)(2,1)S(1)}, f32[4,768]{1,0:T(4,128)S(1)}) custom-call(s32[4]{0:T(128)S(1)} %copy-done.9, f32[640,768]{1,0:T(8,128)S(1)} %get-tuple-element.151.refs_1_, f32[640,768]{1,0:T(8,128)S(1)} %get-tuple-element.152.refs_2_, ...), custom_call_target="tpu_custom_call" | custom-call | flops 35999997952 | bytes 1000 | tf_op jit(solution)/shard_map/mlp_back/pallas_call | solution.py:381
  57.4 5.4 %attn_bwd_0.1.refs_3_ = bf16[640,2304]{1,0:T(8,128)(2,1)S(1)} custom-call(bf16[640,2304]{1,0:T(8,128)(2,1)S(1)} %copy-done.13, bf16[4,6,320,160]{3,2,1,0:T(8,128)(2,1)S(1)} %copy-done.11, bf16[640,768]{1,0:T(8,128)(2,1)S(1)} %get-tuple-element.159.refs_2_), custom_call_target="tpu_custom_call" | custom-call | flops 54999998464 | bytes 1000 | tf_op jit(solution)/shard_map/attn_bwd_0/pallas_call | solution.py:441
  62.8 5.6 %attn_bwd_1.1.grad_ref.refs_0_ = bf16[640,2304]{1,0:T(8,128)(2,1)S(1)} custom-call(bf16[640,2304]{1,0:T(8,128)(2,1)S(1)} %copy-done.13, bf16[4,6,320,160]{3,2,1,0:T(8,128)(2,1)S(1)} %copy-done.11, bf16[640,768]{1,0:T(8,128)(2,1)S(1)} %get-tuple-element.159.refs_2_, bf16[640,2304]{1,0:T(8,128)(2,1)S(1)} %attn_bwd_0.1.refs_3_), custom_call_target="tpu_custom_call", output_to_operand_aliasing={{}: (3, {})} | custom-call | flops 54999998464 | bytes 1000 | tf_op jit(solution)/shard_map/attn_bwd_1/pallas_call | solution.py:441
  68.5 1.3 fusion.18
  69.8 2.6 %attn_grad_0.1 = bf16[2,16,48,768]{3,2,1,0:T(8,128)(2,1)S(1)} custom-call(s32[10]{0:T(128)S(1)} %stack.58.refs_0_.ids_ref, bf16[640,768]{1,0:T(8,128)(2,1)S(1)} %get-tuple-element.163.normed_ref, bf16[640,768]{1,0:T(8,128)(2,1)S(1)} %get-tuple-element.164.mix_ref, bf16[640,2304]{1,0:T(8,128)(2,1)S(1)} %attn_bwd_1.1.grad_ref.refs_0_, ...), custom_call_target="tpu_custom_call" | custom-call | flops 25999998976 | bytes 1000 | tf_op jit(solution)/shard_map/attn_grad_0/pallas_call | solution.py:471
  74.6 2.6 %attn_grad_1.1 = bf16[2,16,48,768]{3,2,1,0:T(8,128)(2,1)S(1)} custom-call(s32[10]{0:T(128)S(1)} %stack.58.refs_0_.ids_ref, bf16[640,768]{1,0:T(8,128)(2,1)S(1)} %get-tuple-element.163.normed_ref, bf16[640,768]{1,0:T(8,128)(2,1)S(1)} %get-tuple-element.164.mix_ref, bf16[640,2304]{1,0:T(8,128)(2,1)S(1)} %attn_bwd_1.1.grad_ref.refs_0_, ...), custom_call_target="tpu_custom_call" | custom-call | flops 25999998976 | bytes 1000 | tf_op jit(solution)/shard_map/attn_grad_1/pallas_call | solution.py:471
  77.2 1.2 collective-permute-start.8
  79.9 7.1 %collective-permute-done.9 = bf16[2,2,48,768]{3,2,1,0:T(8,128)(2,1)S(1)} collective-permute-done((bf16[2,2,48,768]{3,2,1,0:T(8,128)(2,1)S(1)}, bf16[2,2,48,768]{3,2,1,0:T(8,128)(2,1)S(1)}, u32[]{:S(2)}, u32[]{:S(2)}) %collective-permute-start.9) | collective-permute-done | bytes 294944 | tf_op jit(solution)/shard_map/ppermute | solution.py:783
  92.0 5.0 %collective-permute-done.12 = bf16[2,1,48,768]{3,2,1,0:T(8,128)(2,1)S(1)} collective-permute-done((bf16[2,1,48,768]{3,2,1,0:T(8,128)(2,1)S(1)}, bf16[2,1,48,768]{3,2,1,0:T(8,128)(2,1)S(1)}, u32[]{:S(2)}, u32[]{:S(2)}) %collective-permute-start.12) | collective-permute-done | bytes 147488 | tf_op jit(solution)/shard_map/ppermute | solution.py:783
  97.1 4.5 %collective-permute-done.16 = bf16[2,2,48,768]{3,2,1,0:T(8,128)(2,1)S(1)} collective-permute-done((bf16[2,2,48,768]{3,2,1,0:T(8,128)(2,1)S(1)}, bf16[2,2,48,768]{3,2,1,0:T(8,128)(2,1)S(1)}, u32[]{:S(2)}, u32[]{:S(2)}) %collective-permute-start.16) | collective-permute-done | bytes 294944 | tf_op jit(solution)/shard_map/ppermute | solution.py:783
  101.7 1.9 collective-permute-start.20
  103.6 2.4 %collective-permute-done.15 = bf16[2,1,48,768]{3,2,1,0:T(8,128)(2,1)S(1)} collective-permute-done((bf16[2,1,48,768]{3,2,1,0:T(8,128)(2,1)S(1)}, bf16[2,1,48,768]{3,2,1,0:T(8,128)(2,1)S(1)}, u32[]{:S(2)}, u32[]{:S(2)}) %collective-permute-start.15) | collective-permute-done | bytes 147488 | tf_op jit(solution)/shard_map/ppermute | solution.py:783
  106.2 2.0 collective-permute-start.18
  108.6 3.7 %collective-permute-done.20 = bf16[2,1,48,768]{3,2,1,0:T(8,128)(2,1)S(1)} collective-permute-done((bf16[2,1,48,768]{3,2,1,0:T(8,128)(2,1)S(1)}, bf16[2,1,48,768]{3,2,1,0:T(8,128)(2,1)S(1)}, u32[]{:S(2)}, u32[]{:S(2)}) %collective-permute-start.20) | collective-permute-done | bytes 147488 | tf_op jit(solution)/shard_map/ppermute | solution.py:783
  112.4 3.5 %collective-permute-done.19 = bf16[2,2,48,768]{3,2,1,0:T(8,128)(2,1)S(1)} collective-permute-done((bf16[2,2,48,768]{3,2,1,0:T(8,128)(2,1)S(1)}, bf16[2,2,48,768]{3,2,1,0:T(8,128)(2,1)S(1)}, u32[]{:S(2)}, u32[]{:S(2)}) %collective-permute-start.19) | collective-permute-done | bytes 294944 | tf_op jit(solution)/shard_map/ppermute | solution.py:783
  116.1 1.6 collective-permute-start.24
  118.3 3.9 %collective-permute-done.24 = bf16[4,48,768]{2,1,0:T(8,128)(2,1)S(1)} collective-permute-done((bf16[4,48,768]{2,1,0:T(8,128)(2,1)S(1)}, bf16[4,48,768]{2,1,0:T(8,128)(2,1)S(1)}, u32[]{:S(2)}, u32[]{:S(2)}) %collective-permute-start.24) | collective-permute-done | bytes 294944 | tf_op jit(solution)/shard_map/ppermute | solution.py:783
  122.2 1.4 collective-permute-done.23
  123.8 2.0 collective-permute-done.21
  127.0 5.4 %first_back.1 = (bf16[640,768]{1,0:T(8,128)(2,1)}, f32[8,768]{1,0:T(8,128)S(1)}) custom-call(bf16[640,2304]{1,0:T(8,128)(2,1)S(1)} %attn_bwd_1.1.grad_ref.refs_0_, bf16[768,2304]{1,0:T(8,128)(2,1)S(1)} %copy-done.2, bf16[640,768]{1,0:T(8,128)(2,1)S(1)} %bitcast.151, f32[640,768]{1,0:T(8,128)S(1)} %get-tuple-element.188.refs_3_, f32[768]{0:T(1024)S(1)} %copy-done.8), custom_call_target="tpu_custom_call" | custom-call | flops 56000000000 | bytes 1000 | tf_op jit(solution)/shard_map/first_back/pallas_call | solution.py:516
  132.6 2.1 collective-permute-start.26
  135.7 1.6 collective-permute-start.29
  137.2 8.5 %collective-permute-done.26 = bf16[3,48,768]{2,1,0:T(8,128)(2,1)S(1)} collective-permute-done((bf16[3,48,768]{2,1,0:T(8,128)(2,1)S(1)}, bf16[3,48,768]{2,1,0:T(8,128)(2,1)S(1)}, u32[]{:S(2)}, u32[]{:S(2)}) %collective-permute-start.26) | collective-permute-done | bytes 221216 | tf_op jit(solution)/shard_map/ppermute | solution.py:783
  146.2 1.3 collective-permute-start.33
  148.0 1.3 collective-permute-start.37
  149.3 5.8 %collective-permute-done.28 = bf16[5,48,768]{2,1,0:T(8,128)(2,1)S(1)} collective-permute-done((bf16[5,48,768]{2,1,0:T(8,128)(2,1)S(1)}, bf16[5,48,768]{2,1,0:T(8,128)(2,1)S(1)}, u32[]{:S(2)}, u32[]{:S(2)}) %collective-permute-start.28) | collective-permute-done | bytes 368672 | tf_op jit(solution)/shard_map/ppermute | solution.py:783
  155.7 4.6 %collective-permute-done.34 = bf16[8,48,768]{2,1,0:T(8,128)(2,1)S(1)} collective-permute-done((bf16[8,48,768]{2,1,0:T(8,128)(2,1)S(1)}, bf16[8,48,768]{2,1,0:T(8,128)(2,1)S(1)}, u32[]{:S(2)}, u32[]{:S(2)}) %collective-permute-start.34) | collective-permute-done | bytes 589856 | tf_op jit(solution)/shard_map/ppermute | solution.py:783
  160.6 3.1 %finish_mlp_0_0.1 = (f32[3072,768]{1,0:T(8,128)}, f32[768,3072]{1,0:T(8,128)}) custom-call(s32[10]{0:T(128)S(1)} %stack.58.refs_0_.ids_ref, bf16[16,48,768]{2,1,0:T(8,128)(2,1)S(1)} %pad_maximum_fusion.1.refs_1_, bf16[16,48,768]{2,1,0:T(8,128)(2,1)S(1)} %pad_maximum_fusion.2.refs_2_), custom_call_target="tpu_custom_call" | custom-call | flops 32000000000 | bytes 1000 | tf_op jit(solution)/shard_map/finish_mlp_0_0/pallas_call | solution.py:558
  163.7 17.1 %collective-permute-done.31 = bf16[5,48,768]{2,1,0:T(8,128)(2,1)S(1)} collective-permute-done((bf16[5,48,768]{2,1,0:T(8,128)(2,1)S(1)}, bf16[5,48,768]{2,1,0:T(8,128)(2,1)S(1)}, u32[]{:S(2)}, u32[]{:S(2)}) %collective-permute-start.31) | collective-permute-done | bytes 368672 | tf_op jit(solution)/shard_map/ppermute | solution.py:783
  181.2 5.2 %collective-permute-start.40 = (bf16[16,48,768]{2,1,0:T(8,128)(2,1)S(1)}, bf16[16,48,768]{2,1,0:T(8,128)(2,1)S(1)}, u32[]{:S(2)}, u32[]{:S(2)}) collective-permute-start(bf16[16,48,768]{2,1,0:T(8,128)(2,1)S(1)} %pad_maximum_fusion.1.refs_1_), channel_id=1, source_target_pairs={{0,1},{1,0},{2,3},{3,2},{4,5},{5,4},{6,7},{7,6},{8,9},{9,8},{10,11... | collective-permute-start | bytes 3538952 | tf_op jit(solution)/shard_map/ppermute | solution.py:783
  188.7 4.1 %collective-permute-done.35 = bf16[9,48,768]{2,1,0:T(8,128)(2,1)S(1)} collective-permute-done((bf16[9,48,768]{2,1,0:T(8,128)(2,1)S(1)}, bf16[9,48,768]{2,1,0:T(8,128)(2,1)S(1)}, u32[]{:S(2)}, u32[]{:S(2)}) %collective-permute-start.35) | collective-permute-done | bytes 663584 | tf_op jit(solution)/shard_map/ppermute | solution.py:783
  192.8 5.7 %collective-permute-start.39 = (bf16[16,48,768]{2,1,0:T(8,128)(2,1)S(1)}, bf16[16,48,768]{2,1,0:T(8,128)(2,1)S(1)}, u32[]{:S(2)}, u32[]{:S(2)}) collective-permute-start(bf16[16,48,768]{2,1,0:T(8,128)(2,1)S(1)} %pad_maximum_fusion.3.refs_1_), channel_id=1, source_target_pairs={{0,1},{1,0},{2,3},{3,2},{4,5},{5,4},{6,7},{7,6},{8,9},{9,8},{10,11... | collective-permute-start | bytes 3538952 | tf_op jit(solution)/shard_map/ppermute | solution.py:783
  198.7 3.1 %finish_mlp_0_1.1 = (f32[3072,768]{1,0:T(8,128)}, f32[768,3072]{1,0:T(8,128)}) custom-call(s32[10]{0:T(128)S(1)} %stack.58.refs_0_.ids_ref, bf16[16,48,768]{2,1,0:T(8,128)(2,1)S(1)} %collective-permute-done.40.refs_1_, bf16[16,48,768]{2,1,0:T(8,128)(2,1)S(1)} %collective-permute-done.41.refs_2_, ...), custom_call_target="tpu_custom_call", output_to_operand_aliasing={{0}: (3, {}), {1}: (4, {})} | custom-call | flops 32000000000 | bytes 1000 | tf_op jit(solution)/shard_map/finish_mlp_0_1/pallas_call | solution.py:558
  201.8 3.1 %finish_mlp_1_0.1 = (f32[3072,768]{1,0:T(8,128)}, f32[768,3072]{1,0:T(8,128)}) custom-call(s32[10]{0:T(128)S(1)} %stack.58.refs_0_.ids_ref, bf16[16,48,768]{2,1,0:T(8,128)(2,1)S(1)} %pad_maximum_fusion.3.refs_1_, bf16[16,48,768]{2,1,0:T(8,128)(2,1)S(1)} %pad_maximum_fusion.4.refs_2_, ...), custom_call_target="tpu_custom_call", output_to_operand_aliasing={{0}: (3, {}), {1}: (4, {})} | custom-call | flops 32000000000 | bytes 1000 | tf_op jit(solution)/shard_map/finish_mlp_1_0/pallas_call | solution.py:558
  204.9 3.1 %finish_mlp_1_1.1 = (f32[3072,768]{1,0:T(8,128)}, f32[768,3072]{1,0:T(8,128)}) custom-call(s32[10]{0:T(128)S(1)} %stack.58.refs_0_.ids_ref, bf16[16,48,768]{2,1,0:T(8,128)(2,1)S(1)} %collective-permute-done.39.refs_1_, bf16[16,48,768]{2,1,0:T(8,128)(2,1)S(1)} %collective-permute-done.42.refs_2_, ...), custom_call_target="tpu_custom_call", output_to_operand_aliasing={{0}: (3, {}), {1}: (4, {})} | custom-call | flops 32000000000 | bytes 1000 | tf_op jit(solution)/shard_map/finish_mlp_1_1/pallas_call | solution.py:558
  209.0 2.9 %finish_attn_0.1 = (f32[768,2304]{1,0:T(8,128)}, f32[768,768]{1,0:T(8,128)}) custom-call(s32[10]{0:T(128)S(1)} %stack.58.refs_0_.ids_ref, bf16[16,48,768]{2,1,0:T(8,128)(2,1)S(1)} %pad_maximum_fusion.6.a_ref, bf16[16,48,768]{2,1,0:T(8,128)(2,1)S(1)} %pad_maximum_fusion.5.b_ref), custom_call_target="tpu_custom_call" | custom-call | flops 41999998976 | bytes 1000 | tf_op jit(solution)/shard_map/finish_attn_0/pallas_call | solution.py:598
  213.8 3.0 %finish_attn_1.1 = (f32[768,2304]{1,0:T(8,128)}, f32[768,768]{1,0:T(8,128)}) custom-call(s32[10]{0:T(128)S(1)} %stack.58.refs_0_.ids_ref, bf16[17,48,768]{2,1,0:T(8,128)(2,1)S(1)} %collective-permute-done.43.got_ref.a_ref, bf16[16,48,768]{2,1,0:T(8,128)(2,1)S(1)} %collective-permute-done.44.b_ref, ...), custom_call_target="tpu_custom_call", output_to_operand_aliasing={{0}: (3, {}), {1}: (4, {})} | custom-call | flops 41999998976 | bytes 1000 | tf_op jit(solution)/shard_map/finish_attn_1/pallas_call | solution.py:598
  (181 shorter events, 25.2 us)
Async XLA Ops:
  0.8 15.8 %copy-start.1 = (bf16[3072,768]{1,0:T(8,128)(2,1)S(1)}, bf16[3072,768]{1,0:T(8,128)(2,1)}, u32[]{:S(2)}) copy-start(bf16[3072,768]{1,0:T(8,128)(2,1)} %refs_5_.14) | copy-start | bytes 14155780
  20.8 9.8 %collective-permute-start = (bf16[2,16,48,768]{3,2,1,0:T(8,128)(2,1)S(1)}, bf16[2,16,48,768]{3,2,1,0:T(8,128)(2,1)S(1)}, u32[]{:S(2)}, u32[]{:S(2)}) collective-permute-start(bf16[2,16,48,768]{3,2,1,0:T(8,128)(2,1)S(1)} %get-tuple-element.125), channel_id=1, source_target_pairs={{0,1},{1,0},{2,3},{3,2},{4,5},{5,4},{6,7},{7,6},{8,9},{9,8},{10,11... | collective-permute-start | bytes 7077896 | tf_op jit(solution)/shard_map/ppermute | solution.py:783
  31.2 18.0 %copy-start.14 = (bf16[1,8,48,768]{3,2,1,0:T(8,128)(2,1)}, bf16[1,8,48,768]{3,2,1,0:T(8,128)(2,1)S(1)}, u32[]{:S(2)}) copy-start(bf16[1,8,48,768]{3,2,1,0:T(8,128)(2,1)S(1)} %get-tuple-element.240) | copy-start | bytes 1769476
  31.3 19.1 %copy-start.16 = (bf16[1,8,48,768]{3,2,1,0:T(8,128)(2,1)}, bf16[1,8,48,768]{3,2,1,0:T(8,128)(2,1)S(1)}, u32[]{:S(2)}) copy-start(bf16[1,8,48,768]{3,2,1,0:T(8,128)(2,1)S(1)} %get-tuple-element.241) | copy-start | bytes 1769476
  31.3 17.9 %collective-permute-start.2 = (bf16[8,48,768]{2,1,0:T(8,128)(2,1)S(1)}, bf16[8,48,768]{2,1,0:T(8,128)(2,1)S(1)}, u32[]{:S(2)}, u32[]{:S(2)}) collective-permute-start(bf16[8,48,768]{2,1,0:T(8,128)(2,1)S(1)} %get-tuple-element.242), channel_id=1, source_target_pairs={{0,4},{1,5},{2,6},{3,7},{4,0},{5,1},{6,2},{7,3},{8,12},{9,13},{10,... | collective-permute-start | bytes 1769480 | tf_op jit(solution)/shard_map/ppermute | solution.py:783
  32.6 16.6 %collective-permute-start.1 = (bf16[8,48,768]{2,1,0:T(8,128)(2,1)S(1)}, bf16[8,48,768]{2,1,0:T(8,128)(2,1)S(1)}, u32[]{:S(2)}, u32[]{:S(2)}) collective-permute-start(bf16[8,48,768]{2,1,0:T(8,128)(2,1)S(1)} %get-tuple-element.243), channel_id=1, source_target_pairs={{0,2},{1,3},{2,0},{3,1},{4,6},{5,7},{6,4},{7,5},{8,10},{9,11},{10,... | collective-permute-start | bytes 1769480 | tf_op jit(solution)/shard_map/ppermute | solution.py:783
  42.3 5.1 %collective-permute-start.3 = (bf16[2,16,48,768]{3,2,1,0:T(8,128)(2,1)S(1)}, bf16[2,16,48,768]{3,2,1,0:T(8,128)(2,1)S(1)}, u32[]{:S(2)}, u32[]{:S(2)}) collective-permute-start(bf16[2,16,48,768]{3,2,1,0:T(8,128)(2,1)S(1)} %get-tuple-element.147), channel_id=1, source_target_pairs={{0,1},{1,0},{2,3},{3,2},{4,5},{5,4},{6,7},{7,6},{8,9},{9,8},{10,11... | collective-permute-start | bytes 7077896 | tf_op jit(solution)/shard_map/ppermute | solution.py:783
  50.0 18.4 %collective-permute-start.7 = (bf16[4,48,768]{2,1,0:T(8,128)(2,1)}, bf16[4,48,768]{2,1,0:T(8,128)(2,1)}, u32[]{:S(2)}, u32[]{:S(2)}) collective-permute-start(bf16[4,48,768]{2,1,0:T(8,128)(2,1)} %fusion.16), channel_id=1, source_target_pairs={{0,2},{1,3},{2,0},{3,1},{4,6},{5,7},{6,4},{7,5},{8,10},{9,11},{10,... | collective-permute-start | bytes 884744 | tf_op jit(solution)/shard_map/ppermute | solution.py:783
  51.1 17.3 %collective-permute-start.6 = (bf16[4,48,768]{2,1,0:T(8,128)(2,1)}, bf16[4,48,768]{2,1,0:T(8,128)(2,1)}, u32[]{:S(2)}, u32[]{:S(2)}) collective-permute-start(bf16[4,48,768]{2,1,0:T(8,128)(2,1)} %fusion.17), channel_id=1, source_target_pairs={{0,4},{1,5},{2,6},{3,7},{4,0},{5,1},{6,2},{7,3},{8,12},{9,13},{10,... | collective-permute-start | bytes 884744 | tf_op jit(solution)/shard_map/ppermute | solution.py:783
  51.3 21.1 %collective-permute-start.5 = (bf16[8,48,768]{2,1,0:T(8,128)(2,1)}, bf16[8,48,768]{2,1,0:T(8,128)(2,1)}, u32[]{:S(2)}, u32[]{:S(2)}) collective-permute-start(bf16[8,48,768]{2,1,0:T(8,128)(2,1)} %get-tuple-element.238), channel_id=1, source_target_pairs={{0,4},{1,5},{2,6},{3,7},{4,0},{5,1},{6,2},{7,3},{8,12},{9,13},{10,... | collective-permute-start | bytes 1769480 | tf_op jit(solution)/shard_map/ppermute | solution.py:783
  52.6 19.9 %collective-permute-start.4 = (bf16[8,48,768]{2,1,0:T(8,128)(2,1)}, bf16[8,48,768]{2,1,0:T(8,128)(2,1)}, u32[]{:S(2)}, u32[]{:S(2)}) collective-permute-start(bf16[8,48,768]{2,1,0:T(8,128)(2,1)} %get-tuple-element.239), channel_id=1, source_target_pairs={{0,2},{1,3},{2,0},{3,1},{4,6},{5,7},{6,4},{7,5},{8,10},{9,11},{10,... | collective-permute-start | bytes 1769480 | tf_op jit(solution)/shard_map/ppermute | solution.py:783
  77.2 10.1 %collective-permute-start.8 = (bf16[2,16,48,768]{3,2,1,0:T(8,128)(2,1)S(1)}, bf16[2,16,48,768]{3,2,1,0:T(8,128)(2,1)S(1)}, u32[]{:S(2)}, u32[]{:S(2)}) collective-permute-start(bf16[2,16,48,768]{3,2,1,0:T(8,128)(2,1)S(1)} %attn_grad_0.1), channel_id=1, source_target_pairs={{0,1},{1,0},{2,3},{3,2},{4,5},{5,4},{6,7},{7,6},{8,9},{9,8},{10,11... | collective-permute-start | bytes 7077896 | tf_op jit(solution)/shard_map/ppermute | solution.py:783
  78.5 8.6 %collective-permute-start.9 = (bf16[2,2,48,768]{3,2,1,0:T(8,128)(2,1)S(1)}, bf16[2,2,48,768]{3,2,1,0:T(8,128)(2,1)S(1)}, u32[]{:S(2)}, u32[]{:S(2)}) collective-permute-start(bf16[2,2,48,768]{3,2,1,0:T(8,128)(2,1)S(1)} %fusion.26), channel_id=1, source_target_pairs={{0,8},{8,0},{16,24},{24,16},{1,9},{9,1},{17,25},{25,17},{2,10},{10... | collective-permute-start | bytes 884744 | tf_op jit(solution)/shard_map/ppermute | solution.py:783
  78.7 9.3 %collective-permute-start.14 = (bf16[4,48,768]{2,1,0:T(8,128)(2,1)S(1)}, bf16[4,48,768]{2,1,0:T(8,128)(2,1)S(1)}, u32[]{:S(2)}, u32[]{:S(2)}) collective-permute-start(bf16[4,48,768]{2,1,0:T(8,128)(2,1)S(1)} %fusion.12), channel_id=1, source_target_pairs={{0,2},{1,3},{2,0},{3,1},{4,6},{5,7},{6,4},{7,5},{8,10},{9,11},{10,... | collective-permute-start | bytes 884744 | tf_op jit(solution)/shard_map/ppermute | solution.py:783
  79.7 8.3 %collective-permute-start.13 = (bf16[4,48,768]{2,1,0:T(8,128)(2,1)S(1)}, bf16[4,48,768]{2,1,0:T(8,128)(2,1)S(1)}, u32[]{:S(2)}, u32[]{:S(2)}) collective-permute-start(bf16[4,48,768]{2,1,0:T(8,128)(2,1)S(1)} %fusion.15), channel_id=1, source_target_pairs={{0,4},{1,5},{2,6},{3,7},{4,0},{5,1},{6,2},{7,3},{8,12},{9,13},{10,... | collective-permute-start | bytes 884744 | tf_op jit(solution)/shard_map/ppermute | solution.py:783
  87.2 9.8 %collective-permute-start.12 = (bf16[2,1,48,768]{3,2,1,0:T(8,128)(2,1)S(1)}, bf16[2,1,48,768]{3,2,1,0:T(8,128)(2,1)S(1)}, u32[]{:S(2)}, u32[]{:S(2)}) collective-permute-start(bf16[2,1,48,768]{3,2,1,0:T(8,128)(2,1)S(1)} %slice.417), channel_id=1, source_target_pairs={{0,16},{8,24},{16,0},{24,8},{1,17},{9,25},{17,1},{25,9},{2,18},{10... | collective-permute-start | bytes 442376 | tf_op jit(solution)/shard_map/ppermute | solution.py:783
  90.2 11.4 %collective-permute-start.16 = (bf16[2,2,48,768]{3,2,1,0:T(8,128)(2,1)S(1)}, bf16[2,2,48,768]{3,2,1,0:T(8,128)(2,1)S(1)}, u32[]{:S(2)}, u32[]{:S(2)}) collective-permute-start(bf16[2,2,48,768]{3,2,1,0:T(8,128)(2,1)S(1)} %fusion.25), channel_id=1, source_target_pairs={{0,8},{8,0},{16,24},{24,16},{1,9},{9,1},{17,25},{25,17},{2,10},{10... | collective-permute-start | bytes 884744 | tf_op jit(solution)/shard_map/ppermute | solution.py:783
  91.3 14.8 %collective-permute-start.11 = (bf16[8,48,768]{2,1,0:T(8,128)(2,1)S(1)}, bf16[8,48,768]{2,1,0:T(8,128)(2,1)S(1)}, u32[]{:S(2)}, u32[]{:S(2)}) collective-permute-start(bf16[8,48,768]{2,1,0:T(8,128)(2,1)S(1)} %get-tuple-element.233), channel_id=1, source_target_pairs={{0,4},{1,5},{2,6},{3,7},{4,0},{5,1},{6,2},{7,3},{8,12},{9,13},{10,... | collective-permute-start | bytes 1769480 | tf_op jit(solution)/shard_map/ppermute | solution.py:783
  91.5 14.6 %collective-permute-start.10 = (bf16[8,48,768]{2,1,0:T(8,128)(2,1)S(1)}, bf16[8,48,768]{2,1,0:T(8,128)(2,1)S(1)}, u32[]{:S(2)}, u32[]{:S(2)}) collective-permute-start(bf16[8,48,768]{2,1,0:T(8,128)(2,1)S(1)} %get-tuple-element.234), channel_id=1, source_target_pairs={{0,2},{1,3},{2,0},{3,1},{4,6},{5,7},{6,4},{7,5},{8,10},{9,11},{10,... | collective-permute-start | bytes 1769480 | tf_op jit(solution)/shard_map/ppermute | solution.py:783
  97.0 9.0 %collective-permute-start.15 = (bf16[2,1,48,768]{3,2,1,0:T(8,128)(2,1)S(1)}, bf16[2,1,48,768]{3,2,1,0:T(8,128)(2,1)S(1)}, u32[]{:S(2)}, u32[]{:S(2)}) collective-permute-start(bf16[2,1,48,768]{3,2,1,0:T(8,128)(2,1)S(1)} %add_convert_fusion.23), channel_id=1, source_target_pairs={{0,16},{8,24},{16,0},{24,8},{1,17},{9,25},{17,1},{25,9},{2,18},{10... | collective-permute-start | bytes 442376 | tf_op jit(solution)/shard_map/ppermute | solution.py:783
  101.7 10.6 %collective-permute-start.20 = (bf16[2,1,48,768]{3,2,1,0:T(8,128)(2,1)S(1)}, bf16[2,1,48,768]{3,2,1,0:T(8,128)(2,1)S(1)}, u32[]{:S(2)}, u32[]{:S(2)}) collective-permute-start(bf16[2,1,48,768]{3,2,1,0:T(8,128)(2,1)S(1)} %slice.426), channel_id=1, source_target_pairs={{0,16},{8,24},{16,0},{24,8},{1,17},{9,25},{17,1},{25,9},{2,18},{10... | collective-permute-start | bytes 442376 | tf_op jit(solution)/shard_map/ppermute | solution.py:783
  106.0 9.9 %collective-permute-start.19 = (bf16[2,2,48,768]{3,2,1,0:T(8,128)(2,1)S(1)}, bf16[2,2,48,768]{3,2,1,0:T(8,128)(2,1)S(1)}, u32[]{:S(2)}, u32[]{:S(2)}) collective-permute-start(bf16[2,2,48,768]{3,2,1,0:T(8,128)(2,1)S(1)} %pad_maximum_fusion.21), channel_id=1, source_target_pairs={{0,8},{8,0},{16,24},{24,16},{1,9},{9,1},{17,25},{25,17},{2,10},{10... | collective-permute-start | bytes 884744 | tf_op jit(solution)/shard_map/ppermute | solution.py:783
  106.2 11.7 %collective-permute-start.18 = (bf16[4,48,768]{2,1,0:T(8,128)(2,1)S(1)}, bf16[4,48,768]{2,1,0:T(8,128)(2,1)S(1)}, u32[]{:S(2)}, u32[]{:S(2)}) collective-permute-start(bf16[4,48,768]{2,1,0:T(8,128)(2,1)S(1)} %fusion.7), channel_id=1, source_target_pairs={{0,2},{1,3},{2,0},{3,1},{4,6},{5,7},{6,4},{7,5},{8,10},{9,11},{10,... | collective-permute-start | bytes 884744 | tf_op jit(solution)/shard_map/ppermute | solution.py:783
  108.3 9.6 %collective-permute-start.17 = (bf16[4,48,768]{2,1,0:T(8,128)(2,1)S(1)}, bf16[4,48,768]{2,1,0:T(8,128)(2,1)S(1)}, u32[]{:S(2)}, u32[]{:S(2)}) collective-permute-start(bf16[4,48,768]{2,1,0:T(8,128)(2,1)S(1)} %fusion.8), channel_id=1, source_target_pairs={{0,4},{1,5},{2,6},{3,7},{4,0},{5,1},{6,2},{7,3},{8,12},{9,13},{10,... | collective-permute-start | bytes 884744 | tf_op jit(solution)/shard_map/ppermute | solution.py:783
  112.4 11.3 %collective-permute-start.22 = (bf16[2,1,48,768]{3,2,1,0:T(8,128)(2,1)S(1)}, bf16[2,1,48,768]{3,2,1,0:T(8,128)(2,1)S(1)}, u32[]{:S(2)}, u32[]{:S(2)}) collective-permute-start(bf16[2,1,48,768]{3,2,1,0:T(8,128)(2,1)S(1)} %add_convert_fusion.22), channel_id=1, source_target_pairs={{0,16},{8,24},{16,0},{24,8},{1,17},{9,25},{17,1},{25,9},{2,18},{10... | collective-permute-start | bytes 442376 | tf_op jit(solution)/shard_map/ppermute | solution.py:783
  116.1 6.1 %collective-permute-start.24 = (bf16[4,48,768]{2,1,0:T(8,128)(2,1)S(1)}, bf16[4,48,768]{2,1,0:T(8,128)(2,1)S(1)}, u32[]{:S(2)}, u32[]{:S(2)}) collective-permute-start(bf16[4,48,768]{2,1,0:T(8,128)(2,1)S(1)} %get-tuple-element.250), channel_id=1, source_target_pairs={{0,2},{1,3},{2,0},{3,1},{4,6},{5,7},{6,4},{7,5},{8,10},{9,11},{10,... | collective-permute-start | bytes 884744 | tf_op jit(solution)/shard_map/ppermute | solution.py:783
  117.7 5.9 %collective-permute-start.23 = (bf16[4,48,768]{2,1,0:T(8,128)(2,1)S(1)}, bf16[4,48,768]{2,1,0:T(8,128)(2,1)S(1)}, u32[]{:S(2)}, u32[]{:S(2)}) collective-permute-start(bf16[4,48,768]{2,1,0:T(8,128)(2,1)S(1)} %get-tuple-element.251), channel_id=1, source_target_pairs={{0,4},{1,5},{2,6},{3,7},{4,0},{5,1},{6,2},{7,3},{8,12},{9,13},{10,... | collective-permute-start | bytes 884744 | tf_op jit(solution)/shard_map/ppermute | solution.py:783
  118.2 7.6 %collective-permute-start.21 = (bf16[2,2,48,768]{3,2,0,1:T(8,128)(2,1)S(1)}, bf16[2,2,48,768]{3,2,0,1:T(8,128)(2,1)S(1)}, u32[]{:S(2)}, u32[]{:S(2)}) collective-permute-start(bf16[2,2,48,768]{3,2,0,1:T(8,128)(2,1)S(1)} %pad_maximum_fusion.18), channel_id=1, source_target_pairs={{0,8},{8,0},{16,24},{24,16},{1,9},{9,1},{17,25},{25,17},{2,10},{10... | collective-permute-start | bytes 884744 | tf_op jit(solution)/shard_map/ppermute | solution.py:783
  123.7 11.0 %collective-permute-start.27 = (bf16[2,2,48,768]{3,2,1,0:T(8,128)(2,1)S(1)}, bf16[2,2,48,768]{3,2,1,0:T(8,128)(2,1)S(1)}, u32[]{:S(2)}, u32[]{:S(2)}) collective-permute-start(bf16[2,2,48,768]{3,2,1,0:T(8,128)(2,1)S(1)} %pad_maximum_fusion.22), channel_id=1, source_target_pairs={{0,8},{8,0},{16,24},{24,16},{1,9},{9,1},{17,25},{25,17},{2,10},{10... | collective-permute-start | bytes 884744 | tf_op jit(solution)/shard_map/ppermute | solution.py:783
  126.0 6.6 %collective-permute-start.25 = (bf16[2,1,48,768]{3,2,0,1:T(8,128)(2,1)S(1)}, bf16[2,1,48,768]{3,2,0,1:T(8,128)(2,1)S(1)}, u32[]{:S(2)}, u32[]{:S(2)}) collective-permute-start(bf16[2,1,48,768]{3,2,0,1:T(8,128)(2,1)S(1)} %slice.436), channel_id=1, source_target_pairs={{0,16},{8,24},{16,0},{24,8},{1,17},{9,25},{17,1},{25,9},{2,18},{10... | collective-permute-start | bytes 442376 | tf_op jit(solution)/shard_map/ppermute | solution.py:783
  132.6 13.2 %collective-permute-start.26 = (bf16[3,48,768]{2,1,0:T(8,128)(2,1)S(1)}, bf16[3,48,768]{2,1,0:T(8,128)(2,1)S(1)}, u32[]{:S(2)}, u32[]{:S(2)}) collective-permute-start(bf16[3,48,768]{2,1,0:T(8,128)(2,1)S(1)} %pad_maximum_fusion.24), channel_id=1, source_target_pairs={{0,16},{8,24},{16,0},{24,8},{1,17},{9,25},{17,1},{25,9},{2,18},{10... | collective-permute-start | bytes 663560 | tf_op jit(solution)/shard_map/ppermute | solution.py:783
  134.9 12.6 %collective-permute-start.30 = (bf16[4,48,768]{2,1,0:T(8,128)(2,1)S(1)}, bf16[4,48,768]{2,1,0:T(8,128)(2,1)S(1)}, u32[]{:S(2)}, u32[]{:S(2)}) collective-permute-start(bf16[4,48,768]{2,1,0:T(8,128)(2,1)S(1)} %get-tuple-element.248), channel_id=1, source_target_pairs={{0,2},{1,3},{2,0},{3,1},{4,6},{5,7},{6,4},{7,5},{8,10},{9,11},{10,... | collective-permute-start | bytes 884744 | tf_op jit(solution)/shard_map/ppermute | solution.py:783
  135.7 11.8 %collective-permute-start.29 = (bf16[4,48,768]{2,1,0:T(8,128)(2,1)S(1)}, bf16[4,48,768]{2,1,0:T(8,128)(2,1)S(1)}, u32[]{:S(2)}, u32[]{:S(2)}) collective-permute-start(bf16[4,48,768]{2,1,0:T(8,128)(2,1)S(1)} %get-tuple-element.249), channel_id=1, source_target_pairs={{0,4},{1,5},{2,6},{3,7},{4,0},{5,1},{6,2},{7,3},{8,12},{9,13},{10,... | collective-permute-start | bytes 884744 | tf_op jit(solution)/shard_map/ppermute | solution.py:783
  146.0 9.1 %collective-permute-start.28 = (bf16[5,48,768]{2,1,0:T(8,128)(2,1)S(1)}, bf16[5,48,768]{2,1,0:T(8,128)(2,1)S(1)}, u32[]{:S(2)}, u32[]{:S(2)}) collective-permute-start(bf16[5,48,768]{2,1,0:T(8,128)(2,1)S(1)} %pad_maximum_fusion.16), channel_id=1, source_target_pairs={{0,8},{8,0},{16,24},{24,16},{1,9},{9,1},{17,25},{25,17},{2,10},{10... | collective-permute-start | bytes 1105928 | tf_op jit(solution)/shard_map/ppermute | solution.py:783
  146.1 14.2 %collective-permute-start.34 = (bf16[8,48,768]{2,1,0:T(8,128)(2,1)S(1)}, bf16[8,48,768]{2,1,0:T(8,128)(2,1)S(1)}, u32[]{:S(2)}, u32[]{:S(2)}) collective-permute-start(bf16[8,48,768]{2,1,0:T(8,128)(2,1)S(1)} %pad_maximum_fusion.10), channel_id=1, source_target_pairs={{0,4},{1,5},{2,6},{3,7},{4,0},{5,1},{6,2},{7,3},{8,12},{9,13},{10,... | collective-permute-start | bytes 1769480 | tf_op jit(solution)/shard_map/ppermute | solution.py:783
  146.2 14.2 %collective-permute-start.33 = (bf16[8,48,768]{2,1,0:T(8,128)(2,1)S(1)}, bf16[8,48,768]{2,1,0:T(8,128)(2,1)S(1)}, u32[]{:S(2)}, u32[]{:S(2)}) collective-permute-start(bf16[8,48,768]{2,1,0:T(8,128)(2,1)S(1)} %pad_maximum_fusion.9), channel_id=1, source_target_pairs={{0,2},{1,3},{2,0},{3,1},{4,6},{5,7},{6,4},{7,5},{8,10},{9,11},{10,... | collective-permute-start | bytes 1769480 | tf_op jit(solution)/shard_map/ppermute | solution.py:783
  147.5 38.9 %collective-permute-start.38 = (bf16[8,48,768]{2,1,0:T(8,128)(2,1)S(1)}, bf16[8,48,768]{2,1,0:T(8,128)(2,1)S(1)}, u32[]{:S(2)}, u32[]{:S(2)}) collective-permute-start(bf16[8,48,768]{2,1,0:T(8,128)(2,1)S(1)} %pad_maximum_fusion.13), channel_id=1, source_target_pairs={{0,4},{1,5},{2,6},{3,7},{4,0},{5,1},{6,2},{7,3},{8,12},{9,13},{10,... | collective-permute-start | bytes 1769480 | tf_op jit(solution)/shard_map/ppermute | solution.py:783
  148.0 39.6 %collective-permute-start.37 = (bf16[8,48,768]{2,1,0:T(8,128)(2,1)S(1)}, bf16[8,48,768]{2,1,0:T(8,128)(2,1)S(1)}, u32[]{:S(2)}, u32[]{:S(2)}) collective-permute-start(bf16[8,48,768]{2,1,0:T(8,128)(2,1)S(1)} %pad_maximum_fusion.12), channel_id=1, source_target_pairs={{0,2},{1,3},{2,0},{3,1},{4,6},{5,7},{6,4},{7,5},{8,10},{9,11},{10,... | collective-permute-start | bytes 1769480 | tf_op jit(solution)/shard_map/ppermute | solution.py:783
  155.2 25.7 %collective-permute-start.32 = (bf16[4,48,768]{2,1,0:T(8,128)(2,1)S(1)}, bf16[4,48,768]{2,1,0:T(8,128)(2,1)S(1)}, u32[]{:S(2)}, u32[]{:S(2)}) collective-permute-start(bf16[4,48,768]{2,1,0:T(8,128)(2,1)S(1)} %get-tuple-element.246), channel_id=1, source_target_pairs={{0,2},{1,3},{2,0},{3,1},{4,6},{5,7},{6,4},{7,5},{8,10},{9,11},{10,... | collective-permute-start | bytes 884744 | tf_op jit(solution)/shard_map/ppermute | solution.py:783
  160.3 20.5 %collective-permute-start.31 = (bf16[5,48,768]{2,1,0:T(8,128)(2,1)S(1)}, bf16[5,48,768]{2,1,0:T(8,128)(2,1)S(1)}, u32[]{:S(2)}, u32[]{:S(2)}) collective-permute-start(bf16[5,48,768]{2,1,0:T(8,128)(2,1)S(1)} %pad_maximum_fusion.17), channel_id=1, source_target_pairs={{0,4},{1,5},{2,6},{3,7},{4,0},{5,1},{6,2},{7,3},{8,12},{9,13},{10,... | collective-permute-start | bytes 1105928 | tf_op jit(solution)/shard_map/ppermute | solution.py:783
  181.1 11.7 %collective-permute-start.35 = (bf16[9,48,768]{2,1,0:T(8,128)(2,1)S(1)}, bf16[9,48,768]{2,1,0:T(8,128)(2,1)S(1)}, u32[]{:S(2)}, u32[]{:S(2)}) collective-permute-start(bf16[9,48,768]{2,1,0:T(8,128)(2,1)S(1)} %pad_maximum_fusion.7), channel_id=1, source_target_pairs={{0,2},{1,3},{2,0},{3,1},{4,6},{5,7},{6,4},{7,5},{8,10},{9,11},{10,... | collective-permute-start | bytes 1990664 | tf_op jit(solution)/shard_map/ppermute | solution.py:783
  181.2 17.5 %collective-permute-start.40 = (bf16[16,48,768]{2,1,0:T(8,128)(2,1)S(1)}, bf16[16,48,768]{2,1,0:T(8,128)(2,1)S(1)}, u32[]{:S(2)}, u32[]{:S(2)}) collective-permute-start(bf16[16,48,768]{2,1,0:T(8,128)(2,1)S(1)} %pad_maximum_fusion.1.refs_1_), channel_id=1, source_target_pairs={{0,1},{1,0},{2,3},{3,2},{4,5},{5,4},{6,7},{7,6},{8,9},{9,8},{10,11... | collective-permute-start | bytes 3538952 | tf_op jit(solution)/shard_map/ppermute | solution.py:783
  186.4 12.3 %collective-permute-start.41 = (bf16[16,48,768]{2,1,0:T(8,128)(2,1)S(1)}, bf16[16,48,768]{2,1,0:T(8,128)(2,1)S(1)}, u32[]{:S(2)}, u32[]{:S(2)}) collective-permute-start(bf16[16,48,768]{2,1,0:T(8,128)(2,1)S(1)} %pad_maximum_fusion.2.refs_2_), channel_id=1, source_target_pairs={{0,1},{1,0},{2,3},{3,2},{4,5},{5,4},{6,7},{7,6},{8,9},{9,8},{10,11... | collective-permute-start | bytes 3538952 | tf_op jit(solution)/shard_map/ppermute | solution.py:783
  186.5 21.5 %collective-permute-start.36 = (bf16[8,48,768]{2,1,0:T(8,128)(2,1)S(1)}, bf16[8,48,768]{2,1,0:T(8,128)(2,1)S(1)}, u32[]{:S(2)}, u32[]{:S(2)}) collective-permute-start(bf16[8,48,768]{2,1,0:T(8,128)(2,1)S(1)} %pad_maximum_fusion.15), channel_id=1, source_target_pairs={{0,4},{1,5},{2,6},{3,7},{4,0},{5,1},{6,2},{7,3},{8,12},{9,13},{10,... | collective-permute-start | bytes 1769480 | tf_op jit(solution)/shard_map/ppermute | solution.py:783
  187.8 17.1 %collective-permute-start.42 = (bf16[16,48,768]{2,1,0:T(8,128)(2,1)S(1)}, bf16[16,48,768]{2,1,0:T(8,128)(2,1)S(1)}, u32[]{:S(2)}, u32[]{:S(2)}) collective-permute-start(bf16[16,48,768]{2,1,0:T(8,128)(2,1)S(1)} %pad_maximum_fusion.4.refs_2_), channel_id=1, source_target_pairs={{0,1},{1,0},{2,3},{3,2},{4,5},{5,4},{6,7},{7,6},{8,9},{9,8},{10,11... | collective-permute-start | bytes 3538952 | tf_op jit(solution)/shard_map/ppermute | solution.py:783
  192.8 12.1 %collective-permute-start.39 = (bf16[16,48,768]{2,1,0:T(8,128)(2,1)S(1)}, bf16[16,48,768]{2,1,0:T(8,128)(2,1)S(1)}, u32[]{:S(2)}, u32[]{:S(2)}) collective-permute-start(bf16[16,48,768]{2,1,0:T(8,128)(2,1)S(1)} %pad_maximum_fusion.3.refs_1_), channel_id=1, source_target_pairs={{0,1},{1,0},{2,3},{3,2},{4,5},{5,4},{6,7},{7,6},{8,9},{9,8},{10,11... | collective-permute-start | bytes 3538952 | tf_op jit(solution)/shard_map/ppermute | solution.py:783
  208.4 5.4 %collective-permute-start.44 = (bf16[16,48,768]{2,1,0:T(8,128)(2,1)S(1)}, bf16[16,48,768]{2,1,0:T(8,128)(2,1)S(1)}, u32[]{:S(2)}, u32[]{:S(2)}) collective-permute-start(bf16[16,48,768]{2,1,0:T(8,128)(2,1)S(1)} %pad_maximum_fusion.5.b_ref), channel_id=1, source_target_pairs={{0,1},{1,0},{2,3},{3,2},{4,5},{5,4},{6,7},{7,6},{8,9},{9,8},{10,11... | collective-permute-start | bytes 3538952 | tf_op jit(solution)/shard_map/ppermute | solution.py:783
  208.5 4.6 %collective-permute-start.43 = (bf16[17,48,768]{2,1,0:T(8,128)(2,1)S(1)}, bf16[17,48,768]{2,1,0:T(8,128)(2,1)S(1)}, u32[]{:S(2)}, u32[]{:S(2)}) collective-permute-start(bf16[17,48,768]{2,1,0:T(8,128)(2,1)S(1)} %pad_maximum_fusion), channel_id=1, source_target_pairs={{0,1},{1,0},{2,3},{3,2},{4,5},{5,4},{6,7},{7,6},{8,9},{9,8},{10,11... | collective-permute-start | bytes 3760136 | tf_op jit(solution)/shard_map/ppermute | solution.py:783
  (21 other events, 121.5 us)

commit v2 on v1

--- a/solution.py
+++ b/solution.py
@@ -43,6 +43,15 @@
 
 def pin(value):
     return pltpu.with_memory_space_constraint(value, pltpu.HBM)
+
+
+HERE = pl.BlockSpec(memory_space=pltpu.VMEM)
+
+
+def held(rows, shape, dtype):
+    if rows <= 640:
+        return pltpu.VMEM(shape, dtype)
+    return jax.ShapeDtypeStruct(shape, dtype)
 
 
 def vmem(limit):
@@ -124,8 +133,7 @@
         wm_copy.start()
 
     tok_copy.wait()
-    x = tok_ref[...].astype(F32)
-    xhat, _ = stats(x)
+    xhat, _ = stats(tok_ref[...].astype(F32))
     normed = (xhat * g1_ref[...] + s1_ref[...]).astype(BF)
     normed_ref[...] = normed
     for third in range(3):
@@ -143,7 +151,7 @@
         joined_ref[:, cols] = part.astype(BF)
     cot_copy.wait()
     low = head_masks(slots)
-    key_slot = lax.broadcasted_iota(jnp.int32, (2 * slots, slots), 1)
+    key_slot = lax.broadcasted_iota(jnp.int32, (slots, 2 * slots), 0)
     row_slot = lax.broadcasted_iota(jnp.int32, (slots, D), 0)
 
     def one(item, carry):
@@ -158,11 +166,11 @@
             q = stack_heads(joined_ref[here, cols] * BF(FACTOR), low)
             k = joined_ref[here, D + pair * LANES : D + (pair + 1) * LANES]
             v = joined_ref[here, 2 * D + pair * LANES : 2 * D + (pair + 1) * LANES]
-            scores = jnp.where(allowed, dot_t(q, k), NEG)
-            raised = jnp.exp(scores - jnp.max(scores, axis=-1, keepdims=True))
-            soft = (raised * (1.0 / jnp.sum(raised, axis=-1, keepdims=True))).astype(BF)
+            scores = jnp.where(allowed, dot_t(k, q), NEG)
+            raised = jnp.exp(scores - jnp.max(scores, axis=0, keepdims=True))
+            soft = (raised * (1.0 / jnp.sum(raised, axis=0, keepdims=True))).astype(BF)
             probs_ref[item, pair] = soft
-            mixed = dot(soft, v)
+            mixed = t_dot(soft, v)
             mix_ref[here, cols] = jnp.where(low, mixed[:slots], mixed[slots:]).astype(BF)
         return carry
 
@@ -172,37 +180,29 @@
     def _():
         wm_copy.wait()
 
-    middle = tok_ref[...].astype(F32) + dot(mix_ref[...], wm_ref[...]) + mb_ref[...]
-    middle_ref[...] = middle
-    xhat, _ = stats(middle)
-    second_ref[...] = (xhat * g2_ref[...] + s2_ref[...]).astype(BF)
-
-
-def first_call(group, slots, counts, tok, cot, wj, wm, g1, s1, jb, mb, g2, s2):
+    for part in range(2):
+        here = slice(part * rows // 2, (part + 1) * rows // 2)
+        there = pl.ds(pl.multiple_of(step * rows + part * rows // 2, 16), rows // 2)
+        middle = tok_ref[here, :].astype(F32) + dot(mix_ref[here, :], wm_ref[...]) + mb_ref[...]
+        middle_ref[here, :] = middle
+        xhat, _ = stats(middle)
+        second_ref[here, :] = (xhat * g2_ref[...] + s2_ref[...]).astype(BF)
+
+
+def first_call(slots, counts, tok, cot, wj, wm, g1, s1, jb, mb, g2, s2):
     total = tok.shape[0]
-    rows = group * slots
-    steps = total // rows
-    row = lambda width: pl.BlockSpec((rows, width), lambda i, c: (i, 0))
-    out = lambda width, dt: jax.ShapeDtypeStruct((total, width), dt)
     hbm = pl.BlockSpec(memory_space=pltpu.HBM)
+    out = lambda width, dt: held(total, (total, width), dt)
     return pl.pallas_call(
         lambda *refs: first_body(slots, *refs),
         grid_spec=pltpu.PrefetchScalarGridSpec(
             num_scalar_prefetch=1,
-            grid=(steps,),
+            grid=(1,),
             in_specs=[hbm] * 4 + [full(a.shape) for a in (g1, s1, jb, mb, g2, s2)],
-            out_specs=[
-                row(D),
-                row(3 * D),
-                pl.BlockSpec((group, PAIRS, 2 * slots, slots), lambda i, c: (i, 0, 0, 0)),
-                row(D),
-                row(D),
-                row(D),
-                row(D),
-            ],
+            out_specs=[HERE] * 7,
             scratch_shapes=[
-                pltpu.VMEM((rows, D), BF),
-                pltpu.VMEM((rows, D), BF),
+                pltpu.VMEM((total, D), BF),
+                pltpu.VMEM((total, D), BF),
                 pltpu.VMEM((3, D, D), BF),
                 pltpu.VMEM((D, D), BF),
                 pltpu.SemaphoreType.DMA((6,)),
@@ -211,13 +211,13 @@
         out_shape=[
             out(D, BF),
             out(3 * D, BF),
-            jax.ShapeDtypeStruct((total // slots, PAIRS, 2 * slots, slots), BF),
+            held(total, (total // slots, PAIRS, slots, 2 * slots), BF),
             out(D, BF),
             out(D, F32),
             out(D, BF),
             out(D, BF),
         ],
-        compiler_params=vmem(32 if steps == 1 else 48),
+        compiler_params=vmem(20 if total <= 640 else 56),
         cost_estimate=cost(15),
         name="attn_fwd",
     )(*[pin(a) for a in (counts, tok, cot, wj, wm, g1, s1, jb, mb, g2, s2)])
@@ -245,25 +245,24 @@
 
 def quarter_call(call, ids, second, gout, up, ub, down):
     total = second.shape[0]
-    whole = full((total, D))
     return pl.pallas_call(
         lambda *refs: quarter_body(2, *refs),
         grid_spec=pltpu.PrefetchScalarGridSpec(
             num_scalar_prefetch=1,
             grid=(1,),
             in_specs=[
-                whole,
-                whole,
+                HERE,
+                HERE,
                 pl.BlockSpec((D, D), lambda i, ids: (0, ids[4 + call])),
                 pl.BlockSpec((1, D), lambda i, ids: (0, ids[4 + call])),
                 pl.BlockSpec((D, D), lambda i, ids: (ids[4 + call], 0)),
             ],
-            out_specs=[full((2, BLOCKS, BROWS, D)), whole, whole],
+            out_specs=[HERE] * 3,
         ),
         out_shape=[
-            jax.ShapeDtypeStruct((2, BLOCKS, BROWS, D), BF),
-            jax.ShapeDtypeStruct((total, D), BF),
-            jax.ShapeDtypeStruct((total, D), BF),
+            held(total, (2, BLOCKS, BROWS, D), BF),
+            held(total, (total, D), BF),
+            held(total, (total, D), BF),
         ],
         compiler_params=params(total),
         cost_estimate=cost(4.3),
@@ -299,27 +298,25 @@
 
 def collect_call(chunk, ids, acts, ghs, down, up, kept):
     total = acts[0].shape[0]
-    whole = full((total, D))
-    specs = [whole, whole, full((4, D))]
     return pl.pallas_call(
         lambda *refs: collect_body(chunk, *refs),
         grid_spec=pltpu.PrefetchScalarGridSpec(
             num_scalar_prefetch=1,
             grid=(2,),
-            in_specs=[whole] * 4
+            in_specs=[HERE] * 4
             + [
                 pl.BlockSpec((D, D), lambda i, ids: (ids[4 + 2 * chunk + i], 0)),
                 pl.BlockSpec((D, D), lambda i, ids: (0, ids[4 + 2 * chunk + i])),
             ]
-            + specs * (1 if chunk else 0),
-            out_specs=specs,
+            + [HERE] * (3 if chunk else 0),
+            out_specs=[HERE] * 3,
         ),
         out_shape=[
-            jax.ShapeDtypeStruct((total, D), F32),
-            jax.ShapeDtypeStruct((total, D), F32),
-            jax.ShapeDtypeStruct((4, D), F32),
+            held(total, (total, D), F32),
+            held(total, (total, D), F32),
+            held(total, (4, D), F32),
         ],
-        compiler_params=vmem(24 if total <= 640 else 56),
+        compiler_params=vmem(16 if total <= 640 else 56),
         cost_estimate=cost(4.3),
         name=f"mlp_collect_{chunk}",
     )(ids, *acts, *ghs, down, up, *(kept or ()))
@@ -377,21 +374,21 @@
 
 def middle_call(slots, counts, outer, g, mid, gout, db, g2, wm):
     total = mid.shape[0]
-    whole = full((total, D))
+    hbm = jax.ShapeDtypeStruct((total, D), BF)
     return pl.pallas_call(
         lambda *refs: middle_body(slots, *refs),
         grid_spec=pltpu.PrefetchScalarGridSpec(
             num_scalar_prefetch=1,
             grid=(1,),
-            in_specs=[whole, whole, whole, whole, full(db.shape), full(g2.shape), full((D, D))],
-            out_specs=[whole, whole, whole, whole, full((4, D))],
+            in_specs=[HERE] * 4 + [full(db.shape), full(g2.shape), full((D, D))],
+            out_specs=[full((total, D))] + [HERE] * 4,
         ),
         out_shape=[
-            jax.ShapeDtypeStruct((total, D), BF),
-            jax.ShapeDtypeStruct((total, D), F32),
-            jax.ShapeDtypeStruct((total, D), BF),
-            jax.ShapeDtypeStruct((total, D), BF),
-            jax.ShapeDtypeStruct((4, D), F32),
+            hbm,
+            held(total, (total, D), F32),
+            held(total, (total, D), BF),
+            held(total, (total, D), BF),
+            held(total, (4, D), F32),
         ],
         compiler_params=params(total),
         cost_estimate=cost(3.6),
@@ -399,84 +396,79 @@
     )(counts, outer, g, mid, gout, db, g2, wm)
 
 
-def attn_back_body(joined_ref, probs_ref, gmix_ref, grad_ref):
-    slots = joined_ref.shape[0]
+def attn_back_body(slots, first, joined_ref, probs_ref, gmix_ref, grad_ref):
     low = head_masks(slots)
-    for pair in range(PAIRS):
-        cols = slice(pair * LANES, (pair + 1) * LANES)
-        q = stack_heads(joined_ref[:, cols], low)
-        k = joined_ref[:, D + pair * LANES : D + (pair + 1) * LANES]
-        v = joined_ref[:, 2 * D + pair * LANES : 2 * D + (pair + 1) * LANES]
-        out = stack_heads(gmix_ref[:, cols], low)
-        low_soft = probs_ref[0, pair]
-        soft = low_soft.astype(F32)
-        grad_probs = dot_t(out, v)
-        mean = jnp.sum(soft * grad_probs, axis=-1, keepdims=True)
-        scores = (soft * (grad_probs - mean)).astype(BF)
-        gq = dot(scores, k) * FACTOR
-        grad_ref[:, cols] = jnp.where(low, gq[:slots], gq[slots:]).astype(BF)
-        grad_ref[:, D + pair * LANES : D + (pair + 1) * LANES] = (
-            t_dot(scores, q) * FACTOR
-        ).astype(BF)
-        grad_ref[:, 2 * D + pair * LANES : 2 * D + (pair + 1) * LANES] = t_dot(
-            low_soft, out
-        ).astype(BF)
+    items = joined_ref.shape[0] // slots // 2
+
+    def one(at, carry):
+        item = first * items + at
+        here = pl.ds(pl.multiple_of(item * slots, 16), slots)
+        for pair in range(PAIRS):
+            cols = slice(pair * LANES, (pair + 1) * LANES)
+            key_cols = slice(D + pair * LANES, D + (pair + 1) * LANES)
+            value_cols = slice(2 * D + pair * LANES, 2 * D + (pair + 1) * LANES)
+            q = stack_heads(joined_ref[here, cols] * BF(FACTOR), low)
+            out = stack_heads(gmix_ref[here, cols], low)
+            low_soft = probs_ref[item, pair]
+            soft = low_soft.astype(F32)
+            grad_probs = dot_t(joined_ref[here, value_cols], out)
+            mean = jnp.sum(soft * grad_probs, axis=0, keepdims=True)
+            scores = (soft * (grad_probs - mean)).astype(BF)
+            gq = t_dot(scores, joined_ref[here, key_cols] * BF(FACTOR))
+            grad_ref[here, cols] = jnp.where(low, gq[:slots], gq[slots:]).astype(BF)
+            grad_ref[here, key_cols] = dot(scores, q).astype(BF)
+            grad_ref[here, value_cols] = dot(low_soft, out).astype(BF)
+        return carry
+
+    lax.fori_loop(0, items, one, 0)
 
 
 def attn_back_call(call, slots, joined, probs, gmix, kept):
     total = joined.shape[0]
-    steps = total // slots // 2
-    row = lambda width: pl.BlockSpec((slots, width), lambda i: (call * steps + i, 0))
-    in_specs = [
-        row(3 * D),
-        pl.BlockSpec((1, PAIRS, 2 * slots, slots), lambda i: (call * steps + i, 0, 0, 0)),
-        row(D),
-    ]
     args = [joined, probs, gmix]
     aliases = {}
     if kept is not None:
-        in_specs.append(pl.BlockSpec(memory_space=pl.ANY))
         args.append(kept)
         aliases = {3: 0}
     return pl.pallas_call(
-        lambda *refs: attn_back_body(*refs[:3], refs[-1]),
-        grid=(steps,),
-        in_specs=in_specs,
-        out_specs=row(3 * D),
-        out_shape=jax.ShapeDtypeStruct((total, 3 * D), BF),
+        lambda *refs: attn_back_body(slots, call, *refs[:3], refs[-1]),
+        grid=(1,),
+        in_specs=[HERE] * len(args),
+        out_specs=HERE,
+        out_shape=held(total, (total, 3 * D), BF),
         input_output_aliases=aliases,
-        compiler_params=params(),
+        compiler_params=vmem(8 if total <= 640 else 48),
         cost_estimate=cost(5.5),
         name=f"attn_bwd_{call}",
     )(*args)
 
 
-def attn_grad_body(ids_ref, normed_ref, mix_ref, grad_ref, branch_ref, out_ref):
-    half = BLOCKS // 2
-
-    def put(which, base, mask, value):
-        for k in range(half):
-            out_ref[which, (base + k) ^ mask] = value[k * BROWS : (k + 1) * BROWS, :].astype(BF)
+def attn_grad_body(ids_ref, normed_ref, mix_ref, grad_ref, branch_ref, qk_ref, vm_ref):
+    def put(ref, which, value):
+        mask = ids_ref[which] >> 1
+        for k in range(BLOCKS // 2):
+            ref[which, k ^ mask] = value[k * BROWS : (k + 1) * BROWS, :].astype(BF)
 
     normed = normed_ref[...]
-    put(0, 0, ids_ref[0], t_dot(normed, grad_ref[:, :D]))
-    put(0, half, ids_ref[0], t_dot(normed, grad_ref[:, D : 2 * D]))
-    put(1, 0, ids_ref[1], t_dot(normed, grad_ref[:, 2 * D :]))
-    put(1, half, ids_ref[1], t_dot(mix_ref[...], branch_ref[...]))
+    put(qk_ref, 0, t_dot(normed, grad_ref[:, :D]))
+    put(qk_ref, 1, t_dot(normed, grad_ref[:, D : 2 * D]))
+    put(vm_ref, 0, t_dot(normed, grad_ref[:, 2 * D :]))
+    put(vm_ref, 1, t_dot(mix_ref[...], branch_ref[...]))
 
 
 def attn_grad_call(call, ids, normed, mix, grad, branch):
     total = normed.shape[0]
     half = pl.BlockSpec((total, D // 2), lambda i, ids: (0, ids[8 + call]))
+    shape = (2, BLOCKS // 2, BROWS, D)
     return pl.pallas_call(
         attn_grad_body,
         grid_spec=pltpu.PrefetchScalarGridSpec(
             num_scalar_prefetch=1,
             grid=(1,),
-            in_specs=[half, half, full((total, 3 * D)), full((total, D))],
-            out_specs=full((2, BLOCKS, BROWS, D)),
+            in_specs=[half, half, HERE, HERE],
+            out_specs=[HERE] * 2,
         ),
-        out_shape=jax.ShapeDtypeStruct((2, BLOCKS, BROWS, D), BF),
+        out_shape=[held(total, shape, BF)] * 2,
         compiler_params=params(total),
         cost_estimate=cost(2.6),
         name=f"attn_grad_{call}",
@@ -516,7 +508,7 @@
     return pl.pallas_call(
         lambda *refs: last_body(slots, *refs),
         grid=(1,),
-        in_specs=[full(a.shape) for a in (grad, wj, tok, gmid, g1)],
+        in_specs=[HERE, full(wj.shape), full(tok.shape), HERE, full(g1.shape)],
         out_specs=[full((total, D)), full((8, D))],
         out_shape=[
             jax.ShapeDtypeStruct((total, D), BF),
@@ -524,7 +516,7 @@
         ],
         scratch_shapes=[pltpu.VMEM((total, D), F32)],
         compiler_params=params(total),
-        cost_estimate=cost(5.6),
+        cost_estimate=cost(0.001),
         name="first_back",
     )(grad, wj, tok, gmid, g1)
 
@@ -566,48 +558,55 @@
         out_shape=[jax.ShapeDtypeStruct(shape, F32) for shape in ((FF, D), (D, FF))],
         input_output_aliases=aliases,
         compiler_params=params(),
-        cost_estimate=cost(3.2),
+        cost_estimate=cost(0.001),
         name=f"finish_mlp_{chunk}_{which}",
     )(*args)
 
 
-def finish_attn_body(ids_ref, a_ref, b_ref, *rest):
-    joined_ref, merge_ref = rest[-2:]
-    half = BLOCKS // 2
+def finish_attn_body(chunk, ids_ref, a_ref, b_ref, *rest):
     for ab, in_ref in enumerate((a_ref, b_ref)):
-        mask = ids_ref[ab]
-        for i in range(BLOCKS):
-            block = in_ref[i ^ mask].astype(F32)
-            third, k = 2 * ab + i // half, i % half
+        mask = ids_ref[ab] >> 1
+        for k in range(BLOCKS // 2):
+            block = in_ref[k ^ mask].astype(F32)
             rows = slice(k * BROWS, (k + 1) * BROWS)
-            if third < 3:
-                joined_ref[rows, third * D : (third + 1) * D] = block
+            if chunk == 2:
+                rest[-1][rows, ab * D : (ab + 1) * D] = block
             else:
-                merge_ref[rows, :] = block
-
-
-def finish_attn_call(which, ids, a, b, kept):
-    in_specs = [full(a.shape), full(b.shape)]
+                rest[ab - 2][rows, :] = block
+
+
+def finish_attn_call(chunk, which, ids, a, b, joined, merge):
+    half = (D // 2, D)
+    top = lambda ids: ids[3] ^ which
+    out_specs = [pl.BlockSpec((D // 2, 2 * D), lambda i, ids: (top(ids), 0))]
+    shapes = [(D, 3 * D)]
+    if chunk == 3:
+        out_specs = [
+            pl.BlockSpec(half, lambda i, ids: (top(ids), 2)),
+            pl.BlockSpec(half, lambda i, ids: (top(ids), 0)),
+        ]
+        shapes.append((D, D))
+    kept = [joined, merge][: len(shapes)]
+    aliases = {}
     args = [ids, a, b]
-    aliases = {}
-    if kept is not None:
-        in_specs += [pl.BlockSpec(memory_space=pl.ANY)] * 2
-        args += list(kept)
-        aliases = {3: 0, 4: 1}
-    place = lambda i, ids: (ids[3] ^ which, 0)
+    for at, value in enumerate(kept):
+        if value is not None:
+            aliases[len(args)] = at
+            args.append(value)
     return pl.pallas_call(
-        finish_attn_body,
+        lambda *refs: finish_attn_body(chunk, *refs),
         grid_spec=pltpu.PrefetchScalarGridSpec(
             num_scalar_prefetch=1,
             grid=(1,),
-            in_specs=in_specs,
-            out_specs=[pl.BlockSpec((D // 2, 3 * D), place), pl.BlockSpec((D // 2, D), place)],
+            in_specs=[full(a.shape), full(b.shape)]
+            + [pl.BlockSpec(memory_space=pl.ANY)] * (len(args) - 3),
+            out_specs=out_specs,
         ),
-        out_shape=[jax.ShapeDtypeStruct(s, F32) for s in ((D, 3 * D), (D, D))],
+        out_shape=[jax.ShapeDtypeStruct(s, F32) for s in shapes],
         input_output_aliases=aliases,
         compiler_params=params(),
-        cost_estimate=cost(4.2),
-        name=f"finish_attn_{which}",
+        cost_estimate=cost(0.001),
+        name=f"finish_attn_{chunk}_{which}",
     )(*args)
 
 
@@ -635,7 +634,7 @@
         out_specs=[full(s.shape) for s in shapes],
         out_shape=shapes,
         compiler_params=params(),
-        cost_estimate=cost(1),
+        cost_estimate=cost(0.001),
         name="finish_small",
     )(mine, got)
 
@@ -682,7 +681,6 @@
     def __init__(self, sums, chain):
         self.sums = sums
         self.chain = chain
-        self.down_at = 0
         self.small = None
 
     def first(self, send):
@@ -698,26 +696,38 @@
         self.chain.last = out
         self.got = [self.sums.swap(out[ab], self.sums.stage(ab, at)) for ab in range(2)]
 
-    def tail_down(self, small=None):
-        at = self.down_at
+    def tail(self, at, small=None):
+        rest = self.sums.rest
         got = self.chain.after(self.got)
         if at == 0:
             mine = jnp.stack([add(self.keep[ab], got[ab]) for ab in range(2)])
+            n = mine.shape[1] // 2
+            self.keep, out = mine[:, :n], mine[:, n:]
+            self.chain.last = out
+            self.got = self.sums.swap(out, rest[0])
+        elif at == 1:
+            mine = add(self.keep, got)
+            for stage in rest[1:-1]:
+                mine, out = self.sums.split_rows(stage, mine)
+                mine = add(mine, self.sums.swap(out, stage))
+            self.mine = self.chain.last = mine
+            self.small = small
+            self.up(mine, rest[-1])
+        elif at == 2:
+            self.mine = add(self.mine, got)
+            self.small_sum()
+            for stage in rest[-2:0:-1]:
+                self.up(self.mine, stage)
+                self.small_sum()
+                self.mine = self.sums.join_rows(stage, self.mine, self.got)
+            self.chain.last = self.mine
+            self.up(self.mine, rest[0])
         else:
-            mine = add(self.keep, got)
-        self.down_at += 1
-        if at < len(self.sums.rest):
-            self.keep, out = self.sums.tail_down(at, mine)
-            self.chain.last = out
-            self.got = self.sums.swap(out, self.sums.rest[at])
-            if len(self.sums.rest) > 2 and at >= 1 and at + 1 < len(self.sums.rest):
-                self.tail_down(small)
-            return
-        self.mine = mine
-        self.chain.last = mine
-        self.up_at = at
-        self.small = small
-        self.up(self.mine, self.sums.rest[at - 1])
+            self.mine = jnp.concatenate([self.mine, got], axis=1)
+            self.chain.last = self.mine
+            self.small_sum()
+            self.own = [self.mine[0], self.mine[1]]
+            self.ups([self.sums.stage(ab, 1) for ab in range(2)])
 
     def up(self, value, stage):
         if self.small is None:
@@ -735,29 +745,11 @@
         self.got = self.all[:-1].reshape(-1, D)[: value.size // D].reshape(value.shape)
 
     def small_sum(self):
-        other = self.all[-1, : self.rows.shape[0]]
-        self.small = join_small(self.rows) + join_small(other)
-
-    def tail_up(self):
-        at = self.up_at - 1
-        got = self.chain.after(self.got)
-        self.mine = self.sums.tail_up(at, self.mine, got)
-        self.chain.last = self.mine
-        self.up_at = at
         if self.small is not None:
-            self.small_sum()
-        if at:
-            self.up(self.mine, self.sums.rest[at - 1])
-            if at > 1:
-                self.tail_up()
-            return
-        self.own = [self.mine[0], self.mine[1]]
-        self.ups([self.sums.stage(ab, 1) for ab in range(2)])
+            other = self.all[-1, : self.rows.shape[0]]
+            self.small = join_small(self.rows) + join_small(other)
 
     def ups(self, stages):
-        if self.small is None:
-            self.got = [self.sums.swap(self.own[ab], stages[ab]) for ab in range(2)]
-            return
         self.up(self.own[0], stages[0])
         self.got = [self.got, self.sums.swap(self.own[1], stages[1])]
 
@@ -765,8 +757,7 @@
         got = self.chain.after(self.got)
         self.own = [jnp.concatenate([self.own[ab], got[ab]]) for ab in range(2)]
         self.chain.last = self.own
-        if self.small is not None:
-            self.small_sum()
+        self.small_sum()
         if at:
             self.ups([self.sums.stage(ab, at - 1) for ab in range(2)])
         else:
@@ -793,19 +784,14 @@
         )
         return add(*low), add(*high)
 
-    def tail_down(self, at, mine):
-        if at < 2:
-            n = mine.shape[1] // 2
-            return mine[:, :n], mine[:, n:]
+    def split_rows(self, stage, mine):
         n = mine.shape[2] // 2
-        high = bit_of(self.rest[at]) == 1
+        high = bit_of(stage) == 1
         low_rows, high_rows = mine[:, :, :n], mine[:, :, n:]
         return jnp.where(high, high_rows, low_rows), jnp.where(high, low_rows, high_rows)
 
-    def tail_up(self, at, mine, got):
-        if at < 2:
-            return jnp.concatenate([mine, got], axis=1)
-        high = bit_of(self.rest[at]) == 1
+    def join_rows(self, stage, mine, got):
+        high = bit_of(stage) == 1
         return jnp.concatenate([jnp.where(high, got, mine), jnp.where(high, mine, got)], axis=2)
 
 
@@ -849,9 +835,9 @@
         masks = []
         for two in (sums.pair, sums.pair[::-1]):
             mask = 0
-            for stage in list(two) + list(sums.rest[:2]):
+            for stage in list(two) + list(sums.rest[:1]):
                 mask = 2 * mask + bit_of(stage)
-            masks.append(mask)
+            masks.append(2 * mask)
         core = bit_of(sums.first)
         other = 1 - core
         ids = jnp.stack(
@@ -859,7 +845,6 @@
         ).astype(jnp.int32)
 
         normed, joined, probs, mix, middle, second, gout = first_call(
-            4,
             slots,
             counts,
             tok,
@@ -875,7 +860,7 @@
         )
         chain = Chain()
 
-        acts, ghs = [], []
+        acts, ghs = {}, {}
 
         def quarter(call):
             def step(ids):
@@ -884,37 +869,60 @@
                 )
 
             grad, act, gh = chain.run(step, ids)
-            acts.append(act)
-            ghs.append(gh)
+            acts[call], ghs[call] = act, gh
             return grad
 
         def collect(chunk, kept):
-            pick = slice(2 * chunk, 2 * chunk + 2)
+            pick = (2 * chunk, 2 * chunk + 1)
             return chain.run(
                 lambda ids: collect_call(
-                    chunk, ids, acts[pick], ghs[pick], down_weight, up_weight, kept
+                    chunk,
+                    ids,
+                    [acts[call] for call in pick],
+                    [ghs[call] for call in pick],
+                    down_weight,
+                    up_weight,
+                    kept,
                 ),
                 ids,
             )
 
-        def finish(chunk, which, kept):
+        done = {}
+
+        def finish(chunk, which):
             part = chunks[chunk].got if which else chunks[chunk].own
-            return chain.run(
-                lambda a: finish_mlp_call(chunk, which, ids, a, part[1], kept), part[0]
+            if chunk < 2:
+                done["mlp"] = chain.run(
+                    lambda a: finish_mlp_call(
+                        chunk, which, ids, a, part[1], done.get("mlp")
+                    ),
+                    part[0],
+                )
+                return
+            if chunk == 3 and which:
+                part = chunks[3].all, part[1]
+            out = chain.run(
+                lambda a: finish_attn_call(
+                    chunk, which, ids, a, part[1], done.get("joined"), done.get("merge")
+                ),
+                part[0],
             )
-
-        chunks = [Chunk(sums, chain) for _ in range(3)]
-        one, two, three = chunks
+            done["joined"] = out[0]
+            if chunk == 3:
+                done["merge"] = out[1]
+
+        chunks = [Chunk(sums, chain) for _ in range(4)]
+        one, two, three, four = chunks
         one.first(quarter(0))
-        keep = quarter(1)
+        keep1 = quarter(1)
+        send2 = quarter(2)
+        one.pair(0, keep1)
         kept = collect(0, None)
-        one.pair(0, keep)
-        send = quarter(2)
-        keep = quarter(3)
-        two.first(chain.after(send))
+        keep2 = quarter(3)
+        two.first(chain.after(send2))
         outer, g, small_a = collect(1, kept)
-        two.pair(0, keep)
         one.pair(1)
+        two.pair(0, keep2)
         result, gmid, branch, gmix, small_b = chain.run(
             lambda outer: middle_call(
                 slots, counts, outer, g, middle, gout, down_bias, second_gain, merge_weight
@@ -924,54 +932,62 @@
         grad_joined = chain.run(
             lambda gmix: attn_back_call(0, slots, joined, probs, gmix, None), gmix
         )
+        one.tail(0)
         grad_joined = chain.run(
             lambda gmix: attn_back_call(1, slots, joined, probs, gmix, grad_joined), gmix
         )
-        one.tail_down()
-        attn_grad = lambda call: chain.run(
-            lambda ids: attn_grad_call(call, ids, normed, mix, grad_joined, branch), ids
-        )
-        send = attn_grad(0)
+        send3, send4 = chain.run(
+            lambda ids: attn_grad_call(0, ids, normed, mix, grad_joined, branch), ids
+        )
+        four.first(chain.after(send4))
+        three.first(chain.after(send3))
         two.pair(1)
-        keep = attn_grad(1)
-        three.first(chain.after(send))
-        one.tail_down()
-        three.pair(0, keep)
-        two.tail_down()
-        one.tail_down()
-        two.tail_down()
-        one.tail_up()
+        one.tail(1)
+        keep3, keep4 = chain.run(
+            lambda ids: attn_grad_call(1, ids, normed, mix, grad_joined, branch), ids
+        )
+        three.pair(0, keep3)
+        two.tail(0)
+        four.pair(0, keep4)
+        one.tail(2)
+        two.tail(1)
         three.pair(1)
-        two.tail_down()
-        one.tail_up()
-        three.tail_down()
+        four.pair(1)
+        one.tail(3)
+        three.tail(0)
+        four.tail(0)
+        three.tail(1)
+        two.tail(2)
         one.pair_up(1)
-        two.tail_up()
-        three.tail_down()
+        three.tail(2)
         token_grad, small_c = chain.run(
             lambda grad: last_call(slots, grad, joined_weight, tok, gmid, first_gain),
             grad_joined,
         )
         small = jnp.concatenate([small_a, small_b, small_c[:4]], axis=0)
-        three.tail_down(small)
-        two.tail_up()
-        three.tail_up()
+        two.tail(3)
+        three.tail(3)
+        one.pair_up(0)
+        four.tail(1, small)
+        three.pair_up(1)
         two.pair_up(1)
-        three.tail_up()
-        one.pair_up(0)
-        mlp = finish(0, 0, None)
-        three.pair_up(1)
+        four.tail(2)
+        three.pair_up(0)
+        four.tail(3)
+        finish(0, 0)
+        finish(0, 1)
+        finish(2, 0)
+        four.pair_up(1)
         two.pair_up(0)
-        mlp = finish(0, 1, mlp)
-        mlp = finish(1, 0, mlp)
-        mlp = finish(1, 1, mlp)
-        three.pair_up(0)
-        attn = chain.run(
-            lambda a: finish_attn_call(0, ids, a, three.own[1], None), three.own[0]
-        )
-        small = finish_small_call(three.rows, three.all)
-        joined_grad, merge_grad = finish_attn_call(1, ids, three.all, three.got[1], attn)
-        down_grad, up_grad = mlp
+        finish(1, 0)
+        finish(2, 1)
+        four.pair_up(0)
+        finish(3, 0)
+        finish(1, 1)
+        small = finish_small_call(four.rows, four.all)
+        finish(3, 1)
+        joined_grad, merge_grad = done["joined"], done["merge"]
+        down_grad, up_grad = done["mlp"]
         return (
             result.reshape(tokens.shape),
             token_grad.reshape(tokens.shape),

time: 220 us -> 203 us (0.923)
  the two profiles are of different devices: /device:TPU:25 before, /device:TPU:0 now
where the time goes in v2:
time: 203 us; the launch traced here: 199 us
  Pallas kernels  86.4 us (43%)
  starting transfers between devices  50.2 us (25%)
  waiting for transfers between devices  48.2 us (24%)
  other arithmetic  10.7 us (5%)
    ppermute x56, starting transfers between devices, swap(): lax.ppermute(value, axis, [(i, i ^ 1 << bit) for i in range(self.sizes[ax...  50.2 us
    ppermute x56, waiting for transfers between devices, swap(): lax.ppermute(value, axis, [(i, i ^ 1 << bit) for i in range(self.sizes[ax...  48.2 us
    pallas_call x4, Pallas kernels, quarter_call(): pl.pallas_call(lambda *refs: quarter_body(2, *refs), grid_spec=pltpu.Pref...  17.1 us
    pallas_call x1, Pallas kernels, first_call(): pl.pallas_call(lambda *refs: first_body(slots, *refs), grid_spec=pltpu.Pr...  15.2 us
    pallas_call x4, Pallas kernels, finish_mlp_call(): pl.pallas_call(lambda *refs: finish_mlp_body(groups, *refs), grid_spec=pl...  12.4 us
    pallas_call x2, Pallas kernels, attn_back_call(): pl.pallas_call(lambda *refs: attn_back_body(slots, call, *refs[:3], refs[...  9.28 us
    pallas_call x2, Pallas kernels, collect_call(): pl.pallas_call(lambda *refs: collect_body(chunk, *refs), grid_spec=pltpu....  9.23 us
    pallas_call x4, Pallas kernels, finish_attn_call(): pl.pallas_call(lambda *refs: finish_attn_body(chunk, *refs), grid_spec=pl...  8.25 us
  transfers between devices with their start and end apart: 56, of which 15 were waited for; matrix products, arithmetic and copies ran while one was open for 5% of the time, Pallas kernels for 33%

profile of v2, /device:TPU:0, one launch (start us, length us, event | category | flops | bytes accessed | tf_op | source)
XLA Modules:
  0.0 199.0 jit_solution(12862777696936865765)
XLA Ops:
  0.8 15.2 %attn_fwd.1 = (bf16[640,768]{1,0:T(8,128)(2,1)S(1)}, bf16[640,2304]{1,0:T(8,128)(2,1)S(1)}, bf16[4,6,160,320]{3,2,1,0:T(8,128)(2,1)S(1)}, bf16[640,768]{1,0:T(8,...) custom-call(s32[4]{0:T(128)} %refs_0_.3, ...), custom_call_target="tpu_custom_call" | custom-call | flops 149999992832 | bytes 1000 | tf_op jit(solution)/shard_map/attn_fwd/pallas_call | solution.py:196
  16.0 4.3 %mlp_0.1 = (bf16[2,16,48,768]{3,2,1,0:T(8,128)(2,1)S(1)}, bf16[640,768]{1,0:T(8,128)(2,1)S(1)}, bf16[640,768]{1,0:T(8,128)(2,1)S(1)}) custom-call(s32[10]{0:T(128)S(1)} %stack.67.refs_0_.ids_ref, bf16[640,768]{1,0:T(8,128)(2,1)S(1)} %get-tuple-element.140.refs_1_, bf16[640,768]{1,0:T(8,128)(2,1)S(1)} %get-tuple-element.141.refs_2_.refs_4_, ...), custom_call_target="tpu_custom_call" | custom-call | flops 43000000512 | bytes 1000 | tf_op jit(solution)/shard_map/mlp_0/pallas_call | solution.py:248
  20.8 4.3 %mlp_1.1 = (bf16[2,16,48,768]{3,2,1,0:T(8,128)(2,1)S(1)}, bf16[640,768]{1,0:T(8,128)(2,1)S(1)}, bf16[640,768]{1,0:T(8,128)(2,1)S(1)}) custom-call(s32[10]{0:T(128)S(1)} %stack.67.refs_0_.ids_ref, bf16[640,768]{1,0:T(8,128)(2,1)S(1)} %get-tuple-element.140.refs_1_, bf16[640,768]{1,0:T(8,128)(2,1)S(1)} %get-tuple-element.141.refs_2_.refs_4_, ...), custom_call_target="tpu_custom_call" | custom-call | flops 43000000512 | bytes 1000 | tf_op jit(solution)/shard_map/mlp_1/pallas_call | solution.py:248
  25.7 4.3 %mlp_2.1 = (bf16[2,16,48,768]{3,2,1,0:T(8,128)(2,1)S(1)}, bf16[640,768]{1,0:T(8,128)(2,1)S(1)}, bf16[640,768]{1,0:T(8,128)(2,1)S(1)}) custom-call(s32[10]{0:T(128)S(1)} %stack.67.refs_0_.ids_ref, bf16[640,768]{1,0:T(8,128)(2,1)S(1)} %get-tuple-element.140.refs_1_, bf16[640,768]{1,0:T(8,128)(2,1)S(1)} %get-tuple-element.141.refs_2_.refs_4_, ...), custom_call_target="tpu_custom_call" | custom-call | flops 43000000512 | bytes 1000 | tf_op jit(solution)/shard_map/mlp_2/pallas_call | solution.py:248
  31.6 2.6 %collective-permute-start.3 = (bf16[8,48,768]{2,1,0:T(8,128)(2,1)S(1)}, bf16[8,48,768]{2,1,0:T(8,128)(2,1)S(1)}, u32[]{:S(2)}, u32[]{:S(2)}) collective-permute-start(bf16[8,48,768]{2,1,0:T(8,128)(2,1)S(1)} %get-tuple-element.272), channel_id=1, source_target_pairs={{0,4},{1,5},{2,6},{3,7},{4,0},{5,1},{6,2},{7,3},{8,12},{9,13},{10,... | collective-permute-start | bytes 1769480 | tf_op jit(solution)/shard_map/ppermute | solution.py:774
  34.2 1.5 collective-permute-start.2
  35.7 4.8 %mlp_collect_0.1 = (f32[640,768]{1,0:T(8,128)S(1)}, f32[640,768]{1,0:T(8,128)S(1)}, f32[4,768]{1,0:T(4,128)S(1)}) custom-call(s32[10]{0:T(128)S(1)} %stack.67.refs_0_.ids_ref, bf16[640,768]{1,0:T(8,128)(2,1)S(1)} %get-tuple-element.149.refs_1_, bf16[640,768]{1,0:T(8,128)(2,1)S(1)} %get-tuple-element.150.refs_2_, ...), custom_call_target="tpu_custom_call" | custom-call | flops 43000000512 | bytes 1000 | tf_op jit(solution)/shard_map/mlp_collect_0/pallas_call | solution.py:301
  40.5 4.3 %mlp_3.1 = (bf16[2,16,48,768]{3,2,1,0:T(8,128)(2,1)S(1)}, bf16[640,768]{1,0:T(8,128)(2,1)S(1)}, bf16[640,768]{1,0:T(8,128)(2,1)S(1)}) custom-call(s32[10]{0:T(128)S(1)} %stack.67.refs_0_.ids_ref, bf16[640,768]{1,0:T(8,128)(2,1)S(1)} %get-tuple-element.140.refs_1_, bf16[640,768]{1,0:T(8,128)(2,1)S(1)} %get-tuple-element.141.refs_2_.refs_4_, ...), custom_call_target="tpu_custom_call" | custom-call | flops 43000000512 | bytes 1000 | tf_op jit(solution)/shard_map/mlp_3/pallas_call | solution.py:248
  44.9 4.5 %mlp_collect_1.1 = (f32[640,768]{1,0:T(8,128)S(1)}, f32[640,768]{1,0:T(8,128)S(1)}, f32[4,768]{1,0:T(4,128)S(1)}) custom-call(s32[10]{0:T(128)S(1)} %stack.67.refs_0_.ids_ref, bf16[640,768]{1,0:T(8,128)(2,1)S(1)} %get-tuple-element.157.refs_1_, bf16[640,768]{1,0:T(8,128)(2,1)S(1)} %get-tuple-element.158.refs_2_, bf16[640,768]{1,0:T(8,128)(2,1)S(1)} %copy-done.11, ...), custom_call_target="tpu_custom_call" | custom-call | flops 43000000512 | bytes 1000 | tf_op jit(solution)/shard_map/mlp_collect_1/pallas_call | solution.py:301
  49.7 1.6 collective-permute-start.5
  52.0 1.8 add_convert_fusion
  53.8 1.5 collective-permute-start.8
  55.9 3.5 %mlp_back.1 = (bf16[640,768]{1,0:T(8,128)(2,1)}, f32[640,768]{1,0:T(8,128)S(1)}, bf16[640,768]{1,0:T(8,128)(2,1)S(1)}, bf16[640,768]{1,0:T(8,128)(2,1)S(1)}, f32[4,768]{1,0:T(4,128)S(1)}) custom-call(s32[4]{0:T(128)S(1)} %copy-done.9, f32[640,768]{1,0:T(8,128)S(1)} %get-tuple-element.168.refs_1_, f32[640,768]{1,0:T(8,128)S(1)} %get-tuple-element.169.refs_2_, ...), custom_call_target="tpu_custom_call" | custom-call | flops 35999997952 | bytes 1000 | tf_op jit(solution)/shard_map/mlp_back/pallas_call | solution.py:378
  59.4 4.6 %attn_bwd_0.1.refs_3_ = bf16[640,2304]{1,0:T(8,128)(2,1)S(1)} custom-call(bf16[640,2304]{1,0:T(8,128)(2,1)S(1)} %get-tuple-element.172.refs_0_, bf16[4,6,160,320]{3,2,1,0:T(8,128)(2,1)S(1)} %get-tuple-element.173.refs_1_, bf16[640,768]{1,0:T(8,128)(2,1)S(1)} %get-tuple-element.178.refs_2_), custom_call_target="tpu_custom_call" | custom-call | flops 54999998464 | bytes 1000 | tf_op jit(solution)/shard_map/attn_bwd_0/pallas_call | solution.py:433
  64.3 1.6 collective-permute-start.6
  65.9 4.7 %attn_bwd_1.1.grad_ref.refs_0_ = bf16[640,2304]{1,0:T(8,128)(2,1)S(1)} custom-call(bf16[640,2304]{1,0:T(8,128)(2,1)S(1)} %get-tuple-element.172.refs_0_, bf16[4,6,160,320]{3,2,1,0:T(8,128)(2,1)S(1)} %get-tuple-element.173.refs_1_, bf16[640,768]{1,0:T(8,128)(2,1)S(1)} %get-tuple-element.178.refs_2_, ...), custom_call_target="tpu_custom_call", output_to_operand_aliasing={{}: (3, {})} | custom-call | flops 54999998464 | bytes 1000 | tf_op jit(solution)/shard_map/attn_bwd_1/pallas_call | solution.py:433
  70.7 2.6 %attn_grad_0.1 = (bf16[2,8,48,768]{3,2,1,0:T(8,128)(2,1)S(1)}, bf16[2,8,48,768]{3,2,1,0:T(8,128)(2,1)S(1)}) custom-call(s32[10]{0:T(128)S(1)} %stack.67.refs_0_.ids_ref, bf16[640,768]{1,0:T(8,128)(2,1)S(1)} %get-tuple-element.180.normed_ref, bf16[640,768]{1,0:T(8,128)(2,1)S(1)} %get-tuple-element.181.mix_ref, ...), custom_call_target="tpu_custom_call" | custom-call | flops 25999998976 | bytes 1000 | tf_op jit(solution)/shard_map/attn_grad_0/pallas_call | solution.py:463
  76.1 2.7 %collective-permute-start.15 = (bf16[2,2,48,768]{3,2,1,0:T(8,128)(2,1)S(1)}, bf16[2,2,48,768]{3,2,1,0:T(8,128)(2,1)S(1)}, u32[]{:S(2)}, u32[]{:S(2)}) collective-permute-start(bf16[2,2,48,768]{3,2,1,0:T(8,128)(2,1)S(1)} %add_convert_fusion.21), channel_id=1, source_target_pairs={{0,16},{8,24},{16,0},{24,8},{1,17},{9,25},{17,1},{25,9},{2,18},{10... | collective-permute-start | bytes 884744 | tf_op jit(solution)/shard_map/ppermute | solution.py:774
  80.8 2.6 %attn_grad_1.1 = (bf16[2,8,48,768]{3,2,1,0:T(8,128)(2,1)S(1)}, bf16[2,8,48,768]{3,2,1,0:T(8,128)(2,1)S(1)}) custom-call(s32[10]{0:T(128)S(1)} %stack.67.refs_0_.ids_ref, bf16[640,768]{1,0:T(8,128)(2,1)S(1)} %get-tuple-element.180.normed_ref, bf16[640,768]{1,0:T(8,128)(2,1)S(1)} %get-tuple-element.181.mix_ref, ...), custom_call_target="tpu_custom_call" | custom-call | flops 25999998976 | bytes 1000 | tf_op jit(solution)/shard_map/attn_grad_1/pallas_call | solution.py:463
  83.7 1.6 collective-permute-start.11
  85.3 2.2 %collective-permute-done.13 = bf16[4,48,768]{2,1,0:T(8,128)(2,1)S(1)} collective-permute-done((bf16[4,48,768]{2,1,0:T(8,128)(2,1)S(1)}, bf16[4,48,768]{2,1,0:T(8,128)(2,1)S(1)}, u32[]{:S(2)}, u32[]{:S(2)}) %collective-permute-start.13) | collective-permute-done | bytes 294944 | tf_op jit(solution)/shard_map/ppermute | solution.py:774
  87.5 1.5 collective-permute-start.10
  94.5 5.5 %collective-permute-done.14 = bf16[2,2,48,768]{3,2,1,0:T(8,128)(2,1)S(1)} collective-permute-done((bf16[2,2,48,768]{3,2,1,0:T(8,128)(2,1)S(1)}, bf16[2,2,48,768]{3,2,1,0:T(8,128)(2,1)S(1)}, u32[]{:S(2)}, u32[]{:S(2)}) %collective-permute-start.14) | collective-permute-done | bytes 294944 | tf_op jit(solution)/shard_map/ppermute | solution.py:774
  101.9 1.6 collective-permute-start.18
  104.8 6.0 %collective-permute-done.19 = bf16[2,2,48,768]{3,2,1,0:T(8,128)(2,1)S(1)} collective-permute-done((bf16[2,2,48,768]{3,2,1,0:T(8,128)(2,1)S(1)}, bf16[2,2,48,768]{3,2,1,0:T(8,128)(2,1)S(1)}, u32[]{:S(2)}, u32[]{:S(2)}) %collective-permute-start.19) | collective-permute-done | bytes 294944 | tf_op jit(solution)/shard_map/ppermute | solution.py:774
  111.4 2.1 %collective-permute-start.27 = (bf16[4,48,768]{2,1,0:T(8,128)(2,1)S(1)}, bf16[4,48,768]{2,1,0:T(8,128)(2,1)S(1)}, u32[]{:S(2)}, u32[]{:S(2)}) collective-permute-start(bf16[4,48,768]{2,1,0:T(8,128)(2,1)S(1)} %get-tuple-element.284), channel_id=1, source_target_pairs={{0,2},{1,3},{2,0},{3,1},{4,6},{5,7},{6,4},{7,5},{8,10},{9,11},{10,... | collective-permute-start | bytes 884744 | tf_op jit(solution)/shard_map/ppermute | solution.py:774
  115.1 2.1 %collective-permute-done.23 = bf16[2,48,768]{2,1,0:T(8,128)(2,1)S(1)} collective-permute-done((bf16[2,48,768]{2,1,0:T(8,128)(2,1)S(1)}, bf16[2,48,768]{2,1,0:T(8,128)(2,1)S(1)}, u32[]{:S(2)}, u32[]{:S(2)}) %collective-permute-start.23) | collective-permute-done | bytes 147488 | tf_op jit(solution)/shard_map/ppermute | solution.py:774
  117.4 5.3 %collective-permute-done.22 = bf16[2,1,48,768]{3,2,1,0:T(8,128)(2,1)S(1)} collective-permute-done((bf16[2,1,48,768]{3,2,1,0:T(8,128)(2,1)S(1)}, bf16[2,1,48,768]{3,2,1,0:T(8,128)(2,1)S(1)}, u32[]{:S(2)}, u32[]{:S(2)}) %collective-permute-start.22) | collective-permute-done | bytes 147488 | tf_op jit(solution)/shard_map/ppermute | solution.py:774
  125.2 4.8 %collective-permute-done.25 = bf16[2,1,48,768]{3,2,1,0:T(8,128)(2,1)S(1)} collective-permute-done((bf16[2,1,48,768]{3,2,1,0:T(8,128)(2,1)S(1)}, bf16[2,1,48,768]{3,2,1,0:T(8,128)(2,1)S(1)}, u32[]{:S(2)}, u32[]{:S(2)}) %collective-permute-start.25) | collective-permute-done | bytes 147488 | tf_op jit(solution)/shard_map/ppermute | solution.py:774
  130.2 5.4 %first_back.1 = (bf16[640,768]{1,0:T(8,128)(2,1)}, f32[8,768]{1,0:T(8,128)S(1)}) custom-call(bf16[640,2304]{1,0:T(8,128)(2,1)S(1)} %attn_bwd_1.1.grad_ref.refs_0_, bf16[768,2304]{1,0:T(8,128)(2,1)S(1)} %copy-done, bf16[640,768]{1,0:T(8,128)(2,1)S(1)} %bitcast.184, f32[640,768]{1,0:T(8,128)S(1)} %get-tuple-element.214.refs_3_, f32[768]{0:T(1024)S(1)} %copy-done.2), custom_call_target="tpu_custom_call" | custom-call | flops 10000000 | bytes 1000 | tf_op jit(solution)/shard_map/first_back/pallas_call | solution.py:508
  136.9 2.0 %collective-permute-start.36 = (bf16[4,48,768]{2,1,0:T(8,128)(2,1)S(1)}, bf16[4,48,768]{2,1,0:T(8,128)(2,1)S(1)}, u32[]{:S(2)}, u32[]{:S(2)}) collective-permute-start(bf16[4,48,768]{2,1,0:T(8,128)(2,1)S(1)} %get-tuple-element.282), channel_id=1, source_target_pairs={{0,2},{1,3},{2,0},{3,1},{4,6},{5,7},{6,4},{7,5},{8,10},{9,11},{10,... | collective-permute-start | bytes 884744 | tf_op jit(solution)/shard_map/ppermute | solution.py:774
  141.2 2.0 collective-permute-start.34
  145.8 1.5 collective-permute-start.40
  147.5 7.2 %collective-permute-done.34 = bf16[3,48,768]{2,1,0:T(8,128)(2,1)S(1)} collective-permute-done((bf16[3,48,768]{2,1,0:T(8,128)(2,1)S(1)}, bf16[3,48,768]{2,1,0:T(8,128)(2,1)S(1)}, u32[]{:S(2)}, u32[]{:S(2)}) %collective-permute-start.34) | collective-permute-done | bytes 221216 | tf_op jit(solution)/shard_map/ppermute | solution.py:774
  155.1 6.8 %collective-permute-done.39 = bf16[3,48,768]{2,1,0:T(8,128)(2,1)S(1)} collective-permute-done((bf16[3,48,768]{2,1,0:T(8,128)(2,1)S(1)}, bf16[3,48,768]{2,1,0:T(8,128)(2,1)S(1)}, u32[]{:S(2)}, u32[]{:S(2)}) %collective-permute-start.39) | collective-permute-done | bytes 221216 | tf_op jit(solution)/shard_map/ppermute | solution.py:774
  162.2 1.5 collective-permute-start.42
  164.3 1.8 collective-permute-start.49
  166.0 3.1 %finish_mlp_0_0.1 = (f32[3072,768]{1,0:T(8,128)}, f32[768,3072]{1,0:T(8,128)}) custom-call(s32[10]{0:T(128)S(1)} %stack.67.refs_0_.ids_ref, bf16[16,48,768]{2,1,0:T(8,128)(2,1)S(1)} %pad_maximum_fusion.refs_1_, bf16[16,48,768]{2,1,0:T(8,128)(2,1)S(1)} %pad_maximum_fusion.1.refs_2_), custom_call_target="tpu_custom_call" | custom-call | flops 10000000 | bytes 1000 | tf_op jit(solution)/shard_map/finish_mlp_0_0/pallas_call | solution.py:550
  171.2 1.8 collective-permute-start.43
  173.1 3.1 %finish_mlp_0_1.1 = (f32[3072,768]{1,0:T(8,128)}, f32[768,3072]{1,0:T(8,128)}) custom-call(s32[10]{0:T(128)S(1)} %stack.67.refs_0_.ids_ref, bf16[16,48,768]{2,1,0:T(8,128)(2,1)S(1)} %collective-permute-done.44.refs_1_, bf16[16,48,768]{2,1,0:T(8,128)(2,1)S(1)} %collective-permute-done.45.refs_2_, ...), custom_call_target="tpu_custom_call", output_to_operand_aliasing={{0}: (3, {}), {1}: (4, {})} | custom-call | flops 10000000 | bytes 1000 | tf_op jit(solution)/shard_map/finish_mlp_0_1/pallas_call | solution.py:550
  176.2 2.1 %finish_attn_2_0.1.refs_3_ = f32[768,2304]{1,0:T(8,128)} custom-call(s32[10]{0:T(128)S(1)} %stack.67.refs_0_.ids_ref, bf16[8,48,768]{2,1,0:T(8,128)(2,1)S(1)} %pad_maximum_fusion.11.refs_1_, bf16[8,48,768]{2,1,0:T(8,128)(2,1)S(1)} %pad_maximum_fusion.12.refs_2_), custom_call_target="tpu_custom_call" | custom-call | flops 10000000 | bytes 1000 | tf_op jit(solution)/shard_map/finish_attn_2_0/pallas_call | solution.py:596
  178.3 3.0 %collective-permute-done.43 = bf16[2,48,768]{2,1,0:T(8,128)(2,1)S(1)} collective-permute-done((bf16[2,48,768]{2,1,0:T(8,128)(2,1)S(1)}, bf16[2,48,768]{2,1,0:T(8,128)(2,1)S(1)}, u32[]{:S(2)}, u32[]{:S(2)}) %collective-permute-start.43) | collective-permute-done | bytes 147488 | tf_op jit(solution)/shard_map/ppermute | solution.py:774
  181.4 1.8 collective-permute-start.46
  184.0 3.1 %finish_mlp_1_0.1 = (f32[3072,768]{1,0:T(8,128)}, f32[768,3072]{1,0:T(8,128)}) custom-call(s32[10]{0:T(128)S(1)} %stack.67.refs_0_.ids_ref, bf16[16,48,768]{2,1,0:T(8,128)(2,1)S(1)} %pad_maximum_fusion.2.refs_1_, bf16[16,48,768]{2,1,0:T(8,128)(2,1)S(1)} %pad_maximum_fusion.3.refs_2_, ...), custom_call_target="tpu_custom_call", output_to_operand_aliasing={{0}: (3, {}), {1}: (4, {})} | custom-call | flops 10000000 | bytes 1000 | tf_op jit(solution)/shard_map/finish_mlp_1_0/pallas_call | solution.py:550
  187.6 2.1 %finish_attn_2_1.1.refs_3_ = f32[768,2304]{1,0:T(8,128)} custom-call(s32[10]{0:T(128)S(1)} %stack.67.refs_0_.ids_ref, bf16[8,48,768]{2,1,0:T(8,128)(2,1)S(1)} %collective-permute-done.48.refs_1_, bf16[8,48,768]{2,1,0:T(8,128)(2,1)S(1)} %collective-permute-done.51.refs_2_, f32[768,2304]{1,0:T(8,128)} %finish_attn_2_0.1.refs_3_), custom_call_target="tpu_custom_call", output_to_operand_aliasing={{}: (3, {})} | custom-call | flops 10000000 | bytes 1000 | tf_op jit(solution)/shard_map/finish_attn_2_1/pallas_call | solution.py:596
  190.9 2.0 %finish_attn_3_0.1 = (f32[768,2304]{1,0:T(8,128)}, f32[768,768]{1,0:T(8,128)}) custom-call(s32[10]{0:T(128)S(1)} %stack.67.refs_0_.ids_ref, bf16[8,48,768]{2,1,0:T(8,128)(2,1)S(1)} %pad_maximum_fusion.13.refs_1_, bf16[8,48,768]{2,1,0:T(8,128)(2,1)S(1)} %pad_maximum_fusion.14.refs_2_, f32[768,2304]{1,0:T(8,128)} %finish_attn_2_1.1.refs_3_), custom_call_target="tpu_custom_call", output_to_operand_aliasing={{0}: (3, {})} | custom-call | flops 10000000 | bytes 1000 | tf_op jit(solution)/shard_map/finish_attn_3_0/pallas_call | solution.py:596
  193.7 3.1 %finish_mlp_1_1.1 = (f32[3072,768]{1,0:T(8,128)}, f32[768,3072]{1,0:T(8,128)}) custom-call(s32[10]{0:T(128)S(1)} %stack.67.refs_0_.ids_ref, bf16[16,48,768]{2,1,0:T(8,128)(2,1)S(1)} %collective-permute-done.53.refs_1_, bf16[16,48,768]{2,1,0:T(8,128)(2,1)S(1)} %collective-permute-done.54.refs_2_, ...), custom_call_target="tpu_custom_call", output_to_operand_aliasing={{0}: (3, {}), {1}: (4, {})} | custom-call | flops 10000000 | bytes 1000 | tf_op jit(solution)/shard_map/finish_mlp_1_1/pallas_call | solution.py:550
  196.8 2.0 %finish_attn_3_1.1 = (f32[768,2304]{1,0:T(8,128)}, f32[768,768]{1,0:T(8,128)}) custom-call(s32[10]{0:T(128)S(1)} %stack.67.refs_0_.ids_ref, bf16[9,48,768]{2,1,0:T(8,128)(2,1)S(1)} %collective-permute-done.52.got_ref.refs_1_, bf16[8,48,768]{2,1,0:T(8,128)(2,1)S(1)} %collective-permute-done.55.refs_2_, ...), custom_call_target="tpu_custom_call", output_to_operand_aliasing={{0}: (3, {}), {1}: (4, {})} | custom-call | flops 10000000 | bytes 1000 | tf_op jit(solution)/shard_map/finish_attn_3_1/pallas_call | solution.py:596
  (194 shorter events, 36.2 us)
Async XLA Ops:
  20.3 10.6 %collective-permute-start = (bf16[2,16,48,768]{3,2,1,0:T(8,128)(2,1)S(1)}, bf16[2,16,48,768]{3,2,1,0:T(8,128)(2,1)S(1)}, u32[]{:S(2)}, u32[]{:S(2)}) collective-permute-start(bf16[2,16,48,768]{3,2,1,0:T(8,128)(2,1)S(1)} %get-tuple-element.142), channel_id=1, source_target_pairs={{0,1},{1,0},{2,3},{3,2},{4,5},{5,4},{6,7},{7,6},{8,9},{9,8},{10,11... | collective-permute-start | bytes 7077896 | tf_op jit(solution)/shard_map/ppermute | solution.py:774
  31.6 17.8 %collective-permute-start.3 = (bf16[8,48,768]{2,1,0:T(8,128)(2,1)S(1)}, bf16[8,48,768]{2,1,0:T(8,128)(2,1)S(1)}, u32[]{:S(2)}, u32[]{:S(2)}) collective-permute-start(bf16[8,48,768]{2,1,0:T(8,128)(2,1)S(1)} %get-tuple-element.272), channel_id=1, source_target_pairs={{0,4},{1,5},{2,6},{3,7},{4,0},{5,1},{6,2},{7,3},{8,12},{9,13},{10,... | collective-permute-start | bytes 1769480 | tf_op jit(solution)/shard_map/ppermute | solution.py:774
  34.2 15.5 %collective-permute-start.2 = (bf16[8,48,768]{2,1,0:T(8,128)(2,1)S(1)}, bf16[8,48,768]{2,1,0:T(8,128)(2,1)S(1)}, u32[]{:S(2)}, u32[]{:S(2)}) collective-permute-start(bf16[8,48,768]{2,1,0:T(8,128)(2,1)S(1)} %get-tuple-element.273), channel_id=1, source_target_pairs={{0,2},{1,3},{2,0},{3,1},{4,6},{5,7},{6,4},{7,5},{8,10},{9,11},{10,... | collective-permute-start | bytes 1769480 | tf_op jit(solution)/shard_map/ppermute | solution.py:774
  44.8 7.2 %collective-permute-start.1 = (bf16[2,16,48,768]{3,2,1,0:T(8,128)(2,1)S(1)}, bf16[2,16,48,768]{3,2,1,0:T(8,128)(2,1)S(1)}, u32[]{:S(2)}, u32[]{:S(2)}) collective-permute-start(bf16[2,16,48,768]{3,2,1,0:T(8,128)(2,1)S(1)} %get-tuple-element.164), channel_id=1, source_target_pairs={{0,1},{1,0},{2,3},{3,2},{4,5},{5,4},{6,7},{7,6},{8,9},{9,8},{10,11... | collective-permute-start | bytes 7077896 | tf_op jit(solution)/shard_map/ppermute | solution.py:774
  49.7 14.3 %collective-permute-start.5 = (bf16[4,48,768]{2,1,0:T(8,128)(2,1)S(1)}, bf16[4,48,768]{2,1,0:T(8,128)(2,1)S(1)}, u32[]{:S(2)}, u32[]{:S(2)}) collective-permute-start(bf16[4,48,768]{2,1,0:T(8,128)(2,1)S(1)} %fusion.10), channel_id=1, source_target_pairs={{0,2},{1,3},{2,0},{3,1},{4,6},{5,7},{6,4},{7,5},{8,10},{9,11},{10,... | collective-permute-start | bytes 884744 | tf_op jit(solution)/shard_map/ppermute | solution.py:774
  51.4 12.6 %collective-permute-start.4 = (bf16[4,48,768]{2,1,0:T(8,128)(2,1)S(1)}, bf16[4,48,768]{2,1,0:T(8,128)(2,1)S(1)}, u32[]{:S(2)}, u32[]{:S(2)}) collective-permute-start(bf16[4,48,768]{2,1,0:T(8,128)(2,1)S(1)} %fusion.11), channel_id=1, source_target_pairs={{0,4},{1,5},{2,6},{3,7},{4,0},{5,1},{6,2},{7,3},{8,12},{9,13},{10,... | collective-permute-start | bytes 884744 | tf_op jit(solution)/shard_map/ppermute | solution.py:774
  53.8 20.1 %collective-permute-start.8 = (bf16[8,48,768]{2,1,0:T(8,128)(2,1)}, bf16[8,48,768]{2,1,0:T(8,128)(2,1)}, u32[]{:S(2)}, u32[]{:S(2)}) collective-permute-start(bf16[8,48,768]{2,1,0:T(8,128)(2,1)} %get-tuple-element.268), channel_id=1, source_target_pairs={{0,4},{1,5},{2,6},{3,7},{4,0},{5,1},{6,2},{7,3},{8,12},{9,13},{10,... | collective-permute-start | bytes 1769480 | tf_op jit(solution)/shard_map/ppermute | solution.py:774
  55.3 18.6 %collective-permute-start.7 = (bf16[8,48,768]{2,1,0:T(8,128)(2,1)}, bf16[8,48,768]{2,1,0:T(8,128)(2,1)}, u32[]{:S(2)}, u32[]{:S(2)}) collective-permute-start(bf16[8,48,768]{2,1,0:T(8,128)(2,1)} %get-tuple-element.269), channel_id=1, source_target_pairs={{0,2},{1,3},{2,0},{3,1},{4,6},{5,7},{6,4},{7,5},{8,10},{9,11},{10,... | collective-permute-start | bytes 1769480 | tf_op jit(solution)/shard_map/ppermute | solution.py:774
  64.3 11.7 %collective-permute-start.6 = (bf16[2,2,48,768]{3,2,1,0:T(8,128)(2,1)S(1)}, bf16[2,2,48,768]{3,2,1,0:T(8,128)(2,1)S(1)}, u32[]{:S(2)}, u32[]{:S(2)}) collective-permute-start(bf16[2,2,48,768]{3,2,1,0:T(8,128)(2,1)S(1)} %fusion.21), channel_id=1, source_target_pairs={{0,8},{8,0},{16,24},{24,16},{1,9},{9,1},{17,25},{25,17},{2,10},{10... | collective-permute-start | bytes 884744 | tf_op jit(solution)/shard_map/ppermute | solution.py:774
  73.3 10.1 %collective-permute-start.9 = (bf16[2,8,48,768]{3,2,1,0:T(8,128)(2,1)S(1)}, bf16[2,8,48,768]{3,2,1,0:T(8,128)(2,1)S(1)}, u32[]{:S(2)}, u32[]{:S(2)}) collective-permute-start(bf16[2,8,48,768]{3,2,1,0:T(8,128)(2,1)S(1)} %get-tuple-element.189), channel_id=1, source_target_pairs={{0,1},{1,0},{2,3},{3,2},{4,5},{5,4},{6,7},{7,6},{8,9},{9,8},{10,11... | collective-permute-start | bytes 3538952 | tf_op jit(solution)/shard_map/ppermute | solution.py:774
  73.4 19.5 %collective-permute-start.16 = (bf16[2,8,48,768]{3,2,1,0:T(8,128)(2,1)S(1)}, bf16[2,8,48,768]{3,2,1,0:T(8,128)(2,1)S(1)}, u32[]{:S(2)}, u32[]{:S(2)}) collective-permute-start(bf16[2,8,48,768]{3,2,1,0:T(8,128)(2,1)S(1)} %get-tuple-element.195), channel_id=1, source_target_pairs={{0,1},{1,0},{2,3},{3,2},{4,5},{5,4},{6,7},{7,6},{8,9},{9,8},{10,11... | collective-permute-start | bytes 3538952 | tf_op jit(solution)/shard_map/ppermute | solution.py:774
  76.1 17.7 %collective-permute-start.15 = (bf16[2,2,48,768]{3,2,1,0:T(8,128)(2,1)S(1)}, bf16[2,2,48,768]{3,2,1,0:T(8,128)(2,1)S(1)}, u32[]{:S(2)}, u32[]{:S(2)}) collective-permute-start(bf16[2,2,48,768]{3,2,1,0:T(8,128)(2,1)S(1)} %add_convert_fusion.21), channel_id=1, source_target_pairs={{0,16},{8,24},{16,0},{24,8},{1,17},{9,25},{17,1},{25,9},{2,18},{10... | collective-permute-start | bytes 884744 | tf_op jit(solution)/shard_map/ppermute | solution.py:774
  78.8 8.7 %collective-permute-start.13 = (bf16[4,48,768]{2,1,0:T(8,128)(2,1)S(1)}, bf16[4,48,768]{2,1,0:T(8,128)(2,1)S(1)}, u32[]{:S(2)}, u32[]{:S(2)}) collective-permute-start(bf16[4,48,768]{2,1,0:T(8,128)(2,1)S(1)} %fusion.6), channel_id=1, source_target_pairs={{0,2},{1,3},{2,0},{3,1},{4,6},{5,7},{6,4},{7,5},{8,10},{9,11},{10,... | collective-permute-start | bytes 884744 | tf_op jit(solution)/shard_map/ppermute | solution.py:774
  80.3 9.9 %collective-permute-start.12 = (bf16[4,48,768]{2,1,0:T(8,128)(2,1)S(1)}, bf16[4,48,768]{2,1,0:T(8,128)(2,1)S(1)}, u32[]{:S(2)}, u32[]{:S(2)}) collective-permute-start(bf16[4,48,768]{2,1,0:T(8,128)(2,1)S(1)} %fusion.7), channel_id=1, source_target_pairs={{0,4},{1,5},{2,6},{3,7},{4,0},{5,1},{6,2},{7,3},{8,12},{9,13},{10,... | collective-permute-start | bytes 884744 | tf_op jit(solution)/shard_map/ppermute | solution.py:774
  83.7 16.8 %collective-permute-start.11 = (bf16[4,48,768]{2,1,0:T(8,128)(2,1)S(1)}, bf16[4,48,768]{2,1,0:T(8,128)(2,1)S(1)}, u32[]{:S(2)}, u32[]{:S(2)}) collective-permute-start(bf16[4,48,768]{2,1,0:T(8,128)(2,1)S(1)} %get-tuple-element.279), channel_id=1, source_target_pairs={{0,4},{1,5},{2,6},{3,7},{4,0},{5,1},{6,2},{7,3},{8,12},{9,13},{10,... | collective-permute-start | bytes 884744 | tf_op jit(solution)/shard_map/ppermute | solution.py:774
  87.5 14.4 %collective-permute-start.10 = (bf16[4,48,768]{2,1,0:T(8,128)(2,1)S(1)}, bf16[4,48,768]{2,1,0:T(8,128)(2,1)S(1)}, u32[]{:S(2)}, u32[]{:S(2)}) collective-permute-start(bf16[4,48,768]{2,1,0:T(8,128)(2,1)S(1)} %get-tuple-element.280), channel_id=1, source_target_pairs={{0,2},{1,3},{2,0},{3,1},{4,6},{5,7},{6,4},{7,5},{8,10},{9,11},{10,... | collective-permute-start | bytes 884744 | tf_op jit(solution)/shard_map/ppermute | solution.py:774
  92.4 7.6 %collective-permute-start.14 = (bf16[2,2,48,768]{3,2,1,0:T(8,128)(2,1)S(1)}, bf16[2,2,48,768]{3,2,1,0:T(8,128)(2,1)S(1)}, u32[]{:S(2)}, u32[]{:S(2)}) collective-permute-start(bf16[2,2,48,768]{3,2,1,0:T(8,128)(2,1)S(1)} %pad_maximum_fusion.18), channel_id=1, source_target_pairs={{0,8},{8,0},{16,24},{24,16},{1,9},{9,1},{17,25},{25,17},{2,10},{10... | collective-permute-start | bytes 884744 | tf_op jit(solution)/shard_map/ppermute | solution.py:774
  93.2 10.3 %collective-permute-start.21 = (bf16[4,48,768]{2,1,0:T(8,128)(2,1)S(1)}, bf16[4,48,768]{2,1,0:T(8,128)(2,1)S(1)}, u32[]{:S(2)}, u32[]{:S(2)}) collective-permute-start(bf16[4,48,768]{2,1,0:T(8,128)(2,1)S(1)} %get-tuple-element.276), channel_id=1, source_target_pairs={{0,4},{1,5},{2,6},{3,7},{4,0},{5,1},{6,2},{7,3},{8,12},{9,13},{10,... | collective-permute-start | bytes 884744 | tf_op jit(solution)/shard_map/ppermute | solution.py:774
  93.8 10.3 %collective-permute-start.20 = (bf16[4,48,768]{2,1,0:T(8,128)(2,1)S(1)}, bf16[4,48,768]{2,1,0:T(8,128)(2,1)S(1)}, u32[]{:S(2)}, u32[]{:S(2)}) collective-permute-start(bf16[4,48,768]{2,1,0:T(8,128)(2,1)S(1)} %get-tuple-element.277), channel_id=1, source_target_pairs={{0,2},{1,3},{2,0},{3,1},{4,6},{5,7},{6,4},{7,5},{8,10},{9,11},{10,... | collective-permute-start | bytes 884744 | tf_op jit(solution)/shard_map/ppermute | solution.py:774
  100.0 10.8 %collective-permute-start.19 = (bf16[2,2,48,768]{3,2,1,0:T(8,128)(2,1)S(1)}, bf16[2,2,48,768]{3,2,1,0:T(8,128)(2,1)S(1)}, u32[]{:S(2)}, u32[]{:S(2)}) collective-permute-start(bf16[2,2,48,768]{3,2,1,0:T(8,128)(2,1)S(1)} %add_convert_fusion.13), channel_id=1, source_target_pairs={{0,8},{8,0},{16,24},{24,16},{1,9},{9,1},{17,25},{25,17},{2,10},{10... | collective-permute-start | bytes 884744 | tf_op jit(solution)/shard_map/ppermute | solution.py:774
  100.5 22.3 %collective-permute-start.28 = (bf16[2,2,48,768]{3,2,1,0:T(8,128)(2,1)S(1)}, bf16[2,2,48,768]{3,2,1,0:T(8,128)(2,1)S(1)}, u32[]{:S(2)}, u32[]{:S(2)}) collective-permute-start(bf16[2,2,48,768]{3,2,1,0:T(8,128)(2,1)S(1)} %add_convert_fusion.12), channel_id=1, source_target_pairs={{0,16},{8,24},{16,0},{24,8},{1,17},{9,25},{17,1},{25,9},{2,18},{10... | collective-permute-start | bytes 884744 | tf_op jit(solution)/shard_map/ppermute | solution.py:774
  101.9 9.4 %collective-permute-start.18 = (bf16[2,48,768]{2,1,0:T(8,128)(2,1)S(1)}, bf16[2,48,768]{2,1,0:T(8,128)(2,1)S(1)}, u32[]{:S(2)}, u32[]{:S(2)}) collective-permute-start(bf16[2,48,768]{2,1,0:T(8,128)(2,1)S(1)} %fusion.35), channel_id=1, source_target_pairs={{0,2},{1,3},{2,0},{3,1},{4,6},{5,7},{6,4},{7,5},{8,10},{9,11},{10,... | collective-permute-start | bytes 442376 | tf_op jit(solution)/shard_map/ppermute | solution.py:774
  103.6 9.9 %collective-permute-start.17 = (bf16[2,48,768]{2,1,0:T(8,128)(2,1)S(1)}, bf16[2,48,768]{2,1,0:T(8,128)(2,1)S(1)}, u32[]{:S(2)}, u32[]{:S(2)}) collective-permute-start(bf16[2,48,768]{2,1,0:T(8,128)(2,1)S(1)} %fusion.36), channel_id=1, source_target_pairs={{0,4},{1,5},{2,6},{3,7},{4,0},{5,1},{6,2},{7,3},{8,12},{9,13},{10,... | collective-permute-start | bytes 442376 | tf_op jit(solution)/shard_map/ppermute | solution.py:774
  104.2 10.8 %collective-permute-start.24 = (bf16[2,48,768]{2,1,0:T(8,128)(2,1)S(1)}, bf16[2,48,768]{2,1,0:T(8,128)(2,1)S(1)}, u32[]{:S(2)}, u32[]{:S(2)}) collective-permute-start(bf16[2,48,768]{2,1,0:T(8,128)(2,1)S(1)} %fusion.33), channel_id=1, source_target_pairs={{0,2},{1,3},{2,0},{3,1},{4,6},{5,7},{6,4},{7,5},{8,10},{9,11},{10,... | collective-permute-start | bytes 442376 | tf_op jit(solution)/shard_map/ppermute | solution.py:774
  111.4 12.3 %collective-permute-start.27 = (bf16[4,48,768]{2,1,0:T(8,128)(2,1)S(1)}, bf16[4,48,768]{2,1,0:T(8,128)(2,1)S(1)}, u32[]{:S(2)}, u32[]{:S(2)}) collective-permute-start(bf16[4,48,768]{2,1,0:T(8,128)(2,1)S(1)} %get-tuple-element.284), channel_id=1, source_target_pairs={{0,2},{1,3},{2,0},{3,1},{4,6},{5,7},{6,4},{7,5},{8,10},{9,11},{10,... | collective-permute-start | bytes 884744 | tf_op jit(solution)/shard_map/ppermute | solution.py:774
  113.5 10.2 %collective-permute-start.26 = (bf16[4,48,768]{2,1,0:T(8,128)(2,1)S(1)}, bf16[4,48,768]{2,1,0:T(8,128)(2,1)S(1)}, u32[]{:S(2)}, u32[]{:S(2)}) collective-permute-start(bf16[4,48,768]{2,1,0:T(8,128)(2,1)S(1)} %get-tuple-element.285), channel_id=1, source_target_pairs={{0,4},{1,5},{2,6},{3,7},{4,0},{5,1},{6,2},{7,3},{8,12},{9,13},{10,... | collective-permute-start | bytes 884744 | tf_op jit(solution)/shard_map/ppermute | solution.py:774
  115.0 7.7 %collective-permute-start.22 = (bf16[2,1,48,768]{3,2,1,0:T(8,128)(2,1)S(1)}, bf16[2,1,48,768]{3,2,1,0:T(8,128)(2,1)S(1)}, u32[]{:S(2)}, u32[]{:S(2)}) collective-permute-start(bf16[2,1,48,768]{3,2,1,0:T(8,128)(2,1)S(1)} %pad_maximum_fusion.27), channel_id=1, source_target_pairs={{0,8},{8,0},{16,24},{24,16},{1,9},{9,1},{17,25},{25,17},{2,10},{10... | collective-permute-start | bytes 442376 | tf_op jit(solution)/shard_map/ppermute | solution.py:774
  117.3 23.0 %collective-permute-start.29 = (bf16[2,1,48,768]{3,2,0,1:T(8,128)(2,1)S(1)}, bf16[2,1,48,768]{3,2,0,1:T(8,128)(2,1)S(1)}, u32[]{:S(2)}, u32[]{:S(2)}) collective-permute-start(bf16[2,1,48,768]{3,2,0,1:T(8,128)(2,1)S(1)} %fusion.42), channel_id=1, source_target_pairs={{0,8},{8,0},{16,24},{24,16},{1,9},{9,1},{17,25},{25,17},{2,10},{10... | collective-permute-start | bytes 442376 | tf_op jit(solution)/shard_map/ppermute | solution.py:774
  122.8 7.2 %collective-permute-start.25 = (bf16[2,1,48,768]{3,2,1,0:T(8,128)(2,1)S(1)}, bf16[2,1,48,768]{3,2,1,0:T(8,128)(2,1)S(1)}, u32[]{:S(2)}, u32[]{:S(2)}) collective-permute-start(bf16[2,1,48,768]{3,2,1,0:T(8,128)(2,1)S(1)} %add_convert_fusion.27), channel_id=1, source_target_pairs={{0,16},{8,24},{16,0},{24,8},{1,17},{9,25},{17,1},{25,9},{2,18},{10... | collective-permute-start | bytes 442376 | tf_op jit(solution)/shard_map/ppermute | solution.py:774
  123.0 12.7 %collective-permute-start.33 = (bf16[2,2,48,768]{3,2,1,0:T(8,128)(2,1)S(1)}, bf16[2,2,48,768]{3,2,1,0:T(8,128)(2,1)S(1)}, u32[]{:S(2)}, u32[]{:S(2)}) collective-permute-start(bf16[2,2,48,768]{3,2,1,0:T(8,128)(2,1)S(1)} %add_convert_fusion.8), channel_id=1, source_target_pairs={{0,8},{8,0},{16,24},{24,16},{1,9},{9,1},{17,25},{25,17},{2,10},{10... | collective-permute-start | bytes 884744 | tf_op jit(solution)/shard_map/ppermute | solution.py:774
  123.8 13.1 %collective-permute-start.31 = (bf16[8,48,768]{2,1,0:T(8,128)(2,1)S(1)}, bf16[8,48,768]{2,1,0:T(8,128)(2,1)S(1)}, u32[]{:S(2)}, u32[]{:S(2)}) collective-permute-start(bf16[8,48,768]{2,1,0:T(8,128)(2,1)S(1)} %pad_maximum_fusion.8), channel_id=1, source_target_pairs={{0,4},{1,5},{2,6},{3,7},{4,0},{5,1},{6,2},{7,3},{8,12},{9,13},{10,... | collective-permute-start | bytes 1769480 | tf_op jit(solution)/shard_map/ppermute | solution.py:774
  124.3 14.6 %collective-permute-start.30 = (bf16[8,48,768]{2,1,0:T(8,128)(2,1)S(1)}, bf16[8,48,768]{2,1,0:T(8,128)(2,1)S(1)}, u32[]{:S(2)}, u32[]{:S(2)}) collective-permute-start(bf16[8,48,768]{2,1,0:T(8,128)(2,1)S(1)} %pad_maximum_fusion.7), channel_id=1, source_target_pairs={{0,2},{1,3},{2,0},{3,1},{4,6},{5,7},{6,4},{7,5},{8,10},{9,11},{10,... | collective-permute-start | bytes 1769480 | tf_op jit(solution)/shard_map/ppermute | solution.py:774
  136.9 7.5 %collective-permute-start.36 = (bf16[4,48,768]{2,1,0:T(8,128)(2,1)S(1)}, bf16[4,48,768]{2,1,0:T(8,128)(2,1)S(1)}, u32[]{:S(2)}, u32[]{:S(2)}) collective-permute-start(bf16[4,48,768]{2,1,0:T(8,128)(2,1)S(1)} %get-tuple-element.282), channel_id=1, source_target_pairs={{0,2},{1,3},{2,0},{3,1},{4,6},{5,7},{6,4},{7,5},{8,10},{9,11},{10,... | collective-permute-start | bytes 884744 | tf_op jit(solution)/shard_map/ppermute | solution.py:774
  138.9 6.9 %collective-permute-start.35 = (bf16[4,48,768]{2,1,0:T(8,128)(2,1)S(1)}, bf16[4,48,768]{2,1,0:T(8,128)(2,1)S(1)}, u32[]{:S(2)}, u32[]{:S(2)}) collective-permute-start(bf16[4,48,768]{2,1,0:T(8,128)(2,1)S(1)} %get-tuple-element.283), channel_id=1, source_target_pairs={{0,4},{1,5},{2,6},{3,7},{4,0},{5,1},{6,2},{7,3},{8,12},{9,13},{10,... | collective-permute-start | bytes 884744 | tf_op jit(solution)/shard_map/ppermute | solution.py:774
  140.3 30.4 %collective-permute-start.45 = (bf16[16,48,768]{2,1,0:T(8,128)(2,1)S(1)}, bf16[16,48,768]{2,1,0:T(8,128)(2,1)S(1)}, u32[]{:S(2)}, u32[]{:S(2)}) collective-permute-start(bf16[16,48,768]{2,1,0:T(8,128)(2,1)S(1)} %pad_maximum_fusion.1.refs_2_), channel_id=1, source_target_pairs={{0,1},{1,0},{2,3},{3,2},{4,5},{5,4},{6,7},{7,6},{8,9},{9,8},{10,11... | collective-permute-start | bytes 3538952 | tf_op jit(solution)/shard_map/ppermute | solution.py:774
  141.2 30.0 %collective-permute-start.44 = (bf16[16,48,768]{2,1,0:T(8,128)(2,1)S(1)}, bf16[16,48,768]{2,1,0:T(8,128)(2,1)S(1)}, u32[]{:S(2)}, u32[]{:S(2)}) collective-permute-start(bf16[16,48,768]{2,1,0:T(8,128)(2,1)S(1)} %pad_maximum_fusion.refs_1_), channel_id=1, source_target_pairs={{0,1},{1,0},{2,3},{3,2},{4,5},{5,4},{6,7},{7,6},{8,9},{9,8},{10,11... | collective-permute-start | bytes 3538952 | tf_op jit(solution)/shard_map/ppermute | solution.py:774
  141.2 13.5 %collective-permute-start.34 = (bf16[3,48,768]{2,1,0:T(8,128)(2,1)S(1)}, bf16[3,48,768]{2,1,0:T(8,128)(2,1)S(1)}, u32[]{:S(2)}, u32[]{:S(2)}) collective-permute-start(bf16[3,48,768]{2,1,0:T(8,128)(2,1)S(1)} %pad_maximum_fusion.23), channel_id=1, source_target_pairs={{0,16},{8,24},{16,0},{24,8},{1,17},{9,25},{17,1},{25,9},{2,18},{10... | collective-permute-start | bytes 663560 | tf_op jit(solution)/shard_map/ppermute | solution.py:774
  144.3 10.7 %collective-permute-start.41 = (bf16[4,48,768]{2,1,0:T(8,128)(2,1)S(1)}, bf16[4,48,768]{2,1,0:T(8,128)(2,1)S(1)}, u32[]{:S(2)}, u32[]{:S(2)}) collective-permute-start(bf16[4,48,768]{2,1,0:T(8,128)(2,1)S(1)} %pad_maximum_fusion.21), channel_id=1, source_target_pairs={{0,4},{1,5},{2,6},{3,7},{4,0},{5,1},{6,2},{7,3},{8,12},{9,13},{10,... | collective-permute-start | bytes 884744 | tf_op jit(solution)/shard_map/ppermute | solution.py:774
  145.8 9.2 %collective-permute-start.40 = (bf16[4,48,768]{2,1,0:T(8,128)(2,1)S(1)}, bf16[4,48,768]{2,1,0:T(8,128)(2,1)S(1)}, u32[]{:S(2)}, u32[]{:S(2)}) collective-permute-start(bf16[4,48,768]{2,1,0:T(8,128)(2,1)S(1)} %pad_maximum_fusion.20), channel_id=1, source_target_pairs={{0,2},{1,3},{2,0},{3,1},{4,6},{5,7},{6,4},{7,5},{8,10},{9,11},{10,... | collective-permute-start | bytes 884744 | tf_op jit(solution)/shard_map/ppermute | solution.py:774
  154.9 7.1 %collective-permute-start.39 = (bf16[3,48,768]{2,1,0:T(8,128)(2,1)S(1)}, bf16[3,48,768]{2,1,0:T(8,128)(2,1)S(1)}, u32[]{:S(2)}, u32[]{:S(2)}) collective-permute-start(bf16[3,48,768]{2,1,0:T(8,128)(2,1)S(1)} %pad_maximum_fusion.24), channel_id=1, source_target_pairs={{0,8},{8,0},{16,24},{24,16},{1,9},{9,1},{17,25},{25,17},{2,10},{10... | collective-permute-start | bytes 663560 | tf_op jit(solution)/shard_map/ppermute | solution.py:774
  162.2 8.4 %collective-permute-start.42 = (bf16[3,48,768]{2,1,0:T(8,128)(2,1)S(1)}, bf16[3,48,768]{2,1,0:T(8,128)(2,1)S(1)}, u32[]{:S(2)}, u32[]{:S(2)}) collective-permute-start(bf16[3,48,768]{2,1,0:T(8,128)(2,1)S(1)} %pad_maximum_fusion.25), channel_id=1, source_target_pairs={{0,4},{1,5},{2,6},{3,7},{4,0},{5,1},{6,2},{7,3},{8,12},{9,13},{10,... | collective-permute-start | bytes 663560 | tf_op jit(solution)/shard_map/ppermute | solution.py:774
  163.7 19.5 %collective-permute-start.50 = (bf16[8,48,768]{2,1,0:T(8,128)(2,1)S(1)}, bf16[8,48,768]{2,1,0:T(8,128)(2,1)S(1)}, u32[]{:S(2)}, u32[]{:S(2)}) collective-permute-start(bf16[8,48,768]{2,1,0:T(8,128)(2,1)S(1)} %pad_maximum_fusion.10), channel_id=1, source_target_pairs={{0,4},{1,5},{2,6},{3,7},{4,0},{5,1},{6,2},{7,3},{8,12},{9,13},{10,... | collective-permute-start | bytes 1769480 | tf_op jit(solution)/shard_map/ppermute | solution.py:774
  164.3 19.4 %collective-permute-start.49 = (bf16[8,48,768]{2,1,0:T(8,128)(2,1)S(1)}, bf16[8,48,768]{2,1,0:T(8,128)(2,1)S(1)}, u32[]{:S(2)}, u32[]{:S(2)}) collective-permute-start(bf16[8,48,768]{2,1,0:T(8,128)(2,1)S(1)} %pad_maximum_fusion.9), channel_id=1, source_target_pairs={{0,2},{1,3},{2,0},{3,1},{4,6},{5,7},{6,4},{7,5},{8,10},{9,11},{10,... | collective-permute-start | bytes 1769480 | tf_op jit(solution)/shard_map/ppermute | solution.py:774
  170.6 17.0 %collective-permute-start.51 = (bf16[8,48,768]{2,1,0:T(8,128)(2,1)S(1)}, bf16[8,48,768]{2,1,0:T(8,128)(2,1)S(1)}, u32[]{:S(2)}, u32[]{:S(2)}) collective-permute-start(bf16[8,48,768]{2,1,0:T(8,128)(2,1)S(1)} %pad_maximum_fusion.12.refs_2_), channel_id=1, source_target_pairs={{0,1},{1,0},{2,3},{3,2},{4,5},{5,4},{6,7},{7,6},{8,9},{9,8},{10,11... | collective-permute-start | bytes 1769480 | tf_op jit(solution)/shard_map/ppermute | solution.py:774
  170.7 16.4 %collective-permute-start.48 = (bf16[8,48,768]{2,1,0:T(8,128)(2,1)S(1)}, bf16[8,48,768]{2,1,0:T(8,128)(2,1)S(1)}, u32[]{:S(2)}, u32[]{:S(2)}) collective-permute-start(bf16[8,48,768]{2,1,0:T(8,128)(2,1)S(1)} %pad_maximum_fusion.11.refs_1_), channel_id=1, source_target_pairs={{0,1},{1,0},{2,3},{3,2},{4,5},{5,4},{6,7},{7,6},{8,9},{9,8},{10,11... | collective-permute-start | bytes 1769480 | tf_op jit(solution)/shard_map/ppermute | solution.py:774
  171.2 10.1 %collective-permute-start.43 = (bf16[2,48,768]{2,1,0:T(8,128)(2,1)S(1)}, bf16[2,48,768]{2,1,0:T(8,128)(2,1)S(1)}, u32[]{:S(2)}, u32[]{:S(2)}) collective-permute-start(bf16[2,48,768]{2,1,0:T(8,128)(2,1)S(1)} %get-tuple-element.288), channel_id=1, source_target_pairs={{0,2},{1,3},{2,0},{3,1},{4,6},{5,7},{6,4},{7,5},{8,10},{9,11},{10,... | collective-permute-start | bytes 442376 | tf_op jit(solution)/shard_map/ppermute | solution.py:774
  181.4 8.3 %collective-permute-start.46 = (bf16[5,48,768]{2,1,0:T(8,128)(2,1)S(1)}, bf16[5,48,768]{2,1,0:T(8,128)(2,1)S(1)}, u32[]{:S(2)}, u32[]{:S(2)}) collective-permute-start(bf16[5,48,768]{2,1,0:T(8,128)(2,1)S(1)} %pad_maximum_fusion.17), channel_id=1, source_target_pairs={{0,2},{1,3},{2,0},{3,1},{4,6},{5,7},{6,4},{7,5},{8,10},{9,11},{10,... | collective-permute-start | bytes 1105928 | tf_op jit(solution)/shard_map/ppermute | solution.py:774
  183.9 9.8 %collective-permute-start.54 = (bf16[16,48,768]{2,1,0:T(8,128)(2,1)S(1)}, bf16[16,48,768]{2,1,0:T(8,128)(2,1)S(1)}, u32[]{:S(2)}, u32[]{:S(2)}) collective-permute-start(bf16[16,48,768]{2,1,0:T(8,128)(2,1)S(1)} %pad_maximum_fusion.3.refs_2_), channel_id=1, source_target_pairs={{0,1},{1,0},{2,3},{3,2},{4,5},{5,4},{6,7},{7,6},{8,9},{9,8},{10,11... | collective-permute-start | bytes 3538952 | tf_op jit(solution)/shard_map/ppermute | solution.py:774
  (25 other events, 158.0 us)

commit v3 on v2

--- a/solution.py
+++ b/solution.py
@@ -143,12 +143,14 @@
         def _():
             wj_copies[third].wait()
 
-        part = dot(normed, wj_ref[third])
-        if third == 0:
-            part = part + jb_ref[0:1, :]
-        if third == 2:
-            part = part + jb_ref[1:2, :]
-        joined_ref[:, cols] = part.astype(BF)
+        bias = {0: jb_ref[0:1, :], 2: jb_ref[1:2, :]}.get(third, 0.0)
+
+        def project(part, carry):
+            here = pl.ds(pl.multiple_of(part * (rows // 2), 16), rows // 2)
+            joined_ref[here, cols] = (dot(normed_ref[here, :], wj_ref[third]) + bias).astype(BF)
+            return carry
+
+        lax.fori_loop(0, 2, project, 0)
     cot_copy.wait()
     low = head_masks(slots)
     key_slot = lax.broadcasted_iota(jnp.int32, (slots, 2 * slots), 0)
@@ -180,13 +182,15 @@
     def _():
         wm_copy.wait()
 
-    for part in range(2):
-        here = slice(part * rows // 2, (part + 1) * rows // 2)
-        there = pl.ds(pl.multiple_of(step * rows + part * rows // 2, 16), rows // 2)
+    def finish(part, carry):
+        here = pl.ds(pl.multiple_of(part * (rows // 2), 16), rows // 2)
         middle = tok_ref[here, :].astype(F32) + dot(mix_ref[here, :], wm_ref[...]) + mb_ref[...]
         middle_ref[here, :] = middle
         xhat, _ = stats(middle)
         second_ref[here, :] = (xhat * g2_ref[...] + s2_ref[...]).astype(BF)
+        return carry
+
+    lax.fori_loop(0, 2, finish, 0)
 
 
 def first_call(slots, counts, tok, cot, wj, wm, g1, s1, jb, mb, g2, s2):
@@ -231,14 +235,18 @@
 def quarter_body(parts, ids_ref, sec_ref, gout_ref, up_ref, ub_ref, down_ref, *outs):
     grad_ref, act_ref, gh_ref = outs
     rows = sec_ref.shape[0] // parts
-    for part in range(parts):
-        here = slice(part * rows, (part + 1) * rows)
+
+    def one(part, carry):
+        here = pl.ds(pl.multiple_of(part * rows, 16), rows)
         hidden = dot(sec_ref[here, :], up_ref[...]) + ub_ref[...]
         grad_act = dot_t(gout_ref[here, :], down_ref[...])
         cdf = 0.5 + 0.5 * lax.erf(hidden * (0.5**0.5))
         act_ref[here, :] = (hidden * cdf).astype(BF)
         slope = cdf + hidden * (jnp.exp(-0.5 * hidden * hidden) * ((2 * math.pi) ** -0.5))
         gh_ref[here, :] = (grad_act * slope).astype(BF)
+        return carry
+
+    lax.fori_loop(0, parts, one, 0)
     put_blocks(grad_ref, 0, ids_ref[0], t_dot(act_ref[...], gout_ref[...]))
     put_blocks(grad_ref, 1, ids_ref[1], t_dot(sec_ref[...], gh_ref[...]))
 
@@ -280,17 +288,25 @@
 
         @pl.when(step == at)
         def _():
-            outer = dot(acts[at][...], down_ref[...])
-            g = dot_t(ghs[at][...], up_ref[...])
-            if at:
-                outer = outer + outer_ref[...]
-                g = g + g_ref[...]
-            elif chunk:
-                outer = outer + kept[0][...]
-                g = g + kept[1][...]
+            if chunk and not at:
                 small_ref[...] = kept[2][...]
-            outer_ref[...] = outer
-            g_ref[...] = g
+            rows = outer_ref.shape[0] // 2
+
+            def part(k, carry):
+                here = pl.ds(pl.multiple_of(k * rows, 16), rows)
+                outer = dot(acts[at][here, :], down_ref[...])
+                g = dot_t(ghs[at][here, :], up_ref[...])
+                if at:
+                    outer = outer + outer_ref[here, :]
+                    g = g + g_ref[here, :]
+                elif chunk:
+                    outer = outer + kept[0][here, :]
+                    g = g + kept[1][here, :]
+                outer_ref[here, :] = outer
+                g_ref[here, :] = g
+                return carry
+
+            lax.fori_loop(0, 2, part, 0)
             small_ref[pl.ds(ids_ref[4 + 2 * chunk + at], 1), :] = jnp.sum(
                 ghs[at][...].astype(F32), axis=0, keepdims=True
             )
@@ -399,14 +415,17 @@
 def attn_back_body(slots, first, joined_ref, probs_ref, gmix_ref, grad_ref):
     low = head_masks(slots)
     items = joined_ref.shape[0] // slots // 2
+    group = 3
 
     def one(at, carry):
-        item = first * items + at
+        item = first * items + at // (PAIRS // group)
         here = pl.ds(pl.multiple_of(item * slots, 16), slots)
-        for pair in range(PAIRS):
-            cols = slice(pair * LANES, (pair + 1) * LANES)
-            key_cols = slice(D + pair * LANES, D + (pair + 1) * LANES)
-            value_cols = slice(2 * D + pair * LANES, 2 * D + (pair + 1) * LANES)
+        for step in range(group):
+            pair = at % (PAIRS // group) * group + step
+            start = pair * LANES
+            cols = pl.ds(pl.multiple_of(start, LANES), LANES)
+            key_cols = pl.ds(pl.multiple_of(D + start, LANES), LANES)
+            value_cols = pl.ds(pl.multiple_of(2 * D + start, LANES), LANES)
             q = stack_heads(joined_ref[here, cols] * BF(FACTOR), low)
             out = stack_heads(gmix_ref[here, cols], low)
             low_soft = probs_ref[item, pair]
@@ -420,7 +439,7 @@
             grad_ref[here, value_cols] = dot(low_soft, out).astype(BF)
         return carry
 
-    lax.fori_loop(0, items, one, 0)
+    lax.fori_loop(0, items * (PAIRS // group), one, 0)
 
 
 def attn_back_call(call, slots, joined, probs, gmix, kept):
@@ -478,7 +497,14 @@
 def last_body(slots, grad_ref, wj_ref, tok_ref, gmid_ref, g1_ref, out_ref, small_ref, g_ref):
     rows = tok_ref.shape[0]
     items = rows // slots
-    g_ref[...] = dot_t(grad_ref[...], wj_ref[...])
+    half = rows // 2
+
+    def back(part, carry):
+        here = pl.ds(pl.multiple_of(part * half, 16), half)
+        g_ref[here, :] = dot_t(grad_ref[here, :], wj_ref[...])
+        return carry
+
+    lax.fori_loop(0, 2, back, 0)
 
     def one(item, sums):
         here = pl.ds(pl.multiple_of(item * slots, 16), slots)
@@ -940,8 +966,8 @@
             lambda ids: attn_grad_call(0, ids, normed, mix, grad_joined, branch), ids
         )
         four.first(chain.after(send4))
+        two.pair(1)
         three.first(chain.after(send3))
-        two.pair(1)
         one.tail(1)
         keep3, keep4 = chain.run(
             lambda ids: attn_grad_call(1, ids, normed, mix, grad_joined, branch), ids
@@ -956,9 +982,8 @@
         one.tail(3)
         three.tail(0)
         four.tail(0)
+        two.tail(2)
         three.tail(1)
-        two.tail(2)
-        one.pair_up(1)
         three.tail(2)
         token_grad, small_c = chain.run(
             lambda grad: last_call(slots, grad, joined_weight, tok, gmid, first_gain),
@@ -966,15 +991,16 @@
         )
         small = jnp.concatenate([small_a, small_b, small_c[:4]], axis=0)
         two.tail(3)
+        one.pair_up(1)
         three.tail(3)
         one.pair_up(0)
         four.tail(1, small)
+        finish(0, 0)
         three.pair_up(1)
         two.pair_up(1)
         four.tail(2)
+        four.tail(3)
         three.pair_up(0)
-        four.tail(3)
-        finish(0, 0)
         finish(0, 1)
         finish(2, 0)
         four.pair_up(1)
@@ -983,9 +1009,9 @@
         finish(2, 1)
         four.pair_up(0)
         finish(3, 0)
-        finish(1, 1)
         small = finish_small_call(four.rows, four.all)
         finish(3, 1)
+        finish(1, 1)
         joined_grad, merge_grad = done["joined"], done["merge"]
         down_grad, up_grad = done["mlp"]
         return (

time: 203 us -> 205 us (level); the launches traced: 199 us -> 204 us
  waiting for transfers between devices: 48.2 us -> 52 us
  Pallas kernels: 86.4 us -> 89.1 us
    ppermute x56, waiting for transfers between devices: 48.2 us -> 52 us  [swap(): lax.ppermute(value, axis, [(i, i ^ 1 << bit) for i in range(self.sizes[ax...]
  transfers between devices with their start and end apart: 56 -> 56, of which waited for: 15 -> 13; matrix products, arithmetic and copies ran while one was open for 5% -> 5% of each run, Pallas kernels for 33% -> 32%
where the time goes in v3:
time: 205 us; the launch traced here: 204 us
  Pallas kernels  89.1 us (43%)
  waiting for transfers between devices  52 us (25%)
  starting transfers between devices  49.4 us (24%)
  other arithmetic  10.6 us (5%)
    ppermute x56, waiting for transfers between devices, swap(): lax.ppermute(value, axis, [(i, i ^ 1 << bit) for i in range(self.sizes[ax...  52 us
    ppermute x56, starting transfers between devices, swap(): lax.ppermute(value, axis, [(i, i ^ 1 << bit) for i in range(self.sizes[ax...  49.4 us
    pallas_call x4, Pallas kernels, quarter_call(): pl.pallas_call(lambda *refs: quarter_body(2, *refs), grid_spec=pltpu.Pref...  18.3 us
    pallas_call x1, Pallas kernels, first_call(): pl.pallas_call(lambda *refs: first_body(slots, *refs), grid_spec=pltpu.Pr...  15.4 us
    pallas_call x4, Pallas kernels, finish_mlp_call(): pl.pallas_call(lambda *refs: finish_mlp_body(groups, *refs), grid_spec=pl...  12.4 us
    pallas_call x2, Pallas kernels, collect_call(): pl.pallas_call(lambda *refs: collect_body(chunk, *refs), grid_spec=pltpu....  10.1 us
    pallas_call x2, Pallas kernels, attn_back_call(): pl.pallas_call(lambda *refs: attn_back_body(slots, call, *refs[:3], refs[...  9.51 us
    pallas_call x4, Pallas kernels, finish_attn_call(): pl.pallas_call(lambda *refs: finish_attn_body(chunk, *refs), grid_spec=pl...  8.26 us
  transfers between devices with their start and end apart: 56, of which 13 were waited for; matrix products, arithmetic and copies ran while one was open for 5% of the time, Pallas kernels for 32%

profile of v3, /device:TPU:0, one launch (start us, length us, event | category | flops | bytes accessed | tf_op | source)
XLA Modules:
  0.0 204.4 jit_solution(11327208859963004044)
XLA Ops:
  0.8 15.4 %attn_fwd.1 = (bf16[640,768]{1,0:T(8,128)(2,1)S(1)}, bf16[640,2304]{1,0:T(8,128)(2,1)S(1)}, bf16[4,6,160,320]{3,2,1,0:T(8,128)(2,1)S(1)}, bf16[640,768]{1,0:T(8,...) custom-call(s32[4]{0:T(128)} %refs_0_.3, ...), custom_call_target="tpu_custom_call" | custom-call | flops 149999992832 | bytes 1000 | tf_op jit(solution)/shard_map/attn_fwd/pallas_call | solution.py:200
  16.2 4.6 %mlp_0.1 = (bf16[2,16,48,768]{3,2,1,0:T(8,128)(2,1)S(1)}, bf16[640,768]{1,0:T(8,128)(2,1)S(1)}, bf16[640,768]{1,0:T(8,128)(2,1)S(1)}) custom-call(s32[10]{0:T(128)S(1)} %stack.67.refs_0_.ids_ref, bf16[640,768]{1,0:T(8,128)(2,1)S(1)} %get-tuple-element.140.refs_1_, bf16[640,768]{1,0:T(8,128)(2,1)S(1)} %get-tuple-element.141.refs_2_.refs_4_, ...), custom_call_target="tpu_custom_call" | custom-call | flops 43000000512 | bytes 1000 | tf_op jit(solution)/shard_map/mlp_0/pallas_call | solution.py:256
  21.3 4.6 %mlp_1.1 = (bf16[2,16,48,768]{3,2,1,0:T(8,128)(2,1)S(1)}, bf16[640,768]{1,0:T(8,128)(2,1)S(1)}, bf16[640,768]{1,0:T(8,128)(2,1)S(1)}) custom-call(s32[10]{0:T(128)S(1)} %stack.67.refs_0_.ids_ref, bf16[640,768]{1,0:T(8,128)(2,1)S(1)} %get-tuple-element.140.refs_1_, bf16[640,768]{1,0:T(8,128)(2,1)S(1)} %get-tuple-element.141.refs_2_.refs_4_, ...), custom_call_target="tpu_custom_call" | custom-call | flops 43000000512 | bytes 1000 | tf_op jit(solution)/shard_map/mlp_1/pallas_call | solution.py:256
  26.5 4.6 %mlp_2.1 = (bf16[2,16,48,768]{3,2,1,0:T(8,128)(2,1)S(1)}, bf16[640,768]{1,0:T(8,128)(2,1)S(1)}, bf16[640,768]{1,0:T(8,128)(2,1)S(1)}) custom-call(s32[10]{0:T(128)S(1)} %stack.67.refs_0_.ids_ref, bf16[640,768]{1,0:T(8,128)(2,1)S(1)} %get-tuple-element.140.refs_1_, bf16[640,768]{1,0:T(8,128)(2,1)S(1)} %get-tuple-element.141.refs_2_.refs_4_, ...), custom_call_target="tpu_custom_call" | custom-call | flops 43000000512 | bytes 1000 | tf_op jit(solution)/shard_map/mlp_2/pallas_call | solution.py:256
  32.6 2.6 %collective-permute-start.3 = (bf16[8,48,768]{2,1,0:T(8,128)(2,1)S(1)}, bf16[8,48,768]{2,1,0:T(8,128)(2,1)S(1)}, u32[]{:S(2)}, u32[]{:S(2)}) collective-permute-start(bf16[8,48,768]{2,1,0:T(8,128)(2,1)S(1)} %get-tuple-element.272), channel_id=1, source_target_pairs={{0,4},{1,5},{2,6},{3,7},{4,0},{5,1},{6,2},{7,3},{8,12},{9,13},{10,... | collective-permute-start | bytes 1769480 | tf_op jit(solution)/shard_map/ppermute | solution.py:800
  35.3 1.5 collective-permute-start.2
  36.7 5.1 %mlp_collect_0.1 = (f32[640,768]{1,0:T(8,128)S(1)}, f32[640,768]{1,0:T(8,128)S(1)}, f32[4,768]{1,0:T(4,128)S(1)}) custom-call(s32[10]{0:T(128)S(1)} %stack.67.refs_0_.ids_ref, bf16[640,768]{1,0:T(8,128)(2,1)S(1)} %get-tuple-element.149.refs_1_, bf16[640,768]{1,0:T(8,128)(2,1)S(1)} %get-tuple-element.150.refs_2_, ...), custom_call_target="tpu_custom_call" | custom-call | flops 43000000512 | bytes 1000 | tf_op jit(solution)/shard_map/mlp_collect_0/pallas_call | solution.py:317
  41.9 4.6 %mlp_3.1 = (bf16[2,16,48,768]{3,2,1,0:T(8,128)(2,1)S(1)}, bf16[640,768]{1,0:T(8,128)(2,1)S(1)}, bf16[640,768]{1,0:T(8,128)(2,1)S(1)}) custom-call(s32[10]{0:T(128)S(1)} %stack.67.refs_0_.ids_ref, bf16[640,768]{1,0:T(8,128)(2,1)S(1)} %get-tuple-element.140.refs_1_, bf16[640,768]{1,0:T(8,128)(2,1)S(1)} %get-tuple-element.141.refs_2_.refs_4_, ...), custom_call_target="tpu_custom_call" | custom-call | flops 43000000512 | bytes 1000 | tf_op jit(solution)/shard_map/mlp_3/pallas_call | solution.py:256
  46.5 5.0 %mlp_collect_1.1 = (f32[640,768]{1,0:T(8,128)S(1)}, f32[640,768]{1,0:T(8,128)S(1)}, f32[4,768]{1,0:T(4,128)S(1)}) custom-call(s32[10]{0:T(128)S(1)} %stack.67.refs_0_.ids_ref, bf16[640,768]{1,0:T(8,128)(2,1)S(1)} %get-tuple-element.157.refs_1_, bf16[640,768]{1,0:T(8,128)(2,1)S(1)} %get-tuple-element.158.refs_2_, bf16[640,768]{1,0:T(8,128)(2,1)S(1)} %copy-done.11, ...), custom_call_target="tpu_custom_call" | custom-call | flops 43000000512 | bytes 1000 | tf_op jit(solution)/shard_map/mlp_collect_1/pallas_call | solution.py:317
  53.0 1.8 add_convert_fusion
  54.8 1.5 collective-permute-start.8
  56.4 1.4 collective-permute-start.7
  57.8 3.5 %mlp_back.1 = (bf16[640,768]{1,0:T(8,128)(2,1)}, f32[640,768]{1,0:T(8,128)S(1)}, bf16[640,768]{1,0:T(8,128)(2,1)S(1)}, bf16[640,768]{1,0:T(8,128)(2,1)S(1)}, f32[4,768]{1,0:T(4,128)S(1)}) custom-call(s32[4]{0:T(128)S(1)} %copy-done.9, f32[640,768]{1,0:T(8,128)S(1)} %get-tuple-element.168.refs_1_, f32[640,768]{1,0:T(8,128)S(1)} %get-tuple-element.169.refs_2_, ...), custom_call_target="tpu_custom_call" | custom-call | flops 35999997952 | bytes 1000 | tf_op jit(solution)/shard_map/mlp_back/pallas_call | solution.py:394
  61.4 4.7 %attn_bwd_0.1.refs_3_ = bf16[640,2304]{1,0:T(8,128)(2,1)S(1)} custom-call(bf16[640,2304]{1,0:T(8,128)(2,1)S(1)} %get-tuple-element.172.refs_0_, bf16[4,6,160,320]{3,2,1,0:T(8,128)(2,1)S(1)} %get-tuple-element.173.refs_1_, bf16[640,768]{1,0:T(8,128)(2,1)S(1)} %get-tuple-element.178.refs_2_), custom_call_target="tpu_custom_call" | custom-call | flops 54999998464 | bytes 1000 | tf_op jit(solution)/shard_map/attn_bwd_0/pallas_call | solution.py:452
  66.3 1.6 collective-permute-start.6
  68.0 4.9 %attn_bwd_1.1.grad_ref.refs_0_ = bf16[640,2304]{1,0:T(8,128)(2,1)S(1)} custom-call(bf16[640,2304]{1,0:T(8,128)(2,1)S(1)} %get-tuple-element.172.refs_0_, bf16[4,6,160,320]{3,2,1,0:T(8,128)(2,1)S(1)} %get-tuple-element.173.refs_1_, bf16[640,768]{1,0:T(8,128)(2,1)S(1)} %get-tuple-element.178.refs_2_, ...), custom_call_target="tpu_custom_call", output_to_operand_aliasing={{}: (3, {})} | custom-call | flops 54999998464 | bytes 1000 | tf_op jit(solution)/shard_map/attn_bwd_1/pallas_call | solution.py:452
  72.9 2.6 %attn_grad_0.1 = (bf16[2,8,48,768]{3,2,1,0:T(8,128)(2,1)S(1)}, bf16[2,8,48,768]{3,2,1,0:T(8,128)(2,1)S(1)}) custom-call(s32[10]{0:T(128)S(1)} %stack.67.refs_0_.ids_ref, bf16[640,768]{1,0:T(8,128)(2,1)S(1)} %get-tuple-element.180.normed_ref, bf16[640,768]{1,0:T(8,128)(2,1)S(1)} %get-tuple-element.181.mix_ref, ...), custom_call_target="tpu_custom_call" | custom-call | flops 25999998976 | bytes 1000 | tf_op jit(solution)/shard_map/attn_grad_0/pallas_call | solution.py:482
  77.8 2.7 %collective-permute-start.15 = (bf16[2,2,48,768]{3,2,1,0:T(8,128)(2,1)S(1)}, bf16[2,2,48,768]{3,2,1,0:T(8,128)(2,1)S(1)}, u32[]{:S(2)}, u32[]{:S(2)}) collective-permute-start(bf16[2,2,48,768]{3,2,1,0:T(8,128)(2,1)S(1)} %add_convert_fusion.21), channel_id=1, source_target_pairs={{0,16},{8,24},{16,0},{24,8},{1,17},{9,25},{17,1},{25,9},{2,18},{10... | collective-permute-start | bytes 884744 | tf_op jit(solution)/shard_map/ppermute | solution.py:800
  81.5 2.6 %attn_grad_1.1 = (bf16[2,8,48,768]{3,2,1,0:T(8,128)(2,1)S(1)}, bf16[2,8,48,768]{3,2,1,0:T(8,128)(2,1)S(1)}) custom-call(s32[10]{0:T(128)S(1)} %stack.67.refs_0_.ids_ref, bf16[640,768]{1,0:T(8,128)(2,1)S(1)} %get-tuple-element.180.normed_ref, bf16[640,768]{1,0:T(8,128)(2,1)S(1)} %get-tuple-element.181.mix_ref, ...), custom_call_target="tpu_custom_call" | custom-call | flops 25999998976 | bytes 1000 | tf_op jit(solution)/shard_map/attn_grad_1/pallas_call | solution.py:482
  84.7 1.6 collective-permute-start.11
  86.3 3.3 %collective-permute-done.13 = bf16[4,48,768]{2,1,0:T(8,128)(2,1)S(1)} collective-permute-done((bf16[4,48,768]{2,1,0:T(8,128)(2,1)S(1)}, bf16[4,48,768]{2,1,0:T(8,128)(2,1)S(1)}, u32[]{:S(2)}, u32[]{:S(2)}) %collective-permute-start.13) | collective-permute-done | bytes 294944 | tf_op jit(solution)/shard_map/ppermute | solution.py:800
  94.4 1.6 collective-permute-start.20
  96.1 4.6 %collective-permute-done.14 = bf16[2,2,48,768]{3,2,1,0:T(8,128)(2,1)S(1)} collective-permute-done((bf16[2,2,48,768]{3,2,1,0:T(8,128)(2,1)S(1)}, bf16[2,2,48,768]{3,2,1,0:T(8,128)(2,1)S(1)}, u32[]{:S(2)}, u32[]{:S(2)}) %collective-permute-start.14) | collective-permute-done | bytes 294944 | tf_op jit(solution)/shard_map/ppermute | solution.py:800
  100.8 3.2 %collective-permute-start.23 = (bf16[2,2,48,768]{3,2,1,0:T(8,128)(2,1)S(1)}, bf16[2,2,48,768]{3,2,1,0:T(8,128)(2,1)S(1)}, u32[]{:S(2)}, u32[]{:S(2)}) collective-permute-start(bf16[2,2,48,768]{3,2,1,0:T(8,128)(2,1)S(1)} %add_convert_fusion.12), channel_id=1, source_target_pairs={{0,16},{8,24},{16,0},{24,8},{1,17},{9,25},{17,1},{25,9},{2,18},{10... | collective-permute-start | bytes 884744 | tf_op jit(solution)/shard_map/ppermute | solution.py:800
  105.3 1.5 collective-permute-start.25
  106.9 6.4 %collective-permute-done.19 = bf16[2,2,48,768]{3,2,1,0:T(8,128)(2,1)S(1)} collective-permute-done((bf16[2,2,48,768]{3,2,1,0:T(8,128)(2,1)S(1)}, bf16[2,2,48,768]{3,2,1,0:T(8,128)(2,1)S(1)}, u32[]{:S(2)}, u32[]{:S(2)}) %collective-permute-start.19) | collective-permute-done | bytes 294944 | tf_op jit(solution)/shard_map/ppermute | solution.py:800
  114.8 1.5 collective-permute-start.28
  116.5 2.1 %collective-permute-done.24 = bf16[2,48,768]{2,1,0:T(8,128)(2,1)S(1)} collective-permute-done((bf16[2,48,768]{2,1,0:T(8,128)(2,1)S(1)}, bf16[2,48,768]{2,1,0:T(8,128)(2,1)S(1)}, u32[]{:S(2)}, u32[]{:S(2)}) %collective-permute-start.24) | collective-permute-done | bytes 147488 | tf_op jit(solution)/shard_map/ppermute | solution.py:800
  119.0 2.1 %collective-permute-start.30 = (bf16[2,2,48,768]{3,2,1,0:T(8,128)(2,1)S(1)}, bf16[2,2,48,768]{3,2,1,0:T(8,128)(2,1)S(1)}, u32[]{:S(2)}, u32[]{:S(2)}) collective-permute-start(bf16[2,2,48,768]{3,2,1,0:T(8,128)(2,1)S(1)} %add_convert_fusion.8), channel_id=1, source_target_pairs={{0,8},{8,0},{16,24},{24,16},{1,9},{9,1},{17,25},{25,17},{2,10},{10... | collective-permute-start | bytes 884744 | tf_op jit(solution)/shard_map/ppermute | solution.py:800
  121.1 3.8 %collective-permute-done.22 = bf16[2,1,48,768]{3,2,1,0:T(8,128)(2,1)S(1)} collective-permute-done((bf16[2,1,48,768]{3,2,1,0:T(8,128)(2,1)S(1)}, bf16[2,1,48,768]{3,2,1,0:T(8,128)(2,1)S(1)}, u32[]{:S(2)}, u32[]{:S(2)}) %collective-permute-start.22) | collective-permute-done | bytes 147488 | tf_op jit(solution)/shard_map/ppermute | solution.py:800
  127.0 4.7 %collective-permute-done.26 = bf16[2,1,48,768]{3,2,1,0:T(8,128)(2,1)S(1)} collective-permute-done((bf16[2,1,48,768]{3,2,1,0:T(8,128)(2,1)S(1)}, bf16[2,1,48,768]{3,2,1,0:T(8,128)(2,1)S(1)}, u32[]{:S(2)}, u32[]{:S(2)}) %collective-permute-start.26) | collective-permute-done | bytes 147488 | tf_op jit(solution)/shard_map/ppermute | solution.py:800
  131.8 3.8 %collective-permute-start.33 = (bf16[2,1,48,768]{3,2,1,0:T(8,128)(2,1)S(1)}, bf16[2,1,48,768]{3,2,1,0:T(8,128)(2,1)S(1)}, u32[]{:S(2)}, u32[]{:S(2)}) collective-permute-start(bf16[2,1,48,768]{3,2,1,0:T(8,128)(2,1)S(1)} %add_convert_fusion.26), channel_id=1, source_target_pairs={{0,8},{8,0},{16,24},{24,16},{1,9},{9,1},{17,25},{25,17},{2,10},{10... | collective-permute-start | bytes 442376 | tf_op jit(solution)/shard_map/ppermute | solution.py:800
  135.6 5.6 %first_back.1 = (bf16[640,768]{1,0:T(8,128)(2,1)}, f32[8,768]{1,0:T(8,128)S(1)}) custom-call(bf16[640,2304]{1,0:T(8,128)(2,1)S(1)} %attn_bwd_1.1.grad_ref.refs_0_, bf16[768,2304]{1,0:T(8,128)(2,1)S(1)} %copy-done, bf16[640,768]{1,0:T(8,128)(2,1)S(1)} %bitcast.184, f32[640,768]{1,0:T(8,128)S(1)} %get-tuple-element.212.refs_3_, f32[768]{0:T(1024)S(1)} %copy-done.2), custom_call_target="tpu_custom_call" | custom-call | flops 10000000 | bytes 1000 | tf_op jit(solution)/shard_map/first_back/pallas_call | solution.py:534
  144.2 1.5 collective-permute-start.37
  146.1 3.1 %finish_mlp_0_0.1 = (f32[3072,768]{1,0:T(8,128)}, f32[768,3072]{1,0:T(8,128)}) custom-call(s32[10]{0:T(128)S(1)} %stack.67.refs_0_.ids_ref, bf16[16,48,768]{2,1,0:T(8,128)(2,1)S(1)} %pad_maximum_fusion.refs_1_, bf16[16,48,768]{2,1,0:T(8,128)(2,1)S(1)} %pad_maximum_fusion.1.refs_2_), custom_call_target="tpu_custom_call" | custom-call | flops 10000000 | bytes 1000 | tf_op jit(solution)/shard_map/finish_mlp_0_0/pallas_call | solution.py:576
  149.2 2.1 %collective-permute-done.38 = bf16[2,48,768]{2,1,0:T(8,128)(2,1)S(1)} collective-permute-done((bf16[2,48,768]{2,1,0:T(8,128)(2,1)S(1)}, bf16[2,48,768]{2,1,0:T(8,128)(2,1)S(1)}, u32[]{:S(2)}, u32[]{:S(2)}) %collective-permute-start.38) | collective-permute-done | bytes 147488 | tf_op jit(solution)/shard_map/ppermute | solution.py:800
  151.3 3.0 %collective-permute-done.37 = bf16[2,48,768]{2,1,0:T(8,128)(2,1)S(1)} collective-permute-done((bf16[2,48,768]{2,1,0:T(8,128)(2,1)S(1)}, bf16[2,48,768]{2,1,0:T(8,128)(2,1)S(1)}, u32[]{:S(2)}, u32[]{:S(2)}) %collective-permute-start.37) | collective-permute-done | bytes 147488 | tf_op jit(solution)/shard_map/ppermute | solution.py:800
  156.7 5.9 %collective-permute-done.43 = bf16[4,48,768]{2,1,0:T(8,128)(2,1)S(1)} collective-permute-done((bf16[4,48,768]{2,1,0:T(8,128)(2,1)S(1)}, bf16[4,48,768]{2,1,0:T(8,128)(2,1)S(1)}, u32[]{:S(2)}, u32[]{:S(2)}) %collective-permute-start.43) | collective-permute-done | bytes 294944 | tf_op jit(solution)/shard_map/ppermute | solution.py:800
  163.2 2.5 %collective-permute-start.40 = (bf16[3,48,768]{2,1,0:T(8,128)(2,1)S(1)}, bf16[3,48,768]{2,1,0:T(8,128)(2,1)S(1)}, u32[]{:S(2)}, u32[]{:S(2)}) collective-permute-start(bf16[3,48,768]{2,1,0:T(8,128)(2,1)S(1)} %pad_maximum_fusion.25), channel_id=1, source_target_pairs={{0,4},{1,5},{2,6},{3,7},{4,0},{5,1},{6,2},{7,3},{8,12},{9,13},{10,... | collective-permute-start | bytes 663560 | tf_op jit(solution)/shard_map/ppermute | solution.py:800
  165.9 12.5 %collective-permute-done.40 = bf16[3,48,768]{2,1,0:T(8,128)(2,1)S(1)} collective-permute-done((bf16[3,48,768]{2,1,0:T(8,128)(2,1)S(1)}, bf16[3,48,768]{2,1,0:T(8,128)(2,1)S(1)}, u32[]{:S(2)}, u32[]{:S(2)}) %collective-permute-start.40) | collective-permute-done | bytes 221216 | tf_op jit(solution)/shard_map/ppermute | solution.py:800
  179.9 3.1 %finish_mlp_0_1.1 = (f32[3072,768]{1,0:T(8,128)}, f32[768,3072]{1,0:T(8,128)}) custom-call(s32[10]{0:T(128)S(1)} %stack.67.refs_0_.ids_ref, bf16[16,48,768]{2,1,0:T(8,128)(2,1)S(1)} %collective-permute-done.44.refs_1_, bf16[16,48,768]{2,1,0:T(8,128)(2,1)S(1)} %collective-permute-done.45.refs_2_, ...), custom_call_target="tpu_custom_call", output_to_operand_aliasing={{0}: (3, {}), {1}: (4, {})} | custom-call | flops 10000000 | bytes 1000 | tf_op jit(solution)/shard_map/finish_mlp_0_1/pallas_call | solution.py:576
  183.0 2.1 %finish_attn_2_0.1.refs_3_ = f32[768,2304]{1,0:T(8,128)} custom-call(s32[10]{0:T(128)S(1)} %stack.67.refs_0_.ids_ref, bf16[8,48,768]{2,1,0:T(8,128)(2,1)S(1)} %pad_maximum_fusion.11.refs_1_, bf16[8,48,768]{2,1,0:T(8,128)(2,1)S(1)} %pad_maximum_fusion.12.refs_2_), custom_call_target="tpu_custom_call" | custom-call | flops 10000000 | bytes 1000 | tf_op jit(solution)/shard_map/finish_attn_2_0/pallas_call | solution.py:622
  187.4 3.1 %finish_mlp_1_0.1 = (f32[3072,768]{1,0:T(8,128)}, f32[768,3072]{1,0:T(8,128)}) custom-call(s32[10]{0:T(128)S(1)} %stack.67.refs_0_.ids_ref, bf16[16,48,768]{2,1,0:T(8,128)(2,1)S(1)} %pad_maximum_fusion.2.refs_1_, bf16[16,48,768]{2,1,0:T(8,128)(2,1)S(1)} %pad_maximum_fusion.3.refs_2_, ...), custom_call_target="tpu_custom_call", output_to_operand_aliasing={{0}: (3, {}), {1}: (4, {})} | custom-call | flops 10000000 | bytes 1000 | tf_op jit(solution)/shard_map/finish_mlp_1_0/pallas_call | solution.py:576
  191.0 2.1 %finish_attn_2_1.1.refs_3_ = f32[768,2304]{1,0:T(8,128)} custom-call(s32[10]{0:T(128)S(1)} %stack.67.refs_0_.ids_ref, bf16[8,48,768]{2,1,0:T(8,128)(2,1)S(1)} %collective-permute-done.48.refs_1_, bf16[8,48,768]{2,1,0:T(8,128)(2,1)S(1)} %collective-permute-done.51.refs_2_, f32[768,2304]{1,0:T(8,128)} %finish_attn_2_0.1.refs_3_), custom_call_target="tpu_custom_call", output_to_operand_aliasing={{}: (3, {})} | custom-call | flops 10000000 | bytes 1000 | tf_op jit(solution)/shard_map/finish_attn_2_1/pallas_call | solution.py:622
  193.1 2.5 %collective-permute-done.46 = bf16[5,48,768]{2,1,0:T(8,128)(2,1)S(1)} collective-permute-done((bf16[5,48,768]{2,1,0:T(8,128)(2,1)S(1)}, bf16[5,48,768]{2,1,0:T(8,128)(2,1)S(1)}, u32[]{:S(2)}, u32[]{:S(2)}) %collective-permute-start.46) | collective-permute-done | bytes 368672 | tf_op jit(solution)/shard_map/ppermute | solution.py:800
  196.5 2.0 finish_attn_3_0.1
  199.3 2.0 finish_attn_3_1.1
  201.3 3.1 %finish_mlp_1_1.1 = (f32[3072,768]{1,0:T(8,128)}, f32[768,3072]{1,0:T(8,128)}) custom-call(s32[10]{0:T(128)S(1)} %stack.67.refs_0_.ids_ref, bf16[16,48,768]{2,1,0:T(8,128)(2,1)S(1)} %collective-permute-done.54.refs_1_, bf16[16,48,768]{2,1,0:T(8,128)(2,1)S(1)} %collective-permute-done.55.refs_2_, ...), custom_call_target="tpu_custom_call", output_to_operand_aliasing={{0}: (3, {}), {1}: (4, {})} | custom-call | flops 10000000 | bytes 1000 | tf_op jit(solution)/shard_map/finish_mlp_1_1/pallas_call | solution.py:576
  (194 shorter events, 31.0 us)
Async XLA Ops:
  20.8 11.2 %collective-permute-start = (bf16[2,16,48,768]{3,2,1,0:T(8,128)(2,1)S(1)}, bf16[2,16,48,768]{3,2,1,0:T(8,128)(2,1)S(1)}, u32[]{:S(2)}, u32[]{:S(2)}) collective-permute-start(bf16[2,16,48,768]{3,2,1,0:T(8,128)(2,1)S(1)} %get-tuple-element.142), channel_id=1, source_target_pairs={{0,1},{1,0},{2,3},{3,2},{4,5},{5,4},{6,7},{7,6},{8,9},{9,8},{10,11... | collective-permute-start | bytes 7077896 | tf_op jit(solution)/shard_map/ppermute | solution.py:800
  32.6 18.9 %collective-permute-start.3 = (bf16[8,48,768]{2,1,0:T(8,128)(2,1)S(1)}, bf16[8,48,768]{2,1,0:T(8,128)(2,1)S(1)}, u32[]{:S(2)}, u32[]{:S(2)}) collective-permute-start(bf16[8,48,768]{2,1,0:T(8,128)(2,1)S(1)} %get-tuple-element.272), channel_id=1, source_target_pairs={{0,4},{1,5},{2,6},{3,7},{4,0},{5,1},{6,2},{7,3},{8,12},{9,13},{10,... | collective-permute-start | bytes 1769480 | tf_op jit(solution)/shard_map/ppermute | solution.py:800
  35.3 16.3 %collective-permute-start.2 = (bf16[8,48,768]{2,1,0:T(8,128)(2,1)S(1)}, bf16[8,48,768]{2,1,0:T(8,128)(2,1)S(1)}, u32[]{:S(2)}, u32[]{:S(2)}) collective-permute-start(bf16[8,48,768]{2,1,0:T(8,128)(2,1)S(1)} %get-tuple-element.273), channel_id=1, source_target_pairs={{0,2},{1,3},{2,0},{3,1},{4,6},{5,7},{6,4},{7,5},{8,10},{9,11},{10,... | collective-permute-start | bytes 1769480 | tf_op jit(solution)/shard_map/ppermute | solution.py:800
  51.7 14.4 %collective-permute-start.5 = (bf16[4,48,768]{2,1,0:T(8,128)(2,1)S(1)}, bf16[4,48,768]{2,1,0:T(8,128)(2,1)S(1)}, u32[]{:S(2)}, u32[]{:S(2)}) collective-permute-start(bf16[4,48,768]{2,1,0:T(8,128)(2,1)S(1)} %fusion.10), channel_id=1, source_target_pairs={{0,2},{1,3},{2,0},{3,1},{4,6},{5,7},{6,4},{7,5},{8,10},{9,11},{10,... | collective-permute-start | bytes 884744 | tf_op jit(solution)/shard_map/ppermute | solution.py:800
  52.5 13.6 %collective-permute-start.4 = (bf16[4,48,768]{2,1,0:T(8,128)(2,1)S(1)}, bf16[4,48,768]{2,1,0:T(8,128)(2,1)S(1)}, u32[]{:S(2)}, u32[]{:S(2)}) collective-permute-start(bf16[4,48,768]{2,1,0:T(8,128)(2,1)S(1)} %fusion.11), channel_id=1, source_target_pairs={{0,4},{1,5},{2,6},{3,7},{4,0},{5,1},{6,2},{7,3},{8,12},{9,13},{10,... | collective-permute-start | bytes 884744 | tf_op jit(solution)/shard_map/ppermute | solution.py:800
  54.8 20.7 %collective-permute-start.8 = (bf16[8,48,768]{2,1,0:T(8,128)(2,1)}, bf16[8,48,768]{2,1,0:T(8,128)(2,1)}, u32[]{:S(2)}, u32[]{:S(2)}) collective-permute-start(bf16[8,48,768]{2,1,0:T(8,128)(2,1)} %get-tuple-element.268), channel_id=1, source_target_pairs={{0,4},{1,5},{2,6},{3,7},{4,0},{5,1},{6,2},{7,3},{8,12},{9,13},{10,... | collective-permute-start | bytes 1769480 | tf_op jit(solution)/shard_map/ppermute | solution.py:800
  56.4 19.2 %collective-permute-start.7 = (bf16[8,48,768]{2,1,0:T(8,128)(2,1)}, bf16[8,48,768]{2,1,0:T(8,128)(2,1)}, u32[]{:S(2)}, u32[]{:S(2)}) collective-permute-start(bf16[8,48,768]{2,1,0:T(8,128)(2,1)} %get-tuple-element.269), channel_id=1, source_target_pairs={{0,2},{1,3},{2,0},{3,1},{4,6},{5,7},{6,4},{7,5},{8,10},{9,11},{10,... | collective-permute-start | bytes 1769480 | tf_op jit(solution)/shard_map/ppermute | solution.py:800
  66.3 11.4 %collective-permute-start.6 = (bf16[2,2,48,768]{3,2,1,0:T(8,128)(2,1)S(1)}, bf16[2,2,48,768]{3,2,1,0:T(8,128)(2,1)S(1)}, u32[]{:S(2)}, u32[]{:S(2)}) collective-permute-start(bf16[2,2,48,768]{3,2,1,0:T(8,128)(2,1)S(1)} %fusion.21), channel_id=1, source_target_pairs={{0,8},{8,0},{16,24},{24,16},{1,9},{9,1},{17,25},{25,17},{2,10},{10... | collective-permute-start | bytes 884744 | tf_op jit(solution)/shard_map/ppermute | solution.py:800
  75.5 18.5 %collective-permute-start.16 = (bf16[2,8,48,768]{3,2,1,0:T(8,128)(2,1)S(1)}, bf16[2,8,48,768]{3,2,1,0:T(8,128)(2,1)S(1)}, u32[]{:S(2)}, u32[]{:S(2)}) collective-permute-start(bf16[2,8,48,768]{3,2,1,0:T(8,128)(2,1)S(1)} %get-tuple-element.195), channel_id=1, source_target_pairs={{0,1},{1,0},{2,3},{3,2},{4,5},{5,4},{6,7},{7,6},{8,9},{9,8},{10,11... | collective-permute-start | bytes 3538952 | tf_op jit(solution)/shard_map/ppermute | solution.py:800
  77.8 16.6 %collective-permute-start.15 = (bf16[2,2,48,768]{3,2,1,0:T(8,128)(2,1)S(1)}, bf16[2,2,48,768]{3,2,1,0:T(8,128)(2,1)S(1)}, u32[]{:S(2)}, u32[]{:S(2)}) collective-permute-start(bf16[2,2,48,768]{3,2,1,0:T(8,128)(2,1)S(1)} %add_convert_fusion.21), channel_id=1, source_target_pairs={{0,16},{8,24},{16,0},{24,8},{1,17},{9,25},{17,1},{25,9},{2,18},{10... | collective-permute-start | bytes 884744 | tf_op jit(solution)/shard_map/ppermute | solution.py:800
  80.5 9.1 %collective-permute-start.13 = (bf16[4,48,768]{2,1,0:T(8,128)(2,1)S(1)}, bf16[4,48,768]{2,1,0:T(8,128)(2,1)S(1)}, u32[]{:S(2)}, u32[]{:S(2)}) collective-permute-start(bf16[4,48,768]{2,1,0:T(8,128)(2,1)S(1)} %fusion.6), channel_id=1, source_target_pairs={{0,2},{1,3},{2,0},{3,1},{4,6},{5,7},{6,4},{7,5},{8,10},{9,11},{10,... | collective-permute-start | bytes 884744 | tf_op jit(solution)/shard_map/ppermute | solution.py:800
  81.0 9.9 %collective-permute-start.12 = (bf16[4,48,768]{2,1,0:T(8,128)(2,1)S(1)}, bf16[4,48,768]{2,1,0:T(8,128)(2,1)S(1)}, u32[]{:S(2)}, u32[]{:S(2)}) collective-permute-start(bf16[4,48,768]{2,1,0:T(8,128)(2,1)S(1)} %fusion.7), channel_id=1, source_target_pairs={{0,4},{1,5},{2,6},{3,7},{4,0},{5,1},{6,2},{7,3},{8,12},{9,13},{10,... | collective-permute-start | bytes 884744 | tf_op jit(solution)/shard_map/ppermute | solution.py:800
  84.7 16.1 %collective-permute-start.11 = (bf16[4,48,768]{2,1,0:T(8,128)(2,1)S(1)}, bf16[4,48,768]{2,1,0:T(8,128)(2,1)S(1)}, u32[]{:S(2)}, u32[]{:S(2)}) collective-permute-start(bf16[4,48,768]{2,1,0:T(8,128)(2,1)S(1)} %get-tuple-element.279), channel_id=1, source_target_pairs={{0,4},{1,5},{2,6},{3,7},{4,0},{5,1},{6,2},{7,3},{8,12},{9,13},{10,... | collective-permute-start | bytes 884744 | tf_op jit(solution)/shard_map/ppermute | solution.py:800
  89.6 14.4 %collective-permute-start.10 = (bf16[4,48,768]{2,1,0:T(8,128)(2,1)S(1)}, bf16[4,48,768]{2,1,0:T(8,128)(2,1)S(1)}, u32[]{:S(2)}, u32[]{:S(2)}) collective-permute-start(bf16[4,48,768]{2,1,0:T(8,128)(2,1)S(1)} %get-tuple-element.280), channel_id=1, source_target_pairs={{0,2},{1,3},{2,0},{3,1},{4,6},{5,7},{6,4},{7,5},{8,10},{9,11},{10,... | collective-permute-start | bytes 884744 | tf_op jit(solution)/shard_map/ppermute | solution.py:800
  93.1 7.6 %collective-permute-start.14 = (bf16[2,2,48,768]{3,2,1,0:T(8,128)(2,1)S(1)}, bf16[2,2,48,768]{3,2,1,0:T(8,128)(2,1)S(1)}, u32[]{:S(2)}, u32[]{:S(2)}) collective-permute-start(bf16[2,2,48,768]{3,2,1,0:T(8,128)(2,1)S(1)} %pad_maximum_fusion.18), channel_id=1, source_target_pairs={{0,8},{8,0},{16,24},{24,16},{1,9},{9,1},{17,25},{25,17},{2,10},{10... | collective-permute-start | bytes 884744 | tf_op jit(solution)/shard_map/ppermute | solution.py:800
  94.3 10.5 %collective-permute-start.21 = (bf16[4,48,768]{2,1,0:T(8,128)(2,1)S(1)}, bf16[4,48,768]{2,1,0:T(8,128)(2,1)S(1)}, u32[]{:S(2)}, u32[]{:S(2)}) collective-permute-start(bf16[4,48,768]{2,1,0:T(8,128)(2,1)S(1)} %get-tuple-element.276), channel_id=1, source_target_pairs={{0,4},{1,5},{2,6},{3,7},{4,0},{5,1},{6,2},{7,3},{8,12},{9,13},{10,... | collective-permute-start | bytes 884744 | tf_op jit(solution)/shard_map/ppermute | solution.py:800
  94.4 10.9 %collective-permute-start.20 = (bf16[4,48,768]{2,1,0:T(8,128)(2,1)S(1)}, bf16[4,48,768]{2,1,0:T(8,128)(2,1)S(1)}, u32[]{:S(2)}, u32[]{:S(2)}) collective-permute-start(bf16[4,48,768]{2,1,0:T(8,128)(2,1)S(1)} %get-tuple-element.277), channel_id=1, source_target_pairs={{0,2},{1,3},{2,0},{3,1},{4,6},{5,7},{6,4},{7,5},{8,10},{9,11},{10,... | collective-permute-start | bytes 884744 | tf_op jit(solution)/shard_map/ppermute | solution.py:800
  100.7 12.7 %collective-permute-start.19 = (bf16[2,2,48,768]{3,2,1,0:T(8,128)(2,1)S(1)}, bf16[2,2,48,768]{3,2,1,0:T(8,128)(2,1)S(1)}, u32[]{:S(2)}, u32[]{:S(2)}) collective-permute-start(bf16[2,2,48,768]{3,2,1,0:T(8,128)(2,1)S(1)} %add_convert_fusion.13), channel_id=1, source_target_pairs={{0,8},{8,0},{16,24},{24,16},{1,9},{9,1},{17,25},{25,17},{2,10},{10... | collective-permute-start | bytes 884744 | tf_op jit(solution)/shard_map/ppermute | solution.py:800
  100.8 18.1 %collective-permute-start.23 = (bf16[2,2,48,768]{3,2,1,0:T(8,128)(2,1)S(1)}, bf16[2,2,48,768]{3,2,1,0:T(8,128)(2,1)S(1)}, u32[]{:S(2)}, u32[]{:S(2)}) collective-permute-start(bf16[2,2,48,768]{3,2,1,0:T(8,128)(2,1)S(1)} %add_convert_fusion.12), channel_id=1, source_target_pairs={{0,16},{8,24},{16,0},{24,8},{1,17},{9,25},{17,1},{25,9},{2,18},{10... | collective-permute-start | bytes 884744 | tf_op jit(solution)/shard_map/ppermute | solution.py:800
  104.0 9.9 %collective-permute-start.18 = (bf16[2,48,768]{2,1,0:T(8,128)(2,1)S(1)}, bf16[2,48,768]{2,1,0:T(8,128)(2,1)S(1)}, u32[]{:S(2)}, u32[]{:S(2)}) collective-permute-start(bf16[2,48,768]{2,1,0:T(8,128)(2,1)S(1)} %fusion.35), channel_id=1, source_target_pairs={{0,2},{1,3},{2,0},{3,1},{4,6},{5,7},{6,4},{7,5},{8,10},{9,11},{10,... | collective-permute-start | bytes 442376 | tf_op jit(solution)/shard_map/ppermute | solution.py:800
  104.7 10.0 %collective-permute-start.17 = (bf16[2,48,768]{2,1,0:T(8,128)(2,1)S(1)}, bf16[2,48,768]{2,1,0:T(8,128)(2,1)S(1)}, u32[]{:S(2)}, u32[]{:S(2)}) collective-permute-start(bf16[2,48,768]{2,1,0:T(8,128)(2,1)S(1)} %fusion.36), channel_id=1, source_target_pairs={{0,4},{1,5},{2,6},{3,7},{4,0},{5,1},{6,2},{7,3},{8,12},{9,13},{10,... | collective-permute-start | bytes 442376 | tf_op jit(solution)/shard_map/ppermute | solution.py:800
  105.3 11.1 %collective-permute-start.25 = (bf16[2,48,768]{2,1,0:T(8,128)(2,1)S(1)}, bf16[2,48,768]{2,1,0:T(8,128)(2,1)S(1)}, u32[]{:S(2)}, u32[]{:S(2)}) collective-permute-start(bf16[2,48,768]{2,1,0:T(8,128)(2,1)S(1)} %fusion.33), channel_id=1, source_target_pairs={{0,2},{1,3},{2,0},{3,1},{4,6},{5,7},{6,4},{7,5},{8,10},{9,11},{10,... | collective-permute-start | bytes 442376 | tf_op jit(solution)/shard_map/ppermute | solution.py:800
  113.9 11.1 %collective-permute-start.29 = (bf16[4,48,768]{2,1,0:T(8,128)(2,1)S(1)}, bf16[4,48,768]{2,1,0:T(8,128)(2,1)S(1)}, u32[]{:S(2)}, u32[]{:S(2)}) collective-permute-start(bf16[4,48,768]{2,1,0:T(8,128)(2,1)S(1)} %get-tuple-element.284), channel_id=1, source_target_pairs={{0,2},{1,3},{2,0},{3,1},{4,6},{5,7},{6,4},{7,5},{8,10},{9,11},{10,... | collective-permute-start | bytes 884744 | tf_op jit(solution)/shard_map/ppermute | solution.py:800
  114.8 10.3 %collective-permute-start.28 = (bf16[4,48,768]{2,1,0:T(8,128)(2,1)S(1)}, bf16[4,48,768]{2,1,0:T(8,128)(2,1)S(1)}, u32[]{:S(2)}, u32[]{:S(2)}) collective-permute-start(bf16[4,48,768]{2,1,0:T(8,128)(2,1)S(1)} %get-tuple-element.285), channel_id=1, source_target_pairs={{0,4},{1,5},{2,6},{3,7},{4,0},{5,1},{6,2},{7,3},{8,12},{9,13},{10,... | collective-permute-start | bytes 884744 | tf_op jit(solution)/shard_map/ppermute | solution.py:800
  116.4 8.4 %collective-permute-start.22 = (bf16[2,1,48,768]{3,2,1,0:T(8,128)(2,1)S(1)}, bf16[2,1,48,768]{3,2,1,0:T(8,128)(2,1)S(1)}, u32[]{:S(2)}, u32[]{:S(2)}) collective-permute-start(bf16[2,1,48,768]{3,2,1,0:T(8,128)(2,1)S(1)} %pad_maximum_fusion.27), channel_id=1, source_target_pairs={{0,8},{8,0},{16,24},{24,16},{1,9},{9,1},{17,25},{25,17},{2,10},{10... | collective-permute-start | bytes 442376 | tf_op jit(solution)/shard_map/ppermute | solution.py:800
  118.8 27.1 %collective-permute-start.27 = (bf16[2,1,48,768]{3,2,0,1:T(8,128)(2,1)S(1)}, bf16[2,1,48,768]{3,2,0,1:T(8,128)(2,1)S(1)}, u32[]{:S(2)}, u32[]{:S(2)}) collective-permute-start(bf16[2,1,48,768]{3,2,0,1:T(8,128)(2,1)S(1)} %fusion.42), channel_id=1, source_target_pairs={{0,8},{8,0},{16,24},{24,16},{1,9},{9,1},{17,25},{25,17},{2,10},{10... | collective-permute-start | bytes 442376 | tf_op jit(solution)/shard_map/ppermute | solution.py:800
  119.0 22.4 %collective-permute-start.30 = (bf16[2,2,48,768]{3,2,1,0:T(8,128)(2,1)S(1)}, bf16[2,2,48,768]{3,2,1,0:T(8,128)(2,1)S(1)}, u32[]{:S(2)}, u32[]{:S(2)}) collective-permute-start(bf16[2,2,48,768]{3,2,1,0:T(8,128)(2,1)S(1)} %add_convert_fusion.8), channel_id=1, source_target_pairs={{0,8},{8,0},{16,24},{24,16},{1,9},{9,1},{17,25},{25,17},{2,10},{10... | collective-permute-start | bytes 884744 | tf_op jit(solution)/shard_map/ppermute | solution.py:800
  125.1 18.2 %collective-permute-start.32 = (bf16[8,48,768]{2,1,0:T(8,128)(2,1)S(1)}, bf16[8,48,768]{2,1,0:T(8,128)(2,1)S(1)}, u32[]{:S(2)}, u32[]{:S(2)}) collective-permute-start(bf16[8,48,768]{2,1,0:T(8,128)(2,1)S(1)} %pad_maximum_fusion.8), channel_id=1, source_target_pairs={{0,4},{1,5},{2,6},{3,7},{4,0},{5,1},{6,2},{7,3},{8,12},{9,13},{10,... | collective-permute-start | bytes 1769480 | tf_op jit(solution)/shard_map/ppermute | solution.py:800
  125.7 18.5 %collective-permute-start.31 = (bf16[8,48,768]{2,1,0:T(8,128)(2,1)S(1)}, bf16[8,48,768]{2,1,0:T(8,128)(2,1)S(1)}, u32[]{:S(2)}, u32[]{:S(2)}) collective-permute-start(bf16[8,48,768]{2,1,0:T(8,128)(2,1)S(1)} %pad_maximum_fusion.7), channel_id=1, source_target_pairs={{0,2},{1,3},{2,0},{3,1},{4,6},{5,7},{6,4},{7,5},{8,10},{9,11},{10,... | collective-permute-start | bytes 1769480 | tf_op jit(solution)/shard_map/ppermute | solution.py:800
  131.8 11.0 %collective-permute-start.33 = (bf16[2,1,48,768]{3,2,1,0:T(8,128)(2,1)S(1)}, bf16[2,1,48,768]{3,2,1,0:T(8,128)(2,1)S(1)}, u32[]{:S(2)}, u32[]{:S(2)}) collective-permute-start(bf16[2,1,48,768]{3,2,1,0:T(8,128)(2,1)S(1)} %add_convert_fusion.26), channel_id=1, source_target_pairs={{0,8},{8,0},{16,24},{24,16},{1,9},{9,1},{17,25},{25,17},{2,10},{10... | collective-permute-start | bytes 442376 | tf_op jit(solution)/shard_map/ppermute | solution.py:800
  141.4 14.3 %collective-permute-start.36 = (bf16[4,48,768]{2,1,0:T(8,128)(2,1)S(1)}, bf16[4,48,768]{2,1,0:T(8,128)(2,1)S(1)}, u32[]{:S(2)}, u32[]{:S(2)}) collective-permute-start(bf16[4,48,768]{2,1,0:T(8,128)(2,1)S(1)} %get-tuple-element.282), channel_id=1, source_target_pairs={{0,2},{1,3},{2,0},{3,1},{4,6},{5,7},{6,4},{7,5},{8,10},{9,11},{10,... | collective-permute-start | bytes 884744 | tf_op jit(solution)/shard_map/ppermute | solution.py:800
  142.8 13.0 %collective-permute-start.35 = (bf16[4,48,768]{2,1,0:T(8,128)(2,1)S(1)}, bf16[4,48,768]{2,1,0:T(8,128)(2,1)S(1)}, u32[]{:S(2)}, u32[]{:S(2)}) collective-permute-start(bf16[4,48,768]{2,1,0:T(8,128)(2,1)S(1)} %get-tuple-element.283), channel_id=1, source_target_pairs={{0,4},{1,5},{2,6},{3,7},{4,0},{5,1},{6,2},{7,3},{8,12},{9,13},{10,... | collective-permute-start | bytes 884744 | tf_op jit(solution)/shard_map/ppermute | solution.py:800
  143.3 7.9 %collective-permute-start.38 = (bf16[2,48,768]{2,1,0:T(8,128)(2,1)S(1)}, bf16[2,48,768]{2,1,0:T(8,128)(2,1)S(1)}, u32[]{:S(2)}, u32[]{:S(2)}) collective-permute-start(bf16[2,48,768]{2,1,0:T(8,128)(2,1)S(1)} %get-tuple-element.290), channel_id=1, source_target_pairs={{0,2},{1,3},{2,0},{3,1},{4,6},{5,7},{6,4},{7,5},{8,10},{9,11},{10,... | collective-permute-start | bytes 442376 | tf_op jit(solution)/shard_map/ppermute | solution.py:800
  144.2 10.0 %collective-permute-start.37 = (bf16[2,48,768]{2,1,0:T(8,128)(2,1)S(1)}, bf16[2,48,768]{2,1,0:T(8,128)(2,1)S(1)}, u32[]{:S(2)}, u32[]{:S(2)}) collective-permute-start(bf16[2,48,768]{2,1,0:T(8,128)(2,1)S(1)} %get-tuple-element.291), channel_id=1, source_target_pairs={{0,4},{1,5},{2,6},{3,7},{4,0},{5,1},{6,2},{7,3},{8,12},{9,13},{10,... | collective-permute-start | bytes 442376 | tf_op jit(solution)/shard_map/ppermute | solution.py:800
  146.0 9.9 %collective-permute-start.34 = (bf16[3,48,768]{2,1,0:T(8,128)(2,1)S(1)}, bf16[3,48,768]{2,1,0:T(8,128)(2,1)S(1)}, u32[]{:S(2)}, u32[]{:S(2)}) collective-permute-start(bf16[3,48,768]{2,1,0:T(8,128)(2,1)S(1)} %pad_maximum_fusion.23), channel_id=1, source_target_pairs={{0,16},{8,24},{16,0},{24,8},{1,17},{9,25},{17,1},{25,9},{2,18},{10... | collective-permute-start | bytes 663560 | tf_op jit(solution)/shard_map/ppermute | solution.py:800
  154.3 8.4 %collective-permute-start.43 = (bf16[4,48,768]{2,1,0:T(8,128)(2,1)S(1)}, bf16[4,48,768]{2,1,0:T(8,128)(2,1)S(1)}, u32[]{:S(2)}, u32[]{:S(2)}) collective-permute-start(bf16[4,48,768]{2,1,0:T(8,128)(2,1)S(1)} %pad_maximum_fusion.21), channel_id=1, source_target_pairs={{0,4},{1,5},{2,6},{3,7},{4,0},{5,1},{6,2},{7,3},{8,12},{9,13},{10,... | collective-permute-start | bytes 884744 | tf_op jit(solution)/shard_map/ppermute | solution.py:800
  154.8 7.9 %collective-permute-start.42 = (bf16[4,48,768]{2,1,0:T(8,128)(2,1)S(1)}, bf16[4,48,768]{2,1,0:T(8,128)(2,1)S(1)}, u32[]{:S(2)}, u32[]{:S(2)}) collective-permute-start(bf16[4,48,768]{2,1,0:T(8,128)(2,1)S(1)} %pad_maximum_fusion.20), channel_id=1, source_target_pairs={{0,2},{1,3},{2,0},{3,1},{4,6},{5,7},{6,4},{7,5},{8,10},{9,11},{10,... | collective-permute-start | bytes 884744 | tf_op jit(solution)/shard_map/ppermute | solution.py:800
  156.2 22.3 %collective-permute-start.45 = (bf16[16,48,768]{2,1,0:T(8,128)(2,1)S(1)}, bf16[16,48,768]{2,1,0:T(8,128)(2,1)S(1)}, u32[]{:S(2)}, u32[]{:S(2)}) collective-permute-start(bf16[16,48,768]{2,1,0:T(8,128)(2,1)S(1)} %pad_maximum_fusion.1.refs_2_), channel_id=1, source_target_pairs={{0,1},{1,0},{2,3},{3,2},{4,5},{5,4},{6,7},{7,6},{8,9},{9,8},{10,11... | collective-permute-start | bytes 3538952 | tf_op jit(solution)/shard_map/ppermute | solution.py:800
  156.2 22.8 %collective-permute-start.44 = (bf16[16,48,768]{2,1,0:T(8,128)(2,1)S(1)}, bf16[16,48,768]{2,1,0:T(8,128)(2,1)S(1)}, u32[]{:S(2)}, u32[]{:S(2)}) collective-permute-start(bf16[16,48,768]{2,1,0:T(8,128)(2,1)S(1)} %pad_maximum_fusion.refs_1_), channel_id=1, source_target_pairs={{0,1},{1,0},{2,3},{3,2},{4,5},{5,4},{6,7},{7,6},{8,9},{9,8},{10,11... | collective-permute-start | bytes 3538952 | tf_op jit(solution)/shard_map/ppermute | solution.py:800
  162.7 23.9 %collective-permute-start.50 = (bf16[8,48,768]{2,1,0:T(8,128)(2,1)S(1)}, bf16[8,48,768]{2,1,0:T(8,128)(2,1)S(1)}, u32[]{:S(2)}, u32[]{:S(2)}) collective-permute-start(bf16[8,48,768]{2,1,0:T(8,128)(2,1)S(1)} %pad_maximum_fusion.10), channel_id=1, source_target_pairs={{0,4},{1,5},{2,6},{3,7},{4,0},{5,1},{6,2},{7,3},{8,12},{9,13},{10,... | collective-permute-start | bytes 1769480 | tf_op jit(solution)/shard_map/ppermute | solution.py:800
  162.7 24.4 %collective-permute-start.49 = (bf16[8,48,768]{2,1,0:T(8,128)(2,1)S(1)}, bf16[8,48,768]{2,1,0:T(8,128)(2,1)S(1)}, u32[]{:S(2)}, u32[]{:S(2)}) collective-permute-start(bf16[8,48,768]{2,1,0:T(8,128)(2,1)S(1)} %pad_maximum_fusion.9), channel_id=1, source_target_pairs={{0,2},{1,3},{2,0},{3,1},{4,6},{5,7},{6,4},{7,5},{8,10},{9,11},{10,... | collective-permute-start | bytes 1769480 | tf_op jit(solution)/shard_map/ppermute | solution.py:800
  163.2 15.2 %collective-permute-start.40 = (bf16[3,48,768]{2,1,0:T(8,128)(2,1)S(1)}, bf16[3,48,768]{2,1,0:T(8,128)(2,1)S(1)}, u32[]{:S(2)}, u32[]{:S(2)}) collective-permute-start(bf16[3,48,768]{2,1,0:T(8,128)(2,1)S(1)} %pad_maximum_fusion.25), channel_id=1, source_target_pairs={{0,4},{1,5},{2,6},{3,7},{4,0},{5,1},{6,2},{7,3},{8,12},{9,13},{10,... | collective-permute-start | bytes 663560 | tf_op jit(solution)/shard_map/ppermute | solution.py:800
  178.5 12.5 %collective-permute-start.51 = (bf16[8,48,768]{2,1,0:T(8,128)(2,1)S(1)}, bf16[8,48,768]{2,1,0:T(8,128)(2,1)S(1)}, u32[]{:S(2)}, u32[]{:S(2)}) collective-permute-start(bf16[8,48,768]{2,1,0:T(8,128)(2,1)S(1)} %pad_maximum_fusion.12.refs_2_), channel_id=1, source_target_pairs={{0,1},{1,0},{2,3},{3,2},{4,5},{5,4},{6,7},{7,6},{8,9},{9,8},{10,11... | collective-permute-start | bytes 1769480 | tf_op jit(solution)/shard_map/ppermute | solution.py:800
  178.5 12.0 %collective-permute-start.48 = (bf16[8,48,768]{2,1,0:T(8,128)(2,1)S(1)}, bf16[8,48,768]{2,1,0:T(8,128)(2,1)S(1)}, u32[]{:S(2)}, u32[]{:S(2)}) collective-permute-start(bf16[8,48,768]{2,1,0:T(8,128)(2,1)S(1)} %pad_maximum_fusion.11.refs_1_), channel_id=1, source_target_pairs={{0,1},{1,0},{2,3},{3,2},{4,5},{5,4},{6,7},{7,6},{8,9},{9,8},{10,11... | collective-permute-start | bytes 1769480 | tf_op jit(solution)/shard_map/ppermute | solution.py:800
  185.2 10.4 %collective-permute-start.46 = (bf16[5,48,768]{2,1,0:T(8,128)(2,1)S(1)}, bf16[5,48,768]{2,1,0:T(8,128)(2,1)S(1)}, u32[]{:S(2)}, u32[]{:S(2)}) collective-permute-start(bf16[5,48,768]{2,1,0:T(8,128)(2,1)S(1)} %pad_maximum_fusion.17), channel_id=1, source_target_pairs={{0,2},{1,3},{2,0},{3,1},{4,6},{5,7},{6,4},{7,5},{8,10},{9,11},{10,... | collective-permute-start | bytes 1105928 | tf_op jit(solution)/shard_map/ppermute | solution.py:800
  186.6 9.0 %collective-permute-start.47 = (bf16[4,48,768]{2,1,0:T(8,128)(2,1)S(1)}, bf16[4,48,768]{2,1,0:T(8,128)(2,1)S(1)}, u32[]{:S(2)}, u32[]{:S(2)}) collective-permute-start(bf16[4,48,768]{2,1,0:T(8,128)(2,1)S(1)} %pad_maximum_fusion.22), channel_id=1, source_target_pairs={{0,4},{1,5},{2,6},{3,7},{4,0},{5,1},{6,2},{7,3},{8,12},{9,13},{10,... | collective-permute-start | bytes 884744 | tf_op jit(solution)/shard_map/ppermute | solution.py:800
  187.3 14.0 %collective-permute-start.55 = (bf16[16,48,768]{2,1,0:T(8,128)(2,1)S(1)}, bf16[16,48,768]{2,1,0:T(8,128)(2,1)S(1)}, u32[]{:S(2)}, u32[]{:S(2)}) collective-permute-start(bf16[16,48,768]{2,1,0:T(8,128)(2,1)S(1)} %pad_maximum_fusion.3.refs_2_), channel_id=1, source_target_pairs={{0,1},{1,0},{2,3},{3,2},{4,5},{5,4},{6,7},{7,6},{8,9},{9,8},{10,11... | collective-permute-start | bytes 3538952 | tf_op jit(solution)/shard_map/ppermute | solution.py:800
  190.5 10.8 %collective-permute-start.54 = (bf16[16,48,768]{2,1,0:T(8,128)(2,1)S(1)}, bf16[16,48,768]{2,1,0:T(8,128)(2,1)S(1)}, u32[]{:S(2)}, u32[]{:S(2)}) collective-permute-start(bf16[16,48,768]{2,1,0:T(8,128)(2,1)S(1)} %pad_maximum_fusion.2.refs_1_), channel_id=1, source_target_pairs={{0,1},{1,0},{2,3},{3,2},{4,5},{5,4},{6,7},{7,6},{8,9},{9,8},{10,11... | collective-permute-start | bytes 3538952 | tf_op jit(solution)/shard_map/ppermute | solution.py:800
  (25 other events, 172.4 us)

commit v4 on v3

--- a/solution.py
+++ b/solution.py
@@ -990,11 +990,11 @@
             grad_joined,
         )
         small = jnp.concatenate([small_a, small_b, small_c[:4]], axis=0)
-        two.tail(3)
+        three.tail(3)
         one.pair_up(1)
-        three.tail(3)
         one.pair_up(0)
         four.tail(1, small)
+        two.tail(3)
         finish(0, 0)
         three.pair_up(1)
         two.pair_up(1)
@@ -1002,10 +1002,10 @@
         four.tail(3)
         three.pair_up(0)
         finish(0, 1)
-        finish(2, 0)
         four.pair_up(1)
         two.pair_up(0)
         finish(1, 0)
+        finish(2, 0)
         finish(2, 1)
         four.pair_up(0)
         finish(3, 0)

time: 205 us -> 200 us (0.976)
  waiting for transfers between devices: 52 us -> 48.5 us
    ppermute x56, waiting for transfers between devices: 52 us -> 48.5 us  [swap(): lax.ppermute(value, axis, [(i, i ^ 1 << bit) for i in range(self.sizes[ax...]
  transfers between devices with their start and end apart: 56 -> 56, of which waited for: 13 -> 16; matrix products, arithmetic and copies ran while one was open for 5% -> 5% of each run, Pallas kernels for 32% -> 33%
where the time goes in v4:
time: 200 us
  Pallas kernels  89.1 us (45%)
  starting transfers between devices  48.7 us (24%)
  waiting for transfers between devices  48.5 us (24%)
  other arithmetic  10.6 us (5%)
    ppermute x56, starting transfers between devices, swap(): lax.ppermute(value, axis, [(i, i ^ 1 << bit) for i in range(self.sizes[ax...  48.7 us
    ppermute x56, waiting for transfers between devices, swap(): lax.ppermute(value, axis, [(i, i ^ 1 << bit) for i in range(self.sizes[ax...  48.5 us
    pallas_call x4, Pallas kernels, quarter_call(): pl.pallas_call(lambda *refs: quarter_body(2, *refs), grid_spec=pltpu.Pref...  18.3 us
    pallas_call x1, Pallas kernels, first_call(): pl.pallas_call(lambda *refs: first_body(slots, *refs), grid_spec=pltpu.Pr...  15.4 us
    pallas_call x4, Pallas kernels, finish_mlp_call(): pl.pallas_call(lambda *refs: finish_mlp_body(groups, *refs), grid_spec=pl...  12.4 us
    pallas_call x2, Pallas kernels, collect_call(): pl.pallas_call(lambda *refs: collect_body(chunk, *refs), grid_spec=pltpu....  10.1 us
    pallas_call x2, Pallas kernels, attn_back_call(): pl.pallas_call(lambda *refs: attn_back_body(slots, call, *refs[:3], refs[...  9.51 us
    pallas_call x4, Pallas kernels, finish_attn_call(): pl.pallas_call(lambda *refs: finish_attn_body(chunk, *refs), grid_spec=pl...  8.26 us
  transfers between devices with their start and end apart: 56, of which 16 were waited for; matrix products, arithmetic and copies ran while one was open for 5% of the time, Pallas kernels for 33%

profile of v4, /device:TPU:0, one launch (start us, length us, event | category | flops | bytes accessed | tf_op | source)
XLA Modules:
  0.0 200.2 jit_solution(1713912227625121040)
XLA Ops:
  0.8 15.4 %attn_fwd.1 = (bf16[640,768]{1,0:T(8,128)(2,1)S(1)}, bf16[640,2304]{1,0:T(8,128)(2,1)S(1)}, bf16[4,6,160,320]{3,2,1,0:T(8,128)(2,1)S(1)}, bf16[640,768]{1,0:T(8,...) custom-call(s32[4]{0:T(128)} %refs_0_.3, ...), custom_call_target="tpu_custom_call" | custom-call | flops 149999992832 | bytes 1000 | tf_op jit(solution)/shard_map/attn_fwd/pallas_call | solution.py:200
  16.2 4.6 %mlp_0.1 = (bf16[2,16,48,768]{3,2,1,0:T(8,128)(2,1)S(1)}, bf16[640,768]{1,0:T(8,128)(2,1)S(1)}, bf16[640,768]{1,0:T(8,128)(2,1)S(1)}) custom-call(s32[10]{0:T(128)S(1)} %stack.67.refs_0_.ids_ref, bf16[640,768]{1,0:T(8,128)(2,1)S(1)} %get-tuple-element.140.refs_1_, bf16[640,768]{1,0:T(8,128)(2,1)S(1)} %get-tuple-element.141.refs_2_.refs_4_, ...), custom_call_target="tpu_custom_call" | custom-call | flops 43000000512 | bytes 1000 | tf_op jit(solution)/shard_map/mlp_0/pallas_call | solution.py:256
  21.3 4.6 %mlp_1.1 = (bf16[2,16,48,768]{3,2,1,0:T(8,128)(2,1)S(1)}, bf16[640,768]{1,0:T(8,128)(2,1)S(1)}, bf16[640,768]{1,0:T(8,128)(2,1)S(1)}) custom-call(s32[10]{0:T(128)S(1)} %stack.67.refs_0_.ids_ref, bf16[640,768]{1,0:T(8,128)(2,1)S(1)} %get-tuple-element.140.refs_1_, bf16[640,768]{1,0:T(8,128)(2,1)S(1)} %get-tuple-element.141.refs_2_.refs_4_, ...), custom_call_target="tpu_custom_call" | custom-call | flops 43000000512 | bytes 1000 | tf_op jit(solution)/shard_map/mlp_1/pallas_call | solution.py:256
  26.5 4.6 %mlp_2.1 = (bf16[2,16,48,768]{3,2,1,0:T(8,128)(2,1)S(1)}, bf16[640,768]{1,0:T(8,128)(2,1)S(1)}, bf16[640,768]{1,0:T(8,128)(2,1)S(1)}) custom-call(s32[10]{0:T(128)S(1)} %stack.67.refs_0_.ids_ref, bf16[640,768]{1,0:T(8,128)(2,1)S(1)} %get-tuple-element.140.refs_1_, bf16[640,768]{1,0:T(8,128)(2,1)S(1)} %get-tuple-element.141.refs_2_.refs_4_, ...), custom_call_target="tpu_custom_call" | custom-call | flops 43000000512 | bytes 1000 | tf_op jit(solution)/shard_map/mlp_2/pallas_call | solution.py:256
  32.6 2.6 %collective-permute-start.3 = (bf16[8,48,768]{2,1,0:T(8,128)(2,1)S(1)}, bf16[8,48,768]{2,1,0:T(8,128)(2,1)S(1)}, u32[]{:S(2)}, u32[]{:S(2)}) collective-permute-start(bf16[8,48,768]{2,1,0:T(8,128)(2,1)S(1)} %get-tuple-element.272), channel_id=1, source_target_pairs={{0,4},{1,5},{2,6},{3,7},{4,0},{5,1},{6,2},{7,3},{8,12},{9,13},{10,... | collective-permute-start | bytes 1769480 | tf_op jit(solution)/shard_map/ppermute | solution.py:800
  35.3 1.5 collective-permute-start.2
  36.7 5.1 %mlp_collect_0.1 = (f32[640,768]{1,0:T(8,128)S(1)}, f32[640,768]{1,0:T(8,128)S(1)}, f32[4,768]{1,0:T(4,128)S(1)}) custom-call(s32[10]{0:T(128)S(1)} %stack.67.refs_0_.ids_ref, bf16[640,768]{1,0:T(8,128)(2,1)S(1)} %get-tuple-element.149.refs_1_, bf16[640,768]{1,0:T(8,128)(2,1)S(1)} %get-tuple-element.150.refs_2_, ...), custom_call_target="tpu_custom_call" | custom-call | flops 43000000512 | bytes 1000 | tf_op jit(solution)/shard_map/mlp_collect_0/pallas_call | solution.py:317
  41.9 4.6 %mlp_3.1 = (bf16[2,16,48,768]{3,2,1,0:T(8,128)(2,1)S(1)}, bf16[640,768]{1,0:T(8,128)(2,1)S(1)}, bf16[640,768]{1,0:T(8,128)(2,1)S(1)}) custom-call(s32[10]{0:T(128)S(1)} %stack.67.refs_0_.ids_ref, bf16[640,768]{1,0:T(8,128)(2,1)S(1)} %get-tuple-element.140.refs_1_, bf16[640,768]{1,0:T(8,128)(2,1)S(1)} %get-tuple-element.141.refs_2_.refs_4_, ...), custom_call_target="tpu_custom_call" | custom-call | flops 43000000512 | bytes 1000 | tf_op jit(solution)/shard_map/mlp_3/pallas_call | solution.py:256
  46.5 5.0 %mlp_collect_1.1 = (f32[640,768]{1,0:T(8,128)S(1)}, f32[640,768]{1,0:T(8,128)S(1)}, f32[4,768]{1,0:T(4,128)S(1)}) custom-call(s32[10]{0:T(128)S(1)} %stack.67.refs_0_.ids_ref, bf16[640,768]{1,0:T(8,128)(2,1)S(1)} %get-tuple-element.157.refs_1_, bf16[640,768]{1,0:T(8,128)(2,1)S(1)} %get-tuple-element.158.refs_2_, bf16[640,768]{1,0:T(8,128)(2,1)S(1)} %copy-done.11, ...), custom_call_target="tpu_custom_call" | custom-call | flops 43000000512 | bytes 1000 | tf_op jit(solution)/shard_map/mlp_collect_1/pallas_call | solution.py:317
  53.0 1.8 add_convert_fusion
  54.8 1.5 collective-permute-start.8
  56.4 1.4 collective-permute-start.7
  57.8 3.5 %mlp_back.1 = (bf16[640,768]{1,0:T(8,128)(2,1)}, f32[640,768]{1,0:T(8,128)S(1)}, bf16[640,768]{1,0:T(8,128)(2,1)S(1)}, bf16[640,768]{1,0:T(8,128)(2,1)S(1)}, f32[4,768]{1,0:T(4,128)S(1)}) custom-call(s32[4]{0:T(128)S(1)} %copy-done.9, f32[640,768]{1,0:T(8,128)S(1)} %get-tuple-element.168.refs_1_, f32[640,768]{1,0:T(8,128)S(1)} %get-tuple-element.169.refs_2_, ...), custom_call_target="tpu_custom_call" | custom-call | flops 35999997952 | bytes 1000 | tf_op jit(solution)/shard_map/mlp_back/pallas_call | solution.py:394
  61.4 4.7 %attn_bwd_0.1.refs_3_ = bf16[640,2304]{1,0:T(8,128)(2,1)S(1)} custom-call(bf16[640,2304]{1,0:T(8,128)(2,1)S(1)} %get-tuple-element.172.refs_0_, bf16[4,6,160,320]{3,2,1,0:T(8,128)(2,1)S(1)} %get-tuple-element.173.refs_1_, bf16[640,768]{1,0:T(8,128)(2,1)S(1)} %get-tuple-element.178.refs_2_), custom_call_target="tpu_custom_call" | custom-call | flops 54999998464 | bytes 1000 | tf_op jit(solution)/shard_map/attn_bwd_0/pallas_call | solution.py:452
  66.3 1.6 collective-permute-start.6
  68.0 4.9 %attn_bwd_1.1.grad_ref.refs_0_ = bf16[640,2304]{1,0:T(8,128)(2,1)S(1)} custom-call(bf16[640,2304]{1,0:T(8,128)(2,1)S(1)} %get-tuple-element.172.refs_0_, bf16[4,6,160,320]{3,2,1,0:T(8,128)(2,1)S(1)} %get-tuple-element.173.refs_1_, bf16[640,768]{1,0:T(8,128)(2,1)S(1)} %get-tuple-element.178.refs_2_, ...), custom_call_target="tpu_custom_call", output_to_operand_aliasing={{}: (3, {})} | custom-call | flops 54999998464 | bytes 1000 | tf_op jit(solution)/shard_map/attn_bwd_1/pallas_call | solution.py:452
  72.9 2.6 %attn_grad_0.1 = (bf16[2,8,48,768]{3,2,1,0:T(8,128)(2,1)S(1)}, bf16[2,8,48,768]{3,2,1,0:T(8,128)(2,1)S(1)}) custom-call(s32[10]{0:T(128)S(1)} %stack.67.refs_0_.ids_ref, bf16[640,768]{1,0:T(8,128)(2,1)S(1)} %get-tuple-element.180.normed_ref, bf16[640,768]{1,0:T(8,128)(2,1)S(1)} %get-tuple-element.181.mix_ref, ...), custom_call_target="tpu_custom_call" | custom-call | flops 25999998976 | bytes 1000 | tf_op jit(solution)/shard_map/attn_grad_0/pallas_call | solution.py:482
  77.8 2.7 %collective-permute-start.15 = (bf16[2,2,48,768]{3,2,1,0:T(8,128)(2,1)S(1)}, bf16[2,2,48,768]{3,2,1,0:T(8,128)(2,1)S(1)}, u32[]{:S(2)}, u32[]{:S(2)}) collective-permute-start(bf16[2,2,48,768]{3,2,1,0:T(8,128)(2,1)S(1)} %add_convert_fusion.21), channel_id=1, source_target_pairs={{0,16},{8,24},{16,0},{24,8},{1,17},{9,25},{17,1},{25,9},{2,18},{10... | collective-permute-start | bytes 884744 | tf_op jit(solution)/shard_map/ppermute | solution.py:800
  81.5 2.6 %attn_grad_1.1 = (bf16[2,8,48,768]{3,2,1,0:T(8,128)(2,1)S(1)}, bf16[2,8,48,768]{3,2,1,0:T(8,128)(2,1)S(1)}) custom-call(s32[10]{0:T(128)S(1)} %stack.67.refs_0_.ids_ref, bf16[640,768]{1,0:T(8,128)(2,1)S(1)} %get-tuple-element.180.normed_ref, bf16[640,768]{1,0:T(8,128)(2,1)S(1)} %get-tuple-element.181.mix_ref, ...), custom_call_target="tpu_custom_call" | custom-call | flops 25999998976 | bytes 1000 | tf_op jit(solution)/shard_map/attn_grad_1/pallas_call | solution.py:482
  84.7 1.6 collective-permute-start.11
  86.3 3.3 %collective-permute-done.13 = bf16[4,48,768]{2,1,0:T(8,128)(2,1)S(1)} collective-permute-done((bf16[4,48,768]{2,1,0:T(8,128)(2,1)S(1)}, bf16[4,48,768]{2,1,0:T(8,128)(2,1)S(1)}, u32[]{:S(2)}, u32[]{:S(2)}) %collective-permute-start.13) | collective-permute-done | bytes 294944 | tf_op jit(solution)/shard_map/ppermute | solution.py:800
  94.4 1.6 collective-permute-start.20
  96.1 4.6 %collective-permute-done.14 = bf16[2,2,48,768]{3,2,1,0:T(8,128)(2,1)S(1)} collective-permute-done((bf16[2,2,48,768]{3,2,1,0:T(8,128)(2,1)S(1)}, bf16[2,2,48,768]{3,2,1,0:T(8,128)(2,1)S(1)}, u32[]{:S(2)}, u32[]{:S(2)}) %collective-permute-start.14) | collective-permute-done | bytes 294944 | tf_op jit(solution)/shard_map/ppermute | solution.py:800
  100.8 3.2 %collective-permute-start.23 = (bf16[2,2,48,768]{3,2,1,0:T(8,128)(2,1)S(1)}, bf16[2,2,48,768]{3,2,1,0:T(8,128)(2,1)S(1)}, u32[]{:S(2)}, u32[]{:S(2)}) collective-permute-start(bf16[2,2,48,768]{3,2,1,0:T(8,128)(2,1)S(1)} %add_convert_fusion.12), channel_id=1, source_target_pairs={{0,16},{8,24},{16,0},{24,8},{1,17},{9,25},{17,1},{25,9},{2,18},{10... | collective-permute-start | bytes 884744 | tf_op jit(solution)/shard_map/ppermute | solution.py:800
  105.3 1.5 collective-permute-start.25
  106.9 6.4 %collective-permute-done.19 = bf16[2,2,48,768]{3,2,1,0:T(8,128)(2,1)S(1)} collective-permute-done((bf16[2,2,48,768]{3,2,1,0:T(8,128)(2,1)S(1)}, bf16[2,2,48,768]{3,2,1,0:T(8,128)(2,1)S(1)}, u32[]{:S(2)}, u32[]{:S(2)}) %collective-permute-start.19) | collective-permute-done | bytes 294944 | tf_op jit(solution)/shard_map/ppermute | solution.py:800
  114.8 1.5 collective-permute-start.28
  116.5 2.1 %collective-permute-done.24 = bf16[2,48,768]{2,1,0:T(8,128)(2,1)S(1)} collective-permute-done((bf16[2,48,768]{2,1,0:T(8,128)(2,1)S(1)}, bf16[2,48,768]{2,1,0:T(8,128)(2,1)S(1)}, u32[]{:S(2)}, u32[]{:S(2)}) %collective-permute-start.24) | collective-permute-done | bytes 147488 | tf_op jit(solution)/shard_map/ppermute | solution.py:800
  119.0 2.1 %collective-permute-start.34 = (bf16[2,2,48,768]{3,2,1,0:T(8,128)(2,1)S(1)}, bf16[2,2,48,768]{3,2,1,0:T(8,128)(2,1)S(1)}, u32[]{:S(2)}, u32[]{:S(2)}) collective-permute-start(bf16[2,2,48,768]{3,2,1,0:T(8,128)(2,1)S(1)} %add_convert_fusion.8), channel_id=1, source_target_pairs={{0,8},{8,0},{16,24},{24,16},{1,9},{9,1},{17,25},{25,17},{2,10},{10... | collective-permute-start | bytes 884744 | tf_op jit(solution)/shard_map/ppermute | solution.py:800
  121.1 3.8 %collective-permute-done.22 = bf16[2,1,48,768]{3,2,1,0:T(8,128)(2,1)S(1)} collective-permute-done((bf16[2,1,48,768]{3,2,1,0:T(8,128)(2,1)S(1)}, bf16[2,1,48,768]{3,2,1,0:T(8,128)(2,1)S(1)}, u32[]{:S(2)}, u32[]{:S(2)}) %collective-permute-start.22) | collective-permute-done | bytes 147488 | tf_op jit(solution)/shard_map/ppermute | solution.py:800
  125.7 1.3 collective-permute-start.31
  127.0 4.7 %collective-permute-done.26 = bf16[2,1,48,768]{3,2,1,0:T(8,128)(2,1)S(1)} collective-permute-done((bf16[2,1,48,768]{3,2,1,0:T(8,128)(2,1)S(1)}, bf16[2,1,48,768]{3,2,1,0:T(8,128)(2,1)S(1)}, u32[]{:S(2)}, u32[]{:S(2)}) %collective-permute-start.26) | collective-permute-done | bytes 147488 | tf_op jit(solution)/shard_map/ppermute | solution.py:800
  131.8 3.8 %collective-permute-start.30 = (bf16[2,1,48,768]{3,2,1,0:T(8,128)(2,1)S(1)}, bf16[2,1,48,768]{3,2,1,0:T(8,128)(2,1)S(1)}, u32[]{:S(2)}, u32[]{:S(2)}) collective-permute-start(bf16[2,1,48,768]{3,2,1,0:T(8,128)(2,1)S(1)} %add_convert_fusion.26), channel_id=1, source_target_pairs={{0,8},{8,0},{16,24},{24,16},{1,9},{9,1},{17,25},{25,17},{2,10},{10... | collective-permute-start | bytes 442376 | tf_op jit(solution)/shard_map/ppermute | solution.py:800
  135.6 5.6 %first_back.1 = (bf16[640,768]{1,0:T(8,128)(2,1)}, f32[8,768]{1,0:T(8,128)S(1)}) custom-call(bf16[640,2304]{1,0:T(8,128)(2,1)S(1)} %attn_bwd_1.1.grad_ref.refs_0_, bf16[768,2304]{1,0:T(8,128)(2,1)S(1)} %copy-done, bf16[640,768]{1,0:T(8,128)(2,1)S(1)} %bitcast.184, f32[640,768]{1,0:T(8,128)S(1)} %get-tuple-element.212.refs_3_, f32[768]{0:T(1024)S(1)} %copy-done.2), custom_call_target="tpu_custom_call" | custom-call | flops 10000000 | bytes 1000 | tf_op jit(solution)/shard_map/first_back/pallas_call | solution.py:534
  141.4 1.3 collective-permute-start.38
  144.6 1.5 collective-permute-start.35
  146.1 3.1 %finish_mlp_0_0.1 = (f32[3072,768]{1,0:T(8,128)}, f32[768,3072]{1,0:T(8,128)}) custom-call(s32[10]{0:T(128)S(1)} %stack.67.refs_0_.ids_ref, bf16[16,48,768]{2,1,0:T(8,128)(2,1)S(1)} %pad_maximum_fusion.refs_1_, bf16[16,48,768]{2,1,0:T(8,128)(2,1)S(1)} %pad_maximum_fusion.1.refs_2_), custom_call_target="tpu_custom_call" | custom-call | flops 10000000 | bytes 1000 | tf_op jit(solution)/shard_map/finish_mlp_0_0/pallas_call | solution.py:576
  155.1 2.2 %collective-permute-done.44 = bf16[4,48,768]{2,1,0:T(8,128)(2,1)S(1)} collective-permute-done((bf16[4,48,768]{2,1,0:T(8,128)(2,1)S(1)}, bf16[4,48,768]{2,1,0:T(8,128)(2,1)S(1)}, u32[]{:S(2)}, u32[]{:S(2)}) %collective-permute-start.44) | collective-permute-done | bytes 294944 | tf_op jit(solution)/shard_map/ppermute | solution.py:800
  158.7 1.6 collective-permute-done.39
  161.3 13.7 %collective-permute-done.40 = bf16[3,48,768]{2,1,0:T(8,128)(2,1)S(1)} collective-permute-done((bf16[3,48,768]{2,1,0:T(8,128)(2,1)S(1)}, bf16[3,48,768]{2,1,0:T(8,128)(2,1)S(1)}, u32[]{:S(2)}, u32[]{:S(2)}) %collective-permute-start.40) | collective-permute-done | bytes 221216 | tf_op jit(solution)/shard_map/ppermute | solution.py:800
  176.6 3.1 %finish_mlp_0_1.1 = (f32[3072,768]{1,0:T(8,128)}, f32[768,3072]{1,0:T(8,128)}) custom-call(s32[10]{0:T(128)S(1)} %stack.67.refs_0_.ids_ref, bf16[16,48,768]{2,1,0:T(8,128)(2,1)S(1)} %collective-permute-done.42.refs_1_, bf16[16,48,768]{2,1,0:T(8,128)(2,1)S(1)} %collective-permute-done.45.refs_2_, ...), custom_call_target="tpu_custom_call", output_to_operand_aliasing={{0}: (3, {}), {1}: (4, {})} | custom-call | flops 10000000 | bytes 1000 | tf_op jit(solution)/shard_map/finish_mlp_0_1/pallas_call | solution.py:576
  179.7 1.8 collective-permute-done.41
  183.5 3.1 %finish_mlp_1_0.1 = (f32[3072,768]{1,0:T(8,128)}, f32[768,3072]{1,0:T(8,128)}) custom-call(s32[10]{0:T(128)S(1)} %stack.67.refs_0_.ids_ref, bf16[16,48,768]{2,1,0:T(8,128)(2,1)S(1)} %pad_maximum_fusion.2.refs_1_, bf16[16,48,768]{2,1,0:T(8,128)(2,1)S(1)} %pad_maximum_fusion.3.refs_2_, ...), custom_call_target="tpu_custom_call", output_to_operand_aliasing={{0}: (3, {}), {1}: (4, {})} | custom-call | flops 10000000 | bytes 1000 | tf_op jit(solution)/shard_map/finish_mlp_1_0/pallas_call | solution.py:576
  186.6 2.1 %finish_attn_2_0.1.refs_3_ = f32[768,2304]{1,0:T(8,128)} custom-call(s32[10]{0:T(128)S(1)} %stack.67.refs_0_.ids_ref, bf16[8,48,768]{2,1,0:T(8,128)(2,1)S(1)} %pad_maximum_fusion.11.refs_1_, bf16[8,48,768]{2,1,0:T(8,128)(2,1)S(1)} %pad_maximum_fusion.12.refs_2_), custom_call_target="tpu_custom_call" | custom-call | flops 10000000 | bytes 1000 | tf_op jit(solution)/shard_map/finish_attn_2_0/pallas_call | solution.py:622
  189.2 2.1 %finish_attn_2_1.1.refs_3_ = f32[768,2304]{1,0:T(8,128)} custom-call(s32[10]{0:T(128)S(1)} %stack.67.refs_0_.ids_ref, bf16[8,48,768]{2,1,0:T(8,128)(2,1)S(1)} %collective-permute-done.48.refs_1_, bf16[8,48,768]{2,1,0:T(8,128)(2,1)S(1)} %collective-permute-done.51.refs_2_, f32[768,2304]{1,0:T(8,128)} %finish_attn_2_0.1.refs_3_), custom_call_target="tpu_custom_call", output_to_operand_aliasing={{}: (3, {})} | custom-call | flops 10000000 | bytes 1000 | tf_op jit(solution)/shard_map/finish_attn_2_1/pallas_call | solution.py:622
  192.4 2.0 %finish_attn_3_0.1 = (f32[768,2304]{1,0:T(8,128)}, f32[768,768]{1,0:T(8,128)}) custom-call(s32[10]{0:T(128)S(1)} %stack.67.refs_0_.ids_ref, bf16[8,48,768]{2,1,0:T(8,128)(2,1)S(1)} %pad_maximum_fusion.13.refs_1_, bf16[8,48,768]{2,1,0:T(8,128)(2,1)S(1)} %pad_maximum_fusion.14.refs_2_, f32[768,2304]{1,0:T(8,128)} %finish_attn_2_1.1.refs_3_), custom_call_target="tpu_custom_call", output_to_operand_aliasing={{0}: (3, {})} | custom-call | flops 10000000 | bytes 1000 | tf_op jit(solution)/shard_map/finish_attn_3_0/pallas_call | solution.py:622
  195.1 2.0 %finish_attn_3_1.1 = (f32[768,2304]{1,0:T(8,128)}, f32[768,768]{1,0:T(8,128)}) custom-call(s32[10]{0:T(128)S(1)} %stack.67.refs_0_.ids_ref, bf16[9,48,768]{2,1,0:T(8,128)(2,1)S(1)} %collective-permute-done.52.got_ref.refs_1_, bf16[8,48,768]{2,1,0:T(8,128)(2,1)S(1)} %collective-permute-done.53.refs_2_, ...), custom_call_target="tpu_custom_call", output_to_operand_aliasing={{0}: (3, {}), {1}: (4, {})} | custom-call | flops 10000000 | bytes 1000 | tf_op jit(solution)/shard_map/finish_attn_3_1/pallas_call | solution.py:622
  197.1 3.1 %finish_mlp_1_1.1 = (f32[3072,768]{1,0:T(8,128)}, f32[768,3072]{1,0:T(8,128)}) custom-call(s32[10]{0:T(128)S(1)} %stack.67.refs_0_.ids_ref, bf16[16,48,768]{2,1,0:T(8,128)(2,1)S(1)} %collective-permute-done.54.refs_1_, bf16[16,48,768]{2,1,0:T(8,128)(2,1)S(1)} %collective-permute-done.55.refs_2_, ...), custom_call_target="tpu_custom_call", output_to_operand_aliasing={{0}: (3, {}), {1}: (4, {})} | custom-call | flops 10000000 | bytes 1000 | tf_op jit(solution)/shard_map/finish_mlp_1_1/pallas_call | solution.py:576
  (194 shorter events, 33.3 us)
Async XLA Ops:
  20.8 11.2 %collective-permute-start = (bf16[2,16,48,768]{3,2,1,0:T(8,128)(2,1)S(1)}, bf16[2,16,48,768]{3,2,1,0:T(8,128)(2,1)S(1)}, u32[]{:S(2)}, u32[]{:S(2)}) collective-permute-start(bf16[2,16,48,768]{3,2,1,0:T(8,128)(2,1)S(1)} %get-tuple-element.142), channel_id=1, source_target_pairs={{0,1},{1,0},{2,3},{3,2},{4,5},{5,4},{6,7},{7,6},{8,9},{9,8},{10,11... | collective-permute-start | bytes 7077896 | tf_op jit(solution)/shard_map/ppermute | solution.py:800
  32.6 18.9 %collective-permute-start.3 = (bf16[8,48,768]{2,1,0:T(8,128)(2,1)S(1)}, bf16[8,48,768]{2,1,0:T(8,128)(2,1)S(1)}, u32[]{:S(2)}, u32[]{:S(2)}) collective-permute-start(bf16[8,48,768]{2,1,0:T(8,128)(2,1)S(1)} %get-tuple-element.272), channel_id=1, source_target_pairs={{0,4},{1,5},{2,6},{3,7},{4,0},{5,1},{6,2},{7,3},{8,12},{9,13},{10,... | collective-permute-start | bytes 1769480 | tf_op jit(solution)/shard_map/ppermute | solution.py:800
  35.3 16.3 %collective-permute-start.2 = (bf16[8,48,768]{2,1,0:T(8,128)(2,1)S(1)}, bf16[8,48,768]{2,1,0:T(8,128)(2,1)S(1)}, u32[]{:S(2)}, u32[]{:S(2)}) collective-permute-start(bf16[8,48,768]{2,1,0:T(8,128)(2,1)S(1)} %get-tuple-element.273), channel_id=1, source_target_pairs={{0,2},{1,3},{2,0},{3,1},{4,6},{5,7},{6,4},{7,5},{8,10},{9,11},{10,... | collective-permute-start | bytes 1769480 | tf_op jit(solution)/shard_map/ppermute | solution.py:800
  51.7 14.4 %collective-permute-start.5 = (bf16[4,48,768]{2,1,0:T(8,128)(2,1)S(1)}, bf16[4,48,768]{2,1,0:T(8,128)(2,1)S(1)}, u32[]{:S(2)}, u32[]{:S(2)}) collective-permute-start(bf16[4,48,768]{2,1,0:T(8,128)(2,1)S(1)} %fusion.10), channel_id=1, source_target_pairs={{0,2},{1,3},{2,0},{3,1},{4,6},{5,7},{6,4},{7,5},{8,10},{9,11},{10,... | collective-permute-start | bytes 884744 | tf_op jit(solution)/shard_map/ppermute | solution.py:800
  52.5 13.6 %collective-permute-start.4 = (bf16[4,48,768]{2,1,0:T(8,128)(2,1)S(1)}, bf16[4,48,768]{2,1,0:T(8,128)(2,1)S(1)}, u32[]{:S(2)}, u32[]{:S(2)}) collective-permute-start(bf16[4,48,768]{2,1,0:T(8,128)(2,1)S(1)} %fusion.11), channel_id=1, source_target_pairs={{0,4},{1,5},{2,6},{3,7},{4,0},{5,1},{6,2},{7,3},{8,12},{9,13},{10,... | collective-permute-start | bytes 884744 | tf_op jit(solution)/shard_map/ppermute | solution.py:800
  54.8 20.7 %collective-permute-start.8 = (bf16[8,48,768]{2,1,0:T(8,128)(2,1)}, bf16[8,48,768]{2,1,0:T(8,128)(2,1)}, u32[]{:S(2)}, u32[]{:S(2)}) collective-permute-start(bf16[8,48,768]{2,1,0:T(8,128)(2,1)} %get-tuple-element.268), channel_id=1, source_target_pairs={{0,4},{1,5},{2,6},{3,7},{4,0},{5,1},{6,2},{7,3},{8,12},{9,13},{10,... | collective-permute-start | bytes 1769480 | tf_op jit(solution)/shard_map/ppermute | solution.py:800
  56.4 19.2 %collective-permute-start.7 = (bf16[8,48,768]{2,1,0:T(8,128)(2,1)}, bf16[8,48,768]{2,1,0:T(8,128)(2,1)}, u32[]{:S(2)}, u32[]{:S(2)}) collective-permute-start(bf16[8,48,768]{2,1,0:T(8,128)(2,1)} %get-tuple-element.269), channel_id=1, source_target_pairs={{0,2},{1,3},{2,0},{3,1},{4,6},{5,7},{6,4},{7,5},{8,10},{9,11},{10,... | collective-permute-start | bytes 1769480 | tf_op jit(solution)/shard_map/ppermute | solution.py:800
  66.3 11.4 %collective-permute-start.6 = (bf16[2,2,48,768]{3,2,1,0:T(8,128)(2,1)S(1)}, bf16[2,2,48,768]{3,2,1,0:T(8,128)(2,1)S(1)}, u32[]{:S(2)}, u32[]{:S(2)}) collective-permute-start(bf16[2,2,48,768]{3,2,1,0:T(8,128)(2,1)S(1)} %fusion.21), channel_id=1, source_target_pairs={{0,8},{8,0},{16,24},{24,16},{1,9},{9,1},{17,25},{25,17},{2,10},{10... | collective-permute-start | bytes 884744 | tf_op jit(solution)/shard_map/ppermute | solution.py:800
  75.5 18.5 %collective-permute-start.16 = (bf16[2,8,48,768]{3,2,1,0:T(8,128)(2,1)S(1)}, bf16[2,8,48,768]{3,2,1,0:T(8,128)(2,1)S(1)}, u32[]{:S(2)}, u32[]{:S(2)}) collective-permute-start(bf16[2,8,48,768]{3,2,1,0:T(8,128)(2,1)S(1)} %get-tuple-element.195), channel_id=1, source_target_pairs={{0,1},{1,0},{2,3},{3,2},{4,5},{5,4},{6,7},{7,6},{8,9},{9,8},{10,11... | collective-permute-start | bytes 3538952 | tf_op jit(solution)/shard_map/ppermute | solution.py:800
  77.8 16.6 %collective-permute-start.15 = (bf16[2,2,48,768]{3,2,1,0:T(8,128)(2,1)S(1)}, bf16[2,2,48,768]{3,2,1,0:T(8,128)(2,1)S(1)}, u32[]{:S(2)}, u32[]{:S(2)}) collective-permute-start(bf16[2,2,48,768]{3,2,1,0:T(8,128)(2,1)S(1)} %add_convert_fusion.21), channel_id=1, source_target_pairs={{0,16},{8,24},{16,0},{24,8},{1,17},{9,25},{17,1},{25,9},{2,18},{10... | collective-permute-start | bytes 884744 | tf_op jit(solution)/shard_map/ppermute | solution.py:800
  80.5 9.1 %collective-permute-start.13 = (bf16[4,48,768]{2,1,0:T(8,128)(2,1)S(1)}, bf16[4,48,768]{2,1,0:T(8,128)(2,1)S(1)}, u32[]{:S(2)}, u32[]{:S(2)}) collective-permute-start(bf16[4,48,768]{2,1,0:T(8,128)(2,1)S(1)} %fusion.6), channel_id=1, source_target_pairs={{0,2},{1,3},{2,0},{3,1},{4,6},{5,7},{6,4},{7,5},{8,10},{9,11},{10,... | collective-permute-start | bytes 884744 | tf_op jit(solution)/shard_map/ppermute | solution.py:800
  81.0 9.9 %collective-permute-start.12 = (bf16[4,48,768]{2,1,0:T(8,128)(2,1)S(1)}, bf16[4,48,768]{2,1,0:T(8,128)(2,1)S(1)}, u32[]{:S(2)}, u32[]{:S(2)}) collective-permute-start(bf16[4,48,768]{2,1,0:T(8,128)(2,1)S(1)} %fusion.7), channel_id=1, source_target_pairs={{0,4},{1,5},{2,6},{3,7},{4,0},{5,1},{6,2},{7,3},{8,12},{9,13},{10,... | collective-permute-start | bytes 884744 | tf_op jit(solution)/shard_map/ppermute | solution.py:800
  84.7 16.1 %collective-permute-start.11 = (bf16[4,48,768]{2,1,0:T(8,128)(2,1)S(1)}, bf16[4,48,768]{2,1,0:T(8,128)(2,1)S(1)}, u32[]{:S(2)}, u32[]{:S(2)}) collective-permute-start(bf16[4,48,768]{2,1,0:T(8,128)(2,1)S(1)} %get-tuple-element.279), channel_id=1, source_target_pairs={{0,4},{1,5},{2,6},{3,7},{4,0},{5,1},{6,2},{7,3},{8,12},{9,13},{10,... | collective-permute-start | bytes 884744 | tf_op jit(solution)/shard_map/ppermute | solution.py:800
  89.6 14.4 %collective-permute-start.10 = (bf16[4,48,768]{2,1,0:T(8,128)(2,1)S(1)}, bf16[4,48,768]{2,1,0:T(8,128)(2,1)S(1)}, u32[]{:S(2)}, u32[]{:S(2)}) collective-permute-start(bf16[4,48,768]{2,1,0:T(8,128)(2,1)S(1)} %get-tuple-element.280), channel_id=1, source_target_pairs={{0,2},{1,3},{2,0},{3,1},{4,6},{5,7},{6,4},{7,5},{8,10},{9,11},{10,... | collective-permute-start | bytes 884744 | tf_op jit(solution)/shard_map/ppermute | solution.py:800
  93.1 7.6 %collective-permute-start.14 = (bf16[2,2,48,768]{3,2,1,0:T(8,128)(2,1)S(1)}, bf16[2,2,48,768]{3,2,1,0:T(8,128)(2,1)S(1)}, u32[]{:S(2)}, u32[]{:S(2)}) collective-permute-start(bf16[2,2,48,768]{3,2,1,0:T(8,128)(2,1)S(1)} %pad_maximum_fusion.18), channel_id=1, source_target_pairs={{0,8},{8,0},{16,24},{24,16},{1,9},{9,1},{17,25},{25,17},{2,10},{10... | collective-permute-start | bytes 884744 | tf_op jit(solution)/shard_map/ppermute | solution.py:800
  94.3 10.5 %collective-permute-start.21 = (bf16[4,48,768]{2,1,0:T(8,128)(2,1)S(1)}, bf16[4,48,768]{2,1,0:T(8,128)(2,1)S(1)}, u32[]{:S(2)}, u32[]{:S(2)}) collective-permute-start(bf16[4,48,768]{2,1,0:T(8,128)(2,1)S(1)} %get-tuple-element.276), channel_id=1, source_target_pairs={{0,4},{1,5},{2,6},{3,7},{4,0},{5,1},{6,2},{7,3},{8,12},{9,13},{10,... | collective-permute-start | bytes 884744 | tf_op jit(solution)/shard_map/ppermute | solution.py:800
  94.4 10.9 %collective-permute-start.20 = (bf16[4,48,768]{2,1,0:T(8,128)(2,1)S(1)}, bf16[4,48,768]{2,1,0:T(8,128)(2,1)S(1)}, u32[]{:S(2)}, u32[]{:S(2)}) collective-permute-start(bf16[4,48,768]{2,1,0:T(8,128)(2,1)S(1)} %get-tuple-element.277), channel_id=1, source_target_pairs={{0,2},{1,3},{2,0},{3,1},{4,6},{5,7},{6,4},{7,5},{8,10},{9,11},{10,... | collective-permute-start | bytes 884744 | tf_op jit(solution)/shard_map/ppermute | solution.py:800
  100.7 12.7 %collective-permute-start.19 = (bf16[2,2,48,768]{3,2,1,0:T(8,128)(2,1)S(1)}, bf16[2,2,48,768]{3,2,1,0:T(8,128)(2,1)S(1)}, u32[]{:S(2)}, u32[]{:S(2)}) collective-permute-start(bf16[2,2,48,768]{3,2,1,0:T(8,128)(2,1)S(1)} %add_convert_fusion.13), channel_id=1, source_target_pairs={{0,8},{8,0},{16,24},{24,16},{1,9},{9,1},{17,25},{25,17},{2,10},{10... | collective-permute-start | bytes 884744 | tf_op jit(solution)/shard_map/ppermute | solution.py:800
  100.8 18.1 %collective-permute-start.23 = (bf16[2,2,48,768]{3,2,1,0:T(8,128)(2,1)S(1)}, bf16[2,2,48,768]{3,2,1,0:T(8,128)(2,1)S(1)}, u32[]{:S(2)}, u32[]{:S(2)}) collective-permute-start(bf16[2,2,48,768]{3,2,1,0:T(8,128)(2,1)S(1)} %add_convert_fusion.12), channel_id=1, source_target_pairs={{0,16},{8,24},{16,0},{24,8},{1,17},{9,25},{17,1},{25,9},{2,18},{10... | collective-permute-start | bytes 884744 | tf_op jit(solution)/shard_map/ppermute | solution.py:800
  104.0 9.9 %collective-permute-start.18 = (bf16[2,48,768]{2,1,0:T(8,128)(2,1)S(1)}, bf16[2,48,768]{2,1,0:T(8,128)(2,1)S(1)}, u32[]{:S(2)}, u32[]{:S(2)}) collective-permute-start(bf16[2,48,768]{2,1,0:T(8,128)(2,1)S(1)} %fusion.35), channel_id=1, source_target_pairs={{0,2},{1,3},{2,0},{3,1},{4,6},{5,7},{6,4},{7,5},{8,10},{9,11},{10,... | collective-permute-start | bytes 442376 | tf_op jit(solution)/shard_map/ppermute | solution.py:800
  104.7 10.0 %collective-permute-start.17 = (bf16[2,48,768]{2,1,0:T(8,128)(2,1)S(1)}, bf16[2,48,768]{2,1,0:T(8,128)(2,1)S(1)}, u32[]{:S(2)}, u32[]{:S(2)}) collective-permute-start(bf16[2,48,768]{2,1,0:T(8,128)(2,1)S(1)} %fusion.36), channel_id=1, source_target_pairs={{0,4},{1,5},{2,6},{3,7},{4,0},{5,1},{6,2},{7,3},{8,12},{9,13},{10,... | collective-permute-start | bytes 442376 | tf_op jit(solution)/shard_map/ppermute | solution.py:800
  105.3 11.1 %collective-permute-start.25 = (bf16[2,48,768]{2,1,0:T(8,128)(2,1)S(1)}, bf16[2,48,768]{2,1,0:T(8,128)(2,1)S(1)}, u32[]{:S(2)}, u32[]{:S(2)}) collective-permute-start(bf16[2,48,768]{2,1,0:T(8,128)(2,1)S(1)} %fusion.33), channel_id=1, source_target_pairs={{0,2},{1,3},{2,0},{3,1},{4,6},{5,7},{6,4},{7,5},{8,10},{9,11},{10,... | collective-permute-start | bytes 442376 | tf_op jit(solution)/shard_map/ppermute | solution.py:800
  113.9 11.1 %collective-permute-start.29 = (bf16[4,48,768]{2,1,0:T(8,128)(2,1)S(1)}, bf16[4,48,768]{2,1,0:T(8,128)(2,1)S(1)}, u32[]{:S(2)}, u32[]{:S(2)}) collective-permute-start(bf16[4,48,768]{2,1,0:T(8,128)(2,1)S(1)} %get-tuple-element.284), channel_id=1, source_target_pairs={{0,2},{1,3},{2,0},{3,1},{4,6},{5,7},{6,4},{7,5},{8,10},{9,11},{10,... | collective-permute-start | bytes 884744 | tf_op jit(solution)/shard_map/ppermute | solution.py:800
  114.8 10.3 %collective-permute-start.28 = (bf16[4,48,768]{2,1,0:T(8,128)(2,1)S(1)}, bf16[4,48,768]{2,1,0:T(8,128)(2,1)S(1)}, u32[]{:S(2)}, u32[]{:S(2)}) collective-permute-start(bf16[4,48,768]{2,1,0:T(8,128)(2,1)S(1)} %get-tuple-element.285), channel_id=1, source_target_pairs={{0,4},{1,5},{2,6},{3,7},{4,0},{5,1},{6,2},{7,3},{8,12},{9,13},{10,... | collective-permute-start | bytes 884744 | tf_op jit(solution)/shard_map/ppermute | solution.py:800
  116.5 8.4 %collective-permute-start.22 = (bf16[2,1,48,768]{3,2,1,0:T(8,128)(2,1)S(1)}, bf16[2,1,48,768]{3,2,1,0:T(8,128)(2,1)S(1)}, u32[]{:S(2)}, u32[]{:S(2)}) collective-permute-start(bf16[2,1,48,768]{3,2,1,0:T(8,128)(2,1)S(1)} %pad_maximum_fusion.27), channel_id=1, source_target_pairs={{0,8},{8,0},{16,24},{24,16},{1,9},{9,1},{17,25},{25,17},{2,10},{10... | collective-permute-start | bytes 442376 | tf_op jit(solution)/shard_map/ppermute | solution.py:800
  118.8 24.7 %collective-permute-start.27 = (bf16[2,1,48,768]{3,2,0,1:T(8,128)(2,1)S(1)}, bf16[2,1,48,768]{3,2,0,1:T(8,128)(2,1)S(1)}, u32[]{:S(2)}, u32[]{:S(2)}) collective-permute-start(bf16[2,1,48,768]{3,2,0,1:T(8,128)(2,1)S(1)} %fusion.42), channel_id=1, source_target_pairs={{0,8},{8,0},{16,24},{24,16},{1,9},{9,1},{17,25},{25,17},{2,10},{10... | collective-permute-start | bytes 442376 | tf_op jit(solution)/shard_map/ppermute | solution.py:800
  119.0 24.6 %collective-permute-start.34 = (bf16[2,2,48,768]{3,2,1,0:T(8,128)(2,1)S(1)}, bf16[2,2,48,768]{3,2,1,0:T(8,128)(2,1)S(1)}, u32[]{:S(2)}, u32[]{:S(2)}) collective-permute-start(bf16[2,2,48,768]{3,2,1,0:T(8,128)(2,1)S(1)} %add_convert_fusion.8), channel_id=1, source_target_pairs={{0,8},{8,0},{16,24},{24,16},{1,9},{9,1},{17,25},{25,17},{2,10},{10... | collective-permute-start | bytes 884744 | tf_op jit(solution)/shard_map/ppermute | solution.py:800
  125.0 6.8 %collective-permute-start.26 = (bf16[2,1,48,768]{3,2,1,0:T(8,128)(2,1)S(1)}, bf16[2,1,48,768]{3,2,1,0:T(8,128)(2,1)S(1)}, u32[]{:S(2)}, u32[]{:S(2)}) collective-permute-start(bf16[2,1,48,768]{3,2,1,0:T(8,128)(2,1)S(1)} %add_convert_fusion.27), channel_id=1, source_target_pairs={{0,16},{8,24},{16,0},{24,8},{1,17},{9,25},{17,1},{25,9},{2,18},{10... | collective-permute-start | bytes 442376 | tf_op jit(solution)/shard_map/ppermute | solution.py:800
  125.1 17.7 %collective-permute-start.32 = (bf16[8,48,768]{2,1,0:T(8,128)(2,1)S(1)}, bf16[8,48,768]{2,1,0:T(8,128)(2,1)S(1)}, u32[]{:S(2)}, u32[]{:S(2)}) collective-permute-start(bf16[8,48,768]{2,1,0:T(8,128)(2,1)S(1)} %pad_maximum_fusion.8), channel_id=1, source_target_pairs={{0,4},{1,5},{2,6},{3,7},{4,0},{5,1},{6,2},{7,3},{8,12},{9,13},{10,... | collective-permute-start | bytes 1769480 | tf_op jit(solution)/shard_map/ppermute | solution.py:800
  125.7 17.5 %collective-permute-start.31 = (bf16[8,48,768]{2,1,0:T(8,128)(2,1)S(1)}, bf16[8,48,768]{2,1,0:T(8,128)(2,1)S(1)}, u32[]{:S(2)}, u32[]{:S(2)}) collective-permute-start(bf16[8,48,768]{2,1,0:T(8,128)(2,1)S(1)} %pad_maximum_fusion.7), channel_id=1, source_target_pairs={{0,2},{1,3},{2,0},{3,1},{4,6},{5,7},{6,4},{7,5},{8,10},{9,11},{10,... | collective-permute-start | bytes 1769480 | tf_op jit(solution)/shard_map/ppermute | solution.py:800
  131.8 9.6 %collective-permute-start.30 = (bf16[2,1,48,768]{3,2,1,0:T(8,128)(2,1)S(1)}, bf16[2,1,48,768]{3,2,1,0:T(8,128)(2,1)S(1)}, u32[]{:S(2)}, u32[]{:S(2)}) collective-permute-start(bf16[2,1,48,768]{3,2,1,0:T(8,128)(2,1)S(1)} %add_convert_fusion.26), channel_id=1, source_target_pairs={{0,8},{8,0},{16,24},{24,16},{1,9},{9,1},{17,25},{25,17},{2,10},{10... | collective-permute-start | bytes 442376 | tf_op jit(solution)/shard_map/ppermute | solution.py:800
  141.4 7.8 %collective-permute-start.38 = (bf16[2,48,768]{2,1,0:T(8,128)(2,1)S(1)}, bf16[2,48,768]{2,1,0:T(8,128)(2,1)S(1)}, u32[]{:S(2)}, u32[]{:S(2)}) collective-permute-start(bf16[2,48,768]{2,1,0:T(8,128)(2,1)S(1)} %get-tuple-element.290), channel_id=1, source_target_pairs={{0,2},{1,3},{2,0},{3,1},{4,6},{5,7},{6,4},{7,5},{8,10},{9,11},{10,... | collective-permute-start | bytes 442376 | tf_op jit(solution)/shard_map/ppermute | solution.py:800
  143.6 8.8 %collective-permute-start.33 = (bf16[3,48,768]{2,1,0:T(8,128)(2,1)S(1)}, bf16[3,48,768]{2,1,0:T(8,128)(2,1)S(1)}, u32[]{:S(2)}, u32[]{:S(2)}) collective-permute-start(bf16[3,48,768]{2,1,0:T(8,128)(2,1)S(1)} %pad_maximum_fusion.23), channel_id=1, source_target_pairs={{0,16},{8,24},{16,0},{24,8},{1,17},{9,25},{17,1},{25,9},{2,18},{10... | collective-permute-start | bytes 663560 | tf_op jit(solution)/shard_map/ppermute | solution.py:800
  143.8 9.2 %collective-permute-start.36 = (bf16[4,48,768]{2,1,0:T(8,128)(2,1)S(1)}, bf16[4,48,768]{2,1,0:T(8,128)(2,1)S(1)}, u32[]{:S(2)}, u32[]{:S(2)}) collective-permute-start(bf16[4,48,768]{2,1,0:T(8,128)(2,1)S(1)} %get-tuple-element.282), channel_id=1, source_target_pairs={{0,2},{1,3},{2,0},{3,1},{4,6},{5,7},{6,4},{7,5},{8,10},{9,11},{10,... | collective-permute-start | bytes 884744 | tf_op jit(solution)/shard_map/ppermute | solution.py:800
  144.6 9.5 %collective-permute-start.35 = (bf16[4,48,768]{2,1,0:T(8,128)(2,1)S(1)}, bf16[4,48,768]{2,1,0:T(8,128)(2,1)S(1)}, u32[]{:S(2)}, u32[]{:S(2)}) collective-permute-start(bf16[4,48,768]{2,1,0:T(8,128)(2,1)S(1)} %get-tuple-element.283), channel_id=1, source_target_pairs={{0,4},{1,5},{2,6},{3,7},{4,0},{5,1},{6,2},{7,3},{8,12},{9,13},{10,... | collective-permute-start | bytes 884744 | tf_op jit(solution)/shard_map/ppermute | solution.py:800
  149.5 7.8 %collective-permute-start.44 = (bf16[4,48,768]{2,1,0:T(8,128)(2,1)S(1)}, bf16[4,48,768]{2,1,0:T(8,128)(2,1)S(1)}, u32[]{:S(2)}, u32[]{:S(2)}) collective-permute-start(bf16[4,48,768]{2,1,0:T(8,128)(2,1)S(1)} %pad_maximum_fusion.21), channel_id=1, source_target_pairs={{0,4},{1,5},{2,6},{3,7},{4,0},{5,1},{6,2},{7,3},{8,12},{9,13},{10,... | collective-permute-start | bytes 884744 | tf_op jit(solution)/shard_map/ppermute | solution.py:800
  150.1 7.8 %collective-permute-start.43 = (bf16[4,48,768]{2,1,0:T(8,128)(2,1)S(1)}, bf16[4,48,768]{2,1,0:T(8,128)(2,1)S(1)}, u32[]{:S(2)}, u32[]{:S(2)}) collective-permute-start(bf16[4,48,768]{2,1,0:T(8,128)(2,1)S(1)} %pad_maximum_fusion.20), channel_id=1, source_target_pairs={{0,2},{1,3},{2,0},{3,1},{4,6},{5,7},{6,4},{7,5},{8,10},{9,11},{10,... | collective-permute-start | bytes 884744 | tf_op jit(solution)/shard_map/ppermute | solution.py:800
  154.5 20.5 %collective-permute-start.45 = (bf16[16,48,768]{2,1,0:T(8,128)(2,1)S(1)}, bf16[16,48,768]{2,1,0:T(8,128)(2,1)S(1)}, u32[]{:S(2)}, u32[]{:S(2)}) collective-permute-start(bf16[16,48,768]{2,1,0:T(8,128)(2,1)S(1)} %pad_maximum_fusion.1.refs_2_), channel_id=1, source_target_pairs={{0,1},{1,0},{2,3},{3,2},{4,5},{5,4},{6,7},{7,6},{8,9},{9,8},{10,11... | collective-permute-start | bytes 3538952 | tf_op jit(solution)/shard_map/ppermute | solution.py:800
  154.6 21.1 %collective-permute-start.42 = (bf16[16,48,768]{2,1,0:T(8,128)(2,1)S(1)}, bf16[16,48,768]{2,1,0:T(8,128)(2,1)S(1)}, u32[]{:S(2)}, u32[]{:S(2)}) collective-permute-start(bf16[16,48,768]{2,1,0:T(8,128)(2,1)S(1)} %pad_maximum_fusion.refs_1_), channel_id=1, source_target_pairs={{0,1},{1,0},{2,3},{3,2},{4,5},{5,4},{6,7},{7,6},{8,9},{9,8},{10,11... | collective-permute-start | bytes 3538952 | tf_op jit(solution)/shard_map/ppermute | solution.py:800
  157.3 25.2 %collective-permute-start.50 = (bf16[8,48,768]{2,1,0:T(8,128)(2,1)S(1)}, bf16[8,48,768]{2,1,0:T(8,128)(2,1)S(1)}, u32[]{:S(2)}, u32[]{:S(2)}) collective-permute-start(bf16[8,48,768]{2,1,0:T(8,128)(2,1)S(1)} %pad_maximum_fusion.10), channel_id=1, source_target_pairs={{0,4},{1,5},{2,6},{3,7},{4,0},{5,1},{6,2},{7,3},{8,12},{9,13},{10,... | collective-permute-start | bytes 1769480 | tf_op jit(solution)/shard_map/ppermute | solution.py:800
  157.9 25.3 %collective-permute-start.49 = (bf16[8,48,768]{2,1,0:T(8,128)(2,1)S(1)}, bf16[8,48,768]{2,1,0:T(8,128)(2,1)S(1)}, u32[]{:S(2)}, u32[]{:S(2)}) collective-permute-start(bf16[8,48,768]{2,1,0:T(8,128)(2,1)S(1)} %pad_maximum_fusion.9), channel_id=1, source_target_pairs={{0,2},{1,3},{2,0},{3,1},{4,6},{5,7},{6,4},{7,5},{8,10},{9,11},{10,... | collective-permute-start | bytes 1769480 | tf_op jit(solution)/shard_map/ppermute | solution.py:800
  160.5 14.5 %collective-permute-start.40 = (bf16[3,48,768]{2,1,0:T(8,128)(2,1)S(1)}, bf16[3,48,768]{2,1,0:T(8,128)(2,1)S(1)}, u32[]{:S(2)}, u32[]{:S(2)}) collective-permute-start(bf16[3,48,768]{2,1,0:T(8,128)(2,1)S(1)} %pad_maximum_fusion.25), channel_id=1, source_target_pairs={{0,4},{1,5},{2,6},{3,7},{4,0},{5,1},{6,2},{7,3},{8,12},{9,13},{10,... | collective-permute-start | bytes 663560 | tf_op jit(solution)/shard_map/ppermute | solution.py:800
  175.0 14.2 %collective-permute-start.51 = (bf16[8,48,768]{2,1,0:T(8,128)(2,1)S(1)}, bf16[8,48,768]{2,1,0:T(8,128)(2,1)S(1)}, u32[]{:S(2)}, u32[]{:S(2)}) collective-permute-start(bf16[8,48,768]{2,1,0:T(8,128)(2,1)S(1)} %pad_maximum_fusion.12.refs_2_), channel_id=1, source_target_pairs={{0,1},{1,0},{2,3},{3,2},{4,5},{5,4},{6,7},{7,6},{8,9},{9,8},{10,11... | collective-permute-start | bytes 1769480 | tf_op jit(solution)/shard_map/ppermute | solution.py:800
  175.1 13.6 %collective-permute-start.48 = (bf16[8,48,768]{2,1,0:T(8,128)(2,1)S(1)}, bf16[8,48,768]{2,1,0:T(8,128)(2,1)S(1)}, u32[]{:S(2)}, u32[]{:S(2)}) collective-permute-start(bf16[8,48,768]{2,1,0:T(8,128)(2,1)S(1)} %pad_maximum_fusion.11.refs_1_), channel_id=1, source_target_pairs={{0,1},{1,0},{2,3},{3,2},{4,5},{5,4},{6,7},{7,6},{8,9},{9,8},{10,11... | collective-permute-start | bytes 1769480 | tf_op jit(solution)/shard_map/ppermute | solution.py:800
  181.5 9.8 %collective-permute-start.46 = (bf16[5,48,768]{2,1,0:T(8,128)(2,1)S(1)}, bf16[5,48,768]{2,1,0:T(8,128)(2,1)S(1)}, u32[]{:S(2)}, u32[]{:S(2)}) collective-permute-start(bf16[5,48,768]{2,1,0:T(8,128)(2,1)S(1)} %pad_maximum_fusion.17), channel_id=1, source_target_pairs={{0,2},{1,3},{2,0},{3,1},{4,6},{5,7},{6,4},{7,5},{8,10},{9,11},{10,... | collective-permute-start | bytes 1105928 | tf_op jit(solution)/shard_map/ppermute | solution.py:800
  182.5 8.9 %collective-permute-start.47 = (bf16[4,48,768]{2,1,0:T(8,128)(2,1)S(1)}, bf16[4,48,768]{2,1,0:T(8,128)(2,1)S(1)}, u32[]{:S(2)}, u32[]{:S(2)}) collective-permute-start(bf16[4,48,768]{2,1,0:T(8,128)(2,1)S(1)} %pad_maximum_fusion.22), channel_id=1, source_target_pairs={{0,4},{1,5},{2,6},{3,7},{4,0},{5,1},{6,2},{7,3},{8,12},{9,13},{10,... | collective-permute-start | bytes 884744 | tf_op jit(solution)/shard_map/ppermute | solution.py:800
  183.4 13.7 %collective-permute-start.55 = (bf16[16,48,768]{2,1,0:T(8,128)(2,1)S(1)}, bf16[16,48,768]{2,1,0:T(8,128)(2,1)S(1)}, u32[]{:S(2)}, u32[]{:S(2)}) collective-permute-start(bf16[16,48,768]{2,1,0:T(8,128)(2,1)S(1)} %pad_maximum_fusion.3.refs_2_), channel_id=1, source_target_pairs={{0,1},{1,0},{2,3},{3,2},{4,5},{5,4},{6,7},{7,6},{8,9},{9,8},{10,11... | collective-permute-start | bytes 3538952 | tf_op jit(solution)/shard_map/ppermute | solution.py:800
  188.7 8.4 %collective-permute-start.54 = (bf16[16,48,768]{2,1,0:T(8,128)(2,1)S(1)}, bf16[16,48,768]{2,1,0:T(8,128)(2,1)S(1)}, u32[]{:S(2)}, u32[]{:S(2)}) collective-permute-start(bf16[16,48,768]{2,1,0:T(8,128)(2,1)S(1)} %pad_maximum_fusion.2.refs_1_), channel_id=1, source_target_pairs={{0,1},{1,0},{2,3},{3,2},{4,5},{5,4},{6,7},{7,6},{8,9},{9,8},{10,11... | collective-permute-start | bytes 3538952 | tf_op jit(solution)/shard_map/ppermute | solution.py:800
  (25 other events, 171.2 us)

commit v5 on v3

--- a/solution.py
+++ b/solution.py
@@ -966,8 +966,8 @@
             lambda ids: attn_grad_call(0, ids, normed, mix, grad_joined, branch), ids
         )
         four.first(chain.after(send4))
+        three.first(chain.after(send3))
         two.pair(1)
-        three.first(chain.after(send3))
         one.tail(1)
         keep3, keep4 = chain.run(
             lambda ids: attn_grad_call(1, ids, normed, mix, grad_joined, branch), ids
@@ -977,13 +977,14 @@
         four.pair(0, keep4)
         one.tail(2)
         two.tail(1)
-        three.pair(1)
         four.pair(1)
         one.tail(3)
+        three.pair(1)
         three.tail(0)
         four.tail(0)
+        three.tail(1)
         two.tail(2)
-        three.tail(1)
+        one.pair_up(1)
         three.tail(2)
         token_grad, small_c = chain.run(
             lambda grad: last_call(slots, grad, joined_weight, tok, gmid, first_gain),
@@ -991,16 +992,15 @@
         )
         small = jnp.concatenate([small_a, small_b, small_c[:4]], axis=0)
         two.tail(3)
-        one.pair_up(1)
         three.tail(3)
         one.pair_up(0)
         four.tail(1, small)
-        finish(0, 0)
         three.pair_up(1)
         two.pair_up(1)
+        three.pair_up(0)
         four.tail(2)
         four.tail(3)
-        three.pair_up(0)
+        finish(0, 0)
         finish(0, 1)
         finish(2, 0)
         four.pair_up(1)

time: 205 us -> 194 us (0.946)
  waiting for transfers between devices: 52 us -> 45.8 us
  starting transfers between devices: 49.4 us -> 44.9 us
    ppermute x56, waiting for transfers between devices: 52 us -> 45.8 us  [swap(): lax.ppermute(value, axis, [(i, i ^ 1 << bit) for i in range(self.sizes[ax...]
    ppermute x56, starting transfers between devices: 49.4 us -> 44.9 us  [swap(): lax.ppermute(value, axis, [(i, i ^ 1 << bit) for i in range(self.sizes[ax...]
  transfers between devices with their start and end apart: 56 -> 56, of which waited for: 13 -> 20; matrix products, arithmetic and copies ran while one was open for 5% -> 5% of each run, Pallas kernels for 32% -> 34%
where the time goes in v5:
time: 194 us
  Pallas kernels  89.1 us (46%)
  waiting for transfers between devices  45.8 us (24%)
  starting transfers between devices  44.9 us (23%)
  other arithmetic  10.6 us (5%)
    ppermute x56, waiting for transfers between devices, swap(): lax.ppermute(value, axis, [(i, i ^ 1 << bit) for i in range(self.sizes[ax...  45.8 us
    ppermute x56, starting transfers between devices, swap(): lax.ppermute(value, axis, [(i, i ^ 1 << bit) for i in range(self.sizes[ax...  44.9 us
    pallas_call x4, Pallas kernels, quarter_call(): pl.pallas_call(lambda *refs: quarter_body(2, *refs), grid_spec=pltpu.Pref...  18.3 us
    pallas_call x1, Pallas kernels, first_call(): pl.pallas_call(lambda *refs: first_body(slots, *refs), grid_spec=pltpu.Pr...  15.4 us
    pallas_call x4, Pallas kernels, finish_mlp_call(): pl.pallas_call(lambda *refs: finish_mlp_body(groups, *refs), grid_spec=pl...  12.4 us
    pallas_call x2, Pallas kernels, collect_call(): pl.pallas_call(lambda *refs: collect_body(chunk, *refs), grid_spec=pltpu....  10.1 us
    pallas_call x2, Pallas kernels, attn_back_call(): pl.pallas_call(lambda *refs: attn_back_body(slots, call, *refs[:3], refs[...  9.51 us
    pallas_call x4, Pallas kernels, finish_attn_call(): pl.pallas_call(lambda *refs: finish_attn_body(chunk, *refs), grid_spec=pl...  8.26 us
  transfers between devices with their start and end apart: 56, of which 20 were waited for; matrix products, arithmetic and copies ran while one was open for 5% of the time, Pallas kernels for 34%

profile of v5, /device:TPU:0, one launch (start us, length us, event | category | flops | bytes accessed | tf_op | source)
XLA Modules:
  0.0 193.6 jit_solution(2469828073637341482)
XLA Ops:
  0.8 15.4 %attn_fwd.1 = (bf16[640,768]{1,0:T(8,128)(2,1)S(1)}, bf16[640,2304]{1,0:T(8,128)(2,1)S(1)}, bf16[4,6,160,320]{3,2,1,0:T(8,128)(2,1)S(1)}, bf16[640,768]{1,0:T(8,...) custom-call(s32[4]{0:T(128)} %refs_0_.3, ...), custom_call_target="tpu_custom_call" | custom-call | flops 149999992832 | bytes 1000 | tf_op jit(solution)/shard_map/attn_fwd/pallas_call | solution.py:200
  16.2 4.6 %mlp_0.1 = (bf16[2,16,48,768]{3,2,1,0:T(8,128)(2,1)S(1)}, bf16[640,768]{1,0:T(8,128)(2,1)S(1)}, bf16[640,768]{1,0:T(8,128)(2,1)S(1)}) custom-call(s32[10]{0:T(128)S(1)} %stack.67.refs_0_.ids_ref, bf16[640,768]{1,0:T(8,128)(2,1)S(1)} %get-tuple-element.140.refs_1_, bf16[640,768]{1,0:T(8,128)(2,1)S(1)} %get-tuple-element.141.refs_2_.refs_4_, ...), custom_call_target="tpu_custom_call" | custom-call | flops 43000000512 | bytes 1000 | tf_op jit(solution)/shard_map/mlp_0/pallas_call | solution.py:256
  21.3 4.6 %mlp_1.1 = (bf16[2,16,48,768]{3,2,1,0:T(8,128)(2,1)S(1)}, bf16[640,768]{1,0:T(8,128)(2,1)S(1)}, bf16[640,768]{1,0:T(8,128)(2,1)S(1)}) custom-call(s32[10]{0:T(128)S(1)} %stack.67.refs_0_.ids_ref, bf16[640,768]{1,0:T(8,128)(2,1)S(1)} %get-tuple-element.140.refs_1_, bf16[640,768]{1,0:T(8,128)(2,1)S(1)} %get-tuple-element.141.refs_2_.refs_4_, ...), custom_call_target="tpu_custom_call" | custom-call | flops 43000000512 | bytes 1000 | tf_op jit(solution)/shard_map/mlp_1/pallas_call | solution.py:256
  26.5 4.6 %mlp_2.1 = (bf16[2,16,48,768]{3,2,1,0:T(8,128)(2,1)S(1)}, bf16[640,768]{1,0:T(8,128)(2,1)S(1)}, bf16[640,768]{1,0:T(8,128)(2,1)S(1)}) custom-call(s32[10]{0:T(128)S(1)} %stack.67.refs_0_.ids_ref, bf16[640,768]{1,0:T(8,128)(2,1)S(1)} %get-tuple-element.140.refs_1_, bf16[640,768]{1,0:T(8,128)(2,1)S(1)} %get-tuple-element.141.refs_2_.refs_4_, ...), custom_call_target="tpu_custom_call" | custom-call | flops 43000000512 | bytes 1000 | tf_op jit(solution)/shard_map/mlp_2/pallas_call | solution.py:256
  32.6 2.6 %collective-permute-start.3 = (bf16[8,48,768]{2,1,0:T(8,128)(2,1)S(1)}, bf16[8,48,768]{2,1,0:T(8,128)(2,1)S(1)}, u32[]{:S(2)}, u32[]{:S(2)}) collective-permute-start(bf16[8,48,768]{2,1,0:T(8,128)(2,1)S(1)} %get-tuple-element.272), channel_id=1, source_target_pairs={{0,4},{1,5},{2,6},{3,7},{4,0},{5,1},{6,2},{7,3},{8,12},{9,13},{10,... | collective-permute-start | bytes 1769480 | tf_op jit(solution)/shard_map/ppermute | solution.py:800
  35.3 1.5 collective-permute-start.2
  36.7 5.1 %mlp_collect_0.1 = (f32[640,768]{1,0:T(8,128)S(1)}, f32[640,768]{1,0:T(8,128)S(1)}, f32[4,768]{1,0:T(4,128)S(1)}) custom-call(s32[10]{0:T(128)S(1)} %stack.67.refs_0_.ids_ref, bf16[640,768]{1,0:T(8,128)(2,1)S(1)} %get-tuple-element.149.refs_1_, bf16[640,768]{1,0:T(8,128)(2,1)S(1)} %get-tuple-element.150.refs_2_, ...), custom_call_target="tpu_custom_call" | custom-call | flops 43000000512 | bytes 1000 | tf_op jit(solution)/shard_map/mlp_collect_0/pallas_call | solution.py:317
  41.9 4.6 %mlp_3.1 = (bf16[2,16,48,768]{3,2,1,0:T(8,128)(2,1)S(1)}, bf16[640,768]{1,0:T(8,128)(2,1)S(1)}, bf16[640,768]{1,0:T(8,128)(2,1)S(1)}) custom-call(s32[10]{0:T(128)S(1)} %stack.67.refs_0_.ids_ref, bf16[640,768]{1,0:T(8,128)(2,1)S(1)} %get-tuple-element.140.refs_1_, bf16[640,768]{1,0:T(8,128)(2,1)S(1)} %get-tuple-element.141.refs_2_.refs_4_, ...), custom_call_target="tpu_custom_call" | custom-call | flops 43000000512 | bytes 1000 | tf_op jit(solution)/shard_map/mlp_3/pallas_call | solution.py:256
  46.5 5.0 %mlp_collect_1.1 = (f32[640,768]{1,0:T(8,128)S(1)}, f32[640,768]{1,0:T(8,128)S(1)}, f32[4,768]{1,0:T(4,128)S(1)}) custom-call(s32[10]{0:T(128)S(1)} %stack.67.refs_0_.ids_ref, bf16[640,768]{1,0:T(8,128)(2,1)S(1)} %get-tuple-element.157.refs_1_, bf16[640,768]{1,0:T(8,128)(2,1)S(1)} %get-tuple-element.158.refs_2_, bf16[640,768]{1,0:T(8,128)(2,1)S(1)} %copy-done.11, ...), custom_call_target="tpu_custom_call" | custom-call | flops 43000000512 | bytes 1000 | tf_op jit(solution)/shard_map/mlp_collect_1/pallas_call | solution.py:317
  53.0 1.8 add_convert_fusion
  54.8 1.5 collective-permute-start.8
  56.4 1.4 collective-permute-start.7
  57.8 3.5 %mlp_back.1 = (bf16[640,768]{1,0:T(8,128)(2,1)}, f32[640,768]{1,0:T(8,128)S(1)}, bf16[640,768]{1,0:T(8,128)(2,1)S(1)}, bf16[640,768]{1,0:T(8,128)(2,1)S(1)}, f32[4,768]{1,0:T(4,128)S(1)}) custom-call(s32[4]{0:T(128)S(1)} %copy-done.9, f32[640,768]{1,0:T(8,128)S(1)} %get-tuple-element.168.refs_1_, f32[640,768]{1,0:T(8,128)S(1)} %get-tuple-element.169.refs_2_, ...), custom_call_target="tpu_custom_call" | custom-call | flops 35999997952 | bytes 1000 | tf_op jit(solution)/shard_map/mlp_back/pallas_call | solution.py:394
  61.4 4.7 %attn_bwd_0.1.refs_3_ = bf16[640,2304]{1,0:T(8,128)(2,1)S(1)} custom-call(bf16[640,2304]{1,0:T(8,128)(2,1)S(1)} %get-tuple-element.172.refs_0_, bf16[4,6,160,320]{3,2,1,0:T(8,128)(2,1)S(1)} %get-tuple-element.173.refs_1_, bf16[640,768]{1,0:T(8,128)(2,1)S(1)} %get-tuple-element.178.refs_2_), custom_call_target="tpu_custom_call" | custom-call | flops 54999998464 | bytes 1000 | tf_op jit(solution)/shard_map/attn_bwd_0/pallas_call | solution.py:452
  66.3 1.6 collective-permute-start.6
  68.0 4.9 %attn_bwd_1.1.grad_ref.refs_0_ = bf16[640,2304]{1,0:T(8,128)(2,1)S(1)} custom-call(bf16[640,2304]{1,0:T(8,128)(2,1)S(1)} %get-tuple-element.172.refs_0_, bf16[4,6,160,320]{3,2,1,0:T(8,128)(2,1)S(1)} %get-tuple-element.173.refs_1_, bf16[640,768]{1,0:T(8,128)(2,1)S(1)} %get-tuple-element.178.refs_2_, ...), custom_call_target="tpu_custom_call", output_to_operand_aliasing={{}: (3, {})} | custom-call | flops 54999998464 | bytes 1000 | tf_op jit(solution)/shard_map/attn_bwd_1/pallas_call | solution.py:452
  72.9 2.6 %attn_grad_0.1 = (bf16[2,8,48,768]{3,2,1,0:T(8,128)(2,1)S(1)}, bf16[2,8,48,768]{3,2,1,0:T(8,128)(2,1)S(1)}) custom-call(s32[10]{0:T(128)S(1)} %stack.67.refs_0_.ids_ref, bf16[640,768]{1,0:T(8,128)(2,1)S(1)} %get-tuple-element.180.normed_ref, bf16[640,768]{1,0:T(8,128)(2,1)S(1)} %get-tuple-element.181.mix_ref, ...), custom_call_target="tpu_custom_call" | custom-call | flops 25999998976 | bytes 1000 | tf_op jit(solution)/shard_map/attn_grad_0/pallas_call | solution.py:482
  78.3 2.7 %collective-permute-start.12 = (bf16[2,2,48,768]{3,2,1,0:T(8,128)(2,1)S(1)}, bf16[2,2,48,768]{3,2,1,0:T(8,128)(2,1)S(1)}, u32[]{:S(2)}, u32[]{:S(2)}) collective-permute-start(bf16[2,2,48,768]{3,2,1,0:T(8,128)(2,1)S(1)} %add_convert_fusion.21), channel_id=1, source_target_pairs={{0,16},{8,24},{16,0},{24,8},{1,17},{9,25},{17,1},{25,9},{2,18},{10... | collective-permute-start | bytes 884744 | tf_op jit(solution)/shard_map/ppermute | solution.py:800
  82.0 2.6 %attn_grad_1.1 = (bf16[2,8,48,768]{3,2,1,0:T(8,128)(2,1)S(1)}, bf16[2,8,48,768]{3,2,1,0:T(8,128)(2,1)S(1)}) custom-call(s32[10]{0:T(128)S(1)} %stack.67.refs_0_.ids_ref, bf16[640,768]{1,0:T(8,128)(2,1)S(1)} %get-tuple-element.180.normed_ref, bf16[640,768]{1,0:T(8,128)(2,1)S(1)} %get-tuple-element.181.mix_ref, ...), custom_call_target="tpu_custom_call" | custom-call | flops 25999998976 | bytes 1000 | tf_op jit(solution)/shard_map/attn_grad_1/pallas_call | solution.py:482
  85.0 1.6 collective-permute-start.11
  86.5 3.1 %collective-permute-done.15 = bf16[4,48,768]{2,1,0:T(8,128)(2,1)S(1)} collective-permute-done((bf16[4,48,768]{2,1,0:T(8,128)(2,1)S(1)}, bf16[4,48,768]{2,1,0:T(8,128)(2,1)S(1)}, u32[]{:S(2)}, u32[]{:S(2)}) %collective-permute-start.15) | collective-permute-done | bytes 294944 | tf_op jit(solution)/shard_map/ppermute | solution.py:800
  90.2 1.2 collective-permute-done.14
  99.4 4.3 %collective-permute-done.19 = bf16[2,2,48,768]{3,2,1,0:T(8,128)(2,1)S(1)} collective-permute-done((bf16[2,2,48,768]{3,2,1,0:T(8,128)(2,1)S(1)}, bf16[2,2,48,768]{3,2,1,0:T(8,128)(2,1)S(1)}, u32[]{:S(2)}, u32[]{:S(2)}) %collective-permute-start.19) | collective-permute-done | bytes 294944 | tf_op jit(solution)/shard_map/ppermute | solution.py:800
  105.4 1.2 collective-permute-start.24
  106.6 3.2 %collective-permute-done.16 = bf16[2,2,48,768]{3,2,1,0:T(8,128)(2,1)S(1)} collective-permute-done((bf16[2,2,48,768]{3,2,1,0:T(8,128)(2,1)S(1)}, bf16[2,2,48,768]{3,2,1,0:T(8,128)(2,1)S(1)}, u32[]{:S(2)}, u32[]{:S(2)}) %collective-permute-start.16) | collective-permute-done | bytes 294944 | tf_op jit(solution)/shard_map/ppermute | solution.py:800
  111.3 1.5 collective-permute-start.26
  115.8 5.5 %collective-permute-done.22 = bf16[2,1,48,768]{3,2,1,0:T(8,128)(2,1)S(1)} collective-permute-done((bf16[2,1,48,768]{3,2,1,0:T(8,128)(2,1)S(1)}, bf16[2,1,48,768]{3,2,1,0:T(8,128)(2,1)S(1)}, u32[]{:S(2)}, u32[]{:S(2)}) %collective-permute-start.22) | collective-permute-done | bytes 147488 | tf_op jit(solution)/shard_map/ppermute | solution.py:800
  121.6 2.3 %collective-permute-start.33 = (bf16[2,2,48,768]{3,2,1,0:T(8,128)(2,1)S(1)}, bf16[2,2,48,768]{3,2,1,0:T(8,128)(2,1)S(1)}, u32[]{:S(2)}, u32[]{:S(2)}) collective-permute-start(bf16[2,2,48,768]{3,2,1,0:T(8,128)(2,1)S(1)} %add_convert_fusion.8), channel_id=1, source_target_pairs={{0,8},{8,0},{16,24},{24,16},{1,9},{9,1},{17,25},{25,17},{2,10},{10... | collective-permute-start | bytes 884744 | tf_op jit(solution)/shard_map/ppermute | solution.py:800
  125.1 3.6 %collective-permute-done.25 = bf16[2,1,48,768]{3,2,1,0:T(8,128)(2,1)S(1)} collective-permute-done((bf16[2,1,48,768]{3,2,1,0:T(8,128)(2,1)S(1)}, bf16[2,1,48,768]{3,2,1,0:T(8,128)(2,1)S(1)}, u32[]{:S(2)}, u32[]{:S(2)}) %collective-permute-start.25) | collective-permute-done | bytes 147488 | tf_op jit(solution)/shard_map/ppermute | solution.py:800
  128.8 5.6 %first_back.1 = (bf16[640,768]{1,0:T(8,128)(2,1)}, f32[8,768]{1,0:T(8,128)S(1)}) custom-call(bf16[640,2304]{1,0:T(8,128)(2,1)S(1)} %attn_bwd_1.1.grad_ref.refs_0_, bf16[768,2304]{1,0:T(8,128)(2,1)S(1)} %copy-done, bf16[640,768]{1,0:T(8,128)(2,1)S(1)} %bitcast.184, f32[640,768]{1,0:T(8,128)S(1)} %get-tuple-element.214.refs_3_, f32[768]{0:T(1024)S(1)} %copy-done.2), custom_call_target="tpu_custom_call" | custom-call | flops 10000000 | bytes 1000 | tf_op jit(solution)/shard_map/first_back/pallas_call | solution.py:534
  134.7 1.8 collective-permute-start.36
  137.4 2.2 %collective-permute-done.30 = bf16[8,48,768]{2,1,0:T(8,128)(2,1)S(1)} collective-permute-done((bf16[8,48,768]{2,1,0:T(8,128)(2,1)S(1)}, bf16[8,48,768]{2,1,0:T(8,128)(2,1)S(1)}, u32[]{:S(2)}, u32[]{:S(2)}) %collective-permute-start.30) | collective-permute-done | bytes 589856 | tf_op jit(solution)/shard_map/ppermute | solution.py:800
  139.9 2.8 %collective-permute-done.36 = bf16[2,48,768]{2,1,0:T(8,128)(2,1)S(1)} collective-permute-done((bf16[2,48,768]{2,1,0:T(8,128)(2,1)S(1)}, bf16[2,48,768]{2,1,0:T(8,128)(2,1)S(1)}, u32[]{:S(2)}, u32[]{:S(2)}) %collective-permute-start.36) | collective-permute-done | bytes 147488 | tf_op jit(solution)/shard_map/ppermute | solution.py:800
  144.6 2.1 %collective-permute-start.37 = (bf16[4,48,768]{2,1,0:T(8,128)(2,1)S(1)}, bf16[4,48,768]{2,1,0:T(8,128)(2,1)S(1)}, u32[]{:S(2)}, u32[]{:S(2)}) collective-permute-start(bf16[4,48,768]{2,1,0:T(8,128)(2,1)S(1)} %pad_maximum_fusion.20), channel_id=1, source_target_pairs={{0,2},{1,3},{2,0},{3,1},{4,6},{5,7},{6,4},{7,5},{8,10},{9,11},{10,... | collective-permute-start | bytes 884744 | tf_op jit(solution)/shard_map/ppermute | solution.py:800
  146.7 2.4 %collective-permute-done.40 = bf16[4,48,768]{2,1,0:T(8,128)(2,1)S(1)} collective-permute-done((bf16[4,48,768]{2,1,0:T(8,128)(2,1)S(1)}, bf16[4,48,768]{2,1,0:T(8,128)(2,1)S(1)}, u32[]{:S(2)}, u32[]{:S(2)}) %collective-permute-start.40) | collective-permute-done | bytes 294944 | tf_op jit(solution)/shard_map/ppermute | solution.py:800
  149.2 2.8 %collective-permute-done.34 = bf16[3,48,768]{2,1,0:T(8,128)(2,1)S(1)} collective-permute-done((bf16[3,48,768]{2,1,0:T(8,128)(2,1)S(1)}, bf16[3,48,768]{2,1,0:T(8,128)(2,1)S(1)}, u32[]{:S(2)}, u32[]{:S(2)}) %collective-permute-start.34) | collective-permute-done | bytes 221216 | tf_op jit(solution)/shard_map/ppermute | solution.py:800
  153.9 5.0 %collective-permute-done.41 = bf16[3,48,768]{2,1,0:T(8,128)(2,1)S(1)} collective-permute-done((bf16[3,48,768]{2,1,0:T(8,128)(2,1)S(1)}, bf16[3,48,768]{2,1,0:T(8,128)(2,1)S(1)}, u32[]{:S(2)}, u32[]{:S(2)}) %collective-permute-start.41) | collective-permute-done | bytes 221216 | tf_op jit(solution)/shard_map/ppermute | solution.py:800
  159.7 1.5 collective-permute-start.50
  161.9 3.1 %finish_mlp_0_0.1 = (f32[3072,768]{1,0:T(8,128)}, f32[768,3072]{1,0:T(8,128)}) custom-call(s32[10]{0:T(128)S(1)} %stack.67.refs_0_.ids_ref, bf16[16,48,768]{2,1,0:T(8,128)(2,1)S(1)} %pad_maximum_fusion.refs_1_, bf16[16,48,768]{2,1,0:T(8,128)(2,1)S(1)} %pad_maximum_fusion.1.refs_2_), custom_call_target="tpu_custom_call" | custom-call | flops 10000000 | bytes 1000 | tf_op jit(solution)/shard_map/finish_mlp_0_0/pallas_call | solution.py:576
  165.0 2.6 %collective-permute-done.42 = bf16[3,48,768]{2,1,0:T(8,128)(2,1)S(1)} collective-permute-done((bf16[3,48,768]{2,1,0:T(8,128)(2,1)S(1)}, bf16[3,48,768]{2,1,0:T(8,128)(2,1)S(1)}, u32[]{:S(2)}, u32[]{:S(2)}) %collective-permute-start.42) | collective-permute-done | bytes 221216 | tf_op jit(solution)/shard_map/ppermute | solution.py:800
  168.9 3.1 %finish_mlp_0_1.1 = (f32[3072,768]{1,0:T(8,128)}, f32[768,3072]{1,0:T(8,128)}) custom-call(s32[10]{0:T(128)S(1)} %stack.67.refs_0_.ids_ref, bf16[16,48,768]{2,1,0:T(8,128)(2,1)S(1)} %collective-permute-done.44.refs_1_, bf16[16,48,768]{2,1,0:T(8,128)(2,1)S(1)} %collective-permute-done.45.refs_2_, ...), custom_call_target="tpu_custom_call", output_to_operand_aliasing={{0}: (3, {}), {1}: (4, {})} | custom-call | flops 10000000 | bytes 1000 | tf_op jit(solution)/shard_map/finish_mlp_0_1/pallas_call | solution.py:576
  172.0 2.1 %finish_attn_2_0.1.refs_3_ = f32[768,2304]{1,0:T(8,128)} custom-call(s32[10]{0:T(128)S(1)} %stack.67.refs_0_.ids_ref, bf16[8,48,768]{2,1,0:T(8,128)(2,1)S(1)} %pad_maximum_fusion.11.refs_1_, bf16[8,48,768]{2,1,0:T(8,128)(2,1)S(1)} %pad_maximum_fusion.12.refs_2_), custom_call_target="tpu_custom_call" | custom-call | flops 10000000 | bytes 1000 | tf_op jit(solution)/shard_map/finish_attn_2_0/pallas_call | solution.py:622
  177.2 3.1 %finish_mlp_1_0.1 = (f32[3072,768]{1,0:T(8,128)}, f32[768,3072]{1,0:T(8,128)}) custom-call(s32[10]{0:T(128)S(1)} %stack.67.refs_0_.ids_ref, bf16[16,48,768]{2,1,0:T(8,128)(2,1)S(1)} %pad_maximum_fusion.2.refs_1_, bf16[16,48,768]{2,1,0:T(8,128)(2,1)S(1)} %pad_maximum_fusion.3.refs_2_, ...), custom_call_target="tpu_custom_call", output_to_operand_aliasing={{0}: (3, {}), {1}: (4, {})} | custom-call | flops 10000000 | bytes 1000 | tf_op jit(solution)/shard_map/finish_mlp_1_0/pallas_call | solution.py:576
  180.8 2.1 %finish_attn_2_1.1.refs_3_ = f32[768,2304]{1,0:T(8,128)} custom-call(s32[10]{0:T(128)S(1)} %stack.67.refs_0_.ids_ref, bf16[8,48,768]{2,1,0:T(8,128)(2,1)S(1)} %collective-permute-done.48.refs_1_, bf16[8,48,768]{2,1,0:T(8,128)(2,1)S(1)} %collective-permute-done.51.refs_2_, f32[768,2304]{1,0:T(8,128)} %finish_attn_2_0.1.refs_3_), custom_call_target="tpu_custom_call", output_to_operand_aliasing={{}: (3, {})} | custom-call | flops 10000000 | bytes 1000 | tf_op jit(solution)/shard_map/finish_attn_2_1/pallas_call | solution.py:622
  182.9 1.9 collective-permute-done.46
  185.8 2.0 %finish_attn_3_0.1 = (f32[768,2304]{1,0:T(8,128)}, f32[768,768]{1,0:T(8,128)}) custom-call(s32[10]{0:T(128)S(1)} %stack.67.refs_0_.ids_ref, bf16[8,48,768]{2,1,0:T(8,128)(2,1)S(1)} %pad_maximum_fusion.13.refs_1_, bf16[8,48,768]{2,1,0:T(8,128)(2,1)S(1)} %pad_maximum_fusion.14.refs_2_, f32[768,2304]{1,0:T(8,128)} %finish_attn_2_1.1.refs_3_), custom_call_target="tpu_custom_call", output_to_operand_aliasing={{0}: (3, {})} | custom-call | flops 10000000 | bytes 1000 | tf_op jit(solution)/shard_map/finish_attn_3_0/pallas_call | solution.py:622
  188.5 2.0 %finish_attn_3_1.1 = (f32[768,2304]{1,0:T(8,128)}, f32[768,768]{1,0:T(8,128)}) custom-call(s32[10]{0:T(128)S(1)} %stack.67.refs_0_.ids_ref, bf16[9,48,768]{2,1,0:T(8,128)(2,1)S(1)} %collective-permute-done.52.got_ref.refs_1_, bf16[8,48,768]{2,1,0:T(8,128)(2,1)S(1)} %collective-permute-done.53.refs_2_, ...), custom_call_target="tpu_custom_call", output_to_operand_aliasing={{0}: (3, {}), {1}: (4, {})} | custom-call | flops 10000000 | bytes 1000 | tf_op jit(solution)/shard_map/finish_attn_3_1/pallas_call | solution.py:622
  190.5 3.1 %finish_mlp_1_1.1 = (f32[3072,768]{1,0:T(8,128)}, f32[768,3072]{1,0:T(8,128)}) custom-call(s32[10]{0:T(128)S(1)} %stack.67.refs_0_.ids_ref, bf16[16,48,768]{2,1,0:T(8,128)(2,1)S(1)} %collective-permute-done.54.refs_1_, bf16[16,48,768]{2,1,0:T(8,128)(2,1)S(1)} %collective-permute-done.55.refs_2_, ...), custom_call_target="tpu_custom_call", output_to_operand_aliasing={{0}: (3, {}), {1}: (4, {})} | custom-call | flops 10000000 | bytes 1000 | tf_op jit(solution)/shard_map/finish_mlp_1_1/pallas_call | solution.py:576
  (194 shorter events, 38.0 us)
Async XLA Ops:
  20.8 11.2 %collective-permute-start = (bf16[2,16,48,768]{3,2,1,0:T(8,128)(2,1)S(1)}, bf16[2,16,48,768]{3,2,1,0:T(8,128)(2,1)S(1)}, u32[]{:S(2)}, u32[]{:S(2)}) collective-permute-start(bf16[2,16,48,768]{3,2,1,0:T(8,128)(2,1)S(1)} %get-tuple-element.142), channel_id=1, source_target_pairs={{0,1},{1,0},{2,3},{3,2},{4,5},{5,4},{6,7},{7,6},{8,9},{9,8},{10,11... | collective-permute-start | bytes 7077896 | tf_op jit(solution)/shard_map/ppermute | solution.py:800
  32.6 18.9 %collective-permute-start.3 = (bf16[8,48,768]{2,1,0:T(8,128)(2,1)S(1)}, bf16[8,48,768]{2,1,0:T(8,128)(2,1)S(1)}, u32[]{:S(2)}, u32[]{:S(2)}) collective-permute-start(bf16[8,48,768]{2,1,0:T(8,128)(2,1)S(1)} %get-tuple-element.272), channel_id=1, source_target_pairs={{0,4},{1,5},{2,6},{3,7},{4,0},{5,1},{6,2},{7,3},{8,12},{9,13},{10,... | collective-permute-start | bytes 1769480 | tf_op jit(solution)/shard_map/ppermute | solution.py:800
  35.3 16.3 %collective-permute-start.2 = (bf16[8,48,768]{2,1,0:T(8,128)(2,1)S(1)}, bf16[8,48,768]{2,1,0:T(8,128)(2,1)S(1)}, u32[]{:S(2)}, u32[]{:S(2)}) collective-permute-start(bf16[8,48,768]{2,1,0:T(8,128)(2,1)S(1)} %get-tuple-element.273), channel_id=1, source_target_pairs={{0,2},{1,3},{2,0},{3,1},{4,6},{5,7},{6,4},{7,5},{8,10},{9,11},{10,... | collective-permute-start | bytes 1769480 | tf_op jit(solution)/shard_map/ppermute | solution.py:800
  51.7 14.4 %collective-permute-start.5 = (bf16[4,48,768]{2,1,0:T(8,128)(2,1)S(1)}, bf16[4,48,768]{2,1,0:T(8,128)(2,1)S(1)}, u32[]{:S(2)}, u32[]{:S(2)}) collective-permute-start(bf16[4,48,768]{2,1,0:T(8,128)(2,1)S(1)} %fusion.10), channel_id=1, source_target_pairs={{0,2},{1,3},{2,0},{3,1},{4,6},{5,7},{6,4},{7,5},{8,10},{9,11},{10,... | collective-permute-start | bytes 884744 | tf_op jit(solution)/shard_map/ppermute | solution.py:800
  52.5 13.6 %collective-permute-start.4 = (bf16[4,48,768]{2,1,0:T(8,128)(2,1)S(1)}, bf16[4,48,768]{2,1,0:T(8,128)(2,1)S(1)}, u32[]{:S(2)}, u32[]{:S(2)}) collective-permute-start(bf16[4,48,768]{2,1,0:T(8,128)(2,1)S(1)} %fusion.11), channel_id=1, source_target_pairs={{0,4},{1,5},{2,6},{3,7},{4,0},{5,1},{6,2},{7,3},{8,12},{9,13},{10,... | collective-permute-start | bytes 884744 | tf_op jit(solution)/shard_map/ppermute | solution.py:800
  54.8 21.2 %collective-permute-start.8 = (bf16[8,48,768]{2,1,0:T(8,128)(2,1)}, bf16[8,48,768]{2,1,0:T(8,128)(2,1)}, u32[]{:S(2)}, u32[]{:S(2)}) collective-permute-start(bf16[8,48,768]{2,1,0:T(8,128)(2,1)} %get-tuple-element.268), channel_id=1, source_target_pairs={{0,4},{1,5},{2,6},{3,7},{4,0},{5,1},{6,2},{7,3},{8,12},{9,13},{10,... | collective-permute-start | bytes 1769480 | tf_op jit(solution)/shard_map/ppermute | solution.py:800
  56.4 19.7 %collective-permute-start.7 = (bf16[8,48,768]{2,1,0:T(8,128)(2,1)}, bf16[8,48,768]{2,1,0:T(8,128)(2,1)}, u32[]{:S(2)}, u32[]{:S(2)}) collective-permute-start(bf16[8,48,768]{2,1,0:T(8,128)(2,1)} %get-tuple-element.269), channel_id=1, source_target_pairs={{0,2},{1,3},{2,0},{3,1},{4,6},{5,7},{6,4},{7,5},{8,10},{9,11},{10,... | collective-permute-start | bytes 1769480 | tf_op jit(solution)/shard_map/ppermute | solution.py:800
  66.3 11.9 %collective-permute-start.6 = (bf16[2,2,48,768]{3,2,1,0:T(8,128)(2,1)S(1)}, bf16[2,2,48,768]{3,2,1,0:T(8,128)(2,1)S(1)}, u32[]{:S(2)}, u32[]{:S(2)}) collective-permute-start(bf16[2,2,48,768]{3,2,1,0:T(8,128)(2,1)S(1)} %fusion.21), channel_id=1, source_target_pairs={{0,8},{8,0},{16,24},{24,16},{1,9},{9,1},{17,25},{25,17},{2,10},{10... | collective-permute-start | bytes 884744 | tf_op jit(solution)/shard_map/ppermute | solution.py:800
  75.5 9.2 %collective-permute-start.9 = (bf16[2,8,48,768]{3,2,1,0:T(8,128)(2,1)S(1)}, bf16[2,8,48,768]{3,2,1,0:T(8,128)(2,1)S(1)}, u32[]{:S(2)}, u32[]{:S(2)}) collective-permute-start(bf16[2,8,48,768]{3,2,1,0:T(8,128)(2,1)S(1)} %get-tuple-element.189), channel_id=1, source_target_pairs={{0,1},{1,0},{2,3},{3,2},{4,5},{5,4},{6,7},{7,6},{8,9},{9,8},{10,11... | collective-permute-start | bytes 3538952 | tf_op jit(solution)/shard_map/ppermute | solution.py:800
  75.6 18.9 %collective-permute-start.13 = (bf16[2,8,48,768]{3,2,1,0:T(8,128)(2,1)S(1)}, bf16[2,8,48,768]{3,2,1,0:T(8,128)(2,1)S(1)}, u32[]{:S(2)}, u32[]{:S(2)}) collective-permute-start(bf16[2,8,48,768]{3,2,1,0:T(8,128)(2,1)S(1)} %get-tuple-element.193), channel_id=1, source_target_pairs={{0,1},{1,0},{2,3},{3,2},{4,5},{5,4},{6,7},{7,6},{8,9},{9,8},{10,11... | collective-permute-start | bytes 3538952 | tf_op jit(solution)/shard_map/ppermute | solution.py:800
  78.3 17.1 %collective-permute-start.12 = (bf16[2,2,48,768]{3,2,1,0:T(8,128)(2,1)S(1)}, bf16[2,2,48,768]{3,2,1,0:T(8,128)(2,1)S(1)}, u32[]{:S(2)}, u32[]{:S(2)}) collective-permute-start(bf16[2,2,48,768]{3,2,1,0:T(8,128)(2,1)S(1)} %add_convert_fusion.21), channel_id=1, source_target_pairs={{0,16},{8,24},{16,0},{24,8},{1,17},{9,25},{17,1},{25,9},{2,18},{10... | collective-permute-start | bytes 884744 | tf_op jit(solution)/shard_map/ppermute | solution.py:800
  80.9 8.7 %collective-permute-start.15 = (bf16[4,48,768]{2,1,0:T(8,128)(2,1)S(1)}, bf16[4,48,768]{2,1,0:T(8,128)(2,1)S(1)}, u32[]{:S(2)}, u32[]{:S(2)}) collective-permute-start(bf16[4,48,768]{2,1,0:T(8,128)(2,1)S(1)} %fusion.6), channel_id=1, source_target_pairs={{0,2},{1,3},{2,0},{3,1},{4,6},{5,7},{6,4},{7,5},{8,10},{9,11},{10,... | collective-permute-start | bytes 884744 | tf_op jit(solution)/shard_map/ppermute | solution.py:800
  81.5 9.9 %collective-permute-start.14 = (bf16[4,48,768]{2,1,0:T(8,128)(2,1)S(1)}, bf16[4,48,768]{2,1,0:T(8,128)(2,1)S(1)}, u32[]{:S(2)}, u32[]{:S(2)}) collective-permute-start(bf16[4,48,768]{2,1,0:T(8,128)(2,1)S(1)} %fusion.7), channel_id=1, source_target_pairs={{0,4},{1,5},{2,6},{3,7},{4,0},{5,1},{6,2},{7,3},{8,12},{9,13},{10,... | collective-permute-start | bytes 884744 | tf_op jit(solution)/shard_map/ppermute | solution.py:800
  85.0 12.8 %collective-permute-start.11 = (bf16[4,48,768]{2,1,0:T(8,128)(2,1)S(1)}, bf16[4,48,768]{2,1,0:T(8,128)(2,1)S(1)}, u32[]{:S(2)}, u32[]{:S(2)}) collective-permute-start(bf16[4,48,768]{2,1,0:T(8,128)(2,1)S(1)} %get-tuple-element.279), channel_id=1, source_target_pairs={{0,4},{1,5},{2,6},{3,7},{4,0},{5,1},{6,2},{7,3},{8,12},{9,13},{10,... | collective-permute-start | bytes 884744 | tf_op jit(solution)/shard_map/ppermute | solution.py:800
  89.6 8.6 %collective-permute-start.10 = (bf16[4,48,768]{2,1,0:T(8,128)(2,1)S(1)}, bf16[4,48,768]{2,1,0:T(8,128)(2,1)S(1)}, u32[]{:S(2)}, u32[]{:S(2)}) collective-permute-start(bf16[4,48,768]{2,1,0:T(8,128)(2,1)S(1)} %get-tuple-element.280), channel_id=1, source_target_pairs={{0,2},{1,3},{2,0},{3,1},{4,6},{5,7},{6,4},{7,5},{8,10},{9,11},{10,... | collective-permute-start | bytes 884744 | tf_op jit(solution)/shard_map/ppermute | solution.py:800
  93.7 10.0 %collective-permute-start.19 = (bf16[2,2,48,768]{3,2,1,0:T(8,128)(2,1)S(1)}, bf16[2,2,48,768]{3,2,1,0:T(8,128)(2,1)S(1)}, u32[]{:S(2)}, u32[]{:S(2)}) collective-permute-start(bf16[2,2,48,768]{3,2,1,0:T(8,128)(2,1)S(1)} %fusion.20), channel_id=1, source_target_pairs={{0,8},{8,0},{16,24},{24,16},{1,9},{9,1},{17,25},{25,17},{2,10},{10... | collective-permute-start | bytes 884744 | tf_op jit(solution)/shard_map/ppermute | solution.py:800
  94.8 9.5 %collective-permute-start.18 = (bf16[4,48,768]{2,1,0:T(8,128)(2,1)S(1)}, bf16[4,48,768]{2,1,0:T(8,128)(2,1)S(1)}, u32[]{:S(2)}, u32[]{:S(2)}) collective-permute-start(bf16[4,48,768]{2,1,0:T(8,128)(2,1)S(1)} %get-tuple-element.276), channel_id=1, source_target_pairs={{0,4},{1,5},{2,6},{3,7},{4,0},{5,1},{6,2},{7,3},{8,12},{9,13},{10,... | collective-permute-start | bytes 884744 | tf_op jit(solution)/shard_map/ppermute | solution.py:800
  95.4 9.9 %collective-permute-start.17 = (bf16[4,48,768]{2,1,0:T(8,128)(2,1)S(1)}, bf16[4,48,768]{2,1,0:T(8,128)(2,1)S(1)}, u32[]{:S(2)}, u32[]{:S(2)}) collective-permute-start(bf16[4,48,768]{2,1,0:T(8,128)(2,1)S(1)} %get-tuple-element.277), channel_id=1, source_target_pairs={{0,2},{1,3},{2,0},{3,1},{4,6},{5,7},{6,4},{7,5},{8,10},{9,11},{10,... | collective-permute-start | bytes 884744 | tf_op jit(solution)/shard_map/ppermute | solution.py:800
  97.8 12.0 %collective-permute-start.16 = (bf16[2,2,48,768]{3,2,1,0:T(8,128)(2,1)S(1)}, bf16[2,2,48,768]{3,2,1,0:T(8,128)(2,1)S(1)}, u32[]{:S(2)}, u32[]{:S(2)}) collective-permute-start(bf16[2,2,48,768]{3,2,1,0:T(8,128)(2,1)S(1)} %add_convert_fusion.13), channel_id=1, source_target_pairs={{0,8},{8,0},{16,24},{24,16},{1,9},{9,1},{17,25},{25,17},{2,10},{10... | collective-permute-start | bytes 884744 | tf_op jit(solution)/shard_map/ppermute | solution.py:800
  98.3 11.9 %collective-permute-start.21 = (bf16[2,48,768]{2,1,0:T(8,128)(2,1)S(1)}, bf16[2,48,768]{2,1,0:T(8,128)(2,1)S(1)}, u32[]{:S(2)}, u32[]{:S(2)}) collective-permute-start(bf16[2,48,768]{2,1,0:T(8,128)(2,1)S(1)} %fusion.33), channel_id=1, source_target_pairs={{0,2},{1,3},{2,0},{3,1},{4,6},{5,7},{6,4},{7,5},{8,10},{9,11},{10,... | collective-permute-start | bytes 442376 | tf_op jit(solution)/shard_map/ppermute | solution.py:800
  103.7 7.7 %collective-permute-start.20 = (bf16[2,48,768]{2,1,0:T(8,128)(2,1)S(1)}, bf16[2,48,768]{2,1,0:T(8,128)(2,1)S(1)}, u32[]{:S(2)}, u32[]{:S(2)}) collective-permute-start(bf16[2,48,768]{2,1,0:T(8,128)(2,1)S(1)} %fusion.34), channel_id=1, source_target_pairs={{0,4},{1,5},{2,6},{3,7},{4,0},{5,1},{6,2},{7,3},{8,12},{9,13},{10,... | collective-permute-start | bytes 442376 | tf_op jit(solution)/shard_map/ppermute | solution.py:800
  104.3 17.2 %collective-permute-start.28 = (bf16[2,2,48,768]{3,2,1,0:T(8,128)(2,1)S(1)}, bf16[2,2,48,768]{3,2,1,0:T(8,128)(2,1)S(1)}, u32[]{:S(2)}, u32[]{:S(2)}) collective-permute-start(bf16[2,2,48,768]{3,2,1,0:T(8,128)(2,1)S(1)} %add_convert_fusion.11), channel_id=1, source_target_pairs={{0,16},{8,24},{16,0},{24,8},{1,17},{9,25},{17,1},{25,9},{2,18},{10... | collective-permute-start | bytes 884744 | tf_op jit(solution)/shard_map/ppermute | solution.py:800
  105.4 7.6 %collective-permute-start.24 = (bf16[2,48,768]{2,1,0:T(8,128)(2,1)S(1)}, bf16[2,48,768]{2,1,0:T(8,128)(2,1)S(1)}, u32[]{:S(2)}, u32[]{:S(2)}) collective-permute-start(bf16[2,48,768]{2,1,0:T(8,128)(2,1)S(1)} %fusion.35), channel_id=1, source_target_pairs={{0,2},{1,3},{2,0},{3,1},{4,6},{5,7},{6,4},{7,5},{8,10},{9,11},{10,... | collective-permute-start | bytes 442376 | tf_op jit(solution)/shard_map/ppermute | solution.py:800
  110.2 13.7 %collective-permute-start.27 = (bf16[4,48,768]{2,1,0:T(8,128)(2,1)S(1)}, bf16[4,48,768]{2,1,0:T(8,128)(2,1)S(1)}, u32[]{:S(2)}, u32[]{:S(2)}) collective-permute-start(bf16[4,48,768]{2,1,0:T(8,128)(2,1)S(1)} %get-tuple-element.284), channel_id=1, source_target_pairs={{0,2},{1,3},{2,0},{3,1},{4,6},{5,7},{6,4},{7,5},{8,10},{9,11},{10,... | collective-permute-start | bytes 884744 | tf_op jit(solution)/shard_map/ppermute | solution.py:800
  111.3 12.6 %collective-permute-start.26 = (bf16[4,48,768]{2,1,0:T(8,128)(2,1)S(1)}, bf16[4,48,768]{2,1,0:T(8,128)(2,1)S(1)}, u32[]{:S(2)}, u32[]{:S(2)}) collective-permute-start(bf16[4,48,768]{2,1,0:T(8,128)(2,1)S(1)} %get-tuple-element.285), channel_id=1, source_target_pairs={{0,4},{1,5},{2,6},{3,7},{4,0},{5,1},{6,2},{7,3},{8,12},{9,13},{10,... | collective-permute-start | bytes 884744 | tf_op jit(solution)/shard_map/ppermute | solution.py:800
  113.0 8.3 %collective-permute-start.22 = (bf16[2,1,48,768]{3,2,1,0:T(8,128)(2,1)S(1)}, bf16[2,1,48,768]{3,2,1,0:T(8,128)(2,1)S(1)}, u32[]{:S(2)}, u32[]{:S(2)}) collective-permute-start(bf16[2,1,48,768]{3,2,1,0:T(8,128)(2,1)S(1)} %pad_maximum_fusion.27), channel_id=1, source_target_pairs={{0,8},{8,0},{16,24},{24,16},{1,9},{9,1},{17,25},{25,17},{2,10},{10... | collective-permute-start | bytes 442376 | tf_op jit(solution)/shard_map/ppermute | solution.py:800
  115.1 24.7 %collective-permute-start.29 = (bf16[2,1,48,768]{3,2,0,1:T(8,128)(2,1)S(1)}, bf16[2,1,48,768]{3,2,0,1:T(8,128)(2,1)S(1)}, u32[]{:S(2)}, u32[]{:S(2)}) collective-permute-start(bf16[2,1,48,768]{3,2,0,1:T(8,128)(2,1)S(1)} %fusion.42), channel_id=1, source_target_pairs={{0,8},{8,0},{16,24},{24,16},{1,9},{9,1},{17,25},{25,17},{2,10},{10... | collective-permute-start | bytes 442376 | tf_op jit(solution)/shard_map/ppermute | solution.py:800
  121.4 7.3 %collective-permute-start.25 = (bf16[2,1,48,768]{3,2,1,0:T(8,128)(2,1)S(1)}, bf16[2,1,48,768]{3,2,1,0:T(8,128)(2,1)S(1)}, u32[]{:S(2)}, u32[]{:S(2)}) collective-permute-start(bf16[2,1,48,768]{3,2,1,0:T(8,128)(2,1)S(1)} %add_convert_fusion.27), channel_id=1, source_target_pairs={{0,16},{8,24},{16,0},{24,8},{1,17},{9,25},{17,1},{25,9},{2,18},{10... | collective-permute-start | bytes 442376 | tf_op jit(solution)/shard_map/ppermute | solution.py:800
  121.6 13.0 %collective-permute-start.33 = (bf16[2,2,48,768]{3,2,1,0:T(8,128)(2,1)S(1)}, bf16[2,2,48,768]{3,2,1,0:T(8,128)(2,1)S(1)}, u32[]{:S(2)}, u32[]{:S(2)}) collective-permute-start(bf16[2,2,48,768]{3,2,1,0:T(8,128)(2,1)S(1)} %add_convert_fusion.8), channel_id=1, source_target_pairs={{0,8},{8,0},{16,24},{24,16},{1,9},{9,1},{17,25},{25,17},{2,10},{10... | collective-permute-start | bytes 884744 | tf_op jit(solution)/shard_map/ppermute | solution.py:800
  124.0 12.9 %collective-permute-start.31 = (bf16[8,48,768]{2,1,0:T(8,128)(2,1)S(1)}, bf16[8,48,768]{2,1,0:T(8,128)(2,1)S(1)}, u32[]{:S(2)}, u32[]{:S(2)}) collective-permute-start(bf16[8,48,768]{2,1,0:T(8,128)(2,1)S(1)} %pad_maximum_fusion.8), channel_id=1, source_target_pairs={{0,4},{1,5},{2,6},{3,7},{4,0},{5,1},{6,2},{7,3},{8,12},{9,13},{10,... | collective-permute-start | bytes 1769480 | tf_op jit(solution)/shard_map/ppermute | solution.py:800
  124.8 14.8 %collective-permute-start.30 = (bf16[8,48,768]{2,1,0:T(8,128)(2,1)S(1)}, bf16[8,48,768]{2,1,0:T(8,128)(2,1)S(1)}, u32[]{:S(2)}, u32[]{:S(2)}) collective-permute-start(bf16[8,48,768]{2,1,0:T(8,128)(2,1)S(1)} %pad_maximum_fusion.7), channel_id=1, source_target_pairs={{0,2},{1,3},{2,0},{3,1},{4,6},{5,7},{6,4},{7,5},{8,10},{9,11},{10,... | collective-permute-start | bytes 1769480 | tf_op jit(solution)/shard_map/ppermute | solution.py:800
  134.7 8.1 %collective-permute-start.36 = (bf16[2,48,768]{2,1,0:T(8,128)(2,1)S(1)}, bf16[2,48,768]{2,1,0:T(8,128)(2,1)S(1)}, u32[]{:S(2)}, u32[]{:S(2)}) collective-permute-start(bf16[2,48,768]{2,1,0:T(8,128)(2,1)S(1)} %get-tuple-element.290), channel_id=1, source_target_pairs={{0,2},{1,3},{2,0},{3,1},{4,6},{5,7},{6,4},{7,5},{8,10},{9,11},{10,... | collective-permute-start | bytes 442376 | tf_op jit(solution)/shard_map/ppermute | solution.py:800
  136.8 12.3 %collective-permute-start.40 = (bf16[4,48,768]{2,1,0:T(8,128)(2,1)S(1)}, bf16[4,48,768]{2,1,0:T(8,128)(2,1)S(1)}, u32[]{:S(2)}, u32[]{:S(2)}) collective-permute-start(bf16[4,48,768]{2,1,0:T(8,128)(2,1)S(1)} %get-tuple-element.282), channel_id=1, source_target_pairs={{0,2},{1,3},{2,0},{3,1},{4,6},{5,7},{6,4},{7,5},{8,10},{9,11},{10,... | collective-permute-start | bytes 884744 | tf_op jit(solution)/shard_map/ppermute | solution.py:800
  139.6 9.5 %collective-permute-start.39 = (bf16[4,48,768]{2,1,0:T(8,128)(2,1)S(1)}, bf16[4,48,768]{2,1,0:T(8,128)(2,1)S(1)}, u32[]{:S(2)}, u32[]{:S(2)}) collective-permute-start(bf16[4,48,768]{2,1,0:T(8,128)(2,1)S(1)} %get-tuple-element.283), channel_id=1, source_target_pairs={{0,4},{1,5},{2,6},{3,7},{4,0},{5,1},{6,2},{7,3},{8,12},{9,13},{10,... | collective-permute-start | bytes 884744 | tf_op jit(solution)/shard_map/ppermute | solution.py:800
  142.8 9.2 %collective-permute-start.34 = (bf16[3,48,768]{2,1,0:T(8,128)(2,1)S(1)}, bf16[3,48,768]{2,1,0:T(8,128)(2,1)S(1)}, u32[]{:S(2)}, u32[]{:S(2)}) collective-permute-start(bf16[3,48,768]{2,1,0:T(8,128)(2,1)S(1)} %pad_maximum_fusion.23), channel_id=1, source_target_pairs={{0,16},{8,24},{16,0},{24,8},{1,17},{9,25},{17,1},{25,9},{2,18},{10... | collective-permute-start | bytes 663560 | tf_op jit(solution)/shard_map/ppermute | solution.py:800
  143.9 8.2 %collective-permute-start.38 = (bf16[4,48,768]{2,1,0:T(8,128)(2,1)S(1)}, bf16[4,48,768]{2,1,0:T(8,128)(2,1)S(1)}, u32[]{:S(2)}, u32[]{:S(2)}) collective-permute-start(bf16[4,48,768]{2,1,0:T(8,128)(2,1)S(1)} %pad_maximum_fusion.21), channel_id=1, source_target_pairs={{0,4},{1,5},{2,6},{3,7},{4,0},{5,1},{6,2},{7,3},{8,12},{9,13},{10,... | collective-permute-start | bytes 884744 | tf_op jit(solution)/shard_map/ppermute | solution.py:800
  144.6 8.1 %collective-permute-start.37 = (bf16[4,48,768]{2,1,0:T(8,128)(2,1)S(1)}, bf16[4,48,768]{2,1,0:T(8,128)(2,1)S(1)}, u32[]{:S(2)}, u32[]{:S(2)}) collective-permute-start(bf16[4,48,768]{2,1,0:T(8,128)(2,1)S(1)} %pad_maximum_fusion.20), channel_id=1, source_target_pairs={{0,2},{1,3},{2,0},{3,1},{4,6},{5,7},{6,4},{7,5},{8,10},{9,11},{10,... | collective-permute-start | bytes 884744 | tf_op jit(solution)/shard_map/ppermute | solution.py:800
  153.4 14.2 %collective-permute-start.45 = (bf16[16,48,768]{2,1,0:T(8,128)(2,1)S(1)}, bf16[16,48,768]{2,1,0:T(8,128)(2,1)S(1)}, u32[]{:S(2)}, u32[]{:S(2)}) collective-permute-start(bf16[16,48,768]{2,1,0:T(8,128)(2,1)S(1)} %pad_maximum_fusion.1.refs_2_), channel_id=1, source_target_pairs={{0,1},{1,0},{2,3},{3,2},{4,5},{5,4},{6,7},{7,6},{8,9},{9,8},{10,11... | collective-permute-start | bytes 3538952 | tf_op jit(solution)/shard_map/ppermute | solution.py:800
  153.4 14.8 %collective-permute-start.44 = (bf16[16,48,768]{2,1,0:T(8,128)(2,1)S(1)}, bf16[16,48,768]{2,1,0:T(8,128)(2,1)S(1)}, u32[]{:S(2)}, u32[]{:S(2)}) collective-permute-start(bf16[16,48,768]{2,1,0:T(8,128)(2,1)S(1)} %pad_maximum_fusion.refs_1_), channel_id=1, source_target_pairs={{0,1},{1,0},{2,3},{3,2},{4,5},{5,4},{6,7},{7,6},{8,9},{9,8},{10,11... | collective-permute-start | bytes 3538952 | tf_op jit(solution)/shard_map/ppermute | solution.py:800
  159.1 8.4 %collective-permute-start.42 = (bf16[3,48,768]{2,1,0:T(8,128)(2,1)S(1)}, bf16[3,48,768]{2,1,0:T(8,128)(2,1)S(1)}, u32[]{:S(2)}, u32[]{:S(2)}) collective-permute-start(bf16[3,48,768]{2,1,0:T(8,128)(2,1)S(1)} %pad_maximum_fusion.25), channel_id=1, source_target_pairs={{0,4},{1,5},{2,6},{3,7},{4,0},{5,1},{6,2},{7,3},{8,12},{9,13},{10,... | collective-permute-start | bytes 663560 | tf_op jit(solution)/shard_map/ppermute | solution.py:800
  159.7 16.0 %collective-permute-start.50 = (bf16[8,48,768]{2,1,0:T(8,128)(2,1)S(1)}, bf16[8,48,768]{2,1,0:T(8,128)(2,1)S(1)}, u32[]{:S(2)}, u32[]{:S(2)}) collective-permute-start(bf16[8,48,768]{2,1,0:T(8,128)(2,1)S(1)} %pad_maximum_fusion.10), channel_id=1, source_target_pairs={{0,4},{1,5},{2,6},{3,7},{4,0},{5,1},{6,2},{7,3},{8,12},{9,13},{10,... | collective-permute-start | bytes 1769480 | tf_op jit(solution)/shard_map/ppermute | solution.py:800
  161.2 15.7 %collective-permute-start.49 = (bf16[8,48,768]{2,1,0:T(8,128)(2,1)S(1)}, bf16[8,48,768]{2,1,0:T(8,128)(2,1)S(1)}, u32[]{:S(2)}, u32[]{:S(2)}) collective-permute-start(bf16[8,48,768]{2,1,0:T(8,128)(2,1)S(1)} %pad_maximum_fusion.9), channel_id=1, source_target_pairs={{0,2},{1,3},{2,0},{3,1},{4,6},{5,7},{6,4},{7,5},{8,10},{9,11},{10,... | collective-permute-start | bytes 1769480 | tf_op jit(solution)/shard_map/ppermute | solution.py:800
  167.5 13.2 %collective-permute-start.51 = (bf16[8,48,768]{2,1,0:T(8,128)(2,1)S(1)}, bf16[8,48,768]{2,1,0:T(8,128)(2,1)S(1)}, u32[]{:S(2)}, u32[]{:S(2)}) collective-permute-start(bf16[8,48,768]{2,1,0:T(8,128)(2,1)S(1)} %pad_maximum_fusion.12.refs_2_), channel_id=1, source_target_pairs={{0,1},{1,0},{2,3},{3,2},{4,5},{5,4},{6,7},{7,6},{8,9},{9,8},{10,11... | collective-permute-start | bytes 1769480 | tf_op jit(solution)/shard_map/ppermute | solution.py:800
  167.6 12.7 %collective-permute-start.48 = (bf16[8,48,768]{2,1,0:T(8,128)(2,1)S(1)}, bf16[8,48,768]{2,1,0:T(8,128)(2,1)S(1)}, u32[]{:S(2)}, u32[]{:S(2)}) collective-permute-start(bf16[8,48,768]{2,1,0:T(8,128)(2,1)S(1)} %pad_maximum_fusion.11.refs_1_), channel_id=1, source_target_pairs={{0,1},{1,0},{2,3},{3,2},{4,5},{5,4},{6,7},{7,6},{8,9},{9,8},{10,11... | collective-permute-start | bytes 1769480 | tf_op jit(solution)/shard_map/ppermute | solution.py:800
  175.3 9.4 %collective-permute-start.46 = (bf16[5,48,768]{2,1,0:T(8,128)(2,1)S(1)}, bf16[5,48,768]{2,1,0:T(8,128)(2,1)S(1)}, u32[]{:S(2)}, u32[]{:S(2)}) collective-permute-start(bf16[5,48,768]{2,1,0:T(8,128)(2,1)S(1)} %pad_maximum_fusion.17), channel_id=1, source_target_pairs={{0,2},{1,3},{2,0},{3,1},{4,6},{5,7},{6,4},{7,5},{8,10},{9,11},{10,... | collective-permute-start | bytes 1105928 | tf_op jit(solution)/shard_map/ppermute | solution.py:800
  175.8 9.1 %collective-permute-start.47 = (bf16[4,48,768]{2,1,0:T(8,128)(2,1)S(1)}, bf16[4,48,768]{2,1,0:T(8,128)(2,1)S(1)}, u32[]{:S(2)}, u32[]{:S(2)}) collective-permute-start(bf16[4,48,768]{2,1,0:T(8,128)(2,1)S(1)} %pad_maximum_fusion.22), channel_id=1, source_target_pairs={{0,4},{1,5},{2,6},{3,7},{4,0},{5,1},{6,2},{7,3},{8,12},{9,13},{10,... | collective-permute-start | bytes 884744 | tf_op jit(solution)/shard_map/ppermute | solution.py:800
  177.1 13.4 %collective-permute-start.55 = (bf16[16,48,768]{2,1,0:T(8,128)(2,1)S(1)}, bf16[16,48,768]{2,1,0:T(8,128)(2,1)S(1)}, u32[]{:S(2)}, u32[]{:S(2)}) collective-permute-start(bf16[16,48,768]{2,1,0:T(8,128)(2,1)S(1)} %pad_maximum_fusion.3.refs_2_), channel_id=1, source_target_pairs={{0,1},{1,0},{2,3},{3,2},{4,5},{5,4},{6,7},{7,6},{8,9},{9,8},{10,11... | collective-permute-start | bytes 3538952 | tf_op jit(solution)/shard_map/ppermute | solution.py:800
  180.3 10.2 %collective-permute-start.54 = (bf16[16,48,768]{2,1,0:T(8,128)(2,1)S(1)}, bf16[16,48,768]{2,1,0:T(8,128)(2,1)S(1)}, u32[]{:S(2)}, u32[]{:S(2)}) collective-permute-start(bf16[16,48,768]{2,1,0:T(8,128)(2,1)S(1)} %pad_maximum_fusion.2.refs_1_), channel_id=1, source_target_pairs={{0,1},{1,0},{2,3},{3,2},{4,5},{5,4},{6,7},{7,6},{8,9},{9,8},{10,11... | collective-permute-start | bytes 3538952 | tf_op jit(solution)/shard_map/ppermute | solution.py:800
  (25 other events, 160.0 us)
